TPU v7x, 256 devices: a whole 4x4x8 slice. The times are simulated.
256 devices in a mesh: section: 8 (over x, y_lo), dp: 32 (over z, y_hi, core).
Axes of the slice: x: 4, y: 4 (y_hi: 2, y_lo: 2; y = y_hi * 2 + y_lo), z: 8, core: 2. Of those that a mesh axis runs over, the one named last changes fastest.
Arguments:
- acts: bfloat16 [8, 9, 128, 32, 128], P('section', None, 'dp'), may hold values from -6 to 6
- kernels: bfloat16 [8, 3, 3, 3, 128, 128], P('section'), may hold values from -0.078125 to 0.078125
- cotangent: bfloat16 [9, 128, 32, 128], P(None, 'dp'), may hold values from -6 to 6
Outputs:
- input_grads: bfloat16 [8, 9, 128, 32, 128], P('section', None, 'dp')
- kernel_grads: float32 [8, 128, 27, 128], P('section', 'dp')
All inputs are finite; a program needn't handle non-finite values.
Results may differ from a plain program's by a relative error of at most 0.03.
Values may be sent and summed in bfloat16 or wider, within the bound.
No kernel may reach another device: no remote copies, remote signals or barrier semaphores. Data moves between devices by JAX's collectives and lax.ppermute only.
A program may use at most 128 MiB of HBM per device.

v0:
```python
import math

import jax
import jax.numpy as jnp
from jax import lax
from jax.sharding import PartitionSpec as P


def padded_2(block, sides, width):
    for axis, dim in sides:
        count = lax.axis_size(axis)
        forward = [(i, i + 1) for i in range(count - 1)]
        backward = [(target, source) for source, target in forward]
        low = lax.ppermute(
            lax.slice_in_dim(block, block.shape[dim] - width, None, axis=dim), axis, forward
        )
        high = lax.ppermute(lax.slice_in_dim(block, 0, width, axis=dim), axis, backward)
        block = jnp.concatenate([low, block, high], axis=dim)
    return block


def shifted(block, axis, distance):
    devices = range(lax.axis_size(axis))
    route = [(i - distance, i) for i in devices if i - distance in devices]
    return lax.ppermute(block, axis, route)


def grad_update(padded, kern, grad, slope, col_pad):
    flipped = jnp.swapaxes(kern[::-1, ::-1, ::-1], 3, 4)
    back = lax.conv_general_dilated(
        padded[None],
        flipped,
        (1, 1, 1),
        ((0, 2), (0, 0), (col_pad, col_pad)),
        dimension_numbers=("NDHWC", "DHWIO", "NDHWC"),
        preferred_element_type=jnp.float32,
    )[0]
    return (grad.astype(jnp.float32) + slope * back).astype(jnp.bfloat16)


def tap_terms(act_pad, grad_flat, count):
    frames = act_pad.shape[0] - 2
    rows_here = act_pad.shape[1] - 2
    columns = act_pad.shape[2] - 2
    tap_list = [(i, j, k) for i in range(3) for j in range(3) for k in range(3)]
    per_block = max(1, 128 // count)
    blocks = []
    for tap_start in range(0, 27, per_block):
        pieces = [
            act_pad[i : i + frames, j : j + rows_here, k : k + columns].reshape(-1, count)
            for i, j, k in tap_list[tap_start : tap_start + per_block]
        ]
        stacked = pieces[0]
        blocks.append(
            lax.dot_general(
                stacked, grad_flat, (((0,), (0,)), ((), ())), preferred_element_type=jnp.float32
            )
        )
    joined = jnp.concatenate(blocks, axis=0).reshape(27, count, grad_flat.shape[1])
    return jnp.transpose(joined, (1, 0, 2))


def local(acts, kernels, cotangent):
    frames, rows_here, columns, chans = cotangent.shape
    sections = lax.axis_size("section")
    my_section = lax.axis_index("section")
    groups = lax.axis_size("dp")
    scale = 1.0 / math.sqrt(frames * rows_here * groups * columns)
    share = chans // groups
    xval = acts[0].astype(jnp.float32)
    kern = kernels[0]
    sig = jax.nn.sigmoid(xval)
    slope = sig * (1.0 + xval * (1.0 - sig))
    activ = (xval * sig).astype(jnp.bfloat16)

    def grad_step(padded, grad):
        return grad_update(padded, kern, grad, slope, 1)

    def skip_step(padded, grad):
        return jnp.zeros_like(grad)

    buffer = cotangent
    kept_dx = jnp.zeros_like(cotangent)
    kept_grad = jnp.zeros_like(cotangent)
    for tick in range(sections):
        live = my_section == sections - 1 - tick
        padded = padded_2(buffer, (("dp", 1),), 1)
        result = lax.cond(live, grad_step, skip_step, padded, buffer)
        kept_dx = jnp.where(live, result, kept_dx)
        kept_grad = jnp.where(live, buffer, kept_grad)
        if tick + 1 < sections:
            buffer = shifted(result, "section", -1)
    act_pad = padded_2(activ, (("dp", 1),), 1)
    act_pad = jnp.pad(act_pad, ((2, 0), (0, 0), (1, 1), (0, 0)))
    grad_flat = kept_grad.reshape(-1, chans)
    summed = lax.psum(
        (tap_terms(act_pad, grad_flat, chans) * scale).astype(jnp.bfloat16), "dp"
    ).astype(jnp.float32)
    kernel_part = lax.dynamic_slice_in_dim(summed, lax.axis_index("dp") * share, share, 0)
    return (kept_dx[None], kernel_part[None])


def solution(mesh):
    return jax.shard_map(
        local,
        mesh=mesh,
        in_specs=(
            P("section", None, "dp", None, None),
            P("section", None, None, None, None, None),
            P(None, "dp", None, None),
        ),
        out_specs=(P("section", None, "dp", None, None), P("section", "dp", None, None)),
        check_vma=False,
    )
```

profile of v0, /device:TPU:8, one launch (start us, length us, event | category | flops | bytes accessed | tf_op | source)
XLA Modules:
  0.0 478.9 jit_solution(7574003332460891124)
XLA Ops:
  7.2 1.2 copy.29
  8.7 1.7 collective-permute-start
  10.5 1.3 collective-permute-start.1
  11.8 1.2 fusion.154
  13.0 2.8 collective-permute-done.1
  15.8 0.5 pad_maximum_fusion
  16.4 3.3 collective-permute-start.2
  19.7 6.3 %collective-permute-done.2 = bf16[9,4,32,128]{3,2,1,0:T(8,128)(2,1)S(1)} collective-permute-done((bf16[9,4,32,128]{3,2,1,0:T(8,128)(2,1)S(1)}, bf16[9,4,32,128]{3,2,1,0:T(8,128)(2,1)S(1)}, u32[]{:S(2)}, u32[]{:S(2)}) %collective-permute-start.2) | collective-permute-done | bytes 294944 | tf_op jit(solution)/shard_map/ppermute | solution.py:25
  25.9 6.0 %collective-permute-start.3 = (bf16[9,1,32,128]{3,2,1,0:T(8,128)(2,1)S(1)}, bf16[9,1,32,128]{3,2,1,0:T(8,128)(2,1)S(1)}, u32[]{:S(2)}, u32[]{:S(2)}) collective-permute-start(bf16[9,1,32,128]{3,2,1,0:T(8,128)(2,1)S(1)} %get-tuple-element.178), channel_id=1, source_target_pairs={{0,1},{1,2},{2,3},{3,4},{4,5},{5,6},{6,7},{7,8},{8,9},{9,10},{10,1... | collective-permute-start | bytes 221192 | tf_op jit(solution)/shard_map/ppermute | solution.py:14
  31.9 1.3 collective-permute-start.4
  33.2 2.7 collective-permute-done.4
  36.0 2.8 collective-permute-start.5
  38.8 6.7 %collective-permute-done.5 = bf16[9,4,32,128]{3,2,1,0:T(8,128)(2,1)S(1)} collective-permute-done((bf16[9,4,32,128]{3,2,1,0:T(8,128)(2,1)S(1)}, bf16[9,4,32,128]{3,2,1,0:T(8,128)(2,1)S(1)}, u32[]{:S(2)}, u32[]{:S(2)}) %collective-permute-start.5) | collective-permute-done | bytes 294944 | tf_op jit(solution)/shard_map/ppermute | solution.py:25
  45.6 5.3 %collective-permute-start.6 = (bf16[9,1,32,128]{3,2,1,0:T(8,128)(2,1)S(1)}, bf16[9,1,32,128]{3,2,1,0:T(8,128)(2,1)S(1)}, u32[]{:S(2)}, u32[]{:S(2)}) collective-permute-start(bf16[9,1,32,128]{3,2,1,0:T(8,128)(2,1)S(1)} %get-tuple-element.176), channel_id=1, source_target_pairs={{0,1},{1,2},{2,3},{3,4},{4,5},{5,6},{6,7},{7,8},{8,9},{9,10},{10,1... | collective-permute-start | bytes 221192 | tf_op jit(solution)/shard_map/ppermute | solution.py:14
  50.8 1.3 collective-permute-start.7
  52.2 3.8 collective-permute-done.7
  56.3 1.9 collective-permute-start.8
  58.2 8.4 %collective-permute-done.8 = bf16[9,4,32,128]{3,2,1,0:T(8,128)(2,1)S(1)} collective-permute-done((bf16[9,4,32,128]{3,2,1,0:T(8,128)(2,1)S(1)}, bf16[9,4,32,128]{3,2,1,0:T(8,128)(2,1)S(1)}, u32[]{:S(2)}, u32[]{:S(2)}) %collective-permute-start.8) | collective-permute-done | bytes 294944 | tf_op jit(solution)/shard_map/ppermute | solution.py:25
  66.6 5.6 %collective-permute-start.9 = (bf16[9,1,32,128]{3,2,1,0:T(8,128)(2,1)S(1)}, bf16[9,1,32,128]{3,2,1,0:T(8,128)(2,1)S(1)}, u32[]{:S(2)}, u32[]{:S(2)}) collective-permute-start(bf16[9,1,32,128]{3,2,1,0:T(8,128)(2,1)S(1)} %get-tuple-element.174), channel_id=1, source_target_pairs={{0,1},{1,2},{2,3},{3,4},{4,5},{5,6},{6,7},{7,8},{8,9},{9,10},{10,1... | collective-permute-start | bytes 221192 | tf_op jit(solution)/shard_map/ppermute | solution.py:14
  72.2 1.3 collective-permute-start.10
  73.5 4.0 collective-permute-done.10
  77.7 1.9 collective-permute-start.11
  79.6 8.4 %collective-permute-done.11 = bf16[9,4,32,128]{3,2,1,0:T(8,128)(2,1)S(1)} collective-permute-done((bf16[9,4,32,128]{3,2,1,0:T(8,128)(2,1)S(1)}, bf16[9,4,32,128]{3,2,1,0:T(8,128)(2,1)S(1)}, u32[]{:S(2)}, u32[]{:S(2)}) %collective-permute-start.11) | collective-permute-done | bytes 294944 | tf_op jit(solution)/shard_map/ppermute | solution.py:25
  88.0 5.6 %collective-permute-start.12 = (bf16[9,1,32,128]{3,2,1,0:T(8,128)(2,1)S(1)}, bf16[9,1,32,128]{3,2,1,0:T(8,128)(2,1)S(1)}, u32[]{:S(2)}, u32[]{:S(2)}) collective-permute-start(bf16[9,1,32,128]{3,2,1,0:T(8,128)(2,1)S(1)} %get-tuple-element.172), channel_id=1, source_target_pairs={{0,1},{1,2},{2,3},{3,4},{4,5},{5,6},{6,7},{7,8},{8,9},{9,10},{10,1... | collective-permute-start | bytes 221192 | tf_op jit(solution)/shard_map/ppermute | solution.py:14
  93.6 1.3 collective-permute-start.13
  94.9 3.2 collective-permute-done.13
  98.5 1.9 collective-permute-start.14
  100.4 8.4 %collective-permute-done.14 = bf16[9,4,32,128]{3,2,1,0:T(8,128)(2,1)S(1)} collective-permute-done((bf16[9,4,32,128]{3,2,1,0:T(8,128)(2,1)S(1)}, bf16[9,4,32,128]{3,2,1,0:T(8,128)(2,1)S(1)}, u32[]{:S(2)}, u32[]{:S(2)}) %collective-permute-start.14) | collective-permute-done | bytes 294944 | tf_op jit(solution)/shard_map/ppermute | solution.py:25
  108.8 6.3 %collective-permute-start.15 = (bf16[9,1,32,128]{3,2,1,0:T(8,128)(2,1)S(1)}, bf16[9,1,32,128]{3,2,1,0:T(8,128)(2,1)S(1)}, u32[]{:S(2)}, u32[]{:S(2)}) collective-permute-start(bf16[9,1,32,128]{3,2,1,0:T(8,128)(2,1)S(1)} %get-tuple-element.170), channel_id=1, source_target_pairs={{0,1},{1,2},{2,3},{3,4},{4,5},{5,6},{6,7},{7,8},{8,9},{9,10},{10,1... | collective-permute-start | bytes 221192 | tf_op jit(solution)/shard_map/ppermute | solution.py:14
  115.1 1.3 collective-permute-start.16
  116.4 2.7 collective-permute-done.16
  119.3 1.9 collective-permute-start.17
  121.2 29.9 %collective-permute-done.17 = bf16[9,4,32,128]{3,2,1,0:T(8,128)(2,1)S(1)} collective-permute-done((bf16[9,4,32,128]{3,2,1,0:T(8,128)(2,1)S(1)}, bf16[9,4,32,128]{3,2,1,0:T(8,128)(2,1)S(1)}, u32[]{:S(2)}, u32[]{:S(2)}) %collective-permute-start.17) | collective-permute-done | bytes 294944 | tf_op jit(solution)/shard_map/ppermute | solution.py:25
  151.1 0.7 fusion.190
  151.7 6.9 %collective-permute-start.18 = (bf16[9,1,32,128]{3,2,1,0:T(8,128)(2,1)}, bf16[9,1,32,128]{3,2,1,0:T(8,128)(2,1)}, u32[]{:S(2)}, u32[]{:S(2)}) collective-permute-start(bf16[9,1,32,128]{3,2,1,0:T(8,128)(2,1)} %get-tuple-element.168), channel_id=1, source_target_pairs={{0,1},{1,2},{2,3},{3,4},{4,5},{5,6},{6,7},{7,8},{8,9},{9,10},{10,1... | collective-permute-start | bytes 221192 | tf_op jit(solution)/shard_map/ppermute | solution.py:14
  158.6 1.3 collective-permute-start.19
  159.9 2.2 collective-permute-done.19
  162.1 1.0 pad_maximum_fusion.6
  163.1 6.0 %conditional.14 = (bf16[9,4,32,128]{3,2,1,0:T(8,128)(2,1)}) conditional(s32[]{:T(128)} %convert_element_type.96, () %tuple.57, (bf16[9,4,32,128]{3,2,1,0:T(8,128)(2,1)S(1)}, bf16[9,6,32,128]{3,2,1,0:T(8,128)(2,1)S(1)}, bf16[3,3,3,128,128]{4,3,2,1,0:T(8,128)(2,1)}, f32[9,4,32,128]{3,2,1,0:T(8,128)S(1)}) %tuple.129), branch_computations={%region_12.13_spmd, %region_13.14_spmd} | conditional | flops 1135558656 | bytes 13114634 | solution.py:88
  163.9 0.8 copy-done.16
  164.7 2.8 convolution_select_fusion.6
  167.7 0.6 fusion.93
  168.3 0.8 copy.110
  169.1 1.9 collective-permute-start.20
  171.0 0.7 fusion.188
  171.7 7.9 %collective-permute-start.23 = (bf16[9,1,32,128]{3,2,1,0:T(8,128)(2,1)}, bf16[9,1,32,128]{3,2,1,0:T(8,128)(2,1)}, u32[]{:S(2)}, u32[]{:S(2)}) collective-permute-start(bf16[9,1,32,128]{3,2,1,0:T(8,128)(2,1)} %get-tuple-element.162), channel_id=1, source_target_pairs={{0,1},{1,2},{2,3},{3,4},{4,5},{5,6},{6,7},{7,8},{8,9},{9,10},{10,1... | collective-permute-start | bytes 221192 | tf_op jit(solution)/shard_map/ppermute | solution.py:14
  179.6 1.3 collective-permute-start.24
  180.9 3.3 collective-permute-done.24
  184.2 1.2 fusion.146
  189.3 0.3 fusion.130
  189.6 0.3 fusion.129
  191.1 1.2 fusion.118
  192.9 0.4 fusion.122
  193.3 0.3 fusion.121
  193.9 1.2 fusion.117
  195.3 1.1 multiply_convert_fusion
  196.4 8.5 %collective-permute-start.21 = (bf16[9,1,32,128]{3,2,1,0:T(8,128)(2,1)S(1)}, bf16[9,1,32,128]{3,2,1,0:T(8,128)(2,1)S(1)}, u32[]{:S(2)}, u32[]{:S(2)}) collective-permute-start(bf16[9,1,32,128]{3,2,1,0:T(8,128)(2,1)S(1)} %get-tuple-element.166), channel_id=1, source_target_pairs={{0,1},{1,2},{2,3},{3,4},{4,5},{5,6},{6,7},{7,8},{8,9},{9,10},{10,1... | collective-permute-start | bytes 221192 | tf_op jit(solution)/shard_map/ppermute | solution.py:14
  205.0 1.3 collective-permute-start.22
  206.3 1.8 collective-permute-done.22
  208.3 0.4 conditional.15
  208.6 0.5 copy-done.2
  209.5 1.8 select_bitcast_fusion
  211.3 258.8 %all-reduce.3.cloned.1.call-done = bf16[128,27,128]{2,0,1:T(8,128)(2,1)} async-done(((bf16[128,27,128]{2,0,1:T(8,128)(2,1)}), bf16[128,27,128]{2,0,1:T(8,128)(2,1)}) %all-reduce.3.cloned.1.call-update) | async-done | bytes 884752 | tf_op jit(solution)/shard_map/psum | solution.py:96
  470.1 1.4 convert_bitcast_fusion
  (93 shorter events, 9.1 us)
Async XLA Ops:
  7.2 9.2 %copy-start = (bf16[9,4,32,128]{3,2,1,0:T(8,128)(2,1)S(1)}, bf16[9,4,32,128]{3,2,1,0:T(8,128)(2,1)}, u32[]{:S(2)}) copy-start(bf16[9,4,32,128]{3,2,1,0:T(8,128)(2,1)} %param.21) | copy-start | bytes 884740
  7.2 9.2 %copy-start.12 = (bf16[1,3,3,3,128,128]{5,4,3,2,1,0:T(8,128)(2,1)S(1)}, bf16[1,3,3,3,128,128]{5,4,3,2,1,0:T(8,128)(2,1)}, u32[]{:S(2)}) copy-start(bf16[1,3,3,3,128,128]{5,4,3,2,1,0:T(8,128)(2,1)} %param.20) | copy-start | bytes 2654212
  7.2 462.9 %all-reduce.3.cloned.1.call-start = ((), (), s32[]{:S(2)}) async-start(), calls=%async_computation | async-start | bytes 1769472 | tf_op jit(solution)/shard_map/psum | solution.py:96
  8.7 4.3 collective-permute-start
  10.5 5.3 %collective-permute-start.1 = (bf16[9,1,32,128]{3,1,2,0:T(2,128)(2,1)S(1)}, bf16[9,1,32,128]{3,1,2,0:T(2,128)(2,1)S(1)}, u32[]{:S(2)}, u32[]{:S(2)}) collective-permute-start(bf16[9,1,32,128]{3,1,2,0:T(2,128)(2,1)S(1)} %get-tuple-element.181), channel_id=1, source_target_pairs={{1,0},{2,1},{3,2},{4,3},{5,4},{6,5},{7,6},{8,7},{9,8},{10,9},{11,1... | collective-permute-start | bytes 221192 | tf_op jit(solution)/shard_map/ppermute | solution.py:17
  16.4 9.5 %collective-permute-start.2 = (bf16[9,4,32,128]{3,2,1,0:T(8,128)(2,1)S(1)}, bf16[9,4,32,128]{3,2,1,0:T(8,128)(2,1)S(1)}, u32[]{:S(2)}, u32[]{:S(2)}) collective-permute-start(bf16[9,4,32,128]{3,2,1,0:T(8,128)(2,1)S(1)} %get-tuple-element.154), channel_id=1, source_target_pairs={{32,0},{64,32},{96,64},{128,96},{160,128},{192,160},{224,192},{33,... | collective-permute-start | bytes 884744 | tf_op jit(solution)/shard_map/ppermute | solution.py:25
  25.9 7.3 %collective-permute-start.3 = (bf16[9,1,32,128]{3,2,1,0:T(8,128)(2,1)S(1)}, bf16[9,1,32,128]{3,2,1,0:T(8,128)(2,1)S(1)}, u32[]{:S(2)}, u32[]{:S(2)}) collective-permute-start(bf16[9,1,32,128]{3,2,1,0:T(8,128)(2,1)S(1)} %get-tuple-element.178), channel_id=1, source_target_pairs={{0,1},{1,2},{2,3},{3,4},{4,5},{5,6},{6,7},{7,8},{8,9},{9,10},{10,1... | collective-permute-start | bytes 221192 | tf_op jit(solution)/shard_map/ppermute | solution.py:14
  31.9 4.0 collective-permute-start.4
  36.0 16.1 %copy-start.1 = (bf16[9,4,32,128]{3,2,1,0:T(8,128)(2,1)}, bf16[9,4,32,128]{3,2,1,0:T(8,128)(2,1)S(1)}, u32[]{:S(2)}) copy-start(bf16[9,4,32,128]{3,2,1,0:T(8,128)(2,1)S(1)} %get-tuple-element.155) | copy-start | bytes 884740
  36.0 9.5 %collective-permute-start.5 = (bf16[9,4,32,128]{3,2,1,0:T(8,128)(2,1)S(1)}, bf16[9,4,32,128]{3,2,1,0:T(8,128)(2,1)S(1)}, u32[]{:S(2)}, u32[]{:S(2)}) collective-permute-start(bf16[9,4,32,128]{3,2,1,0:T(8,128)(2,1)S(1)} %get-tuple-element.155), channel_id=1, source_target_pairs={{32,0},{64,32},{96,64},{128,96},{160,128},{192,160},{224,192},{33,... | collective-permute-start | bytes 884744 | tf_op jit(solution)/shard_map/ppermute | solution.py:25
  45.6 6.6 %collective-permute-start.6 = (bf16[9,1,32,128]{3,2,1,0:T(8,128)(2,1)S(1)}, bf16[9,1,32,128]{3,2,1,0:T(8,128)(2,1)S(1)}, u32[]{:S(2)}, u32[]{:S(2)}) collective-permute-start(bf16[9,1,32,128]{3,2,1,0:T(8,128)(2,1)S(1)} %get-tuple-element.176), channel_id=1, source_target_pairs={{0,1},{1,2},{2,3},{3,4},{4,5},{5,6},{6,7},{7,8},{8,9},{9,10},{10,1... | collective-permute-start | bytes 221192 | tf_op jit(solution)/shard_map/ppermute | solution.py:14
  50.8 5.1 %collective-permute-start.7 = (bf16[9,1,32,128]{3,2,1,0:T(8,128)(2,1)S(1)}, bf16[9,1,32,128]{3,2,1,0:T(8,128)(2,1)S(1)}, u32[]{:S(2)}, u32[]{:S(2)}) collective-permute-start(bf16[9,1,32,128]{3,2,1,0:T(8,128)(2,1)S(1)} %get-tuple-element.177), channel_id=1, source_target_pairs={{1,0},{2,1},{3,2},{4,3},{5,4},{6,5},{7,6},{8,7},{9,8},{10,9},{11,1... | collective-permute-start | bytes 221192 | tf_op jit(solution)/shard_map/ppermute | solution.py:17
  56.3 17.3 %copy-start.3 = (bf16[9,4,32,128]{3,2,1,0:T(8,128)(2,1)}, bf16[9,4,32,128]{3,2,1,0:T(8,128)(2,1)S(1)}, u32[]{:S(2)}) copy-start(bf16[9,4,32,128]{3,2,1,0:T(8,128)(2,1)S(1)} %get-tuple-element.156) | copy-start | bytes 884740
  56.3 10.3 %collective-permute-start.8 = (bf16[9,4,32,128]{3,2,1,0:T(8,128)(2,1)S(1)}, bf16[9,4,32,128]{3,2,1,0:T(8,128)(2,1)S(1)}, u32[]{:S(2)}, u32[]{:S(2)}) collective-permute-start(bf16[9,4,32,128]{3,2,1,0:T(8,128)(2,1)S(1)} %get-tuple-element.156), channel_id=1, source_target_pairs={{32,0},{64,32},{96,64},{128,96},{160,128},{192,160},{224,192},{33,... | collective-permute-start | bytes 884744 | tf_op jit(solution)/shard_map/ppermute | solution.py:25
  66.6 6.9 %collective-permute-start.9 = (bf16[9,1,32,128]{3,2,1,0:T(8,128)(2,1)S(1)}, bf16[9,1,32,128]{3,2,1,0:T(8,128)(2,1)S(1)}, u32[]{:S(2)}, u32[]{:S(2)}) collective-permute-start(bf16[9,1,32,128]{3,2,1,0:T(8,128)(2,1)S(1)} %get-tuple-element.174), channel_id=1, source_target_pairs={{0,1},{1,2},{2,3},{3,4},{4,5},{5,6},{6,7},{7,8},{8,9},{9,10},{10,1... | collective-permute-start | bytes 221192 | tf_op jit(solution)/shard_map/ppermute | solution.py:14
  72.2 5.4 %collective-permute-start.10 = (bf16[9,1,32,128]{3,2,1,0:T(8,128)(2,1)S(1)}, bf16[9,1,32,128]{3,2,1,0:T(8,128)(2,1)S(1)}, u32[]{:S(2)}, u32[]{:S(2)}) collective-permute-start(bf16[9,1,32,128]{3,2,1,0:T(8,128)(2,1)S(1)} %get-tuple-element.175), channel_id=1, source_target_pairs={{1,0},{2,1},{3,2},{4,3},{5,4},{6,5},{7,6},{8,7},{9,8},{10,9},{11,1... | collective-permute-start | bytes 221192 | tf_op jit(solution)/shard_map/ppermute | solution.py:17
  77.7 10.3 %copy-start.5 = (bf16[9,4,32,128]{3,2,1,0:T(8,128)(2,1)}, bf16[9,4,32,128]{3,2,1,0:T(8,128)(2,1)S(1)}, u32[]{:S(2)}) copy-start(bf16[9,4,32,128]{3,2,1,0:T(8,128)(2,1)S(1)} %get-tuple-element.157) | copy-start | bytes 884740
  77.7 10.3 %collective-permute-start.11 = (bf16[9,4,32,128]{3,2,1,0:T(8,128)(2,1)S(1)}, bf16[9,4,32,128]{3,2,1,0:T(8,128)(2,1)S(1)}, u32[]{:S(2)}, u32[]{:S(2)}) collective-permute-start(bf16[9,4,32,128]{3,2,1,0:T(8,128)(2,1)S(1)} %get-tuple-element.157), channel_id=1, source_target_pairs={{32,0},{64,32},{96,64},{128,96},{160,128},{192,160},{224,192},{33,... | collective-permute-start | bytes 884744 | tf_op jit(solution)/shard_map/ppermute | solution.py:25
  88.0 6.9 %collective-permute-start.12 = (bf16[9,1,32,128]{3,2,1,0:T(8,128)(2,1)S(1)}, bf16[9,1,32,128]{3,2,1,0:T(8,128)(2,1)S(1)}, u32[]{:S(2)}, u32[]{:S(2)}) collective-permute-start(bf16[9,1,32,128]{3,2,1,0:T(8,128)(2,1)S(1)} %get-tuple-element.172), channel_id=1, source_target_pairs={{0,1},{1,2},{2,3},{3,4},{4,5},{5,6},{6,7},{7,8},{8,9},{9,10},{10,1... | collective-permute-start | bytes 221192 | tf_op jit(solution)/shard_map/ppermute | solution.py:14
  93.6 4.5 collective-permute-start.13
  98.5 10.3 %copy-start.7 = (bf16[9,4,32,128]{3,2,1,0:T(8,128)(2,1)}, bf16[9,4,32,128]{3,2,1,0:T(8,128)(2,1)S(1)}, u32[]{:S(2)}) copy-start(bf16[9,4,32,128]{3,2,1,0:T(8,128)(2,1)S(1)} %get-tuple-element.158) | copy-start | bytes 884740
  98.5 10.3 %collective-permute-start.14 = (bf16[9,4,32,128]{3,2,1,0:T(8,128)(2,1)S(1)}, bf16[9,4,32,128]{3,2,1,0:T(8,128)(2,1)S(1)}, u32[]{:S(2)}, u32[]{:S(2)}) collective-permute-start(bf16[9,4,32,128]{3,2,1,0:T(8,128)(2,1)S(1)} %get-tuple-element.158), channel_id=1, source_target_pairs={{32,0},{64,32},{96,64},{128,96},{160,128},{192,160},{224,192},{33,... | collective-permute-start | bytes 884744 | tf_op jit(solution)/shard_map/ppermute | solution.py:25
  108.8 7.6 %collective-permute-start.15 = (bf16[9,1,32,128]{3,2,1,0:T(8,128)(2,1)S(1)}, bf16[9,1,32,128]{3,2,1,0:T(8,128)(2,1)S(1)}, u32[]{:S(2)}, u32[]{:S(2)}) collective-permute-start(bf16[9,1,32,128]{3,2,1,0:T(8,128)(2,1)S(1)} %get-tuple-element.170), channel_id=1, source_target_pairs={{0,1},{1,2},{2,3},{3,4},{4,5},{5,6},{6,7},{7,8},{8,9},{9,10},{10,1... | collective-permute-start | bytes 221192 | tf_op jit(solution)/shard_map/ppermute | solution.py:14
  115.1 4.0 collective-permute-start.16
  119.3 43.8 %copy-start.9 = (bf16[9,4,32,128]{3,2,1,0:T(8,128)(2,1)}, bf16[9,4,32,128]{3,2,1,0:T(8,128)(2,1)S(1)}, u32[]{:S(2)}) copy-start(bf16[9,4,32,128]{3,2,1,0:T(8,128)(2,1)S(1)} %get-tuple-element.159) | copy-start | bytes 884740
  119.3 31.8 %collective-permute-start.17 = (bf16[9,4,32,128]{3,2,1,0:T(8,128)(2,1)S(1)}, bf16[9,4,32,128]{3,2,1,0:T(8,128)(2,1)S(1)}, u32[]{:S(2)}, u32[]{:S(2)}) collective-permute-start(bf16[9,4,32,128]{3,2,1,0:T(8,128)(2,1)S(1)} %get-tuple-element.159), channel_id=1, source_target_pairs={{32,0},{64,32},{96,64},{128,96},{160,128},{192,160},{224,192},{33,... | collective-permute-start | bytes 884744 | tf_op jit(solution)/shard_map/ppermute | solution.py:25
  151.7 8.2 %collective-permute-start.18 = (bf16[9,1,32,128]{3,2,1,0:T(8,128)(2,1)}, bf16[9,1,32,128]{3,2,1,0:T(8,128)(2,1)}, u32[]{:S(2)}, u32[]{:S(2)}) collective-permute-start(bf16[9,1,32,128]{3,2,1,0:T(8,128)(2,1)} %get-tuple-element.168), channel_id=1, source_target_pairs={{0,1},{1,2},{2,3},{3,4},{4,5},{5,6},{6,7},{7,8},{8,9},{9,10},{10,1... | collective-permute-start | bytes 221192 | tf_op jit(solution)/shard_map/ppermute | solution.py:14
  158.6 3.5 collective-permute-start.19
  163.5 1.2 copy-start.16
  163.6 1.2 copy-start.23
  169.1 16.3 %collective-permute-start.20 = (bf16[9,4,32,128]{3,2,1,0:T(8,128)(2,1)}, bf16[9,4,32,128]{3,2,1,0:T(8,128)(2,1)S(1)}, u32[]{:S(2)}, u32[]{:S(2)}) collective-permute-start(bf16[9,4,32,128]{3,2,1,0:T(8,128)(2,1)} %get-tuple-element.160), channel_id=1, source_target_pairs={{32,0},{64,32},{96,64},{128,96},{160,128},{192,160},{224,192},{33,... | collective-permute-start | bytes 884744 | tf_op jit(solution)/shard_map/ppermute | solution.py:25
  171.7 9.2 %collective-permute-start.23 = (bf16[9,1,32,128]{3,2,1,0:T(8,128)(2,1)}, bf16[9,1,32,128]{3,2,1,0:T(8,128)(2,1)}, u32[]{:S(2)}, u32[]{:S(2)}) collective-permute-start(bf16[9,1,32,128]{3,2,1,0:T(8,128)(2,1)} %get-tuple-element.162), channel_id=1, source_target_pairs={{0,1},{1,2},{2,3},{3,4},{4,5},{5,6},{6,7},{7,8},{8,9},{9,10},{10,1... | collective-permute-start | bytes 221192 | tf_op jit(solution)/shard_map/ppermute | solution.py:14
  179.6 4.6 collective-permute-start.24
  191.1 1.8 copy-start.11
  196.4 9.9 %collective-permute-start.21 = (bf16[9,1,32,128]{3,2,1,0:T(8,128)(2,1)S(1)}, bf16[9,1,32,128]{3,2,1,0:T(8,128)(2,1)S(1)}, u32[]{:S(2)}, u32[]{:S(2)}) collective-permute-start(bf16[9,1,32,128]{3,2,1,0:T(8,128)(2,1)S(1)} %get-tuple-element.166), channel_id=1, source_target_pairs={{0,1},{1,2},{2,3},{3,4},{4,5},{5,6},{6,7},{7,8},{8,9},{9,10},{10,1... | collective-permute-start | bytes 221192 | tf_op jit(solution)/shard_map/ppermute | solution.py:14
  205.0 3.2 collective-permute-start.22
  208.2 1.0 copy-start.2
  208.2 1.0 copy-start.4
  208.2 1.1 copy-start.6
  208.2 1.2 copy-start.8
  208.3 1.3 copy-start.10
Sparse Core Ops, SparseCore 0:
  196.5 273.5 all-reduce.2
where the time goes:
time: 488 us; the launch traced here: 479 us
  waiting for transfers between devices  353 us (72%)
  starting transfers between devices  81.1 us (17%)
  between operations  15.3 us (3%)
  matrix products  12.4 us (3%)
  other arithmetic  9.14 us (2%)
  local copies, waits for them, and re-layouts  6.45 us (1%)
    psum x1, waiting for transfers between devices, local(): lax.psum((tap_terms(act_pad, grad_flat, chans) * scale).astype(jnp.bfloat...  259 us
    ppermute x7, waiting for transfers between devices, shifted(): return lax.ppermute(block, axis, route)  68 us
    ppermute x9, starting transfers between devices, padded_2(): lax.ppermute(lax.slice_in_dim(block, block.shape[dim] - width, None, axis...  53.8 us
    ppermute x9, waiting for transfers between devices, padded_2(): lax.ppermute(lax.slice_in_dim(block, 0, width, axis=dim), axis, backward)  26.5 us
    ppermute x7, starting transfers between devices, shifted(): return lax.ppermute(block, axis, route)  15.7 us
    ppermute x9, starting transfers between devices, padded_2(): lax.ppermute(lax.slice_in_dim(block, 0, width, axis=dim), axis, backward)  11.6 us
  transfers between devices with their start and end apart: 26, of which 16 were waited for; matrix products, arithmetic and copies ran while one was open for 1% of the time, Pallas kernels for 0%

commit v1 on v0

v1 whole, which is shorter than its diff:
```python
import functools
import math

import jax
import jax.numpy as jnp
import numpy as np
from jax import lax
from jax.experimental import pallas as pl
from jax.experimental.pallas import tpu as pltpu
from jax.sharding import PartitionSpec as P

BF = jnp.bfloat16
F32 = jnp.float32
DP = 32
SEC = 8
FRAMES = 9
ROWS = 4
COLS = 32
CH = 128
AXES = ("section", "dp")
HALVING = (1, 2, 4, 8, 16)


def permute(value, hops):
    pairs = [
        (src * DP + d, dst * DP + d + off)
        for src, dst, off in hops
        for d in range(DP)
        if 0 <= d + off < DP
    ]
    return lax.ppermute(value, AXES, pairs)


def fill(x_ref, frame, row, value):
    count = value.shape[0] // COLS
    col = lax.broadcasted_iota(jnp.int32, value.shape, 0) % COLS
    size = value.shape[0]
    after = jnp.where(col == COLS - 1, 0.0, pltpu.roll(value, size - 1, 0))
    before = jnp.where(col == 0, 0.0, pltpu.roll(value, 1, 0))
    for n, part in enumerate((after, value, before)):
        x_ref[frame, row : row + count, :, n * CH : (n + 1) * CH] = part.astype(BF).reshape(
            count, COLS, CH
        )


def back_pass(x_ref, w_ref, slope_ref, rows, emit):
    group = 3
    size = rows * COLS
    one_later = None
    two_later = None
    for start in range(FRAMES - group, -1, -group):
        lhs = jnp.concatenate(
            [x_ref[start : start + group, 2 - j : 2 - j + rows] for j in range(3)], axis=-1
        ).reshape(group * size, 9 * CH)
        part = jnp.dot(lhs, w_ref[...], preferred_element_type=F32)
        for t in range(group - 1, -1, -1):
            here = part[t * size : (t + 1) * size]
            back = here[:, 2 * CH :]
            if one_later is not None:
                back = back + one_later[:, CH : 2 * CH]
            if two_later is not None:
                back = back + two_later[:, :CH]
            frame = start + t
            grad = x_ref[frame, 1 : 1 + rows, :, CH : 2 * CH].reshape(size, CH).astype(F32)
            new = grad + slope_ref[frame].reshape(size, CH) * back
            emit(frame, new.astype(BF))
            two_later = one_later
            one_later = here


def single_kernel(low_ref, own_ref, high_ref, w_ref, slope_ref, out_ref, x_ref):
    for t in range(FRAMES):
        whole = jnp.concatenate([low_ref[t], own_ref[t], high_ref[t]], axis=0)
        fill(x_ref, t, 0, whole.reshape(-1, CH).astype(F32))

    def emit(frame, value):
        out_ref[frame] = value.reshape(ROWS, COLS, CH)

    back_pass(x_ref, w_ref, slope_ref, ROWS, emit)


def double_kernel(
    low_ref, own_ref, high_ref, w1_ref, slope1_ref, w0_ref, slope0_ref, out_ref, x1_ref, x0_ref
):
    for t in range(FRAMES):
        whole = jnp.concatenate([low_ref[t], own_ref[t], high_ref[t]], axis=0)
        fill(x1_ref, t, 0, whole.reshape(-1, CH).astype(F32))

    def emit_mid(frame, value):
        fill(x0_ref, frame, 0, value.astype(F32))

    def emit(frame, value):
        out_ref[frame] = value.reshape(ROWS, COLS, CH)

    back_pass(x1_ref, w1_ref, slope1_ref, ROWS + 2, emit_mid)
    back_pass(x0_ref, w0_ref, slope0_ref, ROWS, emit)


def in_vmem(count):
    return [pl.BlockSpec(memory_space=pltpu.VMEM)] * count


def single(low, own, high, w, slope):
    return pl.pallas_call(
        single_kernel,
        out_shape=jax.ShapeDtypeStruct((FRAMES, ROWS, COLS, CH), BF),
        in_specs=in_vmem(5),
        out_specs=pl.BlockSpec(memory_space=pltpu.VMEM),
        scratch_shapes=[pltpu.VMEM((FRAMES, ROWS + 2, COLS, 3 * CH), BF)],
        compiler_params=pltpu.CompilerParams(vmem_limit_bytes=24 << 20),
        name="one_block",
    )(low, own, high, w, slope)


def double(low, own, high, w1, slope1, w0, slope0):
    return pl.pallas_call(
        double_kernel,
        out_shape=jax.ShapeDtypeStruct((FRAMES, ROWS, COLS, CH), BF),
        in_specs=in_vmem(7),
        out_specs=pl.BlockSpec(memory_space=pltpu.VMEM),
        scratch_shapes=[
            pltpu.VMEM((FRAMES, ROWS + 4, COLS, 3 * CH), BF),
            pltpu.VMEM((FRAMES, ROWS + 2, COLS, 3 * CH), BF),
        ],
        compiler_params=pltpu.CompilerParams(vmem_limit_bytes=24 << 20),
        name="two_blocks",
    )(low, own, high, w1, slope1, w0, slope0)


def taps_kernel(scale, ut_ref, g_ref, out_ref):
    grad = g_ref[...].reshape(FRAMES, ROWS * COLS, CH)
    padded = jnp.concatenate([grad, jnp.zeros((2, ROWS * COLS, CH), BF)], axis=0)
    rhs = jnp.concatenate([padded[2 - i : 2 - i + FRAMES] for i in range(3)], axis=-1).reshape(
        FRAMES * ROWS * COLS, 3 * CH
    )
    step = 3 * CH
    for n in range(3):
        rows = slice(n * step, (n + 1) * step)
        part = jnp.dot(ut_ref[rows, :], rhs, preferred_element_type=F32)
        out_ref[rows, :] = (part * scale).astype(BF)


def taps(ut, grad, scale):
    return pl.pallas_call(
        functools.partial(taps_kernel, scale),
        out_shape=jax.ShapeDtypeStruct((9 * CH, 3 * CH), BF),
        in_specs=in_vmem(2),
        out_specs=pl.BlockSpec(memory_space=pltpu.VMEM),
        compiler_params=pltpu.CompilerParams(vmem_limit_bytes=24 << 20),
        name="kernel_taps",
    )(ut, grad)


def channel_order():
    share = CH // DP
    order = []
    for n in range(CH):
        slot, rest = divmod(n, share)
        d = 0
        for place, bit in enumerate(HALVING):
            if (slot >> (len(HALVING) - 1 - place)) & 1:
                d |= bit
        order.append(d * share + rest)
    matrix = np.zeros((CH, CH), np.float32)
    matrix[np.arange(CH), order] = 1.0
    return matrix


def slope_of(x):
    x = x.astype(F32)
    sig = jax.nn.sigmoid(x)
    return sig * (1.0 + x * (1.0 - sig))


def as_matrix(kern):
    return jnp.transpose(kern, (1, 2, 4, 0, 3)).reshape(9 * CH, 3 * CH)


def local(acts, kernels, cotangent):
    me = lax.axis_index("section")
    dp = lax.axis_index("dp")
    scale = 1.0 / math.sqrt(FRAMES * ROWS * DP * COLS)
    own_acts = acts[0]
    odd = [s for s in range(SEC) if s % 2 == 1]
    every = range(SEC)

    low0 = permute(cotangent[:, -1:], [(7, 7, 1)])
    high0 = permute(cotangent[:, :1], [(7, 7, -1)])
    kern_next = permute(kernels[0], [(s + 1, s, 0) for s in odd[:-1]])
    act_low = permute(own_acts[:, -1:], [(s, s, 1) for s in every])
    act_high = permute(own_acts[:, :1], [(s, s, -1) for s in every])
    act6 = jnp.concatenate([act_low, own_acts, act_high], axis=1)
    act_next = permute(act6, [(s + 1, s, 0) for s in odd[:-1]])
    act_prev = permute(act6, [(s, (s + 1) % SEC, 0) for s in every])

    w = as_matrix(kernels[0])
    w_next = as_matrix(kern_next)
    slope = slope_of(own_acts)
    row = lax.broadcasted_iota(jnp.int32, act_next.shape, 1) + dp * ROWS - 1
    inside = (row >= 0) & (row < DP * ROWS)
    slope_next = jnp.where(inside, slope_of(act_next), 0.0)

    x_prev = act_prev.astype(F32)
    u = jnp.pad(
        (x_prev * jax.nn.sigmoid(x_prev)).astype(BF), ((0, 0), (0, 0), (1, 1), (0, 0))
    )
    shifted = jnp.stack(
        [
            u[:, j : j + ROWS, k : k + COLS].reshape(-1, CH)
            for j in range(3)
            for k in range(3)
        ]
    )
    picked = lax.dot_general(
        jnp.asarray(channel_order(), BF),
        shifted,
        (((1,), (2,)), ((), ())),
        preferred_element_type=F32,
    ).astype(BF)
    ut = picked.reshape(9 * CH, FRAMES * ROWS * COLS)

    result = lax.cond(
        me == 7,
        lambda: single(low0, cotangent, high0, w, slope),
        lambda: jnp.zeros_like(cotangent),
    )
    for s in (5, 3, 1):
        own = permute(result, [(s + 2, s, 0)])
        low = permute(result[:, 2:], [(s + 2, s, 1)])
        high = permute(result[:, :2], [(s + 2, s, -1)])
        result = lax.cond(
            me == s,
            lambda low=low, own=own, high=high: double(
                low, own, high, w_next, slope_next, w, slope
            ),
            lambda result=result: result,
        )

    def even(result, sections):
        hops = [(s + 1, s) for s in sections]
        own = permute(result, [(a, b, 0) for a, b in hops])
        low = permute(result[:, -1:], [(a, b, 1) for a, b in hops])
        high = permute(result[:, :1], [(a, b, -1) for a, b in hops])
        live = functools.reduce(jnp.logical_or, [me == s for s in sections])
        return lax.cond(
            live,
            lambda: single(low, own, high, w, slope),
            lambda: result,
        )

    result = even(result, (6, 4, 2))
    final = even(result, (0,))

    grad = jnp.where(me == 0, cotangent, result)
    part = taps(ut, grad, scale)
    for bit in HALVING:
        half = part.shape[0] // 2
        mine = (dp // bit) % 2
        keep = lax.dynamic_slice_in_dim(part, mine * half, half, 0)
        give = lax.dynamic_slice_in_dim(part, (1 - mine) * half, half, 0)
        got = lax.ppermute(
            give, AXES, [(s * DP + d, s * DP + (d ^ bit)) for s in every for d in range(DP)]
        )
        part = (keep.astype(F32) + got.astype(F32)).astype(BF)
    part = permute(part, [((s + 1) % SEC, s, 0) for s in every]).astype(F32)
    share = CH // DP
    kernel_part = jnp.transpose(part.reshape(share, 9, 3, CH), (0, 2, 1, 3)).reshape(share, 27, CH)
    return (final[None], kernel_part[None])


def solution(mesh):
    return jax.shard_map(
        local,
        mesh=mesh,
        in_specs=(
            P("section", None, "dp", None, None),
            P("section", None, None, None, None, None),
            P(None, "dp", None, None),
        ),
        out_specs=(P("section", None, "dp", None, None), P("section", "dp", None, None)),
        check_vma=False,
    )
```

time: 488 us -> 183 us (0.38)
  the two profiles are of different devices: /device:TPU:8 before, /device:TPU:1 now
where the time goes in v1:
time: 183 us; the launch traced here: 182 us
  waiting for transfers between devices  77.3 us (42%)
  starting transfers between devices  56.9 us (31%)
  local copies, waits for them, and re-layouts  33.1 us (18%)
  other arithmetic  6.81 us (4%)
  Pallas kernels  3.95 us (2%)
  matrix products  2.6 us (1%)
    ppermute x23, waiting for transfers between devices, permute(): return lax.ppermute(value, AXES, pairs)  67.9 us
    ppermute x23, starting transfers between devices, permute(): return lax.ppermute(value, AXES, pairs)  41.9 us
    ppermute x5, starting transfers between devices, local(): lax.ppermute(give, AXES, [(s * DP + d, s * DP + (d ^ bit)) for s in every...  15 us
    ppermute x5, waiting for transfers between devices, local(): lax.ppermute(give, AXES, [(s * DP + d, s * DP + (d ^ bit)) for s in every...  9.38 us
    unnamed x22, local copies, waits for them, and re-layouts  8.45 us
    reshape x1, local copies, waits for them, and re-layouts, local(): ut = picked.reshape(9 * CH, FRAMES * ROWS * COLS)  4.34 us
    transpose x2, local copies, waits for them, and re-layouts, as_matrix(): return jnp.transpose(kern, (1, 2, 4, 0, 3)).reshape(9 * CH, 3 * CH)  4.11 us
    convert_element_type x1, local copies, waits for them, and re-layouts, local(): picked = lax.dot_general(jnp.asarray(channel_order(), BF), shifted, (((1,...  3.82 us
  transfers between devices with their start and end apart: 28, of which 7 were waited for; matrix products, arithmetic and copies ran while one was open for 21% of the time, Pallas kernels for 1%

profile of v1, /device:TPU:1, one launch (start us, length us, event | category | flops | bytes accessed | tf_op | source)
XLA Modules:
  0.0 182.2 jit_solution(1757855053344379194)
XLA Ops:
  0.6 1.0 fusion.20
  1.7 5.1 %collective-permute-start.7 = (bf16[9,1,32,128]{3,2,1,0:T(8,128)(2,1)S(1)}, bf16[9,1,32,128]{3,2,1,0:T(8,128)(2,1)S(1)}, u32[]{:S(2)}, u32[]{:S(2)}) collective-permute-start(bf16[9,1,32,128]{3,2,1,0:T(8,128)(2,1)S(1)} %get-tuple-element.158), channel_id=1, source_target_pairs={{1,0},{2,1},{3,2},{4,3},{5,4},{6,5},{7,6},{8,7},{9,8},{10,9},{11,1... | collective-permute-start | bytes 221192 | tf_op jit(solution)/shard_map/ppermute | solution.py:31
  6.8 3.0 %collective-permute-start.6 = (bf16[9,1,32,128]{3,2,1,0:T(8,128)(2,1)S(1)}, bf16[9,1,32,128]{3,2,1,0:T(8,128)(2,1)S(1)}, u32[]{:S(2)}, u32[]{:S(2)}) collective-permute-start(bf16[9,1,32,128]{3,2,1,0:T(8,128)(2,1)S(1)} %get-tuple-element.157), channel_id=1, source_target_pairs={{0,1},{1,2},{2,3},{3,4},{4,5},{5,6},{6,7},{7,8},{8,9},{9,10},{10,1... | collective-permute-start | bytes 221192 | tf_op jit(solution)/shard_map/ppermute | solution.py:31
  9.8 1.6 fusion.22
  11.4 1.3 collective-permute-start
  12.7 1.3 collective-permute-start.1
  13.9 1.6 collective-permute-start.5
  15.5 1.8 pad_maximum_fusion
  17.3 0.8 collective-permute-start.21
  18.1 1.2 fusion.15
  19.3 0.8 copy.13
  20.4 1.4 collective-permute-start.8
  21.8 0.8 conditional.6
  21.8 0.8 broadcast.27
  22.6 1.4 collective-permute-start.3
  24.0 1.7 fusion.21
  25.7 1.3 collective-permute-start.2
  27.0 28.0 %collective-permute-done.21 = bf16[9,6,32,128]{3,2,1,0:T(8,128)(2,1)} collective-permute-done((bf16[9,6,32,128]{3,2,1,0:T(8,128)(2,1)}, bf16[9,6,32,128]{3,2,1,0:T(8,128)(2,1)}, u32[]{:S(2)}, u32[]{:S(2)}) %collective-permute-start.21) | collective-permute-done | bytes 442400 | tf_op jit(solution)/shard_map/ppermute | solution.py:31
  54.9 1.3 collective-permute-start.4
  56.3 1.3 fusion.10
  57.5 1.3 pad_slice_fusion
  59.5 0.7 constant_dynamic-update-slice_fusion.7
  60.3 0.7 constant_dynamic-update-slice_fusion.6
  61.0 0.7 constant_dynamic-update-slice_fusion.5
  61.7 0.8 constant_dynamic-update-slice_fusion.4
  62.5 1.3 fusion.6
  63.8 0.7 constant_dynamic-update-slice_fusion.3
  65.3 3.3 %copy.14 = bf16[3,3,128,3,128]{4,3,2,1,0:T(4,128)(2,1)} copy(bf16[3,3,128,3,128]{2,4,1,0,3:T(8,128)(2,1)} %bitcast.5) | data formatting | bytes 1769472 | tf_op jit(solution)/shard_map/transpose | solution.py:176
  68.6 1.4 copy.21
  70.0 1.4 collective-permute-start.10
  71.4 1.0 fusion.19
  72.4 1.3 collective-permute-start.9
  73.7 1.3 collective-permute-start.11
  75.1 1.7 constant_dynamic-update-slice_fusion.1
  77.0 1.4 collective-permute-start.13
  78.4 1.0 fusion.18
  79.4 1.3 collective-permute-start.12
  80.7 1.3 collective-permute-start.14
  82.0 0.7 constant_dynamic-update-slice_fusion
  82.8 1.6 fusion.17
  84.4 1.4 collective-permute-start.16
  85.8 1.3 collective-permute-start.15
  87.0 1.3 collective-permute-start.17
  88.3 2.6 %fusion = bf16[128,9,1152]{2,0,1:T(8,128)(2,1)S(1)} fusion(bf16[9,1152,128]{2,1,0:T(8,128)(2,1)} %constant_dynamic-update-slice_fusion, bf16[128,128,1]{1,0,2:T(8,128)(2,1)} %constant.130), kind=kOutput, calls=%fused_computation.1 | convolution fusion | flops 341065728 | bytes 5341184 | tf_op jit(solution)/shard_map/dot_general | solution.py:214
  90.9 3.8 %copy.15 = bf16[128,9,1152]{2,1,0:T(8,128)(2,1)} copy(bf16[128,9,1152]{2,0,1:T(8,128)(2,1)S(1)} %fusion) | data formatting | bytes 5308416 | tf_op jit(solution)/shard_map/convert_element_type | solution.py:219
  94.8 4.3 %reshape.19.ut_ref = bf16[1152,1152]{1,0:T(8,128)(2,1)S(1)} reshape(bf16[128,9,1152]{2,1,0:T(8,128)(2,1)} %copy.15) | data formatting | bytes 5308416 | tf_op jit(solution)/shard_map/reshape | solution.py:220
  99.4 1.0 broadcast_select_fusion.g_ref
  100.4 1.6 kernel_taps.1
  102.4 1.5 collective-permute-done.22
  104.1 2.9 %collective-permute-start.23 = (bf16[288,384]{1,0:T(8,128)(2,1)S(1)}, bf16[288,384]{1,0:T(8,128)(2,1)S(1)}, u32[]{:S(2)}, u32[]{:S(2)}) collective-permute-start(bf16[288,384]{1,0:T(8,128)(2,1)S(1)} %constant_dynamic-slice_fusion.3), channel_id=1, source_target_pairs={{0,2},{1,3},{2,0},{3,1},{4,6},{5,7},{6,4},{7,5},{8,10},{9,11},{10,... | collective-permute-start | bytes 663560 | tf_op jit(solution)/shard_map/ppermute | solution.py:261
  107.0 5.5 %collective-permute-done.23 = bf16[288,384]{1,0:T(8,128)(2,1)S(1)} collective-permute-done((bf16[288,384]{1,0:T(8,128)(2,1)S(1)}, bf16[288,384]{1,0:T(8,128)(2,1)S(1)}, u32[]{:S(2)}, u32[]{:S(2)}) %collective-permute-start.23) | collective-permute-done | bytes 221216 | tf_op jit(solution)/shard_map/ppermute | solution.py:261
  112.6 2.4 %collective-permute-start.24 = (bf16[144,384]{1,0:T(8,128)(2,1)S(1)}, bf16[144,384]{1,0:T(8,128)(2,1)S(1)}, u32[]{:S(2)}, u32[]{:S(2)}) collective-permute-start(bf16[144,384]{1,0:T(8,128)(2,1)S(1)} %constant_dynamic-slice_fusion.2), channel_id=1, source_target_pairs={{0,4},{1,5},{2,6},{3,7},{4,0},{5,1},{6,2},{7,3},{8,12},{9,13},{10,... | collective-permute-start | bytes 331784 | tf_op jit(solution)/shard_map/ppermute | solution.py:261
  115.0 2.1 %collective-permute-done.24 = bf16[144,384]{1,0:T(8,128)(2,1)S(1)} collective-permute-done((bf16[144,384]{1,0:T(8,128)(2,1)S(1)}, bf16[144,384]{1,0:T(8,128)(2,1)S(1)}, u32[]{:S(2)}, u32[]{:S(2)}) %collective-permute-start.24) | collective-permute-done | bytes 110624 | tf_op jit(solution)/shard_map/ppermute | solution.py:261
  117.1 3.1 %collective-permute-start.25 = (bf16[72,384]{1,0:T(8,128)(2,1)S(1)}, bf16[72,384]{1,0:T(8,128)(2,1)S(1)}, u32[]{:S(2)}, u32[]{:S(2)}) collective-permute-start(bf16[72,384]{1,0:T(8,128)(2,1)S(1)} %constant_dynamic-slice_fusion.1), channel_id=1, source_target_pairs={{0,8},{1,9},{2,10},{3,11},{4,12},{5,13},{6,14},{7,15},{8,0},{9,1},... | collective-permute-start | bytes 165896 | tf_op jit(solution)/shard_map/ppermute | solution.py:261
  120.2 1.3 collective-permute-start.19
  121.8 6.3 %collective-permute-start.26 = (bf16[36,384]{1,0:T(8,128)(2,1)S(1)}, bf16[36,384]{1,0:T(8,128)(2,1)S(1)}, u32[]{:S(2)}, u32[]{:S(2)}) collective-permute-start(bf16[36,384]{1,0:T(8,128)(2,1)S(1)} %constant_dynamic-slice_fusion), channel_id=1, source_target_pairs={{0,16},{1,17},{2,18},{3,19},{4,20},{5,21},{6,22},{7,23},{8,24},{9,... | collective-permute-start | bytes 82952 | tf_op jit(solution)/shard_map/ppermute | solution.py:261
  128.1 0.9 fusion.16
  129.1 1.3 collective-permute-start.18
  130.4 1.3 collective-permute-start.20
  131.7 7.6 %collective-permute-start.27 = (bf16[36,384]{1,0:T(8,128)(2,1)S(1)}, bf16[36,384]{1,0:T(8,128)(2,1)S(1)}, u32[]{:S(2)}, u32[]{:S(2)}) collective-permute-start(bf16[36,384]{1,0:T(8,128)(2,1)S(1)} %add_convert_fusion.4), channel_id=1, source_target_pairs={{32,0},{33,1},{34,2},{35,3},{36,4},{37,5},{38,6},{39,7},{40,8},{41... | collective-permute-start | bytes 82952 | tf_op jit(solution)/shard_map/ppermute | solution.py:31
  139.3 37.5 %collective-permute-done.18 = bf16[9,1,32,128]{3,2,1,0:T(8,128)(2,1)S(1)} collective-permute-done((bf16[9,1,32,128]{3,2,1,0:T(8,128)(2,1)S(1)}, bf16[9,1,32,128]{3,2,1,0:T(8,128)(2,1)S(1)}, u32[]{:S(2)}, u32[]{:S(2)}) %collective-permute-start.18) | collective-permute-done | bytes 73760 | tf_op jit(solution)/shard_map/ppermute | solution.py:31
  176.8 2.3 %collective-permute-done.20 = bf16[9,1,32,128]{3,2,1,0:T(8,128)(2,1)S(1)} collective-permute-done((bf16[9,1,32,128]{3,2,1,0:T(8,128)(2,1)S(1)}, bf16[9,1,32,128]{3,2,1,0:T(8,128)(2,1)S(1)}, u32[]{:S(2)}, u32[]{:S(2)}) %collective-permute-start.20) | collective-permute-done | bytes 73760 | tf_op jit(solution)/shard_map/ppermute | solution.py:31
  179.1 2.4 %conditional.11 = (bf16[1,9,4,32,128]{4,3,2,1,0:T(8,128)(2,1)}) conditional(s32[]{:T(128)} %convert_element_type.84, bf16[9,4,32,128]{3,2,1,0:T(8,128)(2,1)} %get-tuple-element.169, (bf16[9,1,32,128]{3,2,1,0:T(8,128)(2,1)S(1)}, bf16[9,4,32,128]{3,2,1,0:T(8,128)(2,1)S(1)}, bf16[9,1,32,128]{3,2,1,0:T(8,128)(2,1)S(1)}, ...), branch_computations={%region_10.11_spmd, %region_11.12_spmd} | conditional | bytes 8 | solution.py:245
  179.1 2.4 %one_block.5 = bf16[9,4,32,128]{3,2,1,0:T(8,128)(2,1)} custom-call(bf16[9,1,32,128]{3,2,1,0:T(8,128)(2,1)S(1)} %get-tuple-element.132.low_ref, bf16[9,4,32,128]{3,2,1,0:T(8,128)(2,1)S(1)} %get-tuple-element.133.own_ref, bf16[9,1,32,128]{3,2,1,0:T(8,128)(2,1)S(1)} %get-tuple-element.134.high_ref, bf16[1152,384]{1,0:T(8,128)(2,1)S(1)} %get-tuple-element.135.w_ref, ...), custom_call_target="tpu_custom_call" | custom-call | tf_op jit(solution)/shard_map/cond/branch_1_fun/one_block/pallas_call | solution.py:104
  (55 shorter events, 3.8 us)
Async XLA Ops:
  0.6 18.7 %copy-start.5 = (bf16[1,3,3,3,128,128]{5,4,3,2,1,0:T(8,128)(2,1)S(1)}, bf16[1,3,3,3,128,128]{5,4,3,2,1,0:T(8,128)(2,1)}, u32[]{:S(2)}) copy-start(bf16[1,3,3,3,128,128]{5,4,3,2,1,0:T(8,128)(2,1)} %param.17) | copy-start | bytes 2654212
  1.7 13.9 %collective-permute-start.7 = (bf16[9,1,32,128]{3,2,1,0:T(8,128)(2,1)S(1)}, bf16[9,1,32,128]{3,2,1,0:T(8,128)(2,1)S(1)}, u32[]{:S(2)}, u32[]{:S(2)}) collective-permute-start(bf16[9,1,32,128]{3,2,1,0:T(8,128)(2,1)S(1)} %get-tuple-element.158), channel_id=1, source_target_pairs={{1,0},{2,1},{3,2},{4,3},{5,4},{6,5},{7,6},{8,7},{9,8},{10,9},{11,1... | collective-permute-start | bytes 221192 | tf_op jit(solution)/shard_map/ppermute | solution.py:31
  6.8 8.7 %collective-permute-start.6 = (bf16[9,1,32,128]{3,2,1,0:T(8,128)(2,1)S(1)}, bf16[9,1,32,128]{3,2,1,0:T(8,128)(2,1)S(1)}, u32[]{:S(2)}, u32[]{:S(2)}) collective-permute-start(bf16[9,1,32,128]{3,2,1,0:T(8,128)(2,1)S(1)} %get-tuple-element.157), channel_id=1, source_target_pairs={{0,1},{1,2},{2,3},{3,4},{4,5},{5,6},{6,7},{7,8},{8,9},{9,10},{10,1... | collective-permute-start | bytes 221192 | tf_op jit(solution)/shard_map/ppermute | solution.py:31
  11.4 10.4 %collective-permute-start = (bf16[9,1,32,128]{3,2,1,0:T(8,128)(2,1)}, bf16[9,1,32,128]{3,2,1,0:T(8,128)(2,1)}, u32[]{:S(2)}, u32[]{:S(2)}) collective-permute-start(bf16[9,1,32,128]{3,2,1,0:T(8,128)(2,1)} %get-tuple-element.162), channel_id=1, source_target_pairs={{224,225},{225,226},{226,227},{227,228},{228,229},{229,230},{230,2... | collective-permute-start | bytes 221192 | tf_op jit(solution)/shard_map/ppermute | solution.py:31
  12.7 9.1 %collective-permute-start.1 = (bf16[9,1,32,128]{3,2,1,0:T(8,128)(2,1)}, bf16[9,1,32,128]{3,2,1,0:T(8,128)(2,1)}, u32[]{:S(2)}, u32[]{:S(2)}) collective-permute-start(bf16[9,1,32,128]{3,2,1,0:T(8,128)(2,1)} %get-tuple-element.161), channel_id=1, source_target_pairs={{225,224},{226,225},{227,226},{228,227},{229,228},{230,229},{231,2... | collective-permute-start | bytes 221192 | tf_op jit(solution)/shard_map/ppermute | solution.py:31
  13.9 51.4 %collective-permute-start.5 = (bf16[3,3,3,128,128]{4,3,2,1,0:T(8,128)(2,1)}, bf16[3,3,3,128,128]{4,3,2,1,0:T(8,128)(2,1)}, u32[]{:S(2)}, u32[]{:S(2)}) collective-permute-start(bf16[3,3,3,128,128]{4,3,2,1,0:T(8,128)(2,1)} %bitcast.56), channel_id=1, source_target_pairs={{64,32},{65,33},{66,34},{67,35},{68,36},{69,37},{70,38},{71,39},{7... | collective-permute-start | bytes 2654216 | tf_op jit(solution)/shard_map/ppermute | solution.py:31
  17.3 4.5 %copy-start.4 = (bf16[9,4,32,128]{3,2,1,0:T(8,128)(2,1)S(1)}, bf16[9,4,32,128]{3,2,1,0:T(8,128)(2,1)}, u32[]{:S(2)}) copy-start(bf16[9,4,32,128]{3,2,1,0:T(8,128)(2,1)} %param.18) | copy-start | bytes 884740
  17.3 37.6 %collective-permute-start.21 = (bf16[9,6,32,128]{3,2,1,0:T(8,128)(2,1)}, bf16[9,6,32,128]{3,2,1,0:T(8,128)(2,1)}, u32[]{:S(2)}, u32[]{:S(2)}) collective-permute-start(bf16[9,6,32,128]{3,2,1,0:T(8,128)(2,1)} %pad_maximum_fusion), channel_id=1, source_target_pairs={{0,32},{1,33},{2,34},{3,35},{4,36},{5,37},{6,38},{7,39},{8,40},{9,... | collective-permute-start | bytes 1327112 | tf_op jit(solution)/shard_map/ppermute | solution.py:31
  19.3 63.5 %copy-start.2 = (f32[9,4,32,128]{3,2,1,0:T(8,128)}, f32[9,4,32,128]{3,2,1,0:T(8,128)S(1)}, u32[]{:S(2)}) copy-start(f32[9,4,32,128]{3,2,1,0:T(8,128)S(1)} %fusion.15) | copy-start | bytes 1769476
  20.3 78.8 %copy-start = (bf16[144,8,3,128]{3,1,2,0:T(8,128)(2,1)}, bf16[144,8,3,128]{3,1,2,0:T(8,128)(2,1)S(1)}, u32[]{:S(2)}) copy-start(bf16[144,8,3,128]{3,1,2,0:T(8,128)(2,1)S(1)} %copy.22) | copy-start | bytes 2654212
  20.4 42.1 %collective-permute-start.8 = (bf16[9,6,32,128]{3,2,1,0:T(8,128)(2,1)}, bf16[9,6,32,128]{3,2,1,0:T(8,128)(2,1)}, u32[]{:S(2)}, u32[]{:S(2)}) collective-permute-start(bf16[9,6,32,128]{3,2,1,0:T(8,128)(2,1)} %pad_maximum_fusion), channel_id=1, source_target_pairs={{64,32},{65,33},{66,34},{67,35},{68,36},{69,37},{70,38},{71,39},{7... | collective-permute-start | bytes 1327112 | tf_op jit(solution)/shard_map/ppermute | solution.py:31
  22.6 47.4 %collective-permute-start.3 = (bf16[9,4,32,128]{3,2,1,0:T(8,128)(2,1)}, bf16[9,4,32,128]{3,2,1,0:T(8,128)(2,1)}, u32[]{:S(2)}, u32[]{:S(2)}) collective-permute-start(bf16[9,4,32,128]{3,2,1,0:T(8,128)(2,1)} %get-tuple-element.165), channel_id=1, source_target_pairs={{224,160},{225,161},{226,162},{227,163},{228,164},{229,165},{230,1... | collective-permute-start | bytes 884744 | tf_op jit(solution)/shard_map/ppermute | solution.py:31
  25.7 44.3 %collective-permute-start.2 = (bf16[9,2,32,128]{3,2,1,0:T(8,128)(2,1)}, bf16[9,2,32,128]{3,2,1,0:T(8,128)(2,1)}, u32[]{:S(2)}, u32[]{:S(2)}) collective-permute-start(bf16[9,2,32,128]{3,2,1,0:T(8,128)(2,1)} %get-tuple-element.160), channel_id=1, source_target_pairs={{224,161},{225,162},{226,163},{227,164},{228,165},{229,166},{230,1... | collective-permute-start | bytes 442376 | tf_op jit(solution)/shard_map/ppermute | solution.py:31
  54.9 15.1 %collective-permute-start.4 = (bf16[9,2,32,128]{3,2,1,0:T(8,128)(2,1)}, bf16[9,2,32,128]{3,2,1,0:T(8,128)(2,1)}, u32[]{:S(2)}, u32[]{:S(2)}) collective-permute-start(bf16[9,2,32,128]{3,2,1,0:T(8,128)(2,1)} %get-tuple-element.159), channel_id=1, source_target_pairs={{225,160},{226,161},{227,162},{228,163},{229,164},{230,165},{231,1... | collective-permute-start | bytes 442376 | tf_op jit(solution)/shard_map/ppermute | solution.py:31
  70.0 6.7 %collective-permute-start.10 = (bf16[9,4,32,128]{3,2,1,0:T(8,128)(2,1)}, bf16[9,4,32,128]{3,2,1,0:T(8,128)(2,1)}, u32[]{:S(2)}, u32[]{:S(2)}) collective-permute-start(bf16[9,4,32,128]{3,2,1,0:T(8,128)(2,1)} %get-tuple-element.166), channel_id=1, source_target_pairs={{160,96},{161,97},{162,98},{163,99},{164,100},{165,101},{166,102},... | collective-permute-start | bytes 884744 | tf_op jit(solution)/shard_map/ppermute | solution.py:31
  72.4 4.4 %collective-permute-start.9 = (bf16[9,2,32,128]{3,2,1,0:T(8,128)(2,1)S(1)}, bf16[9,2,32,128]{3,2,1,0:T(8,128)(2,1)}, u32[]{:S(2)}, u32[]{:S(2)}) collective-permute-start(bf16[9,2,32,128]{3,2,1,0:T(8,128)(2,1)S(1)} %get-tuple-element.156), channel_id=1, source_target_pairs={{160,97},{161,98},{162,99},{163,100},{164,101},{165,102},{166,103}... | collective-permute-start | bytes 442376 | tf_op jit(solution)/shard_map/ppermute | solution.py:31
  73.7 3.0 %collective-permute-start.11 = (bf16[9,2,32,128]{3,2,1,0:T(8,128)(2,1)S(1)}, bf16[9,2,32,128]{3,2,1,0:T(8,128)(2,1)}, u32[]{:S(2)}, u32[]{:S(2)}) collective-permute-start(bf16[9,2,32,128]{3,2,1,0:T(8,128)(2,1)S(1)} %get-tuple-element.155), channel_id=1, source_target_pairs={{161,96},{162,97},{163,98},{164,99},{165,100},{166,101},{167,102},... | collective-permute-start | bytes 442376 | tf_op jit(solution)/shard_map/ppermute | solution.py:31
  77.0 5.8 %collective-permute-start.13 = (bf16[9,4,32,128]{3,2,1,0:T(8,128)(2,1)}, bf16[9,4,32,128]{3,2,1,0:T(8,128)(2,1)}, u32[]{:S(2)}, u32[]{:S(2)}) collective-permute-start(bf16[9,4,32,128]{3,2,1,0:T(8,128)(2,1)} %get-tuple-element.167), channel_id=1, source_target_pairs={{96,32},{97,33},{98,34},{99,35},{100,36},{101,37},{102,38},{103,39... | collective-permute-start | bytes 884744 | tf_op jit(solution)/shard_map/ppermute | solution.py:31
  79.4 3.4 %collective-permute-start.12 = (bf16[9,2,32,128]{3,2,1,0:T(8,128)(2,1)S(1)}, bf16[9,2,32,128]{3,2,1,0:T(8,128)(2,1)}, u32[]{:S(2)}, u32[]{:S(2)}) collective-permute-start(bf16[9,2,32,128]{3,2,1,0:T(8,128)(2,1)S(1)} %get-tuple-element.154), channel_id=1, source_target_pairs={{96,33},{97,34},{98,35},{99,36},{100,37},{101,38},{102,39},{103,40... | collective-permute-start | bytes 442376 | tf_op jit(solution)/shard_map/ppermute | solution.py:31
  80.7 2.1 %collective-permute-start.14 = (bf16[9,2,32,128]{3,2,1,0:T(8,128)(2,1)S(1)}, bf16[9,2,32,128]{3,2,1,0:T(8,128)(2,1)}, u32[]{:S(2)}, u32[]{:S(2)}) collective-permute-start(bf16[9,2,32,128]{3,2,1,0:T(8,128)(2,1)S(1)} %get-tuple-element.153), channel_id=1, source_target_pairs={{97,32},{98,33},{99,34},{100,35},{101,36},{102,37},{103,38},{104,3... | collective-permute-start | bytes 442376 | tf_op jit(solution)/shard_map/ppermute | solution.py:31
  84.4 14.7 %collective-permute-start.16 = (bf16[9,4,32,128]{3,2,1,0:T(8,128)(2,1)}, bf16[9,4,32,128]{3,2,1,0:T(8,128)(2,1)}, u32[]{:S(2)}, u32[]{:S(2)}) collective-permute-start(bf16[9,4,32,128]{3,2,1,0:T(8,128)(2,1)} %get-tuple-element.168), channel_id=1, source_target_pairs={{224,192},{225,193},{226,194},{227,195},{228,196},{229,197},{230,1... | collective-permute-start | bytes 884744 | tf_op jit(solution)/shard_map/ppermute | solution.py:31
  85.8 13.3 %collective-permute-start.15 = (bf16[9,1,32,128]{3,2,1,0:T(8,128)(2,1)}, bf16[9,1,32,128]{3,2,1,0:T(8,128)(2,1)}, u32[]{:S(2)}, u32[]{:S(2)}) collective-permute-start(bf16[9,1,32,128]{3,2,1,0:T(8,128)(2,1)} %get-tuple-element.152), channel_id=1, source_target_pairs={{224,193},{225,194},{226,195},{227,196},{228,197},{229,198},{230,1... | collective-permute-start | bytes 221192 | tf_op jit(solution)/shard_map/ppermute | solution.py:31
  87.0 12.1 %collective-permute-start.17 = (bf16[9,1,32,128]{3,2,1,0:T(8,128)(2,1)}, bf16[9,1,32,128]{3,2,1,0:T(8,128)(2,1)}, u32[]{:S(2)}, u32[]{:S(2)}) collective-permute-start(bf16[9,1,32,128]{3,2,1,0:T(8,128)(2,1)} %get-tuple-element.151), channel_id=1, source_target_pairs={{225,192},{226,193},{227,194},{228,195},{229,196},{230,197},{231,1... | collective-permute-start | bytes 221192 | tf_op jit(solution)/shard_map/ppermute | solution.py:31
  102.0 77.1 %copy-start.1 = (bf16[144,8,3,128]{3,1,2,0:T(8,128)(2,1)S(1)}, bf16[144,8,3,128]{3,1,2,0:T(8,128)(2,1)}, u32[]{:S(2)}) copy-start(bf16[144,8,3,128]{3,1,2,0:T(8,128)(2,1)} %copy-done) | copy-start | bytes 2654212
  102.0 77.1 %copy-start.3 = (f32[9,4,32,128]{3,2,1,0:T(8,128)S(1)}, f32[9,4,32,128]{3,2,1,0:T(8,128)}, u32[]{:S(2)}) copy-start(f32[9,4,32,128]{3,2,1,0:T(8,128)} %copy-done.2) | copy-start | bytes 1769476
  102.1 1.9 %collective-permute-start.22 = (bf16[576,384]{1,0:T(8,128)(2,1)S(1)}, bf16[576,384]{1,0:T(8,128)(2,1)S(1)}, u32[]{:S(2)}, u32[]{:S(2)}) collective-permute-start(bf16[576,384]{1,0:T(8,128)(2,1)S(1)} %constant_dynamic-slice_fusion.4), channel_id=1, source_target_pairs={{0,1},{1,0},{2,3},{3,2},{4,5},{5,4},{6,7},{7,6},{8,9},{9,8},{10,11... | collective-permute-start | bytes 1327112 | tf_op jit(solution)/shard_map/ppermute | solution.py:261
  104.1 8.3 %collective-permute-start.23 = (bf16[288,384]{1,0:T(8,128)(2,1)S(1)}, bf16[288,384]{1,0:T(8,128)(2,1)S(1)}, u32[]{:S(2)}, u32[]{:S(2)}) collective-permute-start(bf16[288,384]{1,0:T(8,128)(2,1)S(1)} %constant_dynamic-slice_fusion.3), channel_id=1, source_target_pairs={{0,2},{1,3},{2,0},{3,1},{4,6},{5,7},{6,4},{7,5},{8,10},{9,11},{10,... | collective-permute-start | bytes 663560 | tf_op jit(solution)/shard_map/ppermute | solution.py:261
  112.6 4.5 %collective-permute-start.24 = (bf16[144,384]{1,0:T(8,128)(2,1)S(1)}, bf16[144,384]{1,0:T(8,128)(2,1)S(1)}, u32[]{:S(2)}, u32[]{:S(2)}) collective-permute-start(bf16[144,384]{1,0:T(8,128)(2,1)S(1)} %constant_dynamic-slice_fusion.2), channel_id=1, source_target_pairs={{0,4},{1,5},{2,6},{3,7},{4,0},{5,1},{6,2},{7,3},{8,12},{9,13},{10,... | collective-permute-start | bytes 331784 | tf_op jit(solution)/shard_map/ppermute | solution.py:261
  117.1 4.6 %collective-permute-start.25 = (bf16[72,384]{1,0:T(8,128)(2,1)S(1)}, bf16[72,384]{1,0:T(8,128)(2,1)S(1)}, u32[]{:S(2)}, u32[]{:S(2)}) collective-permute-start(bf16[72,384]{1,0:T(8,128)(2,1)S(1)} %constant_dynamic-slice_fusion.1), channel_id=1, source_target_pairs={{0,8},{1,9},{2,10},{3,11},{4,12},{5,13},{6,14},{7,15},{8,0},{9,1},... | collective-permute-start | bytes 165896 | tf_op jit(solution)/shard_map/ppermute | solution.py:261
  120.2 58.9 %collective-permute-start.19 = (bf16[9,4,32,128]{3,2,1,0:T(8,128)(2,1)}, bf16[9,4,32,128]{3,2,1,0:T(8,128)(2,1)S(1)}, u32[]{:S(2)}, u32[]{:S(2)}) collective-permute-start(bf16[9,4,32,128]{3,2,1,0:T(8,128)(2,1)} %get-tuple-element.169), channel_id=1, source_target_pairs={{32,0},{33,1},{34,2},{35,3},{36,4},{37,5},{38,6},{39,7},{40,8},{41... | collective-permute-start | bytes 884744 | tf_op jit(solution)/shard_map/ppermute | solution.py:31
  121.8 9.8 %collective-permute-start.26 = (bf16[36,384]{1,0:T(8,128)(2,1)S(1)}, bf16[36,384]{1,0:T(8,128)(2,1)S(1)}, u32[]{:S(2)}, u32[]{:S(2)}) collective-permute-start(bf16[36,384]{1,0:T(8,128)(2,1)S(1)} %constant_dynamic-slice_fusion), channel_id=1, source_target_pairs={{0,16},{1,17},{2,18},{3,19},{4,20},{5,21},{6,22},{7,23},{8,24},{9,... | collective-permute-start | bytes 82952 | tf_op jit(solution)/shard_map/ppermute | solution.py:261
  129.1 47.7 %collective-permute-start.18 = (bf16[9,1,32,128]{3,2,1,0:T(8,128)(2,1)S(1)}, bf16[9,1,32,128]{3,2,1,0:T(8,128)(2,1)S(1)}, u32[]{:S(2)}, u32[]{:S(2)}) collective-permute-start(bf16[9,1,32,128]{3,2,1,0:T(8,128)(2,1)S(1)} %get-tuple-element.150), channel_id=1, source_target_pairs={{32,1},{33,2},{34,3},{35,4},{36,5},{37,6},{38,7},{39,8},{40,9},{41... | collective-permute-start | bytes 221192 | tf_op jit(solution)/shard_map/ppermute | solution.py:31
  130.4 48.8 %collective-permute-start.20 = (bf16[9,1,32,128]{3,2,1,0:T(8,128)(2,1)S(1)}, bf16[9,1,32,128]{3,2,1,0:T(8,128)(2,1)S(1)}, u32[]{:S(2)}, u32[]{:S(2)}) collective-permute-start(bf16[9,1,32,128]{3,2,1,0:T(8,128)(2,1)S(1)} %get-tuple-element.149), channel_id=1, source_target_pairs={{33,0},{34,1},{35,2},{36,3},{37,4},{38,5},{39,6},{40,7},{41,8},{42... | collective-permute-start | bytes 221192 | tf_op jit(solution)/shard_map/ppermute | solution.py:31
  131.7 49.8 %collective-permute-start.27 = (bf16[36,384]{1,0:T(8,128)(2,1)S(1)}, bf16[36,384]{1,0:T(8,128)(2,1)S(1)}, u32[]{:S(2)}, u32[]{:S(2)}) collective-permute-start(bf16[36,384]{1,0:T(8,128)(2,1)S(1)} %add_convert_fusion.4), channel_id=1, source_target_pairs={{32,0},{33,1},{34,2},{35,3},{36,4},{37,5},{38,6},{39,7},{40,8},{41... | collective-permute-start | bytes 82952 | tf_op jit(solution)/shard_map/ppermute | solution.py:31

commit v2 on v1

v2 whole, which is shorter than its diff:
```python
import functools
import math

import jax
import jax.numpy as jnp
import numpy as np
from jax import lax
from jax.experimental import pallas as pl
from jax.experimental.pallas import tpu as pltpu
from jax.sharding import PartitionSpec as P

BF = jnp.bfloat16
F32 = jnp.float32
DP = 32
SEC = 8
FRAMES = 9
ROWS = 4
COLS = 32
CH = 128
AXES = ("section", "dp")
HALVING = (1, 2, 4, 8, 16)


def permute(value, hops):
    pairs = [
        (src * DP + d, dst * DP + d + off)
        for src, dst, off in hops
        for d in range(DP)
        if 0 <= d + off < DP
    ]
    return lax.ppermute(value, AXES, pairs)


def fill(x_ref, frame, row, value):
    count = value.shape[0] // COLS
    col = lax.broadcasted_iota(jnp.int32, value.shape, 0) % COLS
    size = value.shape[0]
    after = jnp.where(col == COLS - 1, 0.0, pltpu.roll(value, size - 1, 0))
    before = jnp.where(col == 0, 0.0, pltpu.roll(value, 1, 0))
    for n, part in enumerate((after, value, before)):
        x_ref[frame, row : row + count, :, n * CH : (n + 1) * CH] = part.astype(BF).reshape(
            count, COLS, CH
        )


def back_pass(x_ref, w_ref, slope_ref, rows, emit):
    group = 3
    size = rows * COLS
    one_later = None
    two_later = None
    for start in range(FRAMES - group, -1, -group):
        lhs = jnp.concatenate(
            [x_ref[start : start + group, 2 - j : 2 - j + rows] for j in range(3)], axis=-1
        ).reshape(group * size, 9 * CH)
        part = jnp.dot(lhs, w_ref[...], preferred_element_type=F32)
        for t in range(group - 1, -1, -1):
            here = part[t * size : (t + 1) * size]
            back = here[:, 2 * CH :]
            if one_later is not None:
                back = back + one_later[:, CH : 2 * CH]
            if two_later is not None:
                back = back + two_later[:, :CH]
            frame = start + t
            grad = x_ref[frame, 1 : 1 + rows, :, CH : 2 * CH].reshape(size, CH).astype(F32)
            new = grad + slope_ref[frame].reshape(size, CH) * back
            emit(frame, new.astype(BF))
            two_later = one_later
            one_later = here


def emit_to(refs):
    out_ref, top_ref, bottom_ref = refs

    def emit(frame, value):
        whole = value.reshape(ROWS, COLS, CH)
        out_ref[frame] = whole
        top_ref[frame] = whole[:2]
        bottom_ref[frame] = whole[2:]

    return emit


def single_kernel(low_ref, own_ref, high_ref, w_ref, slope_ref, *rest):
    *outs, x_ref = rest
    for t in range(FRAMES):
        whole = jnp.concatenate([low_ref[t], own_ref[t], high_ref[t]], axis=0)
        fill(x_ref, t, 0, whole.reshape(-1, CH).astype(F32))
    back_pass(x_ref, w_ref, slope_ref, ROWS, emit_to(outs))


def double_kernel(low_ref, own_ref, high_ref, w1_ref, slope1_ref, w0_ref, slope0_ref, *rest):
    *outs, x1_ref, x0_ref = rest
    for t in range(FRAMES):
        whole = jnp.concatenate([low_ref[t], own_ref[t], high_ref[t]], axis=0)
        fill(x1_ref, t, 0, whole.reshape(-1, CH).astype(F32))

    def emit_mid(frame, value):
        fill(x0_ref, frame, 0, value.astype(F32))

    back_pass(x1_ref, w1_ref, slope1_ref, ROWS + 2, emit_mid)
    back_pass(x0_ref, w0_ref, slope0_ref, ROWS, emit_to(outs))


def in_vmem(count):
    return [pl.BlockSpec(memory_space=pltpu.VMEM)] * count


def gradient_shapes():
    return [
        jax.ShapeDtypeStruct((FRAMES, rows, COLS, CH), BF) for rows in (ROWS, 2, 2)
    ]


def single(low, own, high, w, slope):
    return pl.pallas_call(
        single_kernel,
        out_shape=gradient_shapes(),
        in_specs=in_vmem(5),
        out_specs=in_vmem(3),
        scratch_shapes=[pltpu.VMEM((FRAMES, ROWS + 2, COLS, 3 * CH), BF)],
        compiler_params=pltpu.CompilerParams(vmem_limit_bytes=24 << 20),
        name="one_block",
    )(low, own, high, w, slope)


def double(low, own, high, w1, slope1, w0, slope0):
    return pl.pallas_call(
        double_kernel,
        out_shape=gradient_shapes(),
        in_specs=in_vmem(7),
        out_specs=in_vmem(3),
        scratch_shapes=[
            pltpu.VMEM((FRAMES, ROWS + 4, COLS, 3 * CH), BF),
            pltpu.VMEM((FRAMES, ROWS + 2, COLS, 3 * CH), BF),
        ],
        compiler_params=pltpu.CompilerParams(vmem_limit_bytes=24 << 20),
        name="two_blocks",
    )(low, own, high, w1, slope1, w0, slope0)


def tap_rows_kernel(act_ref, order_ref, out_ref, u_ref):
    for t in range(FRAMES):
        x = act_ref[t].reshape(-1, CH).astype(F32)
        u = (x * jax.nn.sigmoid(x)).astype(BF).astype(F32)
        col = lax.broadcasted_iota(jnp.int32, u.shape, 0) % COLS
        size = u.shape[0]
        before = jnp.where(col == 0, 0.0, pltpu.roll(u, 1, 0))
        after = jnp.where(col == COLS - 1, 0.0, pltpu.roll(u, size - 1, 0))
        for k, part in enumerate((before, u, after)):
            u_ref[k, t] = part.astype(BF).reshape(ROWS + 2, COLS, CH)
    for j in range(3):
        for k in range(3):
            taken = u_ref[k, :, j : j + ROWS].reshape(FRAMES * ROWS * COLS, CH)
            out_ref[3 * j + k] = lax.dot_general(
                order_ref[...], taken, (((1,), (1,)), ((), ())), preferred_element_type=F32
            ).astype(BF)


def tap_rows(act6, order):
    return pl.pallas_call(
        tap_rows_kernel,
        out_shape=jax.ShapeDtypeStruct((9, CH, FRAMES * ROWS * COLS), BF),
        in_specs=in_vmem(2),
        out_specs=pl.BlockSpec(memory_space=pltpu.VMEM),
        scratch_shapes=[pltpu.VMEM((3, FRAMES, ROWS + 2, COLS, CH), BF)],
        compiler_params=pltpu.CompilerParams(vmem_limit_bytes=24 << 20),
        name="tap_rows",
    )(act6, order)


def taps_kernel(scale, ut_ref, g_ref, out_ref):
    grad = g_ref[...].reshape(FRAMES, ROWS * COLS, CH)
    padded = jnp.concatenate([grad, jnp.zeros((2, ROWS * COLS, CH), BF)], axis=0)
    rhs = jnp.concatenate([padded[2 - i : 2 - i + FRAMES] for i in range(3)], axis=-1).reshape(
        FRAMES * ROWS * COLS, 3 * CH
    )
    for n in range(3):
        taps_here = slice(3 * n, 3 * n + 3)
        lhs = ut_ref[taps_here].reshape(3 * CH, FRAMES * ROWS * COLS)
        part = jnp.dot(lhs, rhs, preferred_element_type=F32)
        out_ref[taps_here] = (part * scale).astype(BF).reshape(3, CH, 3 * CH)


def taps(ut, grad, scale):
    return pl.pallas_call(
        functools.partial(taps_kernel, scale),
        out_shape=jax.ShapeDtypeStruct((9, CH, 3 * CH), BF),
        in_specs=in_vmem(2),
        out_specs=pl.BlockSpec(memory_space=pltpu.VMEM),
        compiler_params=pltpu.CompilerParams(vmem_limit_bytes=24 << 20),
        name="kernel_taps",
    )(ut, grad)


def channel_order():
    share = CH // DP
    order = []
    for n in range(CH):
        slot, rest = divmod(n, share)
        d = 0
        for place, bit in enumerate(HALVING):
            if (slot >> (len(HALVING) - 1 - place)) & 1:
                d |= bit
        order.append(d * share + rest)
    matrix = np.zeros((CH, CH), np.float32)
    matrix[np.arange(CH), order] = 1.0
    return matrix


def slope_of(x):
    x = x.astype(F32)
    sig = jax.nn.sigmoid(x)
    return sig * (1.0 + x * (1.0 - sig))


def as_matrix(kern):
    return jnp.transpose(kern, (1, 2, 4, 0, 3)).reshape(9 * CH, 3 * CH)


def local(acts, kernels, cotangent):
    me = lax.axis_index("section")
    dp = lax.axis_index("dp")
    core = dp % 2
    scale = 1.0 / math.sqrt(FRAMES * ROWS * DP * COLS)
    odd = [s for s in range(SEC) if s % 2 == 1]
    every = range(SEC)
    pair = odd[:-1]
    barrier = lax.optimization_barrier

    both = jnp.concatenate([cotangent, acts[0]], axis=0)
    edge_low = permute(both[:, -1:], [(s, s, 1) for s in every])
    edge_high = permute(both[:, :1], [(s, s, -1) for s in every])
    low0, high0 = edge_low[:FRAMES], edge_high[:FRAMES]
    act6 = jnp.concatenate([edge_low[FRAMES:], acts[0], edge_high[FRAMES:]], axis=1)

    w = as_matrix(kernels[0])
    half = w.shape[0] // 2
    w_half = permute(
        lax.dynamic_slice_in_dim(w, core * half, half, 0), [(s + 1, s, 0) for s in pair]
    )
    slope = slope_of(acts[0])
    none = jnp.zeros((FRAMES, 2, COLS, CH), BF)
    state = lax.cond(
        me == 7,
        lambda: tuple(single(low0, cotangent, high0, w, slope)),
        lambda: (cotangent, none, none),
    )

    act6, state = barrier((act6, state))
    act_next = permute(act6, [(s + 1, s, 0) for s in pair])
    w_other = lax.ppermute(
        w_half, AXES, [(s * DP + d, s * DP + (d ^ 1)) for s in pair for d in range(DP)]
    )
    w_next = jnp.where(
        core == 0,
        jnp.concatenate([w_half, w_other], axis=0),
        jnp.concatenate([w_other, w_half], axis=0),
    )
    row = lax.broadcasted_iota(jnp.int32, act_next.shape, 1) + dp * ROWS - 1
    inside = (row >= 0) & (row < DP * ROWS)
    slope_next = jnp.where(inside, slope_of(act_next), 0.0)

    def hop(state, target):
        result, top, bottom = state
        own = permute(result, [(target + 2, target, 0)])
        low = permute(bottom, [(target + 2, target, 1)])
        high = permute(top, [(target + 2, target, -1)])
        return low, own, high

    def stage(state, arrived, section):
        low, own, high = arrived
        return lax.cond(
            me == section,
            lambda: tuple(double(low, own, high, w_next, slope_next, w, slope)),
            lambda: state,
        )

    state = stage(state, hop(state, 5), 5)
    state = stage(state, hop(state, 3), 3)
    act6, state = barrier((act6, state))
    arrived = hop(state, 1)
    act_prev = permute(act6, [(s, (s + 1) % SEC, 0) for s in every])
    ut = tap_rows(act_prev, jnp.asarray(channel_order(), BF))
    ut, arrived = barrier((ut, arrived))
    result, _, _ = stage(state, arrived, 1)

    def even(result, sections):
        hops = [(s + 1, s) for s in sections]
        own = permute(result, [(a, b, 0) for a, b in hops])
        low = permute(result[:, -1:], [(a, b, 1) for a, b in hops])
        high = permute(result[:, :1], [(a, b, -1) for a, b in hops])
        live = functools.reduce(jnp.logical_or, [me == s for s in sections])
        return lax.cond(
            live,
            lambda: single(low, own, high, w, slope)[0],
            lambda: result,
        )

    result = even(result, (6, 4, 2))
    final = even(result, (0,))

    grad = jnp.where(me == 0, cotangent, result)
    part = taps(ut, grad, scale)
    for bit in HALVING:
        size = part.shape[1] // 2
        mine = (dp // bit) % 2
        keep = lax.dynamic_slice_in_dim(part, mine * size, size, 1)
        give = lax.dynamic_slice_in_dim(part, (1 - mine) * size, size, 1)
        shift = 0
        if bit == HALVING[-1]:
            keep = permute(keep, [((s + 1) % SEC, s, 0) for s in every])
            shift = 1
        got = lax.ppermute(
            give,
            AXES,
            [((s + shift) % SEC * DP + d, s * DP + (d ^ bit)) for s in every for d in range(DP)],
        )
        part = keep.astype(F32) + got.astype(F32)
        if not shift:
            part = part.astype(BF)
    share = CH // DP
    kernel_part = jnp.transpose(part.reshape(9, share, 3, CH), (1, 2, 0, 3)).reshape(share, 27, CH)
    return (final[None], kernel_part[None])


def solution(mesh):
    return jax.shard_map(
        local,
        mesh=mesh,
        in_specs=(
            P("section", None, "dp", None, None),
            P("section", None, None, None, None, None),
            P(None, "dp", None, None),
        ),
        out_specs=(P("section", None, "dp", None, None), P("section", "dp", None, None)),
        check_vma=False,
    )
```

time: 183 us -> 136 us (0.74)
  the two profiles are of different devices: /device:TPU:1 before, /device:TPU:8 now
where the time goes in v2:
time: 136 us; the launch traced here: 134 us
  waiting for transfers between devices  76.6 us (56%)
  starting transfers between devices  33.6 us (25%)
  Pallas kernels  9.57 us (7%)
  local copies, waits for them, and re-layouts  7.46 us (5%)
  other arithmetic  5.52 us (4%)
    ppermute x21, waiting for transfers between devices, permute(): return lax.ppermute(value, AXES, pairs)  60 us
    ppermute x21, starting transfers between devices, permute(): return lax.ppermute(value, AXES, pairs)  21.1 us
    ppermute x5, waiting for transfers between devices, local(): lax.ppermute(give, AXES, [((s + shift) % SEC * DP + d, s * DP + (d ^ bit)...  16.6 us
    ppermute x5, starting transfers between devices, local(): lax.ppermute(give, AXES, [((s + shift) % SEC * DP + d, s * DP + (d ^ bit)...  8.76 us
    pallas_call x1, Pallas kernels, double(): pl.pallas_call(double_kernel, out_shape=gradient_shapes(), in_specs=in_vm...  6.83 us
    ppermute x1, starting transfers between devices, local(): lax.ppermute(w_half, AXES, [(s * DP + d, s * DP + (d ^ 1)) for s in pair...  3.71 us
    select_n x1, other arithmetic, local(): jnp.where(core == 0, jnp.concatenate([w_half, w_other], axis=0), jnp.conc...  2.86 us
  transfers between devices with their start and end apart: 27, of which 11 were waited for; matrix products, arithmetic and copies ran while one was open for 6% of the time, Pallas kernels for 1%

profile of v2, /device:TPU:8, one launch (start us, length us, event | category | flops | bytes accessed | tf_op | source)
XLA Modules:
  0.0 134.0 jit_solution(16168846366970981860)
XLA Ops:
  0.6 2.4 %copy.9 = bf16[3,3,128,3,128]{4,3,2,1,0:T(4,128)(2,1)S(1)} copy(bf16[3,3,128,3,128]{2,4,1,0,3:T(8,128)(2,1)} %bitcast.26) | data formatting | bytes 1769472 | tf_op jit(solution)/shard_map/transpose | solution.py:217
  3.1 0.0 copy-start.6
  3.1 0.0 copy-start.7
  3.1 0.1 copy.13
  3.3 0.1 constant_dynamic-slice_fusion.6
  3.4 1.3 collective-permute-start.5
  4.7 1.7 %collective-permute-start = (bf16[18,1,32,128]{3,2,1,0:T(8,128)(2,1)S(1)}, bf16[18,1,32,128]{3,2,1,0:T(8,128)(2,1)S(1)}, u32[]{:S(2)}, u32[]{:S(2)}) collective-permute-start(bf16[18,1,32,128]{3,2,1,0:T(8,128)(2,1)S(1)} %get-tuple-element.190), channel_id=1, source_target_pairs={{0,1},{1,2},{2,3},{3,4},{4,5},{5,6},{6,7},{7,8},{8,9},{9,10},{10,1... | collective-permute-start | bytes 442376 | tf_op jit(solution)/shard_map/ppermute | solution.py:31
  6.5 1.3 collective-permute-start.1
  7.8 0.2 fusion.10
  8.0 0.0 collective-permute-done
  8.0 3.8 %collective-permute-done.1 = bf16[18,1,32,128]{3,2,1,0:T(8,128)(2,1)S(1)} collective-permute-done((bf16[18,1,32,128]{3,2,1,0:T(8,128)(2,1)S(1)}, bf16[18,1,32,128]{3,2,1,0:T(8,128)(2,1)S(1)}, u32[]{:S(2)}, u32[]{:S(2)}) %collective-permute-start.1) | collective-permute-done | bytes 147488 | tf_op jit(solution)/shard_map/ppermute | solution.py:31
  11.8 2.1 %conditional.6 = ((bf16[9,4,32,128]{3,2,1,0:T(8,128)(2,1)}, bf16[9,2,32,128]{3,2,1,0:T(8,128)(2,1)}, bf16[9,2,32,128]{3,2,1,0:T(8,128)(2,1)})) conditional(s32[]{:T(128)} %convert_element_type.69, bf16[9,4,32,128]{3,2,1,0:T(8,128)(2,1)S(1)} %copy-done.6, (bf16[18,1,32,128]{3,2,1,0:T(8,128)(2,1)S(1)}, bf16[18,1,32,128]{3,2,1,0:T(8,128)(2,1)S(1)}, ...), branch_computations={%region_0.1_spmd, %region_1.2_spmd} | conditional | bytes 884772 | solution.py:243
  11.8 0.7 copy.14
  12.5 0.7 broadcast_in_dim.13
  13.2 0.7 broadcast_in_dim.13.clone
  13.9 0.8 pad_maximum_fusion
  14.8 1.3 collective-permute-start.7
  16.0 3.8 %collective-permute-done.5 = bf16[576,384]{1,0:T(8,128)(2,1)} collective-permute-done((bf16[576,384]{1,0:T(8,128)(2,1)S(1)}, bf16[576,384]{1,0:T(8,128)(2,1)}, u32[]{:S(2)}, u32[]{:S(2)}) %collective-permute-start.5) | collective-permute-done | bytes 442400 | tf_op jit(solution)/shard_map/ppermute | solution.py:31
  19.8 3.7 %collective-permute-start.6 = (bf16[576,384]{1,0:T(8,128)(2,1)}, bf16[576,384]{1,0:T(8,128)(2,1)}, u32[]{:S(2)}, u32[]{:S(2)}) collective-permute-start(bf16[576,384]{1,0:T(8,128)(2,1)} %collective-permute-done.5), channel_id=1, source_target_pairs={{32,33},{33,32},{34,35},{35,34},{36,37},{37,36},{38,39},{39,38},{4... | collective-permute-start | bytes 1327112 | tf_op jit(solution)/shard_map/ppermute | solution.py:251
  23.6 0.7 collective-permute-start.3
  24.3 1.3 %collective-permute-start.2 = (bf16[9,2,32,128]{3,2,1,0:T(8,128)(2,1)}, bf16[9,2,32,128]{3,2,1,0:T(8,128)(2,1)}, u32[]{:S(2)}, u32[]{:S(2)}) collective-permute-start(bf16[9,2,32,128]{3,2,1,0:T(8,128)(2,1)} %get-tuple-element.173), channel_id=1, source_target_pairs={{224,161},{225,162},{226,163},{227,164},{228,165},{229,166},{230,1... | collective-permute-start | bytes 442376 | tf_op jit(solution)/shard_map/ppermute | solution.py:31
  25.6 1.3 collective-permute-start.4
  27.0 0.4 collective-permute-done.7
  27.4 0.3 fusion.5
  27.8 2.9 %maximum_select_fusion = bf16[1152,384]{1,0:T(8,128)(2,1)} fusion(bf16[576,384]{1,0:T(8,128)(2,1)} %collective-permute-done.6, bf16[576,384]{1,0:T(8,128)(2,1)} %collective-permute-done.5, pred[]{:T(512)S(6)} %eq.43), kind=kLoop, calls=%fused_computation.9 | loop fusion | flops 3981312 | bytes 1769473 | tf_op jit(solution)/shard_map/jit(_where)/select_n | solution.py:254
  30.6 0.7 collective-permute-start.9
  31.3 0.7 collective-permute-start.10
  32.0 0.7 collective-permute-start.8
  32.8 0.0 copy-start
  32.8 0.1 collective-permute-start.11
  32.9 1.3 collective-permute-start.13
  34.2 1.3 collective-permute-start.12
  35.5 1.5 %collective-permute-start.14 = (bf16[9,2,32,128]{3,2,1,0:T(8,128)(2,1)}, bf16[9,2,32,128]{3,2,1,0:T(8,128)(2,1)}, u32[]{:S(2)}, u32[]{:S(2)}) collective-permute-start(bf16[9,2,32,128]{3,2,1,0:T(8,128)(2,1)} %get-tuple-element.183), channel_id=1, source_target_pairs={{97,32},{98,33},{99,34},{100,35},{101,36},{102,37},{103,38},{104,3... | collective-permute-start | bytes 442376 | tf_op jit(solution)/shard_map/ppermute | solution.py:31
  37.0 4.4 %collective-permute-done.11.act_ref = bf16[9,6,32,128]{3,2,1,0:T(8,128)(2,1)S(1)} collective-permute-done((bf16[9,6,32,128]{3,2,1,0:T(8,128)(2,1)}, bf16[9,6,32,128]{3,2,1,0:T(8,128)(2,1)S(1)}, u32[]{:S(2)}, u32[]{:S(2)}) %collective-permute-start.11) | collective-permute-done | bytes 442400 | tf_op jit(solution)/shard_map/ppermute | solution.py:31
  41.4 1.1 tap_rows.1.ut_ref
  42.5 42.9 %collective-permute-done.14 = bf16[9,2,32,128]{3,2,1,0:T(8,128)(2,1)} collective-permute-done((bf16[9,2,32,128]{3,2,1,0:T(8,128)(2,1)}, bf16[9,2,32,128]{3,2,1,0:T(8,128)(2,1)}, u32[]{:S(2)}, u32[]{:S(2)}) %collective-permute-start.14) | collective-permute-done | bytes 147488 | tf_op jit(solution)/shard_map/ppermute | solution.py:31
  85.4 6.8 %conditional.9 = (bf16[9,4,32,128]{3,2,1,0:T(8,128)(2,1)}) conditional(s32[]{:T(128)} %convert_element_type.68, bf16[9,4,32,128]{3,2,1,0:T(8,128)(2,1)} %get-tuple-element.180, (bf16[9,2,32,128]{3,2,1,0:T(8,128)(2,1)}, bf16[9,4,32,128]{3,2,1,0:T(8,128)(2,1)}, bf16[9,2,32,128]{3,2,1,0:T(8,128)(2,1)}, bf16[1152,384]{1,0:T(8,128)(2,1)}, ...), branch_computations={%region_6.7_spmd, %region_7.8_spmd} | conditional | bytes 8 | solution.py:272
  85.4 6.8 %two_blocks.5 = (bf16[9,4,32,128]{3,2,1,0:T(8,128)(2,1)}, bf16[9,2,32,128]{3,2,1,0:T(8,128)(2,1)}, bf16[9,2,32,128]{3,2,1,0:T(8,128)(2,1)}) custom-call(bf16[9,2,32,128]{3,2,1,0:T(8,128)(2,1)} %get-tuple-element.124.low_ref, bf16[9,4,32,128]{3,2,1,0:T(8,128)(2,1)} %get-tuple-element.125.own_ref, bf16[9,2,32,128]{3,2,1,0:T(8,128)(2,1)} %get-tuple-element.126.high_ref, ...), custom_call_target="tpu_custom_call" | custom-call | tf_op jit(solution)/shard_map/cond/branch_1_fun/two_blocks/pallas_call | solution.py:127
  92.2 0.7 collective-permute-start.16
  92.9 0.9 fusion.12
  93.9 0.7 collective-permute-start.15
  94.5 1.3 collective-permute-start.17
  95.8 1.0 broadcast_select_fusion.g_ref
  96.9 1.6 %kernel_taps.1 = bf16[9,128,384]{2,1,0:T(8,128)(2,1)S(1)} custom-call(bf16[9,128,1152]{2,1,0:T(8,128)(2,1)S(1)} %tap_rows.1.ut_ref, bf16[9,4,32,128]{3,2,1,0:T(8,128)(2,1)S(1)} %broadcast_select_fusion.g_ref), custom_call_target="tpu_custom_call" | custom-call | tf_op jit(solution)/shard_map/kernel_taps/pallas_call | solution.py:185
  98.5 0.1 constant_dynamic-slice_fusion.5
  98.5 0.1 collective-permute-start.21
  98.7 1.7 %collective-permute-done.21 = bf16[9,64,384]{2,1,0:T(8,128)(2,1)S(1)} collective-permute-done((bf16[9,64,384]{2,1,0:T(8,128)(2,1)S(1)}, bf16[9,64,384]{2,1,0:T(8,128)(2,1)S(1)}, u32[]{:S(2)}, u32[]{:S(2)}) %collective-permute-start.21) | collective-permute-done | bytes 442400 | tf_op jit(solution)/shard_map/ppermute | solution.py:313
  100.4 0.1 add_convert_fusion
  100.6 0.9 collective-permute-start.22
  101.4 8.2 %collective-permute-done.22 = bf16[9,32,384]{2,1,0:T(8,128)(2,1)S(1)} collective-permute-done((bf16[9,32,384]{2,1,0:T(8,128)(2,1)S(1)}, bf16[9,32,384]{2,1,0:T(8,128)(2,1)S(1)}, u32[]{:S(2)}, u32[]{:S(2)}) %collective-permute-start.22) | collective-permute-done | bytes 221216 | tf_op jit(solution)/shard_map/ppermute | solution.py:313
  109.6 0.1 add_convert_fusion.1
  109.7 1.8 %collective-permute-start.23 = (bf16[9,16,384]{2,1,0:T(8,128)(2,1)S(1)}, bf16[9,16,384]{2,1,0:T(8,128)(2,1)S(1)}, u32[]{:S(2)}, u32[]{:S(2)}) collective-permute-start(bf16[9,16,384]{2,1,0:T(8,128)(2,1)S(1)} %constant_dynamic-slice_fusion.3), channel_id=1, source_target_pairs={{0,4},{1,5},{2,6},{3,7},{4,0},{5,1},{6,2},{7,3},{8,12},{9,13},{10,... | collective-permute-start | bytes 331784 | tf_op jit(solution)/shard_map/ppermute | solution.py:313
  111.6 1.3 collective-permute-start.19
  112.9 1.7 %collective-permute-done.23 = bf16[9,16,384]{2,1,0:T(8,128)(2,1)S(1)} collective-permute-done((bf16[9,16,384]{2,1,0:T(8,128)(2,1)S(1)}, bf16[9,16,384]{2,1,0:T(8,128)(2,1)S(1)}, u32[]{:S(2)}, u32[]{:S(2)}) %collective-permute-start.23) | collective-permute-done | bytes 110624 | tf_op jit(solution)/shard_map/ppermute | solution.py:313
  114.6 5.9 %collective-permute-start.24 = (bf16[9,8,384]{2,1,0:T(8,128)(2,1)S(1)}, bf16[9,8,384]{2,1,0:T(8,128)(2,1)S(1)}, u32[]{:S(2)}, u32[]{:S(2)}) collective-permute-start(bf16[9,8,384]{2,1,0:T(8,128)(2,1)S(1)} %constant_dynamic-slice_fusion.2), channel_id=1, source_target_pairs={{0,8},{1,9},{2,10},{3,11},{4,12},{5,13},{6,14},{7,15},{8,0},{9,1},... | collective-permute-start | bytes 165896 | tf_op jit(solution)/shard_map/ppermute | solution.py:313
  120.5 0.9 fusion.11
  121.5 1.3 collective-permute-start.18
  122.8 0.7 collective-permute-start.20
  123.5 0.1 collective-permute-start.25
  123.6 0.1 collective-permute-start.26
  123.7 1.3 collective-permute-done.18
  125.0 3.3 %collective-permute-done.25 = bf16[9,4,384]{2,1,0:T(4,128)(2,1)S(1)} collective-permute-done((bf16[9,4,384]{2,1,0:T(4,128)(2,1)S(1)}, bf16[9,4,384]{2,1,0:T(4,128)(2,1)S(1)}, u32[]{:S(2)}, u32[]{:S(2)}) %collective-permute-start.25) | collective-permute-done | bytes 27680 | tf_op jit(solution)/shard_map/ppermute | solution.py:31
  128.4 5.0 %collective-permute-done.26 = bf16[9,4,384]{2,1,0:T(4,128)(2,1)S(1)} collective-permute-done((bf16[9,4,384]{2,1,0:T(4,128)(2,1)S(1)}, bf16[9,4,384]{2,1,0:T(4,128)(2,1)S(1)}, u32[]{:S(2)}, u32[]{:S(2)}) %collective-permute-start.26) | collective-permute-done | bytes 27680 | tf_op jit(solution)/shard_map/ppermute | solution.py:313
  133.3 0.6 copy.10
  (43 shorter events, 0.3 us)
Async XLA Ops:
  3.1 1.6 %copy-start.6 = (bf16[9,4,32,128]{3,2,1,0:T(8,128)(2,1)S(1)}, bf16[9,4,32,128]{3,2,1,0:T(8,128)(2,1)}, u32[]{:S(2)}) copy-start(bf16[9,4,32,128]{3,2,1,0:T(8,128)(2,1)} %param.18) | copy-start | bytes 884740
  3.1 1.6 %copy-start.7 = (bf16[1,9,4,32,128]{4,3,2,1,0:T(8,128)(2,1)S(1)}, bf16[1,9,4,32,128]{4,3,2,1,0:T(8,128)(2,1)}, u32[]{:S(2)}) copy-start(bf16[1,9,4,32,128]{4,3,2,1,0:T(8,128)(2,1)} %param.16) | copy-start | bytes 884740
  3.3 29.4 %copy-start.1 = (bf16[144,8,3,128]{3,1,2,0:T(8,128)(2,1)}, bf16[144,8,3,128]{3,1,2,0:T(8,128)(2,1)S(1)}, u32[]{:S(2)}) copy-start(bf16[144,8,3,128]{3,1,2,0:T(8,128)(2,1)S(1)} %copy.13) | copy-start | bytes 2654212
  3.4 16.5 %collective-permute-start.5 = (bf16[576,384]{1,0:T(8,128)(2,1)S(1)}, bf16[576,384]{1,0:T(8,128)(2,1)}, u32[]{:S(2)}, u32[]{:S(2)}) collective-permute-start(bf16[576,384]{1,0:T(8,128)(2,1)S(1)} %constant_dynamic-slice_fusion.6), channel_id=1, source_target_pairs={{64,32},{65,33},{66,34},{67,35},{68,36},{69,37},{70,38},{71,39},{7... | collective-permute-start | bytes 1327112 | tf_op jit(solution)/shard_map/ppermute | solution.py:31
  4.7 3.3 %collective-permute-start = (bf16[18,1,32,128]{3,2,1,0:T(8,128)(2,1)S(1)}, bf16[18,1,32,128]{3,2,1,0:T(8,128)(2,1)S(1)}, u32[]{:S(2)}, u32[]{:S(2)}) collective-permute-start(bf16[18,1,32,128]{3,2,1,0:T(8,128)(2,1)S(1)} %get-tuple-element.190), channel_id=1, source_target_pairs={{0,1},{1,2},{2,3},{3,4},{4,5},{5,6},{6,7},{7,8},{8,9},{9,10},{10,1... | collective-permute-start | bytes 442376 | tf_op jit(solution)/shard_map/ppermute | solution.py:31
  6.5 5.3 %collective-permute-start.1 = (bf16[18,1,32,128]{3,2,1,0:T(8,128)(2,1)S(1)}, bf16[18,1,32,128]{3,2,1,0:T(8,128)(2,1)S(1)}, u32[]{:S(2)}, u32[]{:S(2)}) collective-permute-start(bf16[18,1,32,128]{3,2,1,0:T(8,128)(2,1)S(1)} %get-tuple-element.191), channel_id=1, source_target_pairs={{1,0},{2,1},{3,2},{4,3},{5,4},{6,5},{7,6},{8,7},{9,8},{10,9},{11,1... | collective-permute-start | bytes 442376 | tf_op jit(solution)/shard_map/ppermute | solution.py:31
  8.0 24.8 %copy-start.3 = (f32[9,4,32,128]{3,2,1,0:T(8,128)}, f32[9,4,32,128]{3,2,1,0:T(8,128)S(1)}, u32[]{:S(2)}) copy-start(f32[9,4,32,128]{3,2,1,0:T(8,128)S(1)} %fusion.10) | copy-start | bytes 1769476
  14.8 12.6 %collective-permute-start.7 = (bf16[9,6,32,128]{3,2,1,0:T(8,128)(2,1)}, bf16[9,6,32,128]{3,2,1,0:T(8,128)(2,1)S(1)}, u32[]{:S(2)}, u32[]{:S(2)}) collective-permute-start(bf16[9,6,32,128]{3,2,1,0:T(8,128)(2,1)} %pad_maximum_fusion), channel_id=1, source_target_pairs={{64,32},{65,33},{66,34},{67,35},{68,36},{69,37},{70,38},{71,39},{7... | collective-permute-start | bytes 1327112 | tf_op jit(solution)/shard_map/ppermute | solution.py:31
  19.8 7.9 %collective-permute-start.6 = (bf16[576,384]{1,0:T(8,128)(2,1)}, bf16[576,384]{1,0:T(8,128)(2,1)}, u32[]{:S(2)}, u32[]{:S(2)}) collective-permute-start(bf16[576,384]{1,0:T(8,128)(2,1)} %collective-permute-done.5), channel_id=1, source_target_pairs={{32,33},{33,32},{34,35},{35,34},{36,37},{37,36},{38,39},{39,38},{4... | collective-permute-start | bytes 1327112 | tf_op jit(solution)/shard_map/ppermute | solution.py:251
  23.6 7.0 %collective-permute-start.3 = (bf16[9,4,32,128]{3,2,1,0:T(8,128)(2,1)}, bf16[9,4,32,128]{3,2,1,0:T(8,128)(2,1)S(1)}, u32[]{:S(2)}, u32[]{:S(2)}) collective-permute-start(bf16[9,4,32,128]{3,2,1,0:T(8,128)(2,1)} %get-tuple-element.171), channel_id=1, source_target_pairs={{224,160},{225,161},{226,162},{227,163},{228,164},{229,165},{230,1... | collective-permute-start | bytes 884744 | tf_op jit(solution)/shard_map/ppermute | solution.py:31
  24.3 6.3 %collective-permute-start.2 = (bf16[9,2,32,128]{3,2,1,0:T(8,128)(2,1)}, bf16[9,2,32,128]{3,2,1,0:T(8,128)(2,1)}, u32[]{:S(2)}, u32[]{:S(2)}) collective-permute-start(bf16[9,2,32,128]{3,2,1,0:T(8,128)(2,1)} %get-tuple-element.173), channel_id=1, source_target_pairs={{224,161},{225,162},{226,163},{227,164},{228,165},{229,166},{230,1... | collective-permute-start | bytes 442376 | tf_op jit(solution)/shard_map/ppermute | solution.py:31
  25.6 5.0 %collective-permute-start.4 = (bf16[9,2,32,128]{3,2,1,0:T(8,128)(2,1)}, bf16[9,2,32,128]{3,2,1,0:T(8,128)(2,1)}, u32[]{:S(2)}, u32[]{:S(2)}) collective-permute-start(bf16[9,2,32,128]{3,2,1,0:T(8,128)(2,1)} %get-tuple-element.172), channel_id=1, source_target_pairs={{225,160},{226,161},{227,162},{228,163},{229,164},{230,165},{231,1... | collective-permute-start | bytes 442376 | tf_op jit(solution)/shard_map/ppermute | solution.py:31
  27.7 5.0 %copy-start.5 = (f32[9,6,32,128]{3,2,1,0:T(8,128)}, f32[9,6,32,128]{3,2,1,0:T(8,128)S(1)}, u32[]{:S(2)}) copy-start(f32[9,6,32,128]{3,2,1,0:T(8,128)S(1)} %fusion.5) | copy-start | bytes 2654212
  30.6 2.1 %collective-permute-start.9 = (bf16[9,4,32,128]{3,2,1,0:T(8,128)(2,1)}, bf16[9,4,32,128]{3,2,1,0:T(8,128)(2,1)S(1)}, u32[]{:S(2)}, u32[]{:S(2)}) collective-permute-start(bf16[9,4,32,128]{3,2,1,0:T(8,128)(2,1)} %get-tuple-element.175), channel_id=1, source_target_pairs={{160,96},{161,97},{162,98},{163,99},{164,100},{165,101},{166,102},... | collective-permute-start | bytes 884744 | tf_op jit(solution)/shard_map/ppermute | solution.py:31
  31.3 1.4 %collective-permute-start.10 = (bf16[9,2,32,128]{3,2,1,0:T(8,128)(2,1)}, bf16[9,2,32,128]{3,2,1,0:T(8,128)(2,1)S(1)}, u32[]{:S(2)}, u32[]{:S(2)}) collective-permute-start(bf16[9,2,32,128]{3,2,1,0:T(8,128)(2,1)} %get-tuple-element.176), channel_id=1, source_target_pairs={{161,96},{162,97},{163,98},{164,99},{165,100},{166,101},{167,102},... | collective-permute-start | bytes 442376 | tf_op jit(solution)/shard_map/ppermute | solution.py:31
  32.0 0.7 collective-permute-start.8
  32.8 8.6 %copy-start = (bf16[128,128]{1,0:T(8,128)(2,1)S(1)}, bf16[128,128]{1,0:T(8,128)(2,1)}, u32[]{:S(2)}) copy-start(bf16[128,128]{1,0:T(8,128)(2,1)} %constant.125.clone.order_ref) | copy-start | bytes 98308
  32.8 8.6 %collective-permute-start.11 = (bf16[9,6,32,128]{3,2,1,0:T(8,128)(2,1)}, bf16[9,6,32,128]{3,2,1,0:T(8,128)(2,1)S(1)}, u32[]{:S(2)}, u32[]{:S(2)}) collective-permute-start(bf16[9,6,32,128]{3,2,1,0:T(8,128)(2,1)} %pad_maximum_fusion), channel_id=1, source_target_pairs={{0,32},{1,33},{2,34},{3,35},{4,36},{5,37},{6,38},{7,39},{8,40},{9,... | collective-permute-start | bytes 1327112 | tf_op jit(solution)/shard_map/ppermute | solution.py:31
  32.9 52.5 %collective-permute-start.13 = (bf16[9,4,32,128]{3,2,1,0:T(8,128)(2,1)}, bf16[9,4,32,128]{3,2,1,0:T(8,128)(2,1)}, u32[]{:S(2)}, u32[]{:S(2)}) collective-permute-start(bf16[9,4,32,128]{3,2,1,0:T(8,128)(2,1)} %get-tuple-element.180), channel_id=1, source_target_pairs={{96,32},{97,33},{98,34},{99,35},{100,36},{101,37},{102,38},{103,39... | collective-permute-start | bytes 884744 | tf_op jit(solution)/shard_map/ppermute | solution.py:31
  34.2 8.3 %collective-permute-start.12 = (bf16[9,2,32,128]{3,2,1,0:T(8,128)(2,1)}, bf16[9,2,32,128]{3,2,1,0:T(8,128)(2,1)}, u32[]{:S(2)}, u32[]{:S(2)}) collective-permute-start(bf16[9,2,32,128]{3,2,1,0:T(8,128)(2,1)} %get-tuple-element.182), channel_id=1, source_target_pairs={{96,33},{97,34},{98,35},{99,36},{100,37},{101,38},{102,39},{103,40... | collective-permute-start | bytes 442376 | tf_op jit(solution)/shard_map/ppermute | solution.py:31
  35.5 49.9 %collective-permute-start.14 = (bf16[9,2,32,128]{3,2,1,0:T(8,128)(2,1)}, bf16[9,2,32,128]{3,2,1,0:T(8,128)(2,1)}, u32[]{:S(2)}, u32[]{:S(2)}) collective-permute-start(bf16[9,2,32,128]{3,2,1,0:T(8,128)(2,1)} %get-tuple-element.183), channel_id=1, source_target_pairs={{97,32},{98,33},{99,34},{100,35},{101,36},{102,37},{103,38},{104,3... | collective-permute-start | bytes 442376 | tf_op jit(solution)/shard_map/ppermute | solution.py:31
  92.2 3.6 %collective-permute-start.16 = (bf16[9,4,32,128]{3,2,1,0:T(8,128)(2,1)}, bf16[9,4,32,128]{3,2,1,0:T(8,128)(2,1)S(1)}, u32[]{:S(2)}, u32[]{:S(2)}) collective-permute-start(bf16[9,4,32,128]{3,2,1,0:T(8,128)(2,1)} %get-tuple-element.221), channel_id=1, source_target_pairs={{224,192},{225,193},{226,194},{227,195},{228,196},{229,197},{230,1... | collective-permute-start | bytes 884744 | tf_op jit(solution)/shard_map/ppermute | solution.py:31
  93.9 2.0 %collective-permute-start.15 = (bf16[9,1,32,128]{3,2,1,0:T(8,128)(2,1)S(1)}, bf16[9,1,32,128]{3,2,1,0:T(8,128)(2,1)S(1)}, u32[]{:S(2)}, u32[]{:S(2)}) collective-permute-start(bf16[9,1,32,128]{3,2,1,0:T(8,128)(2,1)S(1)} %get-tuple-element.195), channel_id=1, source_target_pairs={{224,193},{225,194},{226,195},{227,196},{228,197},{229,198},{230,1... | collective-permute-start | bytes 221192 | tf_op jit(solution)/shard_map/ppermute | solution.py:31
  94.5 1.3 collective-permute-start.17
  98.5 1.9 %collective-permute-start.21 = (bf16[9,64,384]{2,1,0:T(8,128)(2,1)S(1)}, bf16[9,64,384]{2,1,0:T(8,128)(2,1)S(1)}, u32[]{:S(2)}, u32[]{:S(2)}) collective-permute-start(bf16[9,64,384]{2,1,0:T(8,128)(2,1)S(1)} %constant_dynamic-slice_fusion.5), channel_id=1, source_target_pairs={{0,1},{1,0},{2,3},{3,2},{4,5},{5,4},{6,7},{7,6},{8,9},{9,8},{10,11... | collective-permute-start | bytes 1327112 | tf_op jit(solution)/shard_map/ppermute | solution.py:313
  98.7 26.3 %copy-start.2 = (bf16[144,8,3,128]{3,1,2,0:T(8,128)(2,1)S(1)}, bf16[144,8,3,128]{3,1,2,0:T(8,128)(2,1)}, u32[]{:S(2)}) copy-start(bf16[144,8,3,128]{3,1,2,0:T(8,128)(2,1)} %copy-done.1) | copy-start | bytes 2654212
  98.7 26.3 %copy-start.4 = (f32[9,4,32,128]{3,2,1,0:T(8,128)S(1)}, f32[9,4,32,128]{3,2,1,0:T(8,128)}, u32[]{:S(2)}) copy-start(f32[9,4,32,128]{3,2,1,0:T(8,128)} %copy-done.3) | copy-start | bytes 1769476
  100.6 9.1 %collective-permute-start.22 = (bf16[9,32,384]{2,1,0:T(8,128)(2,1)S(1)}, bf16[9,32,384]{2,1,0:T(8,128)(2,1)S(1)}, u32[]{:S(2)}, u32[]{:S(2)}) collective-permute-start(bf16[9,32,384]{2,1,0:T(8,128)(2,1)S(1)} %constant_dynamic-slice_fusion.4), channel_id=1, source_target_pairs={{0,2},{1,3},{2,0},{3,1},{4,6},{5,7},{6,4},{7,5},{8,10},{9,11},{10,... | collective-permute-start | bytes 663560 | tf_op jit(solution)/shard_map/ppermute | solution.py:313
  109.7 4.8 %collective-permute-start.23 = (bf16[9,16,384]{2,1,0:T(8,128)(2,1)S(1)}, bf16[9,16,384]{2,1,0:T(8,128)(2,1)S(1)}, u32[]{:S(2)}, u32[]{:S(2)}) collective-permute-start(bf16[9,16,384]{2,1,0:T(8,128)(2,1)S(1)} %constant_dynamic-slice_fusion.3), channel_id=1, source_target_pairs={{0,4},{1,5},{2,6},{3,7},{4,0},{5,1},{6,2},{7,3},{8,12},{9,13},{10,... | collective-permute-start | bytes 331784 | tf_op jit(solution)/shard_map/ppermute | solution.py:313
  111.6 13.4 %collective-permute-start.19 = (bf16[9,4,32,128]{3,2,1,0:T(8,128)(2,1)}, bf16[9,4,32,128]{3,2,1,0:T(8,128)(2,1)S(1)}, u32[]{:S(2)}, u32[]{:S(2)}) collective-permute-start(bf16[9,4,32,128]{3,2,1,0:T(8,128)(2,1)} %get-tuple-element.222), channel_id=1, source_target_pairs={{32,0},{33,1},{34,2},{35,3},{36,4},{37,5},{38,6},{39,7},{40,8},{41... | collective-permute-start | bytes 884744 | tf_op jit(solution)/shard_map/ppermute | solution.py:31
  114.6 8.8 %collective-permute-start.24 = (bf16[9,8,384]{2,1,0:T(8,128)(2,1)S(1)}, bf16[9,8,384]{2,1,0:T(8,128)(2,1)S(1)}, u32[]{:S(2)}, u32[]{:S(2)}) collective-permute-start(bf16[9,8,384]{2,1,0:T(8,128)(2,1)S(1)} %constant_dynamic-slice_fusion.2), channel_id=1, source_target_pairs={{0,8},{1,9},{2,10},{3,11},{4,12},{5,13},{6,14},{7,15},{8,0},{9,1},... | collective-permute-start | bytes 165896 | tf_op jit(solution)/shard_map/ppermute | solution.py:313
  121.5 3.5 %collective-permute-start.18 = (bf16[9,1,32,128]{3,2,1,0:T(8,128)(2,1)S(1)}, bf16[9,1,32,128]{3,2,1,0:T(8,128)(2,1)S(1)}, u32[]{:S(2)}, u32[]{:S(2)}) collective-permute-start(bf16[9,1,32,128]{3,2,1,0:T(8,128)(2,1)S(1)} %get-tuple-element.193), channel_id=1, source_target_pairs={{32,1},{33,2},{34,3},{35,4},{36,5},{37,6},{38,7},{39,8},{40,9},{41... | collective-permute-start | bytes 221192 | tf_op jit(solution)/shard_map/ppermute | solution.py:31
  122.8 2.2 %collective-permute-start.20 = (bf16[9,1,32,128]{3,2,1,0:T(8,128)(2,1)S(1)}, bf16[9,1,32,128]{3,2,1,0:T(8,128)(2,1)S(1)}, u32[]{:S(2)}, u32[]{:S(2)}) collective-permute-start(bf16[9,1,32,128]{3,2,1,0:T(8,128)(2,1)S(1)} %get-tuple-element.192), channel_id=1, source_target_pairs={{33,0},{34,1},{35,2},{36,3},{37,4},{38,5},{39,6},{40,7},{41,8},{42... | collective-permute-start | bytes 221192 | tf_op jit(solution)/shard_map/ppermute | solution.py:31
  123.5 4.8 %collective-permute-start.25 = (bf16[9,4,384]{2,1,0:T(4,128)(2,1)S(1)}, bf16[9,4,384]{2,1,0:T(4,128)(2,1)S(1)}, u32[]{:S(2)}, u32[]{:S(2)}) collective-permute-start(bf16[9,4,384]{2,1,0:T(4,128)(2,1)S(1)} %get-tuple-element.196), channel_id=1, source_target_pairs={{32,0},{33,1},{34,2},{35,3},{36,4},{37,5},{38,6},{39,7},{40,8},{41... | collective-permute-start | bytes 82952 | tf_op jit(solution)/shard_map/ppermute | solution.py:31
  123.6 9.7 %collective-permute-start.26 = (bf16[9,4,384]{2,1,0:T(4,128)(2,1)S(1)}, bf16[9,4,384]{2,1,0:T(4,128)(2,1)S(1)}, u32[]{:S(2)}, u32[]{:S(2)}) collective-permute-start(bf16[9,4,384]{2,1,0:T(4,128)(2,1)S(1)} %get-tuple-element.197), channel_id=1, source_target_pairs={{32,16},{33,17},{34,18},{35,19},{36,20},{37,21},{38,22},{39,23},{4... | collective-permute-start | bytes 82952 | tf_op jit(solution)/shard_map/ppermute | solution.py:313

commit v3 on v2

--- a/solution.py
+++ b/solution.py
@@ -18,7 +18,7 @@
 COLS = 32
 CH = 128
 AXES = ("section", "dp")
-HALVING = (1, 2, 4, 8, 16)
+HALVING = (1, 4, 2, 8, 16)
 
 
 def permute(value, hops):
@@ -228,12 +228,13 @@
     barrier = lax.optimization_barrier
 
     both = jnp.concatenate([cotangent, acts[0]], axis=0)
-    edge_low = permute(both[:, -1:], [(s, s, 1) for s in every])
-    edge_high = permute(both[:, :1], [(s, s, -1) for s in every])
+    kern, last_row, first_row = barrier((kernels[0], both[:, -1:], both[:, :1]))
+    edge_low = permute(last_row, [(s, s, 1) for s in every])
+    edge_high = permute(first_row, [(s, s, -1) for s in every])
     low0, high0 = edge_low[:FRAMES], edge_high[:FRAMES]
     act6 = jnp.concatenate([edge_low[FRAMES:], acts[0], edge_high[FRAMES:]], axis=1)
 
-    w = as_matrix(kernels[0])
+    w = as_matrix(kern)
     half = w.shape[0] // 2
     w_half = permute(
         lax.dynamic_slice_in_dim(w, core * half, half, 0), [(s + 1, s, 0) for s in pair]
@@ -248,17 +249,6 @@
 
     act6, state = barrier((act6, state))
     act_next = permute(act6, [(s + 1, s, 0) for s in pair])
-    w_other = lax.ppermute(
-        w_half, AXES, [(s * DP + d, s * DP + (d ^ 1)) for s in pair for d in range(DP)]
-    )
-    w_next = jnp.where(
-        core == 0,
-        jnp.concatenate([w_half, w_other], axis=0),
-        jnp.concatenate([w_other, w_half], axis=0),
-    )
-    row = lax.broadcasted_iota(jnp.int32, act_next.shape, 1) + dp * ROWS - 1
-    inside = (row >= 0) & (row < DP * ROWS)
-    slope_next = jnp.where(inside, slope_of(act_next), 0.0)
 
     def hop(state, target):
         result, top, bottom = state
@@ -266,6 +256,20 @@
         low = permute(bottom, [(target + 2, target, 1)])
         high = permute(top, [(target + 2, target, -1)])
         return low, own, high
+
+    low, own, high = hop(state, 5)
+    w_half, low = barrier((w_half, low))
+    w_other = lax.ppermute(
+        w_half, AXES, [(s * DP + d, s * DP + (d ^ 1)) for s in pair for d in range(DP)]
+    )
+    w_next = jnp.where(
+        core == 0,
+        jnp.concatenate([w_half, w_other], axis=0),
+        jnp.concatenate([w_other, w_half], axis=0),
+    )
+    row = lax.broadcasted_iota(jnp.int32, act_next.shape, 1) + dp * ROWS - 1
+    inside = (row >= 0) & (row < DP * ROWS)
+    slope_next = jnp.where(inside, slope_of(act_next), 0.0)
 
     def stage(state, arrived, section):
         low, own, high = arrived
@@ -275,7 +279,7 @@
             lambda: state,
         )
 
-    state = stage(state, hop(state, 5), 5)
+    state = stage(state, (low, own, high), 5)
     state = stage(state, hop(state, 3), 3)
     act6, state = barrier((act6, state))
     arrived = hop(state, 1)
@@ -296,28 +300,37 @@
             lambda: result,
         )
 
+    grad = jnp.where(me == 0, cotangent, result)
+    first = (me % 2 == 1) | (me == 0)
+    part = lax.cond(
+        first,
+        lambda: taps(ut, grad, scale),
+        lambda: jnp.zeros((9, CH, 3 * CH), BF),
+    )
+    result, part = barrier((result, part))
     result = even(result, (6, 4, 2))
     final = even(result, (0,))
-
-    grad = jnp.where(me == 0, cotangent, result)
-    part = taps(ut, grad, scale)
-    for bit in HALVING:
+    part = lax.cond(first, lambda: part, lambda: taps(ut, result, scale))
+    for bit in HALVING[:3]:
         size = part.shape[1] // 2
         mine = (dp // bit) % 2
         keep = lax.dynamic_slice_in_dim(part, mine * size, size, 1)
         give = lax.dynamic_slice_in_dim(part, (1 - mine) * size, size, 1)
-        shift = 0
-        if bit == HALVING[-1]:
-            keep = permute(keep, [((s + 1) % SEC, s, 0) for s in every])
-            shift = 1
         got = lax.ppermute(
-            give,
-            AXES,
-            [((s + shift) % SEC * DP + d, s * DP + (d ^ bit)) for s in every for d in range(DP)],
+            give, AXES, [(s * DP + d, s * DP + (d ^ bit)) for s in every for d in range(DP)]
         )
-        part = keep.astype(F32) + got.astype(F32)
-        if not shift:
-            part = part.astype(BF)
+        part = (keep.astype(F32) + got.astype(F32)).astype(BF)
+    high_bit, low_bit = HALVING[3:]
+    total = 0.0
+    for a, b in ((1, 1), (0, 1), (1, 0), (0, 0)):
+        flip = a * high_bit + b * low_bit
+        slot = ((dp // high_bit + a) % 2) * 2 + (dp // low_bit + b) % 2
+        piece = lax.dynamic_slice_in_dim(part, slot * (CH // DP), CH // DP, 1)
+        pairs = [
+            ((s + 1) % SEC * DP + d, s * DP + (d ^ flip)) for s in every for d in range(DP)
+        ]
+        total = total + lax.ppermute(piece, AXES, pairs).astype(F32)
+    part = total
     share = CH // DP
     kernel_part = jnp.transpose(part.reshape(9, share, 3, CH), (1, 2, 0, 3)).reshape(share, 27, CH)
     return (final[None], kernel_part[None])

time: 136 us -> 147 us (1.081)
  the two profiles are of different devices: /device:TPU:8 before, /device:TPU:10 now
where the time goes in v3:
time: 147 us; the launch traced here: 146 us
  waiting for transfers between devices  70.5 us (48%)
  starting transfers between devices  48.5 us (33%)
  Pallas kernels  11.8 us (8%)
  local copies, waits for them, and re-layouts  9.12 us (6%)
  other arithmetic  5.25 us (4%)
    ppermute x20, waiting for transfers between devices, permute(): return lax.ppermute(value, AXES, pairs)  50.7 us
    ppermute x20, starting transfers between devices, permute(): return lax.ppermute(value, AXES, pairs)  21.6 us
    ppermute x4, starting transfers between devices, local(): total = total + lax.ppermute(piece, AXES, pairs).astype(F32)  14.4 us
    ppermute x3, waiting for transfers between devices, local(): lax.ppermute(give, AXES, [(s * DP + d, s * DP + (d ^ bit)) for s in every...  10.7 us
    ppermute x4, waiting for transfers between devices, local(): total = total + lax.ppermute(piece, AXES, pairs).astype(F32)  9.01 us
    ppermute x3, starting transfers between devices, local(): lax.ppermute(give, AXES, [(s * DP + d, s * DP + (d ^ bit)) for s in every...  6.51 us
    ppermute x1, starting transfers between devices, local(): lax.ppermute(w_half, AXES, [(s * DP + d, s * DP + (d ^ 1)) for s in pair...  6.03 us
    pallas_call x1, Pallas kernels, double(): pl.pallas_call(double_kernel, out_shape=gradient_shapes(), in_specs=in_vm...  5.89 us
  transfers between devices with their start and end apart: 28, of which 10 were waited for; matrix products, arithmetic and copies ran while one was open for 4% of the time, Pallas kernels for 2%

profile of v3, /device:TPU:10, one launch (start us, length us, event | category | flops | bytes accessed | tf_op | source)
XLA Modules:
  0.0 146.5 jit_solution(8084529520406809701)
XLA Ops:
  0.6 1.7 %pad_maximum_fusion.1 = (bf16[18,1,32,128]{3,2,1,0:T(8,128)(2,1)}, bf16[18,1,32,128]{3,2,1,0:T(8,128)(2,1)}) fusion(bf16[9,4,32,128]{3,2,1,0:T(8,128)(2,1)} %bitcast.23, bf16[9,4,32,128]{3,2,1,0:T(8,128)(2,1)} %param.22), kind=kLoop, calls=%fused_computation.22 | loop fusion | flops 147456 | bytes 884736 | tf_op jit(solution)/shard_map/concatenate | solution.py:230
  2.4 2.4 %copy.9 = bf16[3,3,128,3,128]{4,3,2,1,0:T(4,128)(2,1)S(1)} copy(bf16[3,3,128,3,128]{2,4,1,0,3:T(8,128)(2,1)} %bitcast.25) | data formatting | bytes 1769472 | tf_op jit(solution)/shard_map/transpose | solution.py:217
  4.8 0.0 copy-start.4
  4.9 0.1 copy.13
  5.0 0.1 constant_dynamic-slice_fusion.7
  5.1 1.3 collective-permute-start.2
  6.4 1.7 %collective-permute-start = (bf16[18,1,32,128]{3,2,1,0:T(8,128)(2,1)}, bf16[18,1,32,128]{3,2,1,0:T(8,128)(2,1)S(1)}, u32[]{:S(2)}, u32[]{:S(2)}) collective-permute-start(bf16[18,1,32,128]{3,2,1,0:T(8,128)(2,1)} %get-tuple-element.201), channel_id=1, source_target_pairs={{0,1},{1,2},{2,3},{3,4},{4,5},{5,6},{6,7},{7,8},{8,9},{9,10},{10,1... | collective-permute-start | bytes 442376 | tf_op jit(solution)/shard_map/ppermute | solution.py:31
  8.1 1.3 collective-permute-start.1
  9.4 0.2 fusion.10
  9.7 4.0 %collective-permute-done.1 = bf16[18,1,32,128]{3,2,1,0:T(8,128)(2,1)S(1)} collective-permute-done((bf16[18,1,32,128]{3,2,1,0:T(8,128)(2,1)}, bf16[18,1,32,128]{3,2,1,0:T(8,128)(2,1)S(1)}, u32[]{:S(2)}, u32[]{:S(2)}) %collective-permute-start.1) | collective-permute-done | bytes 147488 | tf_op jit(solution)/shard_map/ppermute | solution.py:31
  13.7 2.1 %conditional.8 = ((bf16[9,4,32,128]{3,2,1,0:T(8,128)(2,1)}, bf16[9,2,32,128]{3,2,1,0:T(8,128)(2,1)}, bf16[9,2,32,128]{3,2,1,0:T(8,128)(2,1)})) conditional(s32[]{:T(128)} %convert_element_type.70, bf16[9,4,32,128]{3,2,1,0:T(8,128)(2,1)S(1)} %copy-done.2, (bf16[18,1,32,128]{3,2,1,0:T(8,128)(2,1)S(1)}, bf16[18,1,32,128]{3,2,1,0:T(8,128)(2,1)S(1)}, ...), branch_computations={%region_0.1_spmd, %region_1.2_spmd} | conditional | bytes 884772 | solution.py:244
  13.7 0.7 copy.14
  14.4 0.7 broadcast_in_dim.13
  15.1 0.7 broadcast_in_dim.13.clone
  15.8 0.1 pad_maximum_fusion
  15.9 1.3 collective-permute-start.7
  17.2 0.7 collective-permute-start.3
  17.9 2.0 %collective-permute-done.2 = bf16[576,384]{1,0:T(8,128)(2,1)S(1)} collective-permute-done((bf16[576,384]{1,0:T(8,128)(2,1)S(1)}, bf16[576,384]{1,0:T(8,128)(2,1)S(1)}, u32[]{:S(2)}, u32[]{:S(2)}) %collective-permute-start.2) | collective-permute-done | bytes 442400 | tf_op jit(solution)/shard_map/ppermute | solution.py:31
  19.9 6.0 %collective-permute-start.6 = (bf16[576,384]{1,0:T(8,128)(2,1)S(1)}, bf16[576,384]{1,0:T(8,128)(2,1)}, u32[]{:S(2)}, u32[]{:S(2)}) collective-permute-start(bf16[576,384]{1,0:T(8,128)(2,1)S(1)} %collective-permute-done.2), channel_id=1, source_target_pairs={{32,33},{33,32},{34,35},{35,34},{36,37},{37,36},{38,39},{39,38},{4... | collective-permute-start | bytes 1327112 | tf_op jit(solution)/shard_map/ppermute | solution.py:262
  25.9 1.4 collective-permute-start.4
  27.3 1.3 collective-permute-start.5
  28.6 0.3 fusion.5
  29.0 1.7 %maximum_select_fusion = bf16[1152,384]{1,0:T(8,128)(2,1)S(1)} fusion(bf16[576,384]{1,0:T(8,128)(2,1)} %collective-permute-done.6, bf16[576,384]{1,0:T(8,128)(2,1)} %copy-done.6, pred[]{:T(512)S(6)} %eq.54), kind=kLoop, calls=%fused_computation.10 | loop fusion | flops 3981312 | bytes 1769473 | tf_op jit(solution)/shard_map/jit(_where)/select_n | solution.py:265
  30.7 1.3 collective-permute-start.9
  32.0 1.3 collective-permute-start.10
  33.3 1.3 collective-permute-start.8
  34.7 33.4 %collective-permute-done.10 = bf16[9,2,32,128]{3,2,1,0:T(8,128)(2,1)} collective-permute-done((bf16[9,2,32,128]{3,2,1,0:T(8,128)(2,1)}, bf16[9,2,32,128]{3,2,1,0:T(8,128)(2,1)}, u32[]{:S(2)}, u32[]{:S(2)}) %collective-permute-start.10) | collective-permute-done | bytes 147488 | tf_op jit(solution)/shard_map/ppermute | solution.py:31
  68.1 0.7 copy-done.7
  68.8 5.9 %conditional.10 = ((bf16[9,4,32,128]{3,2,1,0:T(8,128)(2,1)}, bf16[9,2,32,128]{3,2,1,0:T(8,128)(2,1)}, bf16[9,2,32,128]{3,2,1,0:T(8,128)(2,1)})) conditional(s32[]{:T(128)} %convert_element_type.72, (bf16[9,4,32,128]{3,2,1,0:T(8,128)(2,1)}, bf16[9,2,32,128]{3,2,1,0:T(8,128)(2,1)}, bf16[9,2,32,128]{3,2,1,0:T(8,128)(2,1)}) %get-tuple-element.262, ...), branch_computations={%region_4.5_spmd, %region_5.6_spmd} | conditional | bytes 8 | solution.py:276
  68.8 5.9 %two_blocks.4 = (bf16[9,4,32,128]{3,2,1,0:T(8,128)(2,1)}, bf16[9,2,32,128]{3,2,1,0:T(8,128)(2,1)}, bf16[9,2,32,128]{3,2,1,0:T(8,128)(2,1)}) custom-call(bf16[9,2,32,128]{3,2,1,0:T(8,128)(2,1)} %get-tuple-element.138.low_ref, bf16[9,4,32,128]{3,2,1,0:T(8,128)(2,1)} %get-tuple-element.139.own_ref, bf16[9,2,32,128]{3,2,1,0:T(8,128)(2,1)} %get-tuple-element.140.high_ref, ...), custom_call_target="tpu_custom_call" | custom-call | tf_op jit(solution)/shard_map/cond/branch_1_fun/two_blocks/pallas_call | solution.py:127
  74.7 1.3 collective-permute-start.13
  76.0 1.3 collective-permute-start.12
  77.3 0.9 collective-permute-start.14
  78.2 6.9 %collective-permute-done.11.act_ref = bf16[9,6,32,128]{3,2,1,0:T(8,128)(2,1)S(1)} collective-permute-done((bf16[9,6,32,128]{3,2,1,0:T(8,128)(2,1)}, bf16[9,6,32,128]{3,2,1,0:T(8,128)(2,1)S(1)}, u32[]{:S(2)}, u32[]{:S(2)}) %collective-permute-start.11) | collective-permute-done | bytes 442400 | tf_op jit(solution)/shard_map/ppermute | solution.py:31
  85.1 2.6 %tap_rows.1 = bf16[9,128,1152]{2,1,0:T(8,128)(2,1)} custom-call(bf16[9,6,32,128]{3,2,1,0:T(8,128)(2,1)S(1)} %collective-permute-done.11.act_ref, bf16[128,128]{1,0:T(8,128)(2,1)S(1)} %copy-done), custom_call_target="tpu_custom_call" | custom-call | tf_op jit(solution)/shard_map/tap_rows/pallas_call | solution.py:160
  87.8 0.9 copy-done.3
  88.7 4.4 %conditional.12 = (bf16[9,128,384]{2,1,0:T(8,128)(2,1)S(1)}) conditional(s32[]{:T(128)} %convert_element_type.75, () %tuple.82, (pred[]{:T(512)}, bf16[9,4,32,128]{3,2,1,0:T(8,128)(2,1)S(1)}, bf16[9,4,32,128]{3,2,1,0:T(8,128)(2,1)}, bf16[9,128,1152]{2,1,0:T(8,128)(2,1)}) %tuple.131), branch_computations={%region_8.9_spmd, %region_9.10_spmd} | conditional | flops 147456 | bytes 884746 | solution.py:305
  88.7 1.0 broadcast_select_fusion.g_ref
  89.7 3.4 %kernel_taps.2 = bf16[9,128,384]{2,1,0:T(8,128)(2,1)S(1)} custom-call(bf16[9,128,1152]{2,1,0:T(8,128)(2,1)} %get-tuple-element.153.ut_ref, bf16[9,4,32,128]{3,2,1,0:T(8,128)(2,1)S(1)} %broadcast_select_fusion.g_ref), custom_call_target="tpu_custom_call" | custom-call | tf_op jit(solution)/shard_map/cond/branch_1_fun/kernel_taps/pallas_call | solution.py:185
  93.1 1.3 collective-permute-start.16
  94.4 0.9 fusion.12
  95.3 1.3 collective-permute-start.15
  96.6 0.7 collective-permute-start.17
  97.3 4.3 %collective-permute-done.15 = bf16[9,1,32,128]{3,2,1,0:T(8,128)(2,1)S(1)} collective-permute-done((bf16[9,1,32,128]{3,2,1,0:T(8,128)(2,1)S(1)}, bf16[9,1,32,128]{3,2,1,0:T(8,128)(2,1)S(1)}, u32[]{:S(2)}, u32[]{:S(2)}) %collective-permute-start.15) | collective-permute-done | bytes 73760 | tf_op jit(solution)/shard_map/ppermute | solution.py:31
  101.6 0.1 constant_dynamic-slice_fusion.6
  101.7 0.1 collective-permute-start.21
  101.8 1.7 %collective-permute-done.21 = bf16[9,64,384]{2,1,0:T(8,128)(2,1)S(1)} collective-permute-done((bf16[9,64,384]{2,1,0:T(8,128)(2,1)S(1)}, bf16[9,64,384]{2,1,0:T(8,128)(2,1)S(1)}, u32[]{:S(2)}, u32[]{:S(2)}) %collective-permute-start.21) | collective-permute-done | bytes 442400 | tf_op jit(solution)/shard_map/ppermute | solution.py:319
  103.6 0.1 add_convert_fusion
  103.7 6.3 %collective-permute-start.22 = (bf16[9,32,384]{2,1,0:T(8,128)(2,1)S(1)}, bf16[9,32,384]{2,1,0:T(8,128)(2,1)S(1)}, u32[]{:S(2)}, u32[]{:S(2)}) collective-permute-start(bf16[9,32,384]{2,1,0:T(8,128)(2,1)S(1)} %constant_dynamic-slice_fusion.5), channel_id=1, source_target_pairs={{0,4},{1,5},{2,6},{3,7},{4,0},{5,1},{6,2},{7,3},{8,12},{9,13},{10,... | collective-permute-start | bytes 663560 | tf_op jit(solution)/shard_map/ppermute | solution.py:319
  110.1 0.7 collective-permute-start.19
  110.7 5.1 %collective-permute-done.22 = bf16[9,32,384]{2,1,0:T(8,128)(2,1)S(1)} collective-permute-done((bf16[9,32,384]{2,1,0:T(8,128)(2,1)S(1)}, bf16[9,32,384]{2,1,0:T(8,128)(2,1)S(1)}, u32[]{:S(2)}, u32[]{:S(2)}) %collective-permute-start.22) | collective-permute-done | bytes 221216 | tf_op jit(solution)/shard_map/ppermute | solution.py:319
  115.8 0.1 add_convert_fusion.1
  115.9 0.1 collective-permute-start.23
  116.0 0.9 fusion.11
  116.9 0.7 collective-permute-start.18
  117.6 0.7 collective-permute-start.20
  118.3 4.0 %collective-permute-done.23 = bf16[9,16,384]{2,1,0:T(8,128)(2,1)S(1)} collective-permute-done((bf16[9,16,384]{2,1,0:T(8,128)(2,1)S(1)}, bf16[9,16,384]{2,1,0:T(8,128)(2,1)S(1)}, u32[]{:S(2)}, u32[]{:S(2)}) %collective-permute-start.23) | collective-permute-done | bytes 110624 | tf_op jit(solution)/shard_map/ppermute | solution.py:319
  122.3 0.1 constant_dynamic-slice_fusion.3
  122.4 13.9 %collective-permute-start.24 = (bf16[9,4,384]{2,1,0:T(4,128)(2,1)S(1)}, bf16[9,4,384]{2,1,0:T(4,128)(2,1)S(1)}, u32[]{:S(2)}, u32[]{:S(2)}) collective-permute-start(bf16[9,4,384]{2,1,0:T(4,128)(2,1)S(1)} %get-tuple-element.237), channel_id=1, source_target_pairs={{32,24},{33,25},{34,26},{35,27},{36,28},{37,29},{38,30},{39,31},{4... | collective-permute-start | bytes 82952 | tf_op jit(solution)/shard_map/ppermute | solution.py:332
  136.2 0.4 collective-permute-start.25
  136.7 0.1 collective-permute-start.27
  136.8 1.0 collective-permute-done.24
  137.8 8.0 %collective-permute-done.25 = bf16[9,4,384]{2,1,0:T(4,128)(2,1)S(1)} collective-permute-done((bf16[9,4,384]{2,1,0:T(4,128)(2,1)S(1)}, bf16[9,4,384]{2,1,0:T(4,128)(2,1)S(1)}, u32[]{:S(2)}, u32[]{:S(2)}) %collective-permute-start.25) | collective-permute-done | bytes 27680 | tf_op jit(solution)/shard_map/ppermute | solution.py:332
  145.8 0.6 copy.10
  (49 shorter events, 0.3 us)
Async XLA Ops:
  4.8 4.6 %copy-start.4 = (bf16[1,9,4,32,128]{4,3,2,1,0:T(8,128)(2,1)S(1)}, bf16[1,9,4,32,128]{4,3,2,1,0:T(8,128)(2,1)}, u32[]{:S(2)}) copy-start(bf16[1,9,4,32,128]{4,3,2,1,0:T(8,128)(2,1)} %param.20) | copy-start | bytes 884740
  4.8 8.8 %copy-start.2 = (bf16[9,4,32,128]{3,2,1,0:T(8,128)(2,1)S(1)}, bf16[9,4,32,128]{3,2,1,0:T(8,128)(2,1)}, u32[]{:S(2)}) copy-start(bf16[9,4,32,128]{3,2,1,0:T(8,128)(2,1)} %param.22) | copy-start | bytes 884740
  5.1 14.8 %collective-permute-start.2 = (bf16[576,384]{1,0:T(8,128)(2,1)S(1)}, bf16[576,384]{1,0:T(8,128)(2,1)S(1)}, u32[]{:S(2)}, u32[]{:S(2)}) collective-permute-start(bf16[576,384]{1,0:T(8,128)(2,1)S(1)} %constant_dynamic-slice_fusion.7), channel_id=1, source_target_pairs={{64,32},{65,33},{66,34},{67,35},{68,36},{69,37},{70,38},{71,39},{7... | collective-permute-start | bytes 1327112 | tf_op jit(solution)/shard_map/ppermute | solution.py:31
  6.4 3.3 %collective-permute-start = (bf16[18,1,32,128]{3,2,1,0:T(8,128)(2,1)}, bf16[18,1,32,128]{3,2,1,0:T(8,128)(2,1)S(1)}, u32[]{:S(2)}, u32[]{:S(2)}) collective-permute-start(bf16[18,1,32,128]{3,2,1,0:T(8,128)(2,1)} %get-tuple-element.201), channel_id=1, source_target_pairs={{0,1},{1,2},{2,3},{3,4},{4,5},{5,6},{6,7},{7,8},{8,9},{9,10},{10,1... | collective-permute-start | bytes 442376 | tf_op jit(solution)/shard_map/ppermute | solution.py:31
  8.1 5.5 %collective-permute-start.1 = (bf16[18,1,32,128]{3,2,1,0:T(8,128)(2,1)}, bf16[18,1,32,128]{3,2,1,0:T(8,128)(2,1)S(1)}, u32[]{:S(2)}, u32[]{:S(2)}) collective-permute-start(bf16[18,1,32,128]{3,2,1,0:T(8,128)(2,1)} %get-tuple-element.202), channel_id=1, source_target_pairs={{1,0},{2,1},{3,2},{4,3},{5,4},{6,5},{7,6},{8,7},{9,8},{10,9},{11,1... | collective-permute-start | bytes 442376 | tf_op jit(solution)/shard_map/ppermute | solution.py:31
  15.9 12.8 %copy-start.5 = (bf16[9,6,32,128]{3,2,1,0:T(8,128)(2,1)}, bf16[9,6,32,128]{3,2,1,0:T(8,128)(2,1)S(1)}, u32[]{:S(2)}) copy-start(bf16[9,6,32,128]{3,2,1,0:T(8,128)(2,1)S(1)} %pad_maximum_fusion) | copy-start | bytes 1327108
  15.9 12.8 %collective-permute-start.7 = (bf16[9,6,32,128]{3,2,1,0:T(8,128)(2,1)S(1)}, bf16[9,6,32,128]{3,2,1,0:T(8,128)(2,1)S(1)}, u32[]{:S(2)}, u32[]{:S(2)}) collective-permute-start(bf16[9,6,32,128]{3,2,1,0:T(8,128)(2,1)S(1)} %pad_maximum_fusion), channel_id=1, source_target_pairs={{64,32},{65,33},{66,34},{67,35},{68,36},{69,37},{70,38},{71,39},{7... | collective-permute-start | bytes 1327112 | tf_op jit(solution)/shard_map/ppermute | solution.py:31
  17.2 0.7 collective-permute-start.3
  17.9 2.0 %copy-start.8 = (bf16[9,2,32,128]{3,2,1,0:T(8,128)(2,1)}, bf16[9,2,32,128]{3,2,1,0:T(8,128)(2,1)S(1)}, u32[]{:S(2)}) copy-start(bf16[9,2,32,128]{3,2,1,0:T(8,128)(2,1)S(1)} %collective-permute-done.3) | copy-start | bytes 442372
  19.9 9.1 %copy-start.6 = (bf16[576,384]{1,0:T(8,128)(2,1)}, bf16[576,384]{1,0:T(8,128)(2,1)S(1)}, u32[]{:S(2)}) copy-start(bf16[576,384]{1,0:T(8,128)(2,1)S(1)} %collective-permute-done.2) | copy-start | bytes 1327108
  19.9 9.1 %collective-permute-start.6 = (bf16[576,384]{1,0:T(8,128)(2,1)S(1)}, bf16[576,384]{1,0:T(8,128)(2,1)}, u32[]{:S(2)}, u32[]{:S(2)}) collective-permute-start(bf16[576,384]{1,0:T(8,128)(2,1)S(1)} %collective-permute-done.2), channel_id=1, source_target_pairs={{32,33},{33,32},{34,35},{35,34},{36,37},{37,36},{38,39},{39,38},{4... | collective-permute-start | bytes 1327112 | tf_op jit(solution)/shard_map/ppermute | solution.py:262
  25.9 4.8 %collective-permute-start.4 = (bf16[9,4,32,128]{3,2,1,0:T(8,128)(2,1)}, bf16[9,4,32,128]{3,2,1,0:T(8,128)(2,1)}, u32[]{:S(2)}, u32[]{:S(2)}) collective-permute-start(bf16[9,4,32,128]{3,2,1,0:T(8,128)(2,1)} %get-tuple-element.208), channel_id=1, source_target_pairs={{224,160},{225,161},{226,162},{227,163},{228,164},{229,165},{230,1... | collective-permute-start | bytes 884744 | tf_op jit(solution)/shard_map/ppermute | solution.py:31
  27.3 3.4 %collective-permute-start.5 = (bf16[9,2,32,128]{3,2,1,0:T(8,128)(2,1)}, bf16[9,2,32,128]{3,2,1,0:T(8,128)(2,1)}, u32[]{:S(2)}, u32[]{:S(2)}) collective-permute-start(bf16[9,2,32,128]{3,2,1,0:T(8,128)(2,1)} %get-tuple-element.209), channel_id=1, source_target_pairs={{225,160},{226,161},{227,162},{228,163},{229,164},{230,165},{231,1... | collective-permute-start | bytes 442376 | tf_op jit(solution)/shard_map/ppermute | solution.py:31
  29.0 1.7 %copy-start.9 = (bf16[9,2,32,128]{3,2,1,0:T(8,128)(2,1)S(1)}, bf16[9,2,32,128]{3,2,1,0:T(8,128)(2,1)}, u32[]{:S(2)}) copy-start(bf16[9,2,32,128]{3,2,1,0:T(8,128)(2,1)} %copy-done.8) | copy-start | bytes 442372
  30.7 38.1 %copy-start.1 = (bf16[1152,384]{1,0:T(8,128)(2,1)}, bf16[1152,384]{1,0:T(8,128)(2,1)S(1)}, u32[]{:S(2)}) copy-start(bf16[1152,384]{1,0:T(8,128)(2,1)S(1)} %maximum_select_fusion) | copy-start | bytes 2654212
  30.7 37.4 %collective-permute-start.9 = (bf16[9,4,32,128]{3,2,1,0:T(8,128)(2,1)}, bf16[9,4,32,128]{3,2,1,0:T(8,128)(2,1)S(1)}, u32[]{:S(2)}, u32[]{:S(2)}) collective-permute-start(bf16[9,4,32,128]{3,2,1,0:T(8,128)(2,1)} %get-tuple-element.214), channel_id=1, source_target_pairs={{160,96},{161,97},{162,98},{163,99},{164,100},{165,101},{166,102},... | collective-permute-start | bytes 884744 | tf_op jit(solution)/shard_map/ppermute | solution.py:31
  32.0 36.0 %collective-permute-start.10 = (bf16[9,2,32,128]{3,2,1,0:T(8,128)(2,1)}, bf16[9,2,32,128]{3,2,1,0:T(8,128)(2,1)}, u32[]{:S(2)}, u32[]{:S(2)}) collective-permute-start(bf16[9,2,32,128]{3,2,1,0:T(8,128)(2,1)} %get-tuple-element.215), channel_id=1, source_target_pairs={{161,96},{162,97},{163,98},{164,99},{165,100},{166,101},{167,102},... | collective-permute-start | bytes 442376 | tf_op jit(solution)/shard_map/ppermute | solution.py:31
  33.3 34.8 %collective-permute-start.8 = (bf16[9,2,32,128]{3,2,1,0:T(8,128)(2,1)}, bf16[9,2,32,128]{3,2,1,0:T(8,128)(2,1)}, u32[]{:S(2)}, u32[]{:S(2)}) collective-permute-start(bf16[9,2,32,128]{3,2,1,0:T(8,128)(2,1)} %get-tuple-element.213), channel_id=1, source_target_pairs={{160,97},{161,98},{162,99},{163,100},{164,101},{165,102},{166,103}... | collective-permute-start | bytes 442376 | tf_op jit(solution)/shard_map/ppermute | solution.py:31
  68.1 0.7 copy-start.7
  68.8 16.3 %copy-start = (bf16[128,128]{1,0:T(8,128)(2,1)S(1)}, bf16[128,128]{1,0:T(8,128)(2,1)}, u32[]{:S(2)}) copy-start(bf16[128,128]{1,0:T(8,128)(2,1)} %constant.158.clone.order_ref) | copy-start | bytes 98308
  74.7 10.4 %collective-permute-start.11 = (bf16[9,6,32,128]{3,2,1,0:T(8,128)(2,1)}, bf16[9,6,32,128]{3,2,1,0:T(8,128)(2,1)S(1)}, u32[]{:S(2)}, u32[]{:S(2)}) collective-permute-start(bf16[9,6,32,128]{3,2,1,0:T(8,128)(2,1)} %copy-done.5), channel_id=1, source_target_pairs={{0,32},{1,33},{2,34},{3,35},{4,36},{5,37},{6,38},{7,39},{8,40},{9,... | collective-permute-start | bytes 1327112 | tf_op jit(solution)/shard_map/ppermute | solution.py:31
  74.7 13.0 %collective-permute-start.13 = (bf16[9,4,32,128]{3,2,1,0:T(8,128)(2,1)}, bf16[9,4,32,128]{3,2,1,0:T(8,128)(2,1)S(1)}, u32[]{:S(2)}, u32[]{:S(2)}) collective-permute-start(bf16[9,4,32,128]{3,2,1,0:T(8,128)(2,1)} %get-tuple-element.219), channel_id=1, source_target_pairs={{96,32},{97,33},{98,34},{99,35},{100,36},{101,37},{102,38},{103,39... | collective-permute-start | bytes 884744 | tf_op jit(solution)/shard_map/ppermute | solution.py:31
  76.0 11.7 %collective-permute-start.12 = (bf16[9,2,32,128]{3,2,1,0:T(8,128)(2,1)}, bf16[9,2,32,128]{3,2,1,0:T(8,128)(2,1)S(1)}, u32[]{:S(2)}, u32[]{:S(2)}) collective-permute-start(bf16[9,2,32,128]{3,2,1,0:T(8,128)(2,1)} %get-tuple-element.221), channel_id=1, source_target_pairs={{96,33},{97,34},{98,35},{99,36},{100,37},{101,38},{102,39},{103,40... | collective-permute-start | bytes 442376 | tf_op jit(solution)/shard_map/ppermute | solution.py:31
  77.3 10.4 %collective-permute-start.14 = (bf16[9,2,32,128]{3,2,1,0:T(8,128)(2,1)}, bf16[9,2,32,128]{3,2,1,0:T(8,128)(2,1)S(1)}, u32[]{:S(2)}, u32[]{:S(2)}) collective-permute-start(bf16[9,2,32,128]{3,2,1,0:T(8,128)(2,1)} %get-tuple-element.222), channel_id=1, source_target_pairs={{97,32},{98,33},{99,34},{100,35},{101,36},{102,37},{103,38},{104,3... | collective-permute-start | bytes 442376 | tf_op jit(solution)/shard_map/ppermute | solution.py:31
  87.8 1.0 copy-start.3
  93.1 8.6 %collective-permute-start.16 = (bf16[9,4,32,128]{3,2,1,0:T(8,128)(2,1)}, bf16[9,4,32,128]{3,2,1,0:T(8,128)(2,1)S(1)}, u32[]{:S(2)}, u32[]{:S(2)}) collective-permute-start(bf16[9,4,32,128]{3,2,1,0:T(8,128)(2,1)} %get-tuple-element.264), channel_id=1, source_target_pairs={{224,192},{225,193},{226,194},{227,195},{228,196},{229,197},{230,1... | collective-permute-start | bytes 884744 | tf_op jit(solution)/shard_map/ppermute | solution.py:31
  95.3 6.3 %collective-permute-start.15 = (bf16[9,1,32,128]{3,2,1,0:T(8,128)(2,1)S(1)}, bf16[9,1,32,128]{3,2,1,0:T(8,128)(2,1)S(1)}, u32[]{:S(2)}, u32[]{:S(2)}) collective-permute-start(bf16[9,1,32,128]{3,2,1,0:T(8,128)(2,1)S(1)} %get-tuple-element.236), channel_id=1, source_target_pairs={{224,193},{225,194},{226,195},{227,196},{228,197},{229,198},{230,1... | collective-permute-start | bytes 221192 | tf_op jit(solution)/shard_map/ppermute | solution.py:31
  96.6 5.0 %collective-permute-start.17 = (bf16[9,1,32,128]{3,2,1,0:T(8,128)(2,1)S(1)}, bf16[9,1,32,128]{3,2,1,0:T(8,128)(2,1)S(1)}, u32[]{:S(2)}, u32[]{:S(2)}) collective-permute-start(bf16[9,1,32,128]{3,2,1,0:T(8,128)(2,1)S(1)} %get-tuple-element.235), channel_id=1, source_target_pairs={{225,192},{226,193},{227,194},{228,195},{229,196},{230,197},{231,1... | collective-permute-start | bytes 221192 | tf_op jit(solution)/shard_map/ppermute | solution.py:31
  101.7 1.9 %collective-permute-start.21 = (bf16[9,64,384]{2,1,0:T(8,128)(2,1)S(1)}, bf16[9,64,384]{2,1,0:T(8,128)(2,1)S(1)}, u32[]{:S(2)}, u32[]{:S(2)}) collective-permute-start(bf16[9,64,384]{2,1,0:T(8,128)(2,1)S(1)} %constant_dynamic-slice_fusion.6), channel_id=1, source_target_pairs={{0,1},{1,0},{2,3},{3,2},{4,5},{5,4},{6,7},{7,6},{8,9},{9,8},{10,11... | collective-permute-start | bytes 1327112 | tf_op jit(solution)/shard_map/ppermute | solution.py:319
  103.7 12.1 %collective-permute-start.22 = (bf16[9,32,384]{2,1,0:T(8,128)(2,1)S(1)}, bf16[9,32,384]{2,1,0:T(8,128)(2,1)S(1)}, u32[]{:S(2)}, u32[]{:S(2)}) collective-permute-start(bf16[9,32,384]{2,1,0:T(8,128)(2,1)S(1)} %constant_dynamic-slice_fusion.5), channel_id=1, source_target_pairs={{0,4},{1,5},{2,6},{3,7},{4,0},{5,1},{6,2},{7,3},{8,12},{9,13},{10,... | collective-permute-start | bytes 663560 | tf_op jit(solution)/shard_map/ppermute | solution.py:319
  110.1 26.7 %collective-permute-start.19 = (bf16[9,4,32,128]{3,2,1,0:T(8,128)(2,1)}, bf16[9,4,32,128]{3,2,1,0:T(8,128)(2,1)S(1)}, u32[]{:S(2)}, u32[]{:S(2)}) collective-permute-start(bf16[9,4,32,128]{3,2,1,0:T(8,128)(2,1)} %get-tuple-element.266), channel_id=1, source_target_pairs={{32,0},{33,1},{34,2},{35,3},{36,4},{37,5},{38,6},{39,7},{40,8},{41... | collective-permute-start | bytes 884744 | tf_op jit(solution)/shard_map/ppermute | solution.py:31
  115.9 6.3 %collective-permute-start.23 = (bf16[9,16,384]{2,1,0:T(8,128)(2,1)S(1)}, bf16[9,16,384]{2,1,0:T(8,128)(2,1)S(1)}, u32[]{:S(2)}, u32[]{:S(2)}) collective-permute-start(bf16[9,16,384]{2,1,0:T(8,128)(2,1)S(1)} %constant_dynamic-slice_fusion.4), channel_id=1, source_target_pairs={{0,2},{1,3},{2,0},{3,1},{4,6},{5,7},{6,4},{7,5},{8,10},{9,11},{10,... | collective-permute-start | bytes 331784 | tf_op jit(solution)/shard_map/ppermute | solution.py:319
  116.9 19.7 %collective-permute-start.18 = (bf16[9,1,32,128]{3,2,1,0:T(8,128)(2,1)S(1)}, bf16[9,1,32,128]{3,2,1,0:T(8,128)(2,1)S(1)}, u32[]{:S(2)}, u32[]{:S(2)}) collective-permute-start(bf16[9,1,32,128]{3,2,1,0:T(8,128)(2,1)S(1)} %get-tuple-element.234), channel_id=1, source_target_pairs={{32,1},{33,2},{34,3},{35,4},{36,5},{37,6},{38,7},{39,8},{40,9},{41... | collective-permute-start | bytes 221192 | tf_op jit(solution)/shard_map/ppermute | solution.py:31
  117.6 19.1 %collective-permute-start.20 = (bf16[9,1,32,128]{3,2,1,0:T(8,128)(2,1)S(1)}, bf16[9,1,32,128]{3,2,1,0:T(8,128)(2,1)S(1)}, u32[]{:S(2)}, u32[]{:S(2)}) collective-permute-start(bf16[9,1,32,128]{3,2,1,0:T(8,128)(2,1)S(1)} %get-tuple-element.233), channel_id=1, source_target_pairs={{33,0},{34,1},{35,2},{36,3},{37,4},{38,5},{39,6},{40,7},{41,8},{42... | collective-permute-start | bytes 221192 | tf_op jit(solution)/shard_map/ppermute | solution.py:31
  122.4 15.5 %collective-permute-start.24 = (bf16[9,4,384]{2,1,0:T(4,128)(2,1)S(1)}, bf16[9,4,384]{2,1,0:T(4,128)(2,1)S(1)}, u32[]{:S(2)}, u32[]{:S(2)}) collective-permute-start(bf16[9,4,384]{2,1,0:T(4,128)(2,1)S(1)} %get-tuple-element.237), channel_id=1, source_target_pairs={{32,24},{33,25},{34,26},{35,27},{36,28},{37,29},{38,30},{39,31},{4... | collective-permute-start | bytes 82952 | tf_op jit(solution)/shard_map/ppermute | solution.py:332
  136.2 9.6 %collective-permute-start.25 = (bf16[9,4,384]{2,1,0:T(4,128)(2,1)S(1)}, bf16[9,4,384]{2,1,0:T(4,128)(2,1)S(1)}, u32[]{:S(2)}, u32[]{:S(2)}) collective-permute-start(bf16[9,4,384]{2,1,0:T(4,128)(2,1)S(1)} %get-tuple-element.240), channel_id=1, source_target_pairs={{32,16},{33,17},{34,18},{35,19},{36,20},{37,21},{38,22},{39,23},{4... | collective-permute-start | bytes 82952 | tf_op jit(solution)/shard_map/ppermute | solution.py:332
  136.7 9.1 %collective-permute-start.26 = (bf16[9,4,384]{2,1,0:T(4,128)(2,1)S(1)}, bf16[9,4,384]{2,1,0:T(4,128)(2,1)S(1)}, u32[]{:S(2)}, u32[]{:S(2)}) collective-permute-start(bf16[9,4,384]{2,1,0:T(4,128)(2,1)S(1)} %get-tuple-element.239), channel_id=1, source_target_pairs={{32,8},{33,9},{34,10},{35,11},{36,12},{37,13},{38,14},{39,15},{40,... | collective-permute-start | bytes 82952 | tf_op jit(solution)/shard_map/ppermute | solution.py:332
  136.7 9.1 %collective-permute-start.27 = (bf16[9,4,384]{2,1,0:T(4,128)(2,1)S(1)}, bf16[9,4,384]{2,1,0:T(4,128)(2,1)S(1)}, u32[]{:S(2)}, u32[]{:S(2)}) collective-permute-start(bf16[9,4,384]{2,1,0:T(4,128)(2,1)S(1)} %get-tuple-element.238), channel_id=1, source_target_pairs={{32,0},{33,1},{34,2},{35,3},{36,4},{37,5},{38,6},{39,7},{40,8},{41... | collective-permute-start | bytes 82952 | tf_op jit(solution)/shard_map/ppermute | solution.py:332

commit v4 on v2

--- a/solution.py
+++ b/solution.py
@@ -18,7 +18,7 @@
 COLS = 32
 CH = 128
 AXES = ("section", "dp")
-HALVING = (1, 2, 4, 8, 16)
+HALVING = (1, 4, 2, 8, 16)
 
 
 def permute(value, hops):
@@ -43,7 +43,19 @@
         )
 
 
-def back_pass(x_ref, w_ref, slope_ref, rows, emit):
+def weights(w_ref):
+    return jnp.concatenate(
+        [
+            jnp.concatenate(
+                [w_ref[(9 * i + n) * CH : (9 * i + n + 1) * CH, :] for n in range(9)], axis=1
+            )
+            for i in range(3)
+        ],
+        axis=0,
+    )
+
+
+def back_pass(x_ref, rhs, slope_ref, rows, emit):
     group = 3
     size = rows * COLS
     one_later = None
@@ -52,7 +64,9 @@
         lhs = jnp.concatenate(
             [x_ref[start : start + group, 2 - j : 2 - j + rows] for j in range(3)], axis=-1
         ).reshape(group * size, 9 * CH)
-        part = jnp.dot(lhs, w_ref[...], preferred_element_type=F32)
+        part = lax.dot_general(
+            lhs, rhs, (((1,), (1,)), ((), ())), preferred_element_type=F32
+        )
         for t in range(group - 1, -1, -1):
             here = part[t * size : (t + 1) * size]
             back = here[:, 2 * CH :]
@@ -85,11 +99,17 @@
     for t in range(FRAMES):
         whole = jnp.concatenate([low_ref[t], own_ref[t], high_ref[t]], axis=0)
         fill(x_ref, t, 0, whole.reshape(-1, CH).astype(F32))
-    back_pass(x_ref, w_ref, slope_ref, ROWS, emit_to(outs))
-
-
-def double_kernel(low_ref, own_ref, high_ref, w1_ref, slope1_ref, w0_ref, slope0_ref, *rest):
-    *outs, x1_ref, x0_ref = rest
+    back_pass(x_ref, weights(w_ref), slope_ref, ROWS, emit_to(outs))
+
+
+def double_kernel(
+    core_ref, low_ref, own_ref, high_ref, half_ref, other_ref, slope1_ref, w0_ref, slope0_ref, *rest
+):
+    *outs, x1_ref, x0_ref, w1_ref = rest
+    half = half_ref.shape[0]
+    core = core_ref[0]
+    w1_ref[pl.ds(pl.multiple_of(core * half, half), half), :] = half_ref[...]
+    w1_ref[pl.ds(pl.multiple_of((1 - core) * half, half), half), :] = other_ref[...]
     for t in range(FRAMES):
         whole = jnp.concatenate([low_ref[t], own_ref[t], high_ref[t]], axis=0)
         fill(x1_ref, t, 0, whole.reshape(-1, CH).astype(F32))
@@ -97,8 +117,8 @@
     def emit_mid(frame, value):
         fill(x0_ref, frame, 0, value.astype(F32))
 
-    back_pass(x1_ref, w1_ref, slope1_ref, ROWS + 2, emit_mid)
-    back_pass(x0_ref, w0_ref, slope0_ref, ROWS, emit_to(outs))
+    back_pass(x1_ref, weights(w1_ref), slope1_ref, ROWS + 2, emit_mid)
+    back_pass(x0_ref, weights(w0_ref), slope0_ref, ROWS, emit_to(outs))
 
 
 def in_vmem(count):
@@ -123,19 +143,20 @@
     )(low, own, high, w, slope)
 
 
-def double(low, own, high, w1, slope1, w0, slope0):
+def double(core, low, own, high, half, other, slope1, w0, slope0):
     return pl.pallas_call(
         double_kernel,
         out_shape=gradient_shapes(),
-        in_specs=in_vmem(7),
+        in_specs=[pl.BlockSpec(memory_space=pltpu.SMEM)] + in_vmem(8),
         out_specs=in_vmem(3),
         scratch_shapes=[
             pltpu.VMEM((FRAMES, ROWS + 4, COLS, 3 * CH), BF),
             pltpu.VMEM((FRAMES, ROWS + 2, COLS, 3 * CH), BF),
+            pltpu.VMEM((27 * CH, CH), BF),
         ],
         compiler_params=pltpu.CompilerParams(vmem_limit_bytes=24 << 20),
         name="two_blocks",
-    )(low, own, high, w1, slope1, w0, slope0)
+    )(core.reshape(1), low, own, high, half, other, slope1, w0, slope0)
 
 
 def tap_rows_kernel(act_ref, order_ref, out_ref, u_ref):
@@ -213,10 +234,6 @@
     return sig * (1.0 + x * (1.0 - sig))
 
 
-def as_matrix(kern):
-    return jnp.transpose(kern, (1, 2, 4, 0, 3)).reshape(9 * CH, 3 * CH)
-
-
 def local(acts, kernels, cotangent):
     me = lax.axis_index("section")
     dp = lax.axis_index("dp")
@@ -227,17 +244,18 @@
     pair = odd[:-1]
     barrier = lax.optimization_barrier
 
+    w = kernels[0].reshape(27 * CH, CH)
+    half = w.shape[0] // 2
+    w_half = permute(
+        lax.dynamic_slice_in_dim(w, core * half, half, 0), [(s + 1, s, 0) for s in pair]
+    )
+
     both = jnp.concatenate([cotangent, acts[0]], axis=0)
     edge_low = permute(both[:, -1:], [(s, s, 1) for s in every])
     edge_high = permute(both[:, :1], [(s, s, -1) for s in every])
     low0, high0 = edge_low[:FRAMES], edge_high[:FRAMES]
     act6 = jnp.concatenate([edge_low[FRAMES:], acts[0], edge_high[FRAMES:]], axis=1)
 
-    w = as_matrix(kernels[0])
-    half = w.shape[0] // 2
-    w_half = permute(
-        lax.dynamic_slice_in_dim(w, core * half, half, 0), [(s + 1, s, 0) for s in pair]
-    )
     slope = slope_of(acts[0])
     none = jnp.zeros((FRAMES, 2, COLS, CH), BF)
     state = lax.cond(
@@ -246,20 +264,6 @@
         lambda: (cotangent, none, none),
     )
 
-    act6, state = barrier((act6, state))
-    act_next = permute(act6, [(s + 1, s, 0) for s in pair])
-    w_other = lax.ppermute(
-        w_half, AXES, [(s * DP + d, s * DP + (d ^ 1)) for s in pair for d in range(DP)]
-    )
-    w_next = jnp.where(
-        core == 0,
-        jnp.concatenate([w_half, w_other], axis=0),
-        jnp.concatenate([w_other, w_half], axis=0),
-    )
-    row = lax.broadcasted_iota(jnp.int32, act_next.shape, 1) + dp * ROWS - 1
-    inside = (row >= 0) & (row < DP * ROWS)
-    slope_next = jnp.where(inside, slope_of(act_next), 0.0)
-
     def hop(state, target):
         result, top, bottom = state
         own = permute(result, [(target + 2, target, 0)])
@@ -267,22 +271,25 @@
         high = permute(top, [(target + 2, target, -1)])
         return low, own, high
 
+    act6, state = barrier((act6, state))
+    act_next = permute(act6, [(s + 1, s, 0) for s in pair])
+    arrived, w_half = barrier((hop(state, 5), w_half))
+    w_other = lax.ppermute(
+        w_half, AXES, [(s * DP + d, s * DP + (d ^ 1)) for s in pair for d in range(DP)]
+    )
+    row = lax.broadcasted_iota(jnp.int32, act_next.shape, 1) + dp * ROWS - 1
+    inside = (row >= 0) & (row < DP * ROWS)
+    slope_next = jnp.where(inside, slope_of(act_next), 0.0)
+
     def stage(state, arrived, section):
         low, own, high = arrived
         return lax.cond(
             me == section,
-            lambda: tuple(double(low, own, high, w_next, slope_next, w, slope)),
+            lambda: tuple(
+                double(core, low, own, high, w_half, w_other, slope_next, w, slope)
+            ),
             lambda: state,
         )
-
-    state = stage(state, hop(state, 5), 5)
-    state = stage(state, hop(state, 3), 3)
-    act6, state = barrier((act6, state))
-    arrived = hop(state, 1)
-    act_prev = permute(act6, [(s, (s + 1) % SEC, 0) for s in every])
-    ut = tap_rows(act_prev, jnp.asarray(channel_order(), BF))
-    ut, arrived = barrier((ut, arrived))
-    result, _, _ = stage(state, arrived, 1)
 
     def even(result, sections):
         hops = [(s + 1, s) for s in sections]
@@ -296,11 +303,20 @@
             lambda: result,
         )
 
-    result = even(result, (6, 4, 2))
+    state = stage(state, arrived, 5)
+    act6, state = barrier((act6, state))
+    arrived = hop(state, 3)
+    act_prev = permute(act6, [(s, (s + 1) % SEC, 0) for s in every])
+    ut = tap_rows(act_prev, jnp.asarray(channel_order(), BF))
+    ut, arrived = barrier((ut, arrived))
+    state = stage(state, arrived, 3)
+    arrived = hop(state, 1)
+    result = even(state[0], (6, 4, 2))
+    result, arrived = barrier((result, arrived))
+    result, _, _ = stage((result, state[1], state[2]), arrived, 1)
     final = even(result, (0,))
 
-    grad = jnp.where(me == 0, cotangent, result)
-    part = taps(ut, grad, scale)
+    part = taps(ut, jnp.where(me == 0, cotangent, result), scale)
     for bit in HALVING:
         size = part.shape[1] // 2
         mine = (dp // bit) % 2

time: 136 us -> 137 us (level)
  starting transfers between devices: 33.6 us -> 41.5 us
  waiting for transfers between devices: 76.6 us -> 72.3 us
  other arithmetic: 5.52 us -> 3.84 us
    ppermute x21, waiting for transfers between devices: 60 us -> 53.9 us  [permute(): return lax.ppermute(value, AXES, pairs)]
    select_n x2 -> x1, other arithmetic: 3.86 us -> 0.03 us  [local(): part = taps(ut, jnp.where(me == 0, cotangent, result), scale)]
    ppermute x1, starting transfers between devices: 3.71 us -> 7.46 us  [local(): lax.ppermute(w_half, AXES, [(s * DP + d, s * DP + (d ^ 1)) for s in pair...]
    ppermute x5, starting transfers between devices: 8.76 us -> 12.1 us  [local(): lax.ppermute(give, AXES, [((s + shift) % SEC * DP + d, s * DP + (d ^ bit)...]
    transpose x1 -> x0, local copies, waits for them, and re-layouts: 2.45 us -> none  [as_matrix(): return jnp.transpose(kern, (1, 2, 4, 0, 3)).reshape(9 * CH, 3 * CH)]
    ppermute x5, waiting for transfers between devices: 16.6 us -> 18.4 us  [local(): lax.ppermute(give, AXES, [((s + shift) % SEC * DP + d, s * DP + (d ^ bit)...]
  transfers between devices with their start and end apart: 27 -> 27, of which waited for: 11 -> 12; matrix products, arithmetic and copies ran while one was open for 6% -> 6% of each run, Pallas kernels for 1% -> 1%
where the time goes in v4:
time: 137 us; the launch traced here: 135 us
  waiting for transfers between devices  72.3 us (53%)
  starting transfers between devices  41.5 us (30%)
  Pallas kernels  9.49 us (7%)
  local copies, waits for them, and re-layouts  7.09 us (5%)
  other arithmetic  3.84 us (3%)
    ppermute x21, waiting for transfers between devices, permute(): return lax.ppermute(value, AXES, pairs)  53.9 us
    ppermute x21, starting transfers between devices, permute(): return lax.ppermute(value, AXES, pairs)  21.9 us
    ppermute x5, waiting for transfers between devices, local(): lax.ppermute(give, AXES, [((s + shift) % SEC * DP + d, s * DP + (d ^ bit)...  18.4 us
    ppermute x5, starting transfers between devices, local(): lax.ppermute(give, AXES, [((s + shift) % SEC * DP + d, s * DP + (d ^ bit)...  12.1 us
    ppermute x1, starting transfers between devices, local(): lax.ppermute(w_half, AXES, [(s * DP + d, s * DP + (d ^ 1)) for s in pair...  7.46 us
    pallas_call x1, Pallas kernels, double(): pl.pallas_call(double_kernel, out_shape=gradient_shapes(), in_specs=[pl.B...  6.76 us
  transfers between devices with their start and end apart: 27, of which 12 were waited for; matrix products, arithmetic and copies ran while one was open for 6% of the time, Pallas kernels for 1%

profile of v4, /device:TPU:8, one launch (start us, length us, event | category | flops | bytes accessed | tf_op | source)
XLA Modules:
  0.0 135.5 jit_solution(4425491014783733715)
XLA Ops:
  0.6 0.0 copy-start.1
  0.6 0.0 copy-start.5
  0.7 1.1 constant_dynamic-slice_fusion.6
  1.8 0.0 copy-start.6
  1.8 1.4 %collective-permute-start.5 = (bf16[1728,128]{1,0:T(8,128)(2,1)S(1)}, bf16[1728,128]{1,0:T(8,128)(2,1)}, u32[]{:S(2)}, u32[]{:S(2)}) collective-permute-start(bf16[1728,128]{1,0:T(8,128)(2,1)S(1)} %constant_dynamic-slice_fusion.6), channel_id=1, source_target_pairs={{64,32},{65,33},{66,34},{67,35},{68,36},{69,37},{70,38},{71,39},{7... | collective-permute-start | bytes 1327112 | tf_op jit(solution)/shard_map/ppermute | solution.py:31
  3.3 1.0 pad_maximum_fusion.2
  4.3 1.7 %collective-permute-start = (bf16[18,1,32,128]{3,2,1,0:T(8,128)(2,1)S(1)}, bf16[18,1,32,128]{3,2,1,0:T(8,128)(2,1)S(1)}, u32[]{:S(2)}, u32[]{:S(2)}) collective-permute-start(bf16[18,1,32,128]{3,2,1,0:T(8,128)(2,1)S(1)} %get-tuple-element.224), channel_id=1, source_target_pairs={{0,1},{1,2},{2,3},{3,4},{4,5},{5,6},{6,7},{7,8},{8,9},{9,10},{10,1... | collective-permute-start | bytes 442376 | tf_op jit(solution)/shard_map/ppermute | solution.py:31
  6.0 1.3 collective-permute-start.1
  7.3 1.2 fusion.10
  8.5 2.8 %collective-permute-done.1 = bf16[18,1,32,128]{3,2,1,0:T(8,128)(2,1)S(1)} collective-permute-done((bf16[18,1,32,128]{3,2,1,0:T(8,128)(2,1)S(1)}, bf16[18,1,32,128]{3,2,1,0:T(8,128)(2,1)S(1)}, u32[]{:S(2)}, u32[]{:S(2)}) %collective-permute-start.1) | collective-permute-done | bytes 147488 | tf_op jit(solution)/shard_map/ppermute | solution.py:31
  11.4 2.1 %conditional.6 = ((bf16[9,4,32,128]{3,2,1,0:T(8,128)(2,1)}, bf16[9,2,32,128]{3,2,1,0:T(8,128)(2,1)}, bf16[9,2,32,128]{3,2,1,0:T(8,128)(2,1)})) conditional(s32[]{:T(128)} %convert_element_type.70, bf16[9,4,32,128]{3,2,1,0:T(8,128)(2,1)S(1)} %copy-done.5, (bf16[18,1,32,128]{3,2,1,0:T(8,128)(2,1)S(1)}, bf16[18,1,32,128]{3,2,1,0:T(8,128)(2,1)S(1)}, ...), branch_computations={%region_0.1_spmd, %region_1.2_spmd} | conditional | bytes 884772 | solution.py:261
  11.4 0.7 copy.8
  12.1 0.7 broadcast_in_dim.13
  12.8 0.7 broadcast_in_dim.13.clone
  13.5 0.1 pad_maximum_fusion
  13.6 0.0 copy-start
  13.6 0.7 collective-permute-start.3
  14.3 1.3 collective-permute-start.7
  15.6 1.3 collective-permute-start.2
  16.9 0.7 collective-permute-start.4
  17.6 0.3 collective-permute-done.5
  17.8 0.4 copy-done.9
  18.2 7.5 %collective-permute-start.6 = (bf16[1728,128]{1,0:T(8,128)(2,1)}, bf16[1728,128]{1,0:T(8,128)(2,1)}, u32[]{:S(2)}, u32[]{:S(2)}) collective-permute-start(bf16[1728,128]{1,0:T(8,128)(2,1)} %collective-permute-done.5), channel_id=1, source_target_pairs={{32,33},{33,32},{34,35},{35,34},{36,37},{37,36},{38,39},{39,38},{4... | collective-permute-start | bytes 1327112 | tf_op jit(solution)/shard_map/ppermute | solution.py:277
  25.7 1.0 collective-permute-done.7
  26.7 1.3 fusion.5
  28.0 1.4 %collective-permute-start.10 = (bf16[9,4,32,128]{3,2,1,0:T(8,128)(2,1)}, bf16[9,4,32,128]{3,2,1,0:T(8,128)(2,1)}, u32[]{:S(2)}, u32[]{:S(2)}) collective-permute-start(bf16[9,4,32,128]{3,2,1,0:T(8,128)(2,1)} %get-tuple-element.207), channel_id=1, source_target_pairs={{160,96},{161,97},{162,98},{163,99},{164,100},{165,101},{166,102},... | collective-permute-start | bytes 884744 | tf_op jit(solution)/shard_map/ppermute | solution.py:31
  29.4 1.3 collective-permute-start.11
  30.7 1.3 collective-permute-start.9
  32.0 5.3 %collective-permute-done.8.act_ref = bf16[9,6,32,128]{3,2,1,0:T(8,128)(2,1)S(1)} collective-permute-done((bf16[9,6,32,128]{3,2,1,0:T(8,128)(2,1)S(1)}, bf16[9,6,32,128]{3,2,1,0:T(8,128)(2,1)S(1)}, u32[]{:S(2)}, u32[]{:S(2)}) %collective-permute-start.8) | collective-permute-done | bytes 442400 | tf_op jit(solution)/shard_map/ppermute | solution.py:31
  37.3 1.1 tap_rows.1.ut_ref
  38.5 1.4 %collective-permute-start.13 = (bf16[9,4,32,128]{3,2,1,0:T(8,128)(2,1)}, bf16[9,4,32,128]{3,2,1,0:T(8,128)(2,1)}, u32[]{:S(2)}, u32[]{:S(2)}) collective-permute-start(bf16[9,4,32,128]{3,2,1,0:T(8,128)(2,1)} %get-tuple-element.214), channel_id=1, source_target_pairs={{224,192},{225,193},{226,194},{227,195},{228,196},{229,197},{230,1... | collective-permute-start | bytes 884744 | tf_op jit(solution)/shard_map/ppermute | solution.py:31
  39.9 1.5 %collective-permute-start.16 = (bf16[9,4,32,128]{3,2,1,0:T(8,128)(2,1)}, bf16[9,4,32,128]{3,2,1,0:T(8,128)(2,1)}, u32[]{:S(2)}, u32[]{:S(2)}) collective-permute-start(bf16[9,4,32,128]{3,2,1,0:T(8,128)(2,1)} %get-tuple-element.214), channel_id=1, source_target_pairs={{96,32},{97,33},{98,34},{99,35},{100,36},{101,37},{102,38},{103,39... | collective-permute-start | bytes 884744 | tf_op jit(solution)/shard_map/ppermute | solution.py:31
  41.4 0.9 fusion.12
  42.3 0.7 collective-permute-start.12
  43.0 0.7 collective-permute-start.15
  43.7 1.3 collective-permute-start.17
  45.0 0.7 collective-permute-start.14
  45.7 1.0 conditional.9
  45.7 1.0 copy.26
  46.7 39.9 %collective-permute-done.17 = bf16[9,2,32,128]{3,2,1,0:T(8,128)(2,1)} collective-permute-done((bf16[9,2,32,128]{3,2,1,0:T(8,128)(2,1)}, bf16[9,2,32,128]{3,2,1,0:T(8,128)(2,1)}, u32[]{:S(2)}, u32[]{:S(2)}) %collective-permute-start.17) | collective-permute-done | bytes 147488 | tf_op jit(solution)/shard_map/ppermute | solution.py:31
  86.6 6.8 %conditional.10 = (bf16[9,4,32,128]{3,2,1,0:T(8,128)(2,1)S(1)}) conditional(s32[]{:T(128)} %convert_element_type.67, bf16[9,4,32,128]{3,2,1,0:T(8,128)(2,1)S(1)} %get-tuple-element.255, (s32[]{:T(128)}, bf16[9,2,32,128]{3,2,1,0:T(8,128)(2,1)S(1)}, bf16[9,4,32,128]{3,2,1,0:T(8,128)(2,1)}, bf16[9,2,32,128]{3,2,1,0:T(8,128)(2,1)}, ...), branch_computations={%region_8.9_spmd, %region_9.10_spmd} | conditional | bytes 8 | solution.py:286
  86.6 6.8 %two_blocks.5 = (bf16[9,4,32,128]{3,2,1,0:T(8,128)(2,1)S(1)}, bf16[9,2,32,128]{3,2,1,0:T(8,128)(2,1)}, bf16[9,2,32,128]{3,2,1,0:T(8,128)(2,1)}) custom-call(s32[1]{0:T(128)} %bitcast.2.core_ref, bf16[9,2,32,128]{3,2,1,0:T(8,128)(2,1)S(1)} %get-tuple-element.147.low_ref, bf16[9,4,32,128]{3,2,1,0:T(8,128)(2,1)} %get-tuple-element.148.own_ref, ...), custom_call_target="tpu_custom_call" | custom-call | tf_op jit(solution)/shard_map/cond/branch_1_fun/two_blocks/pallas_call | solution.py:147
  93.3 0.7 copy-done.7
  94.1 1.6 %kernel_taps.1 = bf16[9,128,384]{2,1,0:T(8,128)(2,1)S(1)} custom-call(bf16[9,128,1152]{2,1,0:T(8,128)(2,1)S(1)} %tap_rows.1.ut_ref, bf16[9,4,32,128]{3,2,1,0:T(8,128)(2,1)S(1)} %broadcast_select_fusion.g_ref), custom_call_target="tpu_custom_call" | custom-call | tf_op jit(solution)/shard_map/kernel_taps/pallas_call | solution.py:206
  95.7 0.1 constant_dynamic-slice_fusion.5
  95.8 0.6 collective-permute-start.21
  96.4 1.4 %collective-permute-done.21 = bf16[9,64,384]{2,1,0:T(8,128)(2,1)S(1)} collective-permute-done((bf16[9,64,384]{2,1,0:T(8,128)(2,1)S(1)}, bf16[9,64,384]{2,1,0:T(8,128)(2,1)S(1)}, u32[]{:S(2)}, u32[]{:S(2)}) %collective-permute-start.21) | collective-permute-done | bytes 442400 | tf_op jit(solution)/shard_map/ppermute | solution.py:329
  97.8 0.1 add_convert_fusion
  98.0 4.4 %collective-permute-start.22 = (bf16[9,32,384]{2,1,0:T(8,128)(2,1)S(1)}, bf16[9,32,384]{2,1,0:T(8,128)(2,1)S(1)}, u32[]{:S(2)}, u32[]{:S(2)}) collective-permute-start(bf16[9,32,384]{2,1,0:T(8,128)(2,1)S(1)} %constant_dynamic-slice_fusion.4), channel_id=1, source_target_pairs={{0,4},{1,5},{2,6},{3,7},{4,0},{5,1},{6,2},{7,3},{8,12},{9,13},{10,... | collective-permute-start | bytes 663560 | tf_op jit(solution)/shard_map/ppermute | solution.py:329
  102.3 6.0 %collective-permute-done.22 = bf16[9,32,384]{2,1,0:T(8,128)(2,1)S(1)} collective-permute-done((bf16[9,32,384]{2,1,0:T(8,128)(2,1)S(1)}, bf16[9,32,384]{2,1,0:T(8,128)(2,1)S(1)}, u32[]{:S(2)}, u32[]{:S(2)}) %collective-permute-start.22) | collective-permute-done | bytes 221216 | tf_op jit(solution)/shard_map/ppermute | solution.py:329
  108.3 0.1 add_convert_fusion.1
  108.4 0.1 collective-permute-start.23
  108.6 1.3 collective-permute-start.19
  109.9 5.9 %collective-permute-done.23 = bf16[9,16,384]{2,1,0:T(8,128)(2,1)S(1)} collective-permute-done((bf16[9,16,384]{2,1,0:T(8,128)(2,1)S(1)}, bf16[9,16,384]{2,1,0:T(8,128)(2,1)S(1)}, u32[]{:S(2)}, u32[]{:S(2)}) %collective-permute-start.23) | collective-permute-done | bytes 110624 | tf_op jit(solution)/shard_map/ppermute | solution.py:329
  115.9 7.0 %collective-permute-start.24 = (bf16[9,8,384]{2,1,0:T(8,128)(2,1)S(1)}, bf16[9,8,384]{2,1,0:T(8,128)(2,1)S(1)}, u32[]{:S(2)}, u32[]{:S(2)}) collective-permute-start(bf16[9,8,384]{2,1,0:T(8,128)(2,1)S(1)} %constant_dynamic-slice_fusion.2), channel_id=1, source_target_pairs={{0,8},{1,9},{2,10},{3,11},{4,12},{5,13},{6,14},{7,15},{8,0},{9,1},... | collective-permute-start | bytes 165896 | tf_op jit(solution)/shard_map/ppermute | solution.py:329
  122.9 1.3 collective-permute-start.18
  124.2 0.7 collective-permute-start.20
  124.9 0.1 collective-permute-done.24
  125.1 0.1 collective-permute-start.25
  125.2 0.1 collective-permute-start.26
  125.3 0.9 collective-permute-done.18
  126.2 3.7 %collective-permute-done.25 = bf16[9,4,384]{2,1,0:T(4,128)(2,1)S(1)} collective-permute-done((bf16[9,4,384]{2,1,0:T(4,128)(2,1)S(1)}, bf16[9,4,384]{2,1,0:T(4,128)(2,1)S(1)}, u32[]{:S(2)}, u32[]{:S(2)}) %collective-permute-start.25) | collective-permute-done | bytes 27680 | tf_op jit(solution)/shard_map/ppermute | solution.py:31
  129.9 4.9 %collective-permute-done.26 = bf16[9,4,384]{2,1,0:T(4,128)(2,1)S(1)} collective-permute-done((bf16[9,4,384]{2,1,0:T(4,128)(2,1)S(1)}, bf16[9,4,384]{2,1,0:T(4,128)(2,1)S(1)}, u32[]{:S(2)}, u32[]{:S(2)}) %collective-permute-start.26) | collective-permute-done | bytes 27680 | tf_op jit(solution)/shard_map/ppermute | solution.py:329
  134.8 0.6 copy.7
  (45 shorter events, 0.3 us)
Async XLA Ops:
  0.6 10.8 %copy-start.1 = (bf16[1,3,3,3,128,128]{5,4,3,2,1,0:T(8,128)(2,1)S(1)}, bf16[1,3,3,3,128,128]{5,4,3,2,1,0:T(8,128)(2,1)}, u32[]{:S(2)}) copy-start(bf16[1,3,3,3,128,128]{5,4,3,2,1,0:T(8,128)(2,1)} %param.17) | copy-start | bytes 2654212
  0.6 10.7 %copy-start.5 = (bf16[9,4,32,128]{3,2,1,0:T(8,128)(2,1)S(1)}, bf16[9,4,32,128]{3,2,1,0:T(8,128)(2,1)}, u32[]{:S(2)}) copy-start(bf16[9,4,32,128]{3,2,1,0:T(8,128)(2,1)} %param.18) | copy-start | bytes 884740
  1.8 11.7 %copy-start.6 = (bf16[1,9,4,32,128]{4,3,2,1,0:T(8,128)(2,1)S(1)}, bf16[1,9,4,32,128]{4,3,2,1,0:T(8,128)(2,1)}, u32[]{:S(2)}) copy-start(bf16[1,9,4,32,128]{4,3,2,1,0:T(8,128)(2,1)} %param.16) | copy-start | bytes 884740
  1.8 16.0 %collective-permute-start.5 = (bf16[1728,128]{1,0:T(8,128)(2,1)S(1)}, bf16[1728,128]{1,0:T(8,128)(2,1)}, u32[]{:S(2)}, u32[]{:S(2)}) collective-permute-start(bf16[1728,128]{1,0:T(8,128)(2,1)S(1)} %constant_dynamic-slice_fusion.6), channel_id=1, source_target_pairs={{64,32},{65,33},{66,34},{67,35},{68,36},{69,37},{70,38},{71,39},{7... | collective-permute-start | bytes 1327112 | tf_op jit(solution)/shard_map/ppermute | solution.py:31
  4.3 4.2 %collective-permute-start = (bf16[18,1,32,128]{3,2,1,0:T(8,128)(2,1)S(1)}, bf16[18,1,32,128]{3,2,1,0:T(8,128)(2,1)S(1)}, u32[]{:S(2)}, u32[]{:S(2)}) collective-permute-start(bf16[18,1,32,128]{3,2,1,0:T(8,128)(2,1)S(1)} %get-tuple-element.224), channel_id=1, source_target_pairs={{0,1},{1,2},{2,3},{3,4},{4,5},{5,6},{6,7},{7,8},{8,9},{9,10},{10,1... | collective-permute-start | bytes 442376 | tf_op jit(solution)/shard_map/ppermute | solution.py:31
  6.0 5.3 %collective-permute-start.1 = (bf16[18,1,32,128]{3,2,1,0:T(8,128)(2,1)S(1)}, bf16[18,1,32,128]{3,2,1,0:T(8,128)(2,1)S(1)}, u32[]{:S(2)}, u32[]{:S(2)}) collective-permute-start(bf16[18,1,32,128]{3,2,1,0:T(8,128)(2,1)S(1)} %get-tuple-element.225), channel_id=1, source_target_pairs={{1,0},{2,1},{3,2},{4,3},{5,4},{6,5},{7,6},{8,7},{9,8},{10,9},{11,1... | collective-permute-start | bytes 442376 | tf_op jit(solution)/shard_map/ppermute | solution.py:31
  8.5 19.5 %copy-start.3 = (f32[9,4,32,128]{3,2,1,0:T(8,128)}, f32[9,4,32,128]{3,2,1,0:T(8,128)S(1)}, u32[]{:S(2)}) copy-start(f32[9,4,32,128]{3,2,1,0:T(8,128)S(1)} %fusion.10) | copy-start | bytes 1769476
  13.6 23.8 %copy-start = (bf16[128,128]{1,0:T(8,128)(2,1)S(1)}, bf16[128,128]{1,0:T(8,128)(2,1)}, u32[]{:S(2)}) copy-start(bf16[128,128]{1,0:T(8,128)(2,1)} %constant.125.clone.order_ref) | copy-start | bytes 98308
  13.6 4.3 %collective-permute-start.3 = (bf16[9,4,32,128]{3,2,1,0:T(8,128)(2,1)}, bf16[9,4,32,128]{3,2,1,0:T(8,128)(2,1)S(1)}, u32[]{:S(2)}, u32[]{:S(2)}) collective-permute-start(bf16[9,4,32,128]{3,2,1,0:T(8,128)(2,1)} %get-tuple-element.197), channel_id=1, source_target_pairs={{224,160},{225,161},{226,162},{227,163},{228,164},{229,165},{230,1... | collective-permute-start | bytes 884744 | tf_op jit(solution)/shard_map/ppermute | solution.py:31
  14.3 12.5 %collective-permute-start.7 = (bf16[9,6,32,128]{3,2,1,0:T(8,128)(2,1)S(1)}, bf16[9,6,32,128]{3,2,1,0:T(8,128)(2,1)S(1)}, u32[]{:S(2)}, u32[]{:S(2)}) collective-permute-start(bf16[9,6,32,128]{3,2,1,0:T(8,128)(2,1)S(1)} %pad_maximum_fusion), channel_id=1, source_target_pairs={{64,32},{65,33},{66,34},{67,35},{68,36},{69,37},{70,38},{71,39},{7... | collective-permute-start | bytes 1327112 | tf_op jit(solution)/shard_map/ppermute | solution.py:31
  15.6 2.0 %collective-permute-start.2 = (bf16[9,2,32,128]{3,2,1,0:T(8,128)(2,1)}, bf16[9,2,32,128]{3,2,1,0:T(8,128)(2,1)}, u32[]{:S(2)}, u32[]{:S(2)}) collective-permute-start(bf16[9,2,32,128]{3,2,1,0:T(8,128)(2,1)} %get-tuple-element.199), channel_id=1, source_target_pairs={{224,161},{225,162},{226,163},{227,164},{228,165},{229,166},{230,1... | collective-permute-start | bytes 442376 | tf_op jit(solution)/shard_map/ppermute | solution.py:31
  16.9 0.7 collective-permute-start.4
  17.6 0.7 copy-start.9
  18.2 9.8 %collective-permute-start.6 = (bf16[1728,128]{1,0:T(8,128)(2,1)}, bf16[1728,128]{1,0:T(8,128)(2,1)}, u32[]{:S(2)}, u32[]{:S(2)}) collective-permute-start(bf16[1728,128]{1,0:T(8,128)(2,1)} %collective-permute-done.5), channel_id=1, source_target_pairs={{32,33},{33,32},{34,35},{35,34},{36,37},{37,36},{38,39},{39,38},{4... | collective-permute-start | bytes 1327112 | tf_op jit(solution)/shard_map/ppermute | solution.py:277
  28.0 9.3 %collective-permute-start.8 = (bf16[9,6,32,128]{3,2,1,0:T(8,128)(2,1)S(1)}, bf16[9,6,32,128]{3,2,1,0:T(8,128)(2,1)S(1)}, u32[]{:S(2)}, u32[]{:S(2)}) collective-permute-start(bf16[9,6,32,128]{3,2,1,0:T(8,128)(2,1)S(1)} %pad_maximum_fusion), channel_id=1, source_target_pairs={{0,32},{1,33},{2,34},{3,35},{4,36},{5,37},{6,38},{7,39},{8,40},{9,... | collective-permute-start | bytes 1327112 | tf_op jit(solution)/shard_map/ppermute | solution.py:31
  28.0 10.5 %collective-permute-start.10 = (bf16[9,4,32,128]{3,2,1,0:T(8,128)(2,1)}, bf16[9,4,32,128]{3,2,1,0:T(8,128)(2,1)}, u32[]{:S(2)}, u32[]{:S(2)}) collective-permute-start(bf16[9,4,32,128]{3,2,1,0:T(8,128)(2,1)} %get-tuple-element.207), channel_id=1, source_target_pairs={{160,96},{161,97},{162,98},{163,99},{164,100},{165,101},{166,102},... | collective-permute-start | bytes 884744 | tf_op jit(solution)/shard_map/ppermute | solution.py:31
  29.4 9.0 %collective-permute-start.11 = (bf16[9,2,32,128]{3,2,1,0:T(8,128)(2,1)}, bf16[9,2,32,128]{3,2,1,0:T(8,128)(2,1)}, u32[]{:S(2)}, u32[]{:S(2)}) collective-permute-start(bf16[9,2,32,128]{3,2,1,0:T(8,128)(2,1)} %get-tuple-element.208), channel_id=1, source_target_pairs={{161,96},{162,97},{163,98},{164,99},{165,100},{166,101},{167,102},... | collective-permute-start | bytes 442376 | tf_op jit(solution)/shard_map/ppermute | solution.py:31
  30.7 7.7 %collective-permute-start.9 = (bf16[9,2,32,128]{3,2,1,0:T(8,128)(2,1)}, bf16[9,2,32,128]{3,2,1,0:T(8,128)(2,1)}, u32[]{:S(2)}, u32[]{:S(2)}) collective-permute-start(bf16[9,2,32,128]{3,2,1,0:T(8,128)(2,1)} %get-tuple-element.209), channel_id=1, source_target_pairs={{160,97},{161,98},{162,99},{163,100},{164,101},{165,102},{166,103}... | collective-permute-start | bytes 442376 | tf_op jit(solution)/shard_map/ppermute | solution.py:31
  38.5 7.2 %collective-permute-start.13 = (bf16[9,4,32,128]{3,2,1,0:T(8,128)(2,1)}, bf16[9,4,32,128]{3,2,1,0:T(8,128)(2,1)}, u32[]{:S(2)}, u32[]{:S(2)}) collective-permute-start(bf16[9,4,32,128]{3,2,1,0:T(8,128)(2,1)} %get-tuple-element.214), channel_id=1, source_target_pairs={{224,192},{225,193},{226,194},{227,195},{228,196},{229,197},{230,1... | collective-permute-start | bytes 884744 | tf_op jit(solution)/shard_map/ppermute | solution.py:31
  39.9 46.7 %collective-permute-start.16 = (bf16[9,4,32,128]{3,2,1,0:T(8,128)(2,1)}, bf16[9,4,32,128]{3,2,1,0:T(8,128)(2,1)}, u32[]{:S(2)}, u32[]{:S(2)}) collective-permute-start(bf16[9,4,32,128]{3,2,1,0:T(8,128)(2,1)} %get-tuple-element.214), channel_id=1, source_target_pairs={{96,32},{97,33},{98,34},{99,35},{100,36},{101,37},{102,38},{103,39... | collective-permute-start | bytes 884744 | tf_op jit(solution)/shard_map/ppermute | solution.py:31
  42.3 2.7 %collective-permute-start.12 = (bf16[9,1,32,128]{3,2,1,0:T(8,128)(2,1)S(1)}, bf16[9,1,32,128]{3,2,1,0:T(8,128)(2,1)S(1)}, u32[]{:S(2)}, u32[]{:S(2)}) collective-permute-start(bf16[9,1,32,128]{3,2,1,0:T(8,128)(2,1)S(1)} %get-tuple-element.229), channel_id=1, source_target_pairs={{224,193},{225,194},{226,195},{227,196},{228,197},{229,198},{230,1... | collective-permute-start | bytes 221192 | tf_op jit(solution)/shard_map/ppermute | solution.py:31
  43.0 3.7 %collective-permute-start.15 = (bf16[9,2,32,128]{3,2,1,0:T(8,128)(2,1)}, bf16[9,2,32,128]{3,2,1,0:T(8,128)(2,1)S(1)}, u32[]{:S(2)}, u32[]{:S(2)}) collective-permute-start(bf16[9,2,32,128]{3,2,1,0:T(8,128)(2,1)} %get-tuple-element.215), channel_id=1, source_target_pairs={{96,33},{97,34},{98,35},{99,36},{100,37},{101,38},{102,39},{103,40... | collective-permute-start | bytes 442376 | tf_op jit(solution)/shard_map/ppermute | solution.py:31
  43.7 42.9 %collective-permute-start.17 = (bf16[9,2,32,128]{3,2,1,0:T(8,128)(2,1)}, bf16[9,2,32,128]{3,2,1,0:T(8,128)(2,1)}, u32[]{:S(2)}, u32[]{:S(2)}) collective-permute-start(bf16[9,2,32,128]{3,2,1,0:T(8,128)(2,1)} %get-tuple-element.216), channel_id=1, source_target_pairs={{97,32},{98,33},{99,34},{100,35},{101,36},{102,37},{103,38},{104,3... | collective-permute-start | bytes 442376 | tf_op jit(solution)/shard_map/ppermute | solution.py:31
  45.0 0.7 collective-permute-start.14
  93.3 0.7 copy-start.7
  95.7 12.9 %copy-start.8 = (bf16[9,4,32,128]{3,2,1,0:T(8,128)(2,1)S(1)}, bf16[9,4,32,128]{3,2,1,0:T(8,128)(2,1)}, u32[]{:S(2)}) copy-start(bf16[9,4,32,128]{3,2,1,0:T(8,128)(2,1)} %copy-done.7) | copy-start | bytes 884740
  95.7 30.4 %copy-start.2 = (bf16[1,3,3,3,128,128]{5,4,3,2,1,0:T(8,128)(2,1)S(1)}, bf16[1,3,3,3,128,128]{5,4,3,2,1,0:T(8,128)(2,1)}, u32[]{:S(2)}) copy-start(bf16[1,3,3,3,128,128]{5,4,3,2,1,0:T(8,128)(2,1)} %param.17) | copy-start | bytes 2654212
  95.7 30.4 %copy-start.4 = (f32[9,4,32,128]{3,2,1,0:T(8,128)S(1)}, f32[9,4,32,128]{3,2,1,0:T(8,128)}, u32[]{:S(2)}) copy-start(f32[9,4,32,128]{3,2,1,0:T(8,128)} %copy-done.3) | copy-start | bytes 1769476
  95.8 2.0 %collective-permute-start.21 = (bf16[9,64,384]{2,1,0:T(8,128)(2,1)S(1)}, bf16[9,64,384]{2,1,0:T(8,128)(2,1)S(1)}, u32[]{:S(2)}, u32[]{:S(2)}) collective-permute-start(bf16[9,64,384]{2,1,0:T(8,128)(2,1)S(1)} %constant_dynamic-slice_fusion.5), channel_id=1, source_target_pairs={{0,1},{1,0},{2,3},{3,2},{4,5},{5,4},{6,7},{7,6},{8,9},{9,8},{10,11... | collective-permute-start | bytes 1327112 | tf_op jit(solution)/shard_map/ppermute | solution.py:329
  98.0 10.3 %collective-permute-start.22 = (bf16[9,32,384]{2,1,0:T(8,128)(2,1)S(1)}, bf16[9,32,384]{2,1,0:T(8,128)(2,1)S(1)}, u32[]{:S(2)}, u32[]{:S(2)}) collective-permute-start(bf16[9,32,384]{2,1,0:T(8,128)(2,1)S(1)} %constant_dynamic-slice_fusion.4), channel_id=1, source_target_pairs={{0,4},{1,5},{2,6},{3,7},{4,0},{5,1},{6,2},{7,3},{8,12},{9,13},{10,... | collective-permute-start | bytes 663560 | tf_op jit(solution)/shard_map/ppermute | solution.py:329
  108.4 7.4 %collective-permute-start.23 = (bf16[9,16,384]{2,1,0:T(8,128)(2,1)S(1)}, bf16[9,16,384]{2,1,0:T(8,128)(2,1)S(1)}, u32[]{:S(2)}, u32[]{:S(2)}) collective-permute-start(bf16[9,16,384]{2,1,0:T(8,128)(2,1)S(1)} %constant_dynamic-slice_fusion.3), channel_id=1, source_target_pairs={{0,2},{1,3},{2,0},{3,1},{4,6},{5,7},{6,4},{7,5},{8,10},{9,11},{10,... | collective-permute-start | bytes 331784 | tf_op jit(solution)/shard_map/ppermute | solution.py:329
  108.6 17.6 %collective-permute-start.19 = (bf16[9,4,32,128]{3,2,1,0:T(8,128)(2,1)S(1)}, bf16[9,4,32,128]{3,2,1,0:T(8,128)(2,1)S(1)}, u32[]{:S(2)}, u32[]{:S(2)}) collective-permute-start(bf16[9,4,32,128]{3,2,1,0:T(8,128)(2,1)S(1)} %copy-done.8), channel_id=1, source_target_pairs={{32,0},{33,1},{34,2},{35,3},{36,4},{37,5},{38,6},{39,7},{40,8},{41... | collective-permute-start | bytes 884744 | tf_op jit(solution)/shard_map/ppermute | solution.py:31
  115.9 9.1 %collective-permute-start.24 = (bf16[9,8,384]{2,1,0:T(8,128)(2,1)S(1)}, bf16[9,8,384]{2,1,0:T(8,128)(2,1)S(1)}, u32[]{:S(2)}, u32[]{:S(2)}) collective-permute-start(bf16[9,8,384]{2,1,0:T(8,128)(2,1)S(1)} %constant_dynamic-slice_fusion.2), channel_id=1, source_target_pairs={{0,8},{1,9},{2,10},{3,11},{4,12},{5,13},{6,14},{7,15},{8,0},{9,1},... | collective-permute-start | bytes 165896 | tf_op jit(solution)/shard_map/ppermute | solution.py:329
  122.9 3.3 %collective-permute-start.18 = (bf16[9,1,32,128]{3,2,1,0:T(8,128)(2,1)S(1)}, bf16[9,1,32,128]{3,2,1,0:T(8,128)(2,1)S(1)}, u32[]{:S(2)}, u32[]{:S(2)}) collective-permute-start(bf16[9,1,32,128]{3,2,1,0:T(8,128)(2,1)S(1)} %get-tuple-element.227), channel_id=1, source_target_pairs={{32,1},{33,2},{34,3},{35,4},{36,5},{37,6},{38,7},{39,8},{40,9},{41... | collective-permute-start | bytes 221192 | tf_op jit(solution)/shard_map/ppermute | solution.py:31
  124.2 2.0 %collective-permute-start.20 = (bf16[9,1,32,128]{3,2,1,0:T(8,128)(2,1)S(1)}, bf16[9,1,32,128]{3,2,1,0:T(8,128)(2,1)S(1)}, u32[]{:S(2)}, u32[]{:S(2)}) collective-permute-start(bf16[9,1,32,128]{3,2,1,0:T(8,128)(2,1)S(1)} %get-tuple-element.226), channel_id=1, source_target_pairs={{33,0},{34,1},{35,2},{36,3},{37,4},{38,5},{39,6},{40,7},{41,8},{42... | collective-permute-start | bytes 221192 | tf_op jit(solution)/shard_map/ppermute | solution.py:31
  125.1 4.8 %collective-permute-start.25 = (bf16[9,4,384]{2,1,0:T(4,128)(2,1)S(1)}, bf16[9,4,384]{2,1,0:T(4,128)(2,1)S(1)}, u32[]{:S(2)}, u32[]{:S(2)}) collective-permute-start(bf16[9,4,384]{2,1,0:T(4,128)(2,1)S(1)} %get-tuple-element.230), channel_id=1, source_target_pairs={{32,0},{33,1},{34,2},{35,3},{36,4},{37,5},{38,6},{39,7},{40,8},{41... | collective-permute-start | bytes 82952 | tf_op jit(solution)/shard_map/ppermute | solution.py:31
  125.2 9.6 %collective-permute-start.26 = (bf16[9,4,384]{2,1,0:T(4,128)(2,1)S(1)}, bf16[9,4,384]{2,1,0:T(4,128)(2,1)S(1)}, u32[]{:S(2)}, u32[]{:S(2)}) collective-permute-start(bf16[9,4,384]{2,1,0:T(4,128)(2,1)S(1)} %get-tuple-element.231), channel_id=1, source_target_pairs={{32,16},{33,17},{34,18},{35,19},{36,20},{37,21},{38,22},{39,23},{4... | collective-permute-start | bytes 82952 | tf_op jit(solution)/shard_map/ppermute | solution.py:329

commit v5 on v4

--- a/solution.py
+++ b/solution.py
@@ -14,11 +14,12 @@
 DP = 32
 SEC = 8
 FRAMES = 9
+CUT = 4
 ROWS = 4
 COLS = 32
 CH = 128
 AXES = ("section", "dp")
-HALVING = (1, 4, 2, 8, 16)
+HALVING = (1, 2, 4, 8, 16)
 
 
 def permute(value, hops):
@@ -55,12 +56,16 @@
     )
 
 
-def back_pass(x_ref, rhs, slope_ref, rows, emit):
-    group = 3
+def back_pass(x_ref, rhs, slope_ref, rows, first, emit, carry_in=None, carry_out=None):
     size = rows * COLS
-    one_later = None
-    two_later = None
-    for start in range(FRAMES - group, -1, -group):
+    count = x_ref.shape[0]
+    group = count if count <= 5 else 3
+    middle = lower = next_lower = None
+    if carry_in is not None:
+        middle, lower, next_lower = (
+            carry_in[:, n * CH : (n + 1) * CH] for n in range(3)
+        )
+    for start in range(count - group, -1, -group):
         lhs = jnp.concatenate(
             [x_ref[start : start + group, 2 - j : 2 - j + rows] for j in range(3)], axis=-1
         ).reshape(group * size, 9 * CH)
@@ -70,16 +75,26 @@
         for t in range(group - 1, -1, -1):
             here = part[t * size : (t + 1) * size]
             back = here[:, 2 * CH :]
-            if one_later is not None:
-                back = back + one_later[:, CH : 2 * CH]
-            if two_later is not None:
-                back = back + two_later[:, :CH]
+            if middle is not None:
+                back = back + middle
+            if lower is not None:
+                back = back + lower
             frame = start + t
             grad = x_ref[frame, 1 : 1 + rows, :, CH : 2 * CH].reshape(size, CH).astype(F32)
-            new = grad + slope_ref[frame].reshape(size, CH) * back
+            new = grad + slope_ref[first + frame].reshape(size, CH) * back
             emit(frame, new.astype(BF))
-            two_later = one_later
-            one_later = here
+            lower = next_lower
+            next_lower = here[:, :CH]
+            middle = here[:, CH : 2 * CH]
+    if carry_out is not None:
+        for n, value in enumerate((middle, lower, next_lower)):
+            carry_out[:, n * CH : (n + 1) * CH] = value
+
+
+def load(low_ref, own_ref, high_ref, x_ref):
+    for t in range(own_ref.shape[0]):
+        whole = jnp.concatenate([low_ref[t], own_ref[t], high_ref[t]], axis=0)
+        fill(x_ref, t, 0, whole.reshape(-1, CH).astype(F32))
 
 
 def emit_to(refs):
@@ -94,69 +109,128 @@
     return emit
 
 
-def single_kernel(low_ref, own_ref, high_ref, w_ref, slope_ref, *rest):
+def single_kernel(first, last, low_ref, own_ref, high_ref, w_ref, slope_ref, *rest):
     *outs, x_ref = rest
-    for t in range(FRAMES):
-        whole = jnp.concatenate([low_ref[t], own_ref[t], high_ref[t]], axis=0)
-        fill(x_ref, t, 0, whole.reshape(-1, CH).astype(F32))
-    back_pass(x_ref, weights(w_ref), slope_ref, ROWS, emit_to(outs))
+    load(low_ref, own_ref, high_ref, x_ref)
+    back_pass(x_ref, weights(w_ref), slope_ref, ROWS, first, emit_to(outs))
+
+
+def keep(flags_ref, previous, outs):
+    @pl.when(flags_ref[0] == 0)
+    def _():
+        for source, target in zip(previous, outs, strict=True):
+            target[...] = source[...]
+
+
+def first_kernel(first, flags_ref, low_ref, own_ref, high_ref, w_ref, slope_ref, *rest):
+    carry_in = carry_out = None
+    if first == 0:
+        carry_in, *rest = rest
+    *outs, x_ref = rest[3:]
+    if first > 0:
+        *outs, carry_out = outs
+    keep(flags_ref, rest[:3], outs)
+
+    @pl.when(flags_ref[0] == 1)
+    def _():
+        load(low_ref, own_ref, high_ref, x_ref)
+        back_pass(
+            x_ref, weights(w_ref), slope_ref, ROWS, first, emit_to(outs), carry_in, carry_out
+        )
 
 
 def double_kernel(
-    core_ref, low_ref, own_ref, high_ref, half_ref, other_ref, slope1_ref, w0_ref, slope0_ref, *rest
+    first,
+    flags_ref,
+    low_ref,
+    own_ref,
+    high_ref,
+    half_ref,
+    other_ref,
+    slope1_ref,
+    w0_ref,
+    slope0_ref,
+    *rest,
 ):
-    *outs, x1_ref, x0_ref, w1_ref = rest
-    half = half_ref.shape[0]
-    core = core_ref[0]
-    w1_ref[pl.ds(pl.multiple_of(core * half, half), half), :] = half_ref[...]
-    w1_ref[pl.ds(pl.multiple_of((1 - core) * half, half), half), :] = other_ref[...]
-    for t in range(FRAMES):
-        whole = jnp.concatenate([low_ref[t], own_ref[t], high_ref[t]], axis=0)
-        fill(x1_ref, t, 0, whole.reshape(-1, CH).astype(F32))
+    in1 = in0 = out1 = out0 = None
+    if first == 0:
+        in1, in0, *rest = rest
+    *outs, x1_ref, x0_ref, w1_ref = rest[3:]
+    if first > 0:
+        *outs, out1, out0 = outs
+    keep(flags_ref, rest[:3], outs)
 
     def emit_mid(frame, value):
         fill(x0_ref, frame, 0, value.astype(F32))
 
-    back_pass(x1_ref, weights(w1_ref), slope1_ref, ROWS + 2, emit_mid)
-    back_pass(x0_ref, weights(w0_ref), slope0_ref, ROWS, emit_to(outs))
+    @pl.when(flags_ref[0] == 1)
+    def _():
+        half = half_ref.shape[0]
+        core = flags_ref[1]
+        w1_ref[pl.ds(pl.multiple_of(core * half, half), half), :] = half_ref[...]
+        w1_ref[pl.ds(pl.multiple_of((1 - core) * half, half), half), :] = other_ref[...]
+        load(low_ref, own_ref, high_ref, x1_ref)
+        back_pass(x1_ref, weights(w1_ref), slope1_ref, ROWS + 2, first, emit_mid, in1, out1)
+        back_pass(x0_ref, weights(w0_ref), slope0_ref, ROWS, first, emit_to(outs), in0, out0)
 
 
 def in_vmem(count):
     return [pl.BlockSpec(memory_space=pltpu.VMEM)] * count
 
 
-def gradient_shapes():
-    return [
-        jax.ShapeDtypeStruct((FRAMES, rows, COLS, CH), BF) for rows in (ROWS, 2, 2)
-    ]
+def gradient_shapes(count):
+    return [jax.ShapeDtypeStruct((count, rows, COLS, CH), BF) for rows in (ROWS, 2, 2)]
+
+
+def work(rows):
+    positions = rows * COLS
+    return pl.CostEstimate(
+        flops=2 * positions * 27 * CH * CH * 3,
+        bytes_accessed=positions * CH * 8 + 27 * CH * CH * 2,
+        transcendentals=0,
+    )
+
+
+def carry_shape(rows):
+    return jax.ShapeDtypeStruct((rows * COLS, 3 * CH), F32)
 
 
 def single(low, own, high, w, slope):
     return pl.pallas_call(
-        single_kernel,
-        out_shape=gradient_shapes(),
+        functools.partial(single_kernel, 0, FRAMES),
+        out_shape=gradient_shapes(FRAMES),
         in_specs=in_vmem(5),
         out_specs=in_vmem(3),
         scratch_shapes=[pltpu.VMEM((FRAMES, ROWS + 2, COLS, 3 * CH), BF)],
         compiler_params=pltpu.CompilerParams(vmem_limit_bytes=24 << 20),
+        cost_estimate=work(FRAMES * ROWS),
         name="one_block",
     )(low, own, high, w, slope)
 
 
-def double(core, low, own, high, half, other, slope1, w0, slope0):
+def chain_call(kernel, name, first, last, live, core, operands, carry, previous, carries, rows):
+    count = last - first
+    out_shape = gradient_shapes(count)
+    if first:
+        out_shape += [carry_shape(r) for r in carries]
+    scratch = [
+        pltpu.VMEM((count, r + 2, COLS, 3 * CH), BF) for r in rows
+    ]
+    if len(rows) > 1:
+        scratch.append(pltpu.VMEM((27 * CH, CH), BF))
+    before = 1 + len(operands) + len(carry)
+    flags = jnp.stack([live.astype(jnp.int32), core.astype(jnp.int32)])
     return pl.pallas_call(
-        double_kernel,
-        out_shape=gradient_shapes(),
-        in_specs=[pl.BlockSpec(memory_space=pltpu.SMEM)] + in_vmem(8),
-        out_specs=in_vmem(3),
-        scratch_shapes=[
-            pltpu.VMEM((FRAMES, ROWS + 4, COLS, 3 * CH), BF),
-            pltpu.VMEM((FRAMES, ROWS + 2, COLS, 3 * CH), BF),
-            pltpu.VMEM((27 * CH, CH), BF),
-        ],
+        functools.partial(kernel, first),
+        out_shape=out_shape,
+        in_specs=[pl.BlockSpec(memory_space=pltpu.SMEM)] + in_vmem(before - 1 + 3),
+        out_specs=in_vmem(len(out_shape)),
+        scratch_shapes=scratch,
+        input_output_aliases={before + n: n for n in range(3)},
         compiler_params=pltpu.CompilerParams(vmem_limit_bytes=24 << 20),
-        name="two_blocks",
-    )(core.reshape(1), low, own, high, half, other, slope1, w0, slope0)
+        cost_estimate=work(count * sum(rows)),
+        name=f"{name}_{first}_{last}",
+    )(flags, *operands, *carry, *previous)
 
 
 def tap_rows_kernel(act_ref, order_ref, out_ref, u_ref):
@@ -189,8 +263,10 @@
     )(act6, order)
 
 
-def taps_kernel(scale, ut_ref, g_ref, out_ref):
-    grad = g_ref[...].reshape(FRAMES, ROWS * COLS, CH)
+def taps_kernel(scale, ut_ref, early_ref, late_ref, out_ref):
+    grad = jnp.concatenate([early_ref[...], late_ref[...]], axis=0).reshape(
+        FRAMES, ROWS * COLS, CH
+    )
     padded = jnp.concatenate([grad, jnp.zeros((2, ROWS * COLS, CH), BF)], axis=0)
     rhs = jnp.concatenate([padded[2 - i : 2 - i + FRAMES] for i in range(3)], axis=-1).reshape(
         FRAMES * ROWS * COLS, 3 * CH
@@ -202,15 +278,15 @@
         out_ref[taps_here] = (part * scale).astype(BF).reshape(3, CH, 3 * CH)
 
 
-def taps(ut, grad, scale):
+def taps(ut, early, late, scale):
     return pl.pallas_call(
         functools.partial(taps_kernel, scale),
         out_shape=jax.ShapeDtypeStruct((9, CH, 3 * CH), BF),
-        in_specs=in_vmem(2),
+        in_specs=in_vmem(3),
         out_specs=pl.BlockSpec(memory_space=pltpu.VMEM),
         compiler_params=pltpu.CompilerParams(vmem_limit_bytes=24 << 20),
         name="kernel_taps",
-    )(ut, grad)
+    )(ut, early, late)
 
 
 def channel_order():
@@ -257,23 +333,38 @@
     act6 = jnp.concatenate([edge_low[FRAMES:], acts[0], edge_high[FRAMES:]], axis=1)
 
     slope = slope_of(acts[0])
-    none = jnp.zeros((FRAMES, 2, COLS, CH), BF)
-    state = lax.cond(
-        me == 7,
-        lambda: tuple(single(low0, cotangent, high0, w, slope)),
-        lambda: (cotangent, none, none),
-    )
+    chunks = {"late": (CUT, FRAMES), "early": (0, CUT)}
+
+    def blank(count):
+        return tuple(jnp.zeros((count, 2, COLS, CH), BF) for _ in range(2))
+
+    def start_stage(name, carry):
+        first, last = chunks[name]
+        part = slice(first, last)
+        return chain_call(
+            first_kernel,
+            "first_block",
+            first,
+            last,
+            me == 7,
+            core,
+            (low0[part], cotangent[part], high0[part], w, slope),
+            carry,
+            (cotangent[part],) + blank(last - first),
+            (ROWS,),
+            (ROWS,),
+        )
 
     def hop(state, target):
-        result, top, bottom = state
+        result, top, bottom = state[:3]
         own = permute(result, [(target + 2, target, 0)])
         low = permute(bottom, [(target + 2, target, 1)])
         high = permute(top, [(target + 2, target, -1)])
         return low, own, high
 
-    act6, state = barrier((act6, state))
+    late7 = start_stage("late", ())
+    act6, w_half = barrier((act6, w_half))
     act_next = permute(act6, [(s + 1, s, 0) for s in pair])
-    arrived, w_half = barrier((hop(state, 5), w_half))
     w_other = lax.ppermute(
         w_half, AXES, [(s * DP + d, s * DP + (d ^ 1)) for s in pair for d in range(DP)]
     )
@@ -281,42 +372,74 @@
     inside = (row >= 0) & (row < DP * ROWS)
     slope_next = jnp.where(inside, slope_of(act_next), 0.0)
 
-    def stage(state, arrived, section):
-        low, own, high = arrived
-        return lax.cond(
+    def pair_stage(name, section, previous, arrived, carry):
+        first, last = chunks[name]
+        return chain_call(
+            double_kernel,
+            "two_blocks",
+            first,
+            last,
             me == section,
-            lambda: tuple(
-                double(core, low, own, high, w_half, w_other, slope_next, w, slope)
-            ),
-            lambda: state,
-        )
-
-    def even(result, sections):
+            core,
+            (*arrived, w_half, w_other, slope_next, w, slope),
+            carry,
+            tuple(previous[:3]),
+            (ROWS + 2, ROWS),
+            (ROWS + 2, ROWS),
+        )
+
+    def even(early, late, sections):
         hops = [(s + 1, s) for s in sections]
-        own = permute(result, [(a, b, 0) for a, b in hops])
-        low = permute(result[:, -1:], [(a, b, 1) for a, b in hops])
-        high = permute(result[:, :1], [(a, b, -1) for a, b in hops])
+        own, top, bottom = (
+            jnp.concatenate([a, b], axis=0) for a, b in zip(early[:3], late[:3], strict=True)
+        )
+        own = permute(own, [(a, b, 0) for a, b in hops])
+        low = permute(bottom[:, 1:], [(a, b, 1) for a, b in hops])
+        high = permute(top[:, :1], [(a, b, -1) for a, b in hops])
         live = functools.reduce(jnp.logical_or, [me == s for s in sections])
-        return lax.cond(
-            live,
-            lambda: single(low, own, high, w, slope)[0],
-            lambda: result,
-        )
-
-    state = stage(state, arrived, 5)
-    act6, state = barrier((act6, state))
-    arrived = hop(state, 3)
+
+        def run():
+            new = single(low, own, high, w, slope)[0]
+            return new[:CUT], new[CUT:]
+
+        return lax.cond(live, run, lambda: (early[0], late[0]))
+
+    late_in = hop(late7, 5)
+    late5 = pair_stage("late", 5, late7, late_in, ())
+    carry, late5 = barrier((late7[3:], late5))
+    early7 = start_stage("early", carry)
+    early_in = hop(early7, 5)
+
+    late_in = hop(late5, 3)
     act_prev = permute(act6, [(s, (s + 1) % SEC, 0) for s in every])
     ut = tap_rows(act_prev, jnp.asarray(channel_order(), BF))
-    ut, arrived = barrier((ut, arrived))
-    state = stage(state, arrived, 3)
-    arrived = hop(state, 1)
-    result = even(state[0], (6, 4, 2))
-    result, arrived = barrier((result, arrived))
-    result, _, _ = stage((result, state[1], state[2]), arrived, 1)
-    final = even(result, (0,))
-
-    part = taps(ut, jnp.where(me == 0, cotangent, result), scale)
+    ut, late_in = barrier((ut, late_in))
+    late3 = pair_stage("late", 3, late5, late_in, ())
+    carry, late3 = barrier((late5[3:], late3))
+    early5 = pair_stage("early", 5, early7, early_in, carry)
+    early_in = hop(early5, 3)
+
+    late_in = hop(late3, 1)
+    late1 = pair_stage("late", 1, late3, late_in, ())
+    carry, late1 = barrier((late3[3:], late1))
+    early3 = pair_stage("early", 3, early5, early_in, carry)
+    early_in = hop(early3, 1)
+
+    early_even, late_even = even(early3, late3, (6, 4, 2))
+    early_even, early_in = barrier((early_even, early_in))
+    early1 = pair_stage("early", 1, early3, early_in, late1[3:])
+
+    early = lax.select(me % 2 == 1, early1[0], early_even)
+    late = lax.select(me % 2 == 1, late1[0], late_even)
+    is_first = me == 0
+    part = taps(
+        ut,
+        jnp.where(is_first, cotangent[:CUT], early),
+        jnp.where(is_first, cotangent[CUT:], late),
+        scale,
+    )
+    early, late = even((early, *early1[1:3]), (late, *late1[1:3]), (0,))
+    final = jnp.concatenate([early, late], axis=0)
     for bit in HALVING:
         size = part.shape[1] // 2
         mine = (dp // bit) % 2

time: 137 us -> 153 us (1.12)
  waiting for transfers between devices: 72.3 us -> 57.2 us
  other arithmetic: 3.84 us -> 12.6 us
  Pallas kernels: 9.49 us -> 18.2 us
  starting transfers between devices: 41.5 us -> 48.5 us
  local copies, waits for them, and re-layouts: 7.09 us -> 13 us
    ppermute x21 -> x30, waiting for transfers between devices: 53.9 us -> 44.9 us  [permute(): return lax.ppermute(value, AXES, pairs)]
    pallas_call x1 -> x8, Pallas kernels: 6.76 us -> 15.5 us  [chain_call(): pl.pallas_call(functools.partial(kernel, first), out_shape=out_shape, in_...]
    concatenate x0 -> x7, other arithmetic: none -> 6.47 us  [the longest x6 5.38 us: even(): jnp.concatenate([a, b], axis=0)]
    unnamed x20 -> x73, local copies, waits for them, and re-layouts: 1.16 us -> 7.34 us
    ppermute x5, waiting for transfers between devices: 18.4 us -> 12.3 us  [local(): lax.ppermute(give, AXES, [((s + shift) % SEC * DP + d, s * DP + (d ^ bit)...]
    ppermute x21 -> x30, starting transfers between devices: 21.9 us -> 27.4 us  [permute(): return lax.ppermute(value, AXES, pairs)]
    ppermute x5, starting transfers between devices: 12.1 us -> 17.3 us  [local(): lax.ppermute(give, AXES, [((s + shift) % SEC * DP + d, s * DP + (d ^ bit)...]
    ppermute x1, starting transfers between devices: 7.46 us -> 3.81 us  [local(): lax.ppermute(w_half, AXES, [(s * DP + d, s * DP + (d ^ 1)) for s in pair...]
  transfers between devices with their start and end apart: 27 -> 36, of which waited for: 12 -> 11; matrix products, arithmetic and copies ran while one was open for 6% -> 9% of each run, Pallas kernels for 1% -> 7%
where the time goes in v5:
time: 153 us; the launch traced here: 151 us
  waiting for transfers between devices  57.2 us (37%)
  starting transfers between devices  48.5 us (32%)
  Pallas kernels  18.2 us (12%)
  local copies, waits for them, and re-layouts  13 us (8%)
  other arithmetic  12.6 us (8%)
  between operations  1.54 us (1%)
    ppermute x30, waiting for transfers between devices, permute(): return lax.ppermute(value, AXES, pairs)  44.9 us
    ppermute x30, starting transfers between devices, permute(): return lax.ppermute(value, AXES, pairs)  27.4 us
    ppermute x5, starting transfers between devices, local(): lax.ppermute(give, AXES, [((s + shift) % SEC * DP + d, s * DP + (d ^ bit)...  17.3 us
    pallas_call x8, Pallas kernels, chain_call(): pl.pallas_call(functools.partial(kernel, first), out_shape=out_shape, in_...  15.5 us
    ppermute x5, waiting for transfers between devices, local(): lax.ppermute(give, AXES, [((s + shift) % SEC * DP + d, s * DP + (d ^ bit)...  12.3 us
    unnamed x73, local copies, waits for them, and re-layouts  7.34 us
    concatenate x6, other arithmetic, even(): jnp.concatenate([a, b], axis=0)  5.38 us
    ppermute x1, starting transfers between devices, local(): lax.ppermute(w_half, AXES, [(s * DP + d, s * DP + (d ^ 1)) for s in pair...  3.81 us
  transfers between devices with their start and end apart: 36, of which 11 were waited for; matrix products, arithmetic and copies ran while one was open for 9% of the time, Pallas kernels for 7%

profile of v5, /device:TPU:8, one launch (start us, length us, event | category | flops | bytes accessed | tf_op | source)
XLA Modules:
  0.0 151.3 jit_solution(4176453767706486119)
XLA Ops:
  0.7 1.1 pad_maximum_fusion.3
  1.7 1.7 %collective-permute-start = (bf16[18,1,32,128]{3,2,1,0:T(8,128)(2,1)S(1)}, bf16[18,1,32,128]{3,2,1,0:T(8,128)(2,1)S(1)}, u32[]{:S(2)}, u32[]{:S(2)}) collective-permute-start(bf16[18,1,32,128]{3,2,1,0:T(8,128)(2,1)S(1)} %get-tuple-element.177), channel_id=1, source_target_pairs={{0,1},{1,2},{2,3},{3,4},{4,5},{5,6},{6,7},{7,8},{8,9},{9,10},{10,1... | collective-permute-start | bytes 442376 | tf_op jit(solution)/shard_map/ppermute | solution.py:32
  3.5 1.3 collective-permute-start.1
  4.8 1.0 constant_dynamic-slice_fusion.6
  5.9 1.3 collective-permute-start.5
  7.2 1.2 fusion.10.slope_ref.slope0_ref
  9.0 12.2 %collective-permute-done.5.half_ref = bf16[1728,128]{1,0:T(8,128)(2,1)S(1)} collective-permute-done((bf16[1728,128]{1,0:T(8,128)(2,1)S(1)}, bf16[1728,128]{1,0:T(8,128)(2,1)S(1)}, u32[]{:S(2)}, u32[]{:S(2)}) %collective-permute-start.5) | collective-permute-done | bytes 442400 | tf_op jit(solution)/shard_map/ppermute | solution.py:32
  21.2 1.3 collective-permute-start.7
  22.6 3.8 %collective-permute-start.6 = (bf16[1728,128]{1,0:T(8,128)(2,1)S(1)}, bf16[1728,128]{1,0:T(8,128)(2,1)S(1)}, u32[]{:S(2)}, u32[]{:S(2)}) collective-permute-start(bf16[1728,128]{1,0:T(8,128)(2,1)S(1)} %collective-permute-done.5.half_ref), channel_id=1, source_target_pairs={{32,33},{33,32},{34,35},{35,34},{36,37},{37,36},{38,39},{39,38},{4... | collective-permute-start | bytes 1327112 | tf_op jit(solution)/shard_map/ppermute | solution.py:368
  26.6 1.4 first_block_4_9.1
  28.0 0.7 collective-permute-start.2
  28.7 0.7 collective-permute-start.3
  29.3 0.7 collective-permute-start.4
  30.0 6.2 %collective-permute-done.7 = bf16[9,6,32,128]{3,2,1,0:T(8,128)(2,1)} collective-permute-done((bf16[9,6,32,128]{3,2,1,0:T(8,128)(2,1)S(1)}, bf16[9,6,32,128]{3,2,1,0:T(8,128)(2,1)}, u32[]{:S(2)}, u32[]{:S(2)}) %collective-permute-start.7) | collective-permute-done | bytes 442400 | tf_op jit(solution)/shard_map/ppermute | solution.py:32
  36.2 1.3 fusion.5.slope1_ref
  39.8 0.8 slice.78.low_ref
  40.5 0.8 slice.79.high_ref
  42.0 0.7 collective-permute-start.14
  43.9 1.7 %first_block_0_4.1 = (bf16[4,4,32,128]{3,2,1,0:T(8,128)(2,1)}, bf16[4,2,32,128]{3,2,1,0:T(8,128)(2,1)}, bf16[4,2,32,128]{3,2,1,0:T(8,128)(2,1)}) custom-call(s32[2]{0:T(128)S(1)} %pad_add_fusion.3.flags_ref, bf16[4,1,32,128]{3,2,1,0:T(8,128)(2,1)S(1)} %slice.78.low_ref, ...), custom_call_target="tpu_custom_call", output_to_operand_aliasing={{0}: (7, {}), {1}: (8, {}), {2}: (9, {})} | custom-call | flops 1358954496 | bytes 1409024 | tf_op jit(solution)/shard_map/first_block_0_4/pallas_call | solution.py:223
  45.6 0.8 collective-permute-start.8
  46.4 2.6 %collective-permute-done.11.act_ref = bf16[9,6,32,128]{3,2,1,0:T(8,128)(2,1)S(1)} collective-permute-done((bf16[9,6,32,128]{3,2,1,0:T(8,128)(2,1)S(1)}, bf16[9,6,32,128]{3,2,1,0:T(8,128)(2,1)S(1)}, u32[]{:S(2)}, u32[]{:S(2)}) %collective-permute-start.11) | collective-permute-done | bytes 442400 | tf_op jit(solution)/shard_map/ppermute | solution.py:32
  49.7 1.1 tap_rows.1.ut_ref
  52.2 0.7 collective-permute-start.18
  52.9 1.3 collective-permute-start.19
  54.2 1.3 collective-permute-start.20
  55.5 1.7 %two_blocks_0_4.3 = (bf16[4,4,32,128]{3,2,1,0:T(8,128)(2,1)}, bf16[4,2,32,128]{3,2,1,0:T(8,128)(2,1)}, bf16[4,2,32,128]{3,2,1,0:T(8,128)(2,1)}) custom-call(s32[2]{0:T(128)S(1)} %pad_add_fusion.2.flags_ref, bf16[4,2,32,128]{3,2,1,0:T(8,128)(2,1)S(1)} %collective-permute-done.8.low_ref, ...), custom_call_target="tpu_custom_call", output_to_operand_aliasing={{0}: (11, {}), {1}: (12, {}), {2}: (13, {})} | custom-call | flops 3397386240 | bytes 2195456 | tf_op jit(solution)/shard_map/two_blocks_0_4/pallas_call | solution.py:223
  58.0 0.7 collective-permute-start.16
  59.3 10.2 %collective-permute-done.20.high_ref = bf16[5,2,32,128]{3,2,1,0:T(8,128)(2,1)S(1)} collective-permute-done((bf16[5,2,32,128]{3,2,1,0:T(8,128)(2,1)S(1)}, bf16[5,2,32,128]{3,2,1,0:T(8,128)(2,1)S(1)}, u32[]{:S(2)}, u32[]{:S(2)}) %collective-permute-start.20) | collective-permute-done | bytes 81952 | tf_op jit(solution)/shard_map/ppermute | solution.py:32
  69.5 3.3 %two_blocks_4_9.5 = (bf16[5,4,32,128]{3,2,1,0:T(8,128)(2,1)S(1)}, bf16[5,2,32,128]{3,2,1,0:T(8,128)(2,1)S(1)}, bf16[5,2,32,128]{3,2,1,0:T(8,128)(2,1)S(1)}, f32[192,384]{1,0:T(8,128)S(1)}, f32[128,384]{1,0:T(8,128)S(1)}) custom-call(s32[2]{0:T(128)S(1)} %pad_add_fusion.flags_ref, ...), custom_call_target="tpu_custom_call", output_to_operand_aliasing={{0}: (9, {}), {1}: (10, {}), {2}: (11, {})} | custom-call | flops 4246732800 | bytes 2523136 | tf_op jit(solution)/shard_map/two_blocks_4_9/pallas_call | solution.py:223
  74.7 1.9 %two_blocks_0_4.4 = (bf16[4,4,32,128]{3,2,1,0:T(8,128)(2,1)}, bf16[4,2,32,128]{3,2,1,0:T(8,128)(2,1)}, bf16[4,2,32,128]{3,2,1,0:T(8,128)(2,1)}) custom-call(s32[2]{0:T(128)S(1)} %pad_add_fusion.1.flags_ref, bf16[4,2,32,128]{3,2,1,0:T(8,128)(2,1)S(1)} %collective-permute-done.15.low_ref, ...), custom_call_target="tpu_custom_call", output_to_operand_aliasing={{0}: (11, {}), {1}: (12, {}), {2}: (13, {})} | custom-call | flops 3397386240 | bytes 2195456 | tf_op jit(solution)/shard_map/two_blocks_0_4/pallas_call | solution.py:223
  76.6 1.6 %pad_maximum_fusion.1 = bf16[9,4,32,128]{3,2,1,0:T(8,128)(2,1)} fusion(bf16[5,4,32,128]{3,2,1,0:T(8,128)(2,1)S(1)} %get-tuple-element.143, bf16[4,4,32,128]{3,2,1,0:T(8,128)(2,1)} %get-tuple-element.152.rest_2_), kind=kLoop, calls=%fused_computation.18 | loop fusion | flops 147456 | bytes 589824 | tf_op jit(solution)/shard_map/concatenate | solution.py:394
  78.2 1.3 collective-permute-start.25
  79.5 1.4 collective-permute-start.22
  80.9 0.8 pad_maximum_fusion.8
  82.4 1.4 pad_maximum_fusion.7
  83.8 1.3 collective-permute-start.23
  85.1 1.3 collective-permute-start.24
  87.0 1.3 collective-permute-start.26
  88.3 0.9 conditional.2
  88.3 0.9 copy.53
  89.2 13.2 %collective-permute-done.26.high_ref = bf16[4,2,32,128]{3,2,1,0:T(8,128)(2,1)} collective-permute-done((bf16[4,2,32,128]{3,2,1,0:T(8,128)(2,1)}, bf16[4,2,32,128]{3,2,1,0:T(8,128)(2,1)}, u32[]{:S(2)}, u32[]{:S(2)}) %collective-permute-start.26) | collective-permute-done | bytes 65568 | tf_op jit(solution)/shard_map/ppermute | solution.py:32
  102.5 1.0 copy-done.9
  103.5 1.0 copy-done.12
  104.5 1.0 copy-done.14
  105.5 0.9 copy-done.16
  106.4 4.4 %two_blocks_0_4.5 = (bf16[4,4,32,128]{3,2,1,0:T(8,128)(2,1)}, bf16[4,2,32,128]{3,2,1,0:T(8,128)(2,1)}, bf16[4,2,32,128]{3,2,1,0:T(8,128)(2,1)}) custom-call(s32[2]{0:T(128)S(1)} %pad_add_fusion.flags_ref, bf16[4,2,32,128]{3,2,1,0:T(8,128)(2,1)} %collective-permute-done.24.low_ref, ...), custom_call_target="tpu_custom_call", output_to_operand_aliasing={{0}: (11, {}), {1}: (12, {}), {2}: (13, {})} | custom-call | flops 3397386240 | bytes 2195456 | tf_op jit(solution)/shard_map/two_blocks_0_4/pallas_call | solution.py:223
  110.8 1.6 %broadcast_select_fusion.2 = (bf16[4,4,32,128]{3,2,1,0:T(8,128)(2,1)S(1)}, bf16[4,4,32,128]{3,2,1,0:T(8,128)(2,1)}) fusion(pred[]{:T(512)S(6)} %eq.42, bf16[9,4,32,128]{3,2,1,0:T(8,128)(2,1)S(1)} %copy-done.19, bf16[4,4,32,128]{3,2,1,0:T(8,128)(2,1)} %get-tuple-element.161, bf16[4,4,32,128]{3,2,1,0:T(8,128)(2,1)S(1)} %copy-done.28, pred[]{:T(512)S(6)} %eq.43), kind=kLoop, calls=%fused_computation.26 | loop fusion | flops 131072 | bytes 655362 | tf_op jit(solution)/shard_map/jit(_where)/select_n | solution.py:437
  112.4 0.7 broadcast_select_fusion
  113.1 1.6 %kernel_taps.1 = bf16[9,128,384]{2,1,0:T(8,128)(2,1)S(1)} custom-call(bf16[9,128,1152]{2,1,0:T(8,128)(2,1)S(1)} %tap_rows.1.ut_ref, bf16[4,4,32,128]{3,2,1,0:T(8,128)(2,1)S(1)} %get-tuple-element.174.early_ref, bf16[5,4,32,128]{3,2,1,0:T(8,128)(2,1)S(1)} %get-tuple-element.172.late_ref), custom_call_target="tpu_custom_call" | custom-call | tf_op jit(solution)/shard_map/kernel_taps/pallas_call | solution.py:282
  114.8 1.6 %collective-permute-start.30 = (bf16[9,64,384]{2,1,0:T(8,128)(2,1)S(1)}, bf16[9,64,384]{2,1,0:T(8,128)(2,1)S(1)}, u32[]{:S(2)}, u32[]{:S(2)}) collective-permute-start(bf16[9,64,384]{2,1,0:T(8,128)(2,1)S(1)} %constant_dynamic-slice_fusion.5), channel_id=1, source_target_pairs={{0,1},{1,0},{2,3},{3,2},{4,5},{5,4},{6,7},{7,6},{8,9},{9,8},{10,11... | collective-permute-start | bytes 1327112 | tf_op jit(solution)/shard_map/ppermute | solution.py:452
  116.4 1.4 collective-permute-done.30
  118.0 3.5 %collective-permute-start.31 = (bf16[9,32,384]{2,1,0:T(8,128)(2,1)S(1)}, bf16[9,32,384]{2,1,0:T(8,128)(2,1)S(1)}, u32[]{:S(2)}, u32[]{:S(2)}) collective-permute-start(bf16[9,32,384]{2,1,0:T(8,128)(2,1)S(1)} %constant_dynamic-slice_fusion.4), channel_id=1, source_target_pairs={{0,2},{1,3},{2,0},{3,1},{4,6},{5,7},{6,4},{7,5},{8,10},{9,11},{10,... | collective-permute-start | bytes 663560 | tf_op jit(solution)/shard_map/ppermute | solution.py:452
  121.5 0.8 pad_maximum_fusion.6
  122.3 1.3 collective-permute-start.27
  123.6 1.3 collective-permute-start.28
  124.9 2.9 %collective-permute-done.31 = bf16[9,32,384]{2,1,0:T(8,128)(2,1)S(1)} collective-permute-done((bf16[9,32,384]{2,1,0:T(8,128)(2,1)S(1)}, bf16[9,32,384]{2,1,0:T(8,128)(2,1)S(1)}, u32[]{:S(2)}, u32[]{:S(2)}) %collective-permute-start.31) | collective-permute-done | bytes 221216 | tf_op jit(solution)/shard_map/ppermute | solution.py:452
  127.9 2.7 %collective-permute-start.32 = (bf16[9,16,384]{2,1,0:T(8,128)(2,1)S(1)}, bf16[9,16,384]{2,1,0:T(8,128)(2,1)S(1)}, u32[]{:S(2)}, u32[]{:S(2)}) collective-permute-start(bf16[9,16,384]{2,1,0:T(8,128)(2,1)S(1)} %constant_dynamic-slice_fusion.3), channel_id=1, source_target_pairs={{0,4},{1,5},{2,6},{3,7},{4,0},{5,1},{6,2},{7,3},{8,12},{9,13},{10,... | collective-permute-start | bytes 331784 | tf_op jit(solution)/shard_map/ppermute | solution.py:452
  130.7 0.8 pad_maximum_fusion.5
  132.1 1.3 collective-permute-done.32
  133.5 5.1 %collective-permute-start.33 = (bf16[9,8,384]{2,1,0:T(8,128)(2,1)S(1)}, bf16[9,8,384]{2,1,0:T(8,128)(2,1)S(1)}, u32[]{:S(2)}, u32[]{:S(2)}) collective-permute-start(bf16[9,8,384]{2,1,0:T(8,128)(2,1)S(1)} %constant_dynamic-slice_fusion.2), channel_id=1, source_target_pairs={{0,8},{1,9},{2,10},{3,11},{4,12},{5,13},{6,14},{7,15},{8,0},{9,1},... | collective-permute-start | bytes 165896 | tf_op jit(solution)/shard_map/ppermute | solution.py:452
  138.8 2.1 %collective-permute-done.33 = bf16[9,8,384]{2,1,0:T(8,128)(2,1)S(1)} collective-permute-done((bf16[9,8,384]{2,1,0:T(8,128)(2,1)S(1)}, bf16[9,8,384]{2,1,0:T(8,128)(2,1)S(1)}, u32[]{:S(2)}, u32[]{:S(2)}) %collective-permute-start.33) | collective-permute-done | bytes 55328 | tf_op jit(solution)/shard_map/ppermute | solution.py:452
  141.0 4.4 %collective-permute-start.35 = (bf16[9,4,384]{2,1,0:T(4,128)(2,1)S(1)}, bf16[9,4,384]{2,1,0:T(4,128)(2,1)S(1)}, u32[]{:S(2)}, u32[]{:S(2)}) collective-permute-start(bf16[9,4,384]{2,1,0:T(4,128)(2,1)S(1)} %get-tuple-element.179), channel_id=1, source_target_pairs={{32,16},{33,17},{34,18},{35,19},{36,20},{37,21},{38,22},{39,23},{4... | collective-permute-start | bytes 82952 | tf_op jit(solution)/shard_map/ppermute | solution.py:452
  145.5 0.7 maximum_bitcast_fusion
  146.2 4.5 %collective-permute-done.35 = bf16[9,4,384]{2,1,0:T(4,128)(2,1)S(1)} collective-permute-done((bf16[9,4,384]{2,1,0:T(4,128)(2,1)S(1)}, bf16[9,4,384]{2,1,0:T(4,128)(2,1)S(1)}, u32[]{:S(2)}, u32[]{:S(2)}) %collective-permute-start.35) | collective-permute-done | bytes 27680 | tf_op jit(solution)/shard_map/ppermute | solution.py:452
  (136 shorter events, 13.5 us)
Async XLA Ops:
  0.6 25.8 %copy-start.18 = (bf16[9,4,32,128]{3,2,1,0:T(8,128)(2,1)S(1)}, bf16[9,4,32,128]{3,2,1,0:T(8,128)(2,1)}, u32[]{:S(2)}) copy-start(bf16[9,4,32,128]{3,2,1,0:T(8,128)(2,1)} %param.10) | copy-start | bytes 884740
  0.6 8.2 %copy-start.17 = (bf16[1,9,4,32,128]{4,3,2,1,0:T(8,128)(2,1)S(1)}, bf16[1,9,4,32,128]{4,3,2,1,0:T(8,128)(2,1)}, u32[]{:S(2)}) copy-start(bf16[1,9,4,32,128]{4,3,2,1,0:T(8,128)(2,1)} %param.8) | copy-start | bytes 884740
  1.7 7.1 %collective-permute-start = (bf16[18,1,32,128]{3,2,1,0:T(8,128)(2,1)S(1)}, bf16[18,1,32,128]{3,2,1,0:T(8,128)(2,1)S(1)}, u32[]{:S(2)}, u32[]{:S(2)}) collective-permute-start(bf16[18,1,32,128]{3,2,1,0:T(8,128)(2,1)S(1)} %get-tuple-element.177), channel_id=1, source_target_pairs={{0,1},{1,2},{2,3},{3,4},{4,5},{5,6},{6,7},{7,8},{8,9},{9,10},{10,1... | collective-permute-start | bytes 442376 | tf_op jit(solution)/shard_map/ppermute | solution.py:32
  3.5 5.3 %collective-permute-start.1 = (bf16[18,1,32,128]{3,2,1,0:T(8,128)(2,1)S(1)}, bf16[18,1,32,128]{3,2,1,0:T(8,128)(2,1)S(1)}, u32[]{:S(2)}, u32[]{:S(2)}) collective-permute-start(bf16[18,1,32,128]{3,2,1,0:T(8,128)(2,1)S(1)} %get-tuple-element.176), channel_id=1, source_target_pairs={{1,0},{2,1},{3,2},{4,3},{5,4},{6,5},{7,6},{8,7},{9,8},{10,9},{11,1... | collective-permute-start | bytes 442376 | tf_op jit(solution)/shard_map/ppermute | solution.py:32
  5.9 15.3 %collective-permute-start.5 = (bf16[1728,128]{1,0:T(8,128)(2,1)S(1)}, bf16[1728,128]{1,0:T(8,128)(2,1)S(1)}, u32[]{:S(2)}, u32[]{:S(2)}) collective-permute-start(bf16[1728,128]{1,0:T(8,128)(2,1)S(1)} %constant_dynamic-slice_fusion.6), channel_id=1, source_target_pairs={{64,32},{65,33},{66,34},{67,35},{68,36},{69,37},{70,38},{71,39},{7... | collective-permute-start | bytes 1327112 | tf_op jit(solution)/shard_map/ppermute | solution.py:32
  8.3 35.6 %copy-start.24 = (f32[9,4,32,128]{3,2,1,0:T(8,128)}, f32[9,4,32,128]{3,2,1,0:T(8,128)S(1)}, u32[]{:S(2)}) copy-start(f32[9,4,32,128]{3,2,1,0:T(8,128)S(1)} %fusion.10.slope_ref.slope0_ref) | copy-start | bytes 1769476
  8.8 19.1 %copy-start.32 = (bf16[18,1,32,128]{3,2,1,0:T(8,128)(2,1)}, bf16[18,1,32,128]{3,2,1,0:T(8,128)(2,1)S(1)}, u32[]{:S(2)}) copy-start(bf16[18,1,32,128]{3,2,1,0:T(8,128)(2,1)S(1)} %collective-permute-done.1) | copy-start | bytes 442372
  8.9 19.1 %copy-start.31 = (bf16[18,1,32,128]{3,2,1,0:T(8,128)(2,1)}, bf16[18,1,32,128]{3,2,1,0:T(8,128)(2,1)S(1)}, u32[]{:S(2)}) copy-start(bf16[18,1,32,128]{3,2,1,0:T(8,128)(2,1)S(1)} %collective-permute-done) | copy-start | bytes 442372
  21.2 16.4 %copy-start.7 = (bf16[1728,128]{1,0:T(8,128)(2,1)}, bf16[1728,128]{1,0:T(8,128)(2,1)S(1)}, u32[]{:S(2)}) copy-start(bf16[1728,128]{1,0:T(8,128)(2,1)S(1)} %collective-permute-done.5.half_ref) | copy-start | bytes 1327108
  21.2 15.0 %collective-permute-start.7 = (bf16[9,6,32,128]{3,2,1,0:T(8,128)(2,1)S(1)}, bf16[9,6,32,128]{3,2,1,0:T(8,128)(2,1)}, u32[]{:S(2)}, u32[]{:S(2)}) collective-permute-start(bf16[9,6,32,128]{3,2,1,0:T(8,128)(2,1)S(1)} %pad_maximum_fusion), channel_id=1, source_target_pairs={{64,32},{65,33},{66,34},{67,35},{68,36},{69,37},{70,38},{71,39},{7... | collective-permute-start | bytes 1327112 | tf_op jit(solution)/shard_map/ppermute | solution.py:32
  22.6 14.9 %collective-permute-start.6 = (bf16[1728,128]{1,0:T(8,128)(2,1)S(1)}, bf16[1728,128]{1,0:T(8,128)(2,1)S(1)}, u32[]{:S(2)}, u32[]{:S(2)}) collective-permute-start(bf16[1728,128]{1,0:T(8,128)(2,1)S(1)} %collective-permute-done.5.half_ref), channel_id=1, source_target_pairs={{32,33},{33,32},{34,35},{35,34},{36,37},{37,36},{38,39},{39,38},{4... | collective-permute-start | bytes 1327112 | tf_op jit(solution)/shard_map/ppermute | solution.py:368
  26.6 11.0 %copy-start.29 = (bf16[1,3,3,3,128,128]{5,4,3,2,1,0:T(8,128)(2,1)S(1)}, bf16[1,3,3,3,128,128]{5,4,3,2,1,0:T(8,128)(2,1)}, u32[]{:S(2)}) copy-start(bf16[1,3,3,3,128,128]{5,4,3,2,1,0:T(8,128)(2,1)} %param.9) | copy-start | bytes 2654212
  28.0 9.6 %collective-permute-start.2 = (bf16[5,2,32,128]{3,2,1,0:T(8,128)(2,1)S(1)}, bf16[5,2,32,128]{3,2,1,0:T(8,128)(2,1)S(1)}, u32[]{:S(2)}, u32[]{:S(2)}) collective-permute-start(bf16[5,2,32,128]{3,2,1,0:T(8,128)(2,1)S(1)} %get-tuple-element.108.rest_2_), channel_id=1, source_target_pairs={{224,161},{225,162},{226,163},{227,164},{228,165},{229,166},{230,1... | collective-permute-start | bytes 245768 | tf_op jit(solution)/shard_map/ppermute | solution.py:32
  28.7 8.9 %collective-permute-start.3 = (bf16[5,4,32,128]{3,2,1,0:T(8,128)(2,1)S(1)}, bf16[5,4,32,128]{3,2,1,0:T(8,128)(2,1)S(1)}, u32[]{:S(2)}, u32[]{:S(2)}) collective-permute-start(bf16[5,4,32,128]{3,2,1,0:T(8,128)(2,1)S(1)} %get-tuple-element.109.rest_0_), channel_id=1, source_target_pairs={{224,160},{225,161},{226,162},{227,163},{228,164},{229,165},{230,1... | collective-permute-start | bytes 491528 | tf_op jit(solution)/shard_map/ppermute | solution.py:32
  29.3 8.2 %collective-permute-start.4 = (bf16[5,2,32,128]{3,2,1,0:T(8,128)(2,1)S(1)}, bf16[5,2,32,128]{3,2,1,0:T(8,128)(2,1)S(1)}, u32[]{:S(2)}, u32[]{:S(2)}) collective-permute-start(bf16[5,2,32,128]{3,2,1,0:T(8,128)(2,1)S(1)} %get-tuple-element.110.rest_1_), channel_id=1, source_target_pairs={{225,160},{226,161},{227,162},{228,163},{229,164},{230,165},{231,1... | collective-permute-start | bytes 245768 | tf_op jit(solution)/shard_map/ppermute | solution.py:32
  36.2 12.8 %collective-permute-start.11 = (bf16[9,6,32,128]{3,2,1,0:T(8,128)(2,1)S(1)}, bf16[9,6,32,128]{3,2,1,0:T(8,128)(2,1)S(1)}, u32[]{:S(2)}, u32[]{:S(2)}) collective-permute-start(bf16[9,6,32,128]{3,2,1,0:T(8,128)(2,1)S(1)} %pad_maximum_fusion), channel_id=1, source_target_pairs={{0,32},{1,33},{2,34},{3,35},{4,36},{5,37},{6,38},{7,39},{8,40},{9,... | collective-permute-start | bytes 1327112 | tf_op jit(solution)/shard_map/ppermute | solution.py:32
  38.4 13.2 %collective-permute-start.13 = (bf16[5,4,32,128]{3,2,1,0:T(8,128)(2,1)S(1)}, bf16[5,4,32,128]{3,2,1,0:T(8,128)(2,1)S(1)}, u32[]{:S(2)}, u32[]{:S(2)}) collective-permute-start(bf16[5,4,32,128]{3,2,1,0:T(8,128)(2,1)S(1)} %get-tuple-element.125.rest_0_), channel_id=1, source_target_pairs={{160,96},{161,97},{162,98},{163,99},{164,100},{165,101},{166,102},... | collective-permute-start | bytes 491528 | tf_op jit(solution)/shard_map/ppermute | solution.py:32
  39.8 9.9 %copy-start.6 = (bf16[128,128]{1,0:T(8,128)(2,1)S(1)}, bf16[128,128]{1,0:T(8,128)(2,1)}, u32[]{:S(2)}) copy-start(bf16[128,128]{1,0:T(8,128)(2,1)} %constant.132.clone.order_ref) | copy-start | bytes 98308
  41.3 9.5 %collective-permute-start.12 = (bf16[5,2,32,128]{3,2,1,0:T(8,128)(2,1)S(1)}, bf16[5,2,32,128]{3,2,1,0:T(8,128)(2,1)S(1)}, u32[]{:S(2)}, u32[]{:S(2)}) collective-permute-start(bf16[5,2,32,128]{3,2,1,0:T(8,128)(2,1)S(1)} %get-tuple-element.124.rest_2_), channel_id=1, source_target_pairs={{160,97},{161,98},{162,99},{163,100},{164,101},{165,102},{166,103}... | collective-permute-start | bytes 245768 | tf_op jit(solution)/shard_map/ppermute | solution.py:32
  42.0 9.6 %collective-permute-start.14 = (bf16[5,2,32,128]{3,2,1,0:T(8,128)(2,1)S(1)}, bf16[5,2,32,128]{3,2,1,0:T(8,128)(2,1)S(1)}, u32[]{:S(2)}, u32[]{:S(2)}) collective-permute-start(bf16[5,2,32,128]{3,2,1,0:T(8,128)(2,1)S(1)} %get-tuple-element.126.rest_1_), channel_id=1, source_target_pairs={{161,96},{162,97},{163,98},{164,99},{165,100},{166,101},{167,102},... | collective-permute-start | bytes 245768 | tf_op jit(solution)/shard_map/ppermute | solution.py:32
  45.6 6.0 %copy-start.8 = (bf16[1728,128]{1,0:T(8,128)(2,1)S(1)}, bf16[1728,128]{1,0:T(8,128)(2,1)}, u32[]{:S(2)}) copy-start(bf16[1728,128]{1,0:T(8,128)(2,1)} %copy-done.7) | copy-start | bytes 1327108
  45.6 6.0 %copy-start.11 = (bf16[1728,128]{1,0:T(8,128)(2,1)S(1)}, bf16[1728,128]{1,0:T(8,128)(2,1)}, u32[]{:S(2)}) copy-start(bf16[1728,128]{1,0:T(8,128)(2,1)} %copy-done.10) | copy-start | bytes 1327108
  45.6 6.0 %copy-start.25 = (f32[9,4,32,128]{3,2,1,0:T(8,128)S(1)}, f32[9,4,32,128]{3,2,1,0:T(8,128)}, u32[]{:S(2)}) copy-start(f32[9,4,32,128]{3,2,1,0:T(8,128)} %copy-done.24) | copy-start | bytes 1769476
  45.6 8.6 %collective-permute-start.8 = (bf16[4,2,32,128]{3,2,1,0:T(8,128)(2,1)}, bf16[4,2,32,128]{3,2,1,0:T(8,128)(2,1)S(1)}, u32[]{:S(2)}, u32[]{:S(2)}) collective-permute-start(bf16[4,2,32,128]{3,2,1,0:T(8,128)(2,1)} %get-tuple-element.119.rest_4_), channel_id=1, source_target_pairs={{224,161},{225,162},{226,163},{227,164},{228,165},{229,166},{230,1... | collective-permute-start | bytes 196616 | tf_op jit(solution)/shard_map/ppermute | solution.py:32
  49.0 6.5 %collective-permute-start.9 = (bf16[4,4,32,128]{3,2,1,0:T(8,128)(2,1)}, bf16[4,4,32,128]{3,2,1,0:T(8,128)(2,1)S(1)}, u32[]{:S(2)}, u32[]{:S(2)}) collective-permute-start(bf16[4,4,32,128]{3,2,1,0:T(8,128)(2,1)} %get-tuple-element.120.rest_2_), channel_id=1, source_target_pairs={{224,160},{225,161},{226,162},{227,163},{228,164},{229,165},{230,1... | collective-permute-start | bytes 393224 | tf_op jit(solution)/shard_map/ppermute | solution.py:32
  50.9 4.7 %collective-permute-start.10 = (bf16[4,2,32,128]{3,2,1,0:T(8,128)(2,1)}, bf16[4,2,32,128]{3,2,1,0:T(8,128)(2,1)S(1)}, u32[]{:S(2)}, u32[]{:S(2)}) collective-permute-start(bf16[4,2,32,128]{3,2,1,0:T(8,128)(2,1)} %get-tuple-element.121.rest_3_), channel_id=1, source_target_pairs={{225,160},{226,161},{227,162},{228,163},{229,164},{230,165},{231,1... | collective-permute-start | bytes 196616 | tf_op jit(solution)/shard_map/ppermute | solution.py:32
  52.2 24.4 %copy-start.20 = (bf16[5,4,32,128]{3,2,1,0:T(8,128)(2,1)}, bf16[5,4,32,128]{3,2,1,0:T(8,128)(2,1)S(1)}, u32[]{:S(2)}) copy-start(bf16[5,4,32,128]{3,2,1,0:T(8,128)(2,1)S(1)} %get-tuple-element.143) | copy-start | bytes 491524
  52.2 6.4 %collective-permute-start.18 = (bf16[5,2,32,128]{3,2,1,0:T(8,128)(2,1)S(1)}, bf16[5,2,32,128]{3,2,1,0:T(8,128)(2,1)S(1)}, u32[]{:S(2)}, u32[]{:S(2)}) collective-permute-start(bf16[5,2,32,128]{3,2,1,0:T(8,128)(2,1)S(1)} %get-tuple-element.142), channel_id=1, source_target_pairs={{96,33},{97,34},{98,35},{99,36},{100,37},{101,38},{102,39},{103,40... | collective-permute-start | bytes 245768 | tf_op jit(solution)/shard_map/ppermute | solution.py:32
  52.9 16.6 %collective-permute-start.19 = (bf16[5,4,32,128]{3,2,1,0:T(8,128)(2,1)S(1)}, bf16[5,4,32,128]{3,2,1,0:T(8,128)(2,1)S(1)}, u32[]{:S(2)}, u32[]{:S(2)}) collective-permute-start(bf16[5,4,32,128]{3,2,1,0:T(8,128)(2,1)S(1)} %get-tuple-element.143), channel_id=1, source_target_pairs={{96,32},{97,33},{98,34},{99,35},{100,36},{101,37},{102,38},{103,39... | collective-permute-start | bytes 491528 | tf_op jit(solution)/shard_map/ppermute | solution.py:32
  54.2 15.3 %collective-permute-start.20 = (bf16[5,2,32,128]{3,2,1,0:T(8,128)(2,1)S(1)}, bf16[5,2,32,128]{3,2,1,0:T(8,128)(2,1)S(1)}, u32[]{:S(2)}, u32[]{:S(2)}) collective-permute-start(bf16[5,2,32,128]{3,2,1,0:T(8,128)(2,1)S(1)} %get-tuple-element.144), channel_id=1, source_target_pairs={{97,32},{98,33},{99,34},{100,35},{101,36},{102,37},{103,38},{104,3... | collective-permute-start | bytes 245768 | tf_op jit(solution)/shard_map/ppermute | solution.py:32
  57.3 17.4 %collective-permute-start.15 = (bf16[4,2,32,128]{3,2,1,0:T(8,128)(2,1)}, bf16[4,2,32,128]{3,2,1,0:T(8,128)(2,1)S(1)}, u32[]{:S(2)}, u32[]{:S(2)}) collective-permute-start(bf16[4,2,32,128]{3,2,1,0:T(8,128)(2,1)} %get-tuple-element.137.rest_4_), channel_id=1, source_target_pairs={{160,97},{161,98},{162,99},{163,100},{164,101},{165,102},{166,103}... | collective-permute-start | bytes 196616 | tf_op jit(solution)/shard_map/ppermute | solution.py:32
  58.0 16.8 %collective-permute-start.16 = (bf16[4,4,32,128]{3,2,1,0:T(8,128)(2,1)}, bf16[4,4,32,128]{3,2,1,0:T(8,128)(2,1)S(1)}, u32[]{:S(2)}, u32[]{:S(2)}) collective-permute-start(bf16[4,4,32,128]{3,2,1,0:T(8,128)(2,1)} %get-tuple-element.138.rest_2_), channel_id=1, source_target_pairs={{160,96},{161,97},{162,98},{163,99},{164,100},{165,101},{166,102},... | collective-permute-start | bytes 393224 | tf_op jit(solution)/shard_map/ppermute | solution.py:32
  58.6 16.1 %collective-permute-start.17 = (bf16[4,2,32,128]{3,2,1,0:T(8,128)(2,1)}, bf16[4,2,32,128]{3,2,1,0:T(8,128)(2,1)S(1)}, u32[]{:S(2)}, u32[]{:S(2)}) collective-permute-start(bf16[4,2,32,128]{3,2,1,0:T(8,128)(2,1)} %get-tuple-element.139.rest_3_), channel_id=1, source_target_pairs={{161,96},{162,97},{163,98},{164,99},{165,100},{166,101},{167,102},... | collective-permute-start | bytes 196616 | tf_op jit(solution)/shard_map/ppermute | solution.py:32
  74.7 1.9 %copy-start.13 = (f32[192,384]{1,0:T(8,128)}, f32[192,384]{1,0:T(8,128)S(1)}, u32[]{:S(2)}) copy-start(f32[192,384]{1,0:T(8,128)S(1)} %get-tuple-element.159.rest_0_) | copy-start | bytes 884740
  74.7 1.9 %copy-start.15 = (f32[128,384]{1,0:T(8,128)}, f32[128,384]{1,0:T(8,128)S(1)}, u32[]{:S(2)}) copy-start(f32[128,384]{1,0:T(8,128)S(1)} %get-tuple-element.160.rest_1_) | copy-start | bytes 589828
  78.2 24.2 %collective-permute-start.25 = (bf16[4,4,32,128]{3,2,1,0:T(8,128)(2,1)}, bf16[4,4,32,128]{3,2,1,0:T(8,128)(2,1)}, u32[]{:S(2)}, u32[]{:S(2)}) collective-permute-start(bf16[4,4,32,128]{3,2,1,0:T(8,128)(2,1)} %get-tuple-element.152.rest_2_), channel_id=1, source_target_pairs={{96,32},{97,33},{98,34},{99,35},{100,36},{101,37},{102,38},{103,39... | collective-permute-start | bytes 393224 | tf_op jit(solution)/shard_map/ppermute | solution.py:32
  79.5 8.8 %collective-permute-start.22 = (bf16[9,4,32,128]{3,2,1,0:T(8,128)(2,1)}, bf16[9,4,32,128]{3,2,1,0:T(8,128)(2,1)}, u32[]{:S(2)}, u32[]{:S(2)}) collective-permute-start(bf16[9,4,32,128]{3,2,1,0:T(8,128)(2,1)} %pad_maximum_fusion.1), channel_id=1, source_target_pairs={{224,192},{225,193},{226,194},{227,195},{228,196},{229,197},{230,1... | collective-permute-start | bytes 884744 | tf_op jit(solution)/shard_map/ppermute | solution.py:32
  81.7 4.6 %collective-permute-start.21 = (bf16[9,1,32,128]{3,2,1,0:T(8,128)(2,1)S(1)}, bf16[9,1,32,128]{3,2,1,0:T(8,128)(2,1)S(1)}, u32[]{:S(2)}, u32[]{:S(2)}) collective-permute-start(bf16[9,1,32,128]{3,2,1,0:T(8,128)(2,1)S(1)} %pad_maximum_fusion.8), channel_id=1, source_target_pairs={{224,193},{225,194},{226,195},{227,196},{228,197},{229,198},{230,1... | collective-permute-start | bytes 221192 | tf_op jit(solution)/shard_map/ppermute | solution.py:32
  83.8 4.5 %collective-permute-start.23 = (bf16[9,1,32,128]{3,2,1,0:T(8,128)(2,1)}, bf16[9,1,32,128]{3,2,1,0:T(8,128)(2,1)}, u32[]{:S(2)}, u32[]{:S(2)}) collective-permute-start(bf16[9,1,32,128]{3,2,1,0:T(8,128)(2,1)} %pad_maximum_fusion.7), channel_id=1, source_target_pairs={{225,192},{226,193},{227,194},{228,195},{229,196},{230,197},{231,1... | collective-permute-start | bytes 221192 | tf_op jit(solution)/shard_map/ppermute | solution.py:32
  85.1 4.2 %collective-permute-start.24 = (bf16[4,2,32,128]{3,2,1,0:T(8,128)(2,1)}, bf16[4,2,32,128]{3,2,1,0:T(8,128)(2,1)}, u32[]{:S(2)}, u32[]{:S(2)}) collective-permute-start(bf16[4,2,32,128]{3,2,1,0:T(8,128)(2,1)} %get-tuple-element.153.rest_4_), channel_id=1, source_target_pairs={{96,33},{97,34},{98,35},{99,36},{100,37},{101,38},{102,39},{103,40... | collective-permute-start | bytes 196616 | tf_op jit(solution)/shard_map/ppermute | solution.py:32
  87.0 15.5 %collective-permute-start.26 = (bf16[4,2,32,128]{3,2,1,0:T(8,128)(2,1)}, bf16[4,2,32,128]{3,2,1,0:T(8,128)(2,1)}, u32[]{:S(2)}, u32[]{:S(2)}) collective-permute-start(bf16[4,2,32,128]{3,2,1,0:T(8,128)(2,1)} %get-tuple-element.154.rest_3_), channel_id=1, source_target_pairs={{97,32},{98,33},{99,34},{100,35},{101,36},{102,37},{103,38},{104,3... | collective-permute-start | bytes 196616 | tf_op jit(solution)/shard_map/ppermute | solution.py:32
  89.2 13.2 %copy-start.27 = (bf16[4,4,32,128]{3,2,1,0:T(8,128)(2,1)}, bf16[4,4,32,128]{3,2,1,0:T(8,128)(2,1)S(1)}, u32[]{:S(2)}) copy-start(bf16[4,4,32,128]{3,2,1,0:T(8,128)(2,1)S(1)} %get-tuple-element.162) | copy-start | bytes 393220
  102.5 1.0 copy-start.9
  103.5 1.0 copy-start.12
  104.5 1.0 copy-start.14
  106.4 4.4 %copy-start.19 = (bf16[9,4,32,128]{3,2,1,0:T(8,128)(2,1)S(1)}, bf16[9,4,32,128]{3,2,1,0:T(8,128)(2,1)}, u32[]{:S(2)}) copy-start(bf16[9,4,32,128]{3,2,1,0:T(8,128)(2,1)} %param.10) | copy-start | bytes 884740
  106.4 4.4 %copy-start.28 = (bf16[4,4,32,128]{3,2,1,0:T(8,128)(2,1)S(1)}, bf16[4,4,32,128]{3,2,1,0:T(8,128)(2,1)}, u32[]{:S(2)}) copy-start(bf16[4,4,32,128]{3,2,1,0:T(8,128)(2,1)} %copy-done.27) | copy-start | bytes 393220
  106.4 6.0 %copy-start.1 = (bf16[5,4,32,128]{3,2,1,0:T(8,128)(2,1)S(1)}, bf16[5,4,32,128]{3,2,1,0:T(8,128)(2,1)}, u32[]{:S(2)}) copy-start(bf16[5,4,32,128]{3,2,1,0:T(8,128)(2,1)} %copy-done) | copy-start | bytes 491524
  106.4 6.0 %copy-start.21 = (bf16[5,4,32,128]{3,2,1,0:T(8,128)(2,1)S(1)}, bf16[5,4,32,128]{3,2,1,0:T(8,128)(2,1)}, u32[]{:S(2)}) copy-start(bf16[5,4,32,128]{3,2,1,0:T(8,128)(2,1)} %get-tuple-element.164) | copy-start | bytes 491524
  114.7 6.8 %copy-start.5 = (bf16[5,2,32,128]{3,2,1,0:T(8,128)(2,1)S(1)}, bf16[5,2,32,128]{3,2,1,0:T(8,128)(2,1)}, u32[]{:S(2)}) copy-start(bf16[5,2,32,128]{3,2,1,0:T(8,128)(2,1)} %copy-done.4) | copy-start | bytes 245764
  114.7 8.8 %copy-start.22 = (bf16[5,4,32,128]{3,2,1,0:T(8,128)(2,1)S(1)}, bf16[5,4,32,128]{3,2,1,0:T(8,128)(2,1)}, u32[]{:S(2)}) copy-start(bf16[5,4,32,128]{3,2,1,0:T(8,128)(2,1)} %get-tuple-element.173) | copy-start | bytes 491524
  114.7 8.8 %copy-start.23 = (bf16[4,4,32,128]{3,2,1,0:T(8,128)(2,1)S(1)}, bf16[4,4,32,128]{3,2,1,0:T(8,128)(2,1)}, u32[]{:S(2)}) copy-start(bf16[4,4,32,128]{3,2,1,0:T(8,128)(2,1)} %get-tuple-element.175) | copy-start | bytes 393220
  114.7 15.9 %copy-start.3 = (bf16[5,2,32,128]{3,2,1,0:T(8,128)(2,1)S(1)}, bf16[5,2,32,128]{3,2,1,0:T(8,128)(2,1)}, u32[]{:S(2)}) copy-start(bf16[5,2,32,128]{3,2,1,0:T(8,128)(2,1)} %copy-done.2) | copy-start | bytes 245764
  114.7 23.8 %copy-start.26 = (f32[9,4,32,128]{3,2,1,0:T(8,128)S(1)}, f32[9,4,32,128]{3,2,1,0:T(8,128)}, u32[]{:S(2)}) copy-start(f32[9,4,32,128]{3,2,1,0:T(8,128)} %copy-done.24) | copy-start | bytes 1769476
  114.8 3.0 %collective-permute-start.30 = (bf16[9,64,384]{2,1,0:T(8,128)(2,1)S(1)}, bf16[9,64,384]{2,1,0:T(8,128)(2,1)S(1)}, u32[]{:S(2)}, u32[]{:S(2)}) collective-permute-start(bf16[9,64,384]{2,1,0:T(8,128)(2,1)S(1)} %constant_dynamic-slice_fusion.5), channel_id=1, source_target_pairs={{0,1},{1,0},{2,3},{3,2},{4,5},{5,4},{6,7},{7,6},{8,9},{9,8},{10,11... | collective-permute-start | bytes 1327112 | tf_op jit(solution)/shard_map/ppermute | solution.py:452
  118.0 20.6 %copy-start.30 = (bf16[1,3,3,3,128,128]{5,4,3,2,1,0:T(8,128)(2,1)S(1)}, bf16[1,3,3,3,128,128]{5,4,3,2,1,0:T(8,128)(2,1)}, u32[]{:S(2)}) copy-start(bf16[1,3,3,3,128,128]{5,4,3,2,1,0:T(8,128)(2,1)} %param.9) | copy-start | bytes 2654212
  118.0 9.8 %collective-permute-start.31 = (bf16[9,32,384]{2,1,0:T(8,128)(2,1)S(1)}, bf16[9,32,384]{2,1,0:T(8,128)(2,1)S(1)}, u32[]{:S(2)}, u32[]{:S(2)}) collective-permute-start(bf16[9,32,384]{2,1,0:T(8,128)(2,1)S(1)} %constant_dynamic-slice_fusion.4), channel_id=1, source_target_pairs={{0,2},{1,3},{2,0},{3,1},{4,6},{5,7},{6,4},{7,5},{8,10},{9,11},{10,... | collective-permute-start | bytes 663560 | tf_op jit(solution)/shard_map/ppermute | solution.py:452
  122.3 16.3 %collective-permute-start.27 = (bf16[9,1,32,128]{3,2,1,0:T(8,128)(2,1)S(1)}, bf16[9,1,32,128]{3,2,1,0:T(8,128)(2,1)S(1)}, u32[]{:S(2)}, u32[]{:S(2)}) collective-permute-start(bf16[9,1,32,128]{3,2,1,0:T(8,128)(2,1)S(1)} %pad_maximum_fusion.6), channel_id=1, source_target_pairs={{32,1},{33,2},{34,3},{35,4},{36,5},{37,6},{38,7},{39,8},{40,9},{41... | collective-permute-start | bytes 221192 | tf_op jit(solution)/shard_map/ppermute | solution.py:32
  123.6 15.0 %collective-permute-start.28 = (bf16[9,4,32,128]{3,2,1,0:T(8,128)(2,1)S(1)}, bf16[9,4,32,128]{3,2,1,0:T(8,128)(2,1)S(1)}, u32[]{:S(2)}, u32[]{:S(2)}) collective-permute-start(bf16[9,4,32,128]{3,2,1,0:T(8,128)(2,1)S(1)} %pad_maximum_fusion.2), channel_id=1, source_target_pairs={{32,0},{33,1},{34,2},{35,3},{36,4},{37,5},{38,6},{39,7},{40,8},{41... | collective-permute-start | bytes 884744 | tf_op jit(solution)/shard_map/ppermute | solution.py:32
  127.9 5.5 %collective-permute-start.32 = (bf16[9,16,384]{2,1,0:T(8,128)(2,1)S(1)}, bf16[9,16,384]{2,1,0:T(8,128)(2,1)S(1)}, u32[]{:S(2)}, u32[]{:S(2)}) collective-permute-start(bf16[9,16,384]{2,1,0:T(8,128)(2,1)S(1)} %constant_dynamic-slice_fusion.3), channel_id=1, source_target_pairs={{0,4},{1,5},{2,6},{3,7},{4,0},{5,1},{6,2},{7,3},{8,12},{9,13},{10,... | collective-permute-start | bytes 331784 | tf_op jit(solution)/shard_map/ppermute | solution.py:452
  131.4 7.1 %collective-permute-start.29 = (bf16[9,1,32,128]{3,2,1,0:T(8,128)(2,1)S(1)}, bf16[9,1,32,128]{3,2,1,0:T(8,128)(2,1)S(1)}, u32[]{:S(2)}, u32[]{:S(2)}) collective-permute-start(bf16[9,1,32,128]{3,2,1,0:T(8,128)(2,1)S(1)} %pad_maximum_fusion.5), channel_id=1, source_target_pairs={{33,0},{34,1},{35,2},{36,3},{37,4},{38,5},{39,6},{40,7},{41,8},{42... | collective-permute-start | bytes 221192 | tf_op jit(solution)/shard_map/ppermute | solution.py:32
  133.5 7.5 %collective-permute-start.33 = (bf16[9,8,384]{2,1,0:T(8,128)(2,1)S(1)}, bf16[9,8,384]{2,1,0:T(8,128)(2,1)S(1)}, u32[]{:S(2)}, u32[]{:S(2)}) collective-permute-start(bf16[9,8,384]{2,1,0:T(8,128)(2,1)S(1)} %constant_dynamic-slice_fusion.2), channel_id=1, source_target_pairs={{0,8},{1,9},{2,10},{3,11},{4,12},{5,13},{6,14},{7,15},{8,0},{9,1},... | collective-permute-start | bytes 165896 | tf_op jit(solution)/shard_map/ppermute | solution.py:452
  141.0 9.6 %collective-permute-start.35 = (bf16[9,4,384]{2,1,0:T(4,128)(2,1)S(1)}, bf16[9,4,384]{2,1,0:T(4,128)(2,1)S(1)}, u32[]{:S(2)}, u32[]{:S(2)}) collective-permute-start(bf16[9,4,384]{2,1,0:T(4,128)(2,1)S(1)} %get-tuple-element.179), channel_id=1, source_target_pairs={{32,16},{33,17},{34,18},{35,19},{36,20},{37,21},{38,22},{39,23},{4... | collective-permute-start | bytes 82952 | tf_op jit(solution)/shard_map/ppermute | solution.py:452
  145.5 5.2 %collective-permute-start.34 = (bf16[9,4,384]{2,1,0:T(4,128)(2,1)S(1)}, bf16[9,4,384]{2,1,0:T(4,128)(2,1)S(1)}, u32[]{:S(2)}, u32[]{:S(2)}) collective-permute-start(bf16[9,4,384]{2,1,0:T(4,128)(2,1)S(1)} %get-tuple-element.178), channel_id=1, source_target_pairs={{32,0},{33,1},{34,2},{35,3},{36,4},{37,5},{38,6},{39,7},{40,8},{41... | collective-permute-start | bytes 82952 | tf_op jit(solution)/shard_map/ppermute | solution.py:32
  (6 other events, 4.2 us)

commit v6 on v4

--- a/solution.py
+++ b/solution.py
@@ -18,7 +18,7 @@
 COLS = 32
 CH = 128
 AXES = ("section", "dp")
-HALVING = (1, 4, 2, 8, 16)
+HALVING = (1, 2, 4, 8, 16)
 
 
 def permute(value, hops):
@@ -82,42 +82,53 @@
             one_later = here
 
 
+def load(low_ref, own_ref, high_ref, x_ref):
+    for t in range(FRAMES):
+        whole = jnp.concatenate([low_ref[t], own_ref[t], high_ref[t]], axis=0)
+        fill(x_ref, t, 0, whole.reshape(-1, CH).astype(F32))
+
+
 def emit_to(refs):
     out_ref, top_ref, bottom_ref = refs
+    edge = top_ref.shape[1]
 
     def emit(frame, value):
         whole = value.reshape(ROWS, COLS, CH)
         out_ref[frame] = whole
-        top_ref[frame] = whole[:2]
-        bottom_ref[frame] = whole[2:]
+        top_ref[frame] = whole[:edge]
+        bottom_ref[frame] = whole[ROWS - edge :]
 
     return emit
 
 
 def single_kernel(low_ref, own_ref, high_ref, w_ref, slope_ref, *rest):
     *outs, x_ref = rest
-    for t in range(FRAMES):
-        whole = jnp.concatenate([low_ref[t], own_ref[t], high_ref[t]], axis=0)
-        fill(x_ref, t, 0, whole.reshape(-1, CH).astype(F32))
+    load(low_ref, own_ref, high_ref, x_ref)
     back_pass(x_ref, weights(w_ref), slope_ref, ROWS, emit_to(outs))
 
 
-def double_kernel(
-    core_ref, low_ref, own_ref, high_ref, half_ref, other_ref, slope1_ref, w0_ref, slope0_ref, *rest
-):
-    *outs, x1_ref, x0_ref, w1_ref = rest
-    half = half_ref.shape[0]
-    core = core_ref[0]
-    w1_ref[pl.ds(pl.multiple_of(core * half, half), half), :] = half_ref[...]
-    w1_ref[pl.ds(pl.multiple_of((1 - core) * half, half), half), :] = other_ref[...]
-    for t in range(FRAMES):
-        whole = jnp.concatenate([low_ref[t], own_ref[t], high_ref[t]], axis=0)
-        fill(x1_ref, t, 0, whole.reshape(-1, CH).astype(F32))
-
-    def emit_mid(frame, value):
+def wide_kernel(low_ref, own_ref, high_ref, w_ref, slope_ref, *rest):
+    own_out, low_out, high_out, x_ref = rest
+    load(low_ref, own_ref, high_ref, x_ref)
+
+    def emit(frame, value):
+        whole = value.reshape(ROWS + 2, COLS, CH)
+        low_out[frame] = whole[:1]
+        own_out[frame] = whole[1 : 1 + ROWS]
+        high_out[frame] = whole[1 + ROWS :]
+
+    back_pass(x_ref, weights(w_ref), slope_ref, ROWS + 2, emit)
+
+
+def double_kernel(low_ref, own_ref, high_ref, w1_ref, slope1_ref, w0_ref, slope0_ref, *rest):
+    *outs, middle_ref, x1_ref, x0_ref = rest
+    load(low_ref, own_ref, high_ref, x1_ref)
+
+    def emit_middle(frame, value):
         fill(x0_ref, frame, 0, value.astype(F32))
-
-    back_pass(x1_ref, weights(w1_ref), slope1_ref, ROWS + 2, emit_mid)
+        middle_ref[frame] = value.reshape(ROWS + 2, COLS, CH)[1 : 1 + ROWS]
+
+    back_pass(x1_ref, weights(w1_ref), slope1_ref, ROWS + 2, emit_middle)
     back_pass(x0_ref, weights(w0_ref), slope0_ref, ROWS, emit_to(outs))
 
 
@@ -125,38 +136,50 @@
     return [pl.BlockSpec(memory_space=pltpu.VMEM)] * count
 
 
-def gradient_shapes():
-    return [
-        jax.ShapeDtypeStruct((FRAMES, rows, COLS, CH), BF) for rows in (ROWS, 2, 2)
-    ]
-
-
-def single(low, own, high, w, slope):
+def rows_shape(rows):
+    return jax.ShapeDtypeStruct((FRAMES, rows, COLS, CH), BF)
+
+
+def block_call(kernel, name, operands, outs, halos):
     return pl.pallas_call(
+        kernel,
+        out_shape=[rows_shape(r) for r in outs],
+        in_specs=in_vmem(len(operands)),
+        out_specs=in_vmem(len(outs)),
+        scratch_shapes=[pltpu.VMEM((FRAMES, r, COLS, 3 * CH), BF) for r in halos],
+        compiler_params=pltpu.CompilerParams(vmem_limit_bytes=24 << 20),
+        name=name,
+    )(*operands)
+
+
+def single(low, own, high, w, slope, edge):
+    return block_call(
         single_kernel,
-        out_shape=gradient_shapes(),
-        in_specs=in_vmem(5),
-        out_specs=in_vmem(3),
-        scratch_shapes=[pltpu.VMEM((FRAMES, ROWS + 2, COLS, 3 * CH), BF)],
-        compiler_params=pltpu.CompilerParams(vmem_limit_bytes=24 << 20),
-        name="one_block",
-    )(low, own, high, w, slope)
-
-
-def double(core, low, own, high, half, other, slope1, w0, slope0):
-    return pl.pallas_call(
+        f"one_block_{edge}",
+        (low, own, high, w, slope),
+        (ROWS, edge, edge),
+        (ROWS + 2,),
+    )
+
+
+def wide(low, own, high, w, slope):
+    return block_call(
+        wide_kernel,
+        "wide_block",
+        (low, own, high, w, slope),
+        (ROWS, 1, 1),
+        (ROWS + 4,),
+    )
+
+
+def double(low, own, high, w1, slope1, w0, slope0):
+    return block_call(
         double_kernel,
-        out_shape=gradient_shapes(),
-        in_specs=[pl.BlockSpec(memory_space=pltpu.SMEM)] + in_vmem(8),
-        out_specs=in_vmem(3),
-        scratch_shapes=[
-            pltpu.VMEM((FRAMES, ROWS + 4, COLS, 3 * CH), BF),
-            pltpu.VMEM((FRAMES, ROWS + 2, COLS, 3 * CH), BF),
-            pltpu.VMEM((27 * CH, CH), BF),
-        ],
-        compiler_params=pltpu.CompilerParams(vmem_limit_bytes=24 << 20),
-        name="two_blocks",
-    )(core.reshape(1), low, own, high, half, other, slope1, w0, slope0)
+        "two_blocks",
+        (low, own, high, w1, slope1, w0, slope0),
+        (ROWS, 2, 2, ROWS),
+        (ROWS + 4, ROWS + 2),
+    )
 
 
 def tap_rows_kernel(act_ref, order_ref, out_ref, u_ref):
@@ -237,18 +260,13 @@
 def local(acts, kernels, cotangent):
     me = lax.axis_index("section")
     dp = lax.axis_index("dp")
-    core = dp % 2
     scale = 1.0 / math.sqrt(FRAMES * ROWS * DP * COLS)
-    odd = [s for s in range(SEC) if s % 2 == 1]
     every = range(SEC)
-    pair = odd[:-1]
+    pairs = (4, 2, 0)
     barrier = lax.optimization_barrier
 
-    w = kernels[0].reshape(27 * CH, CH)
-    half = w.shape[0] // 2
-    w_half = permute(
-        lax.dynamic_slice_in_dim(w, core * half, half, 0), [(s + 1, s, 0) for s in pair]
-    )
+    def blank(rows):
+        return jnp.zeros((FRAMES, rows, COLS, CH), BF)
 
     both = jnp.concatenate([cotangent, acts[0]], axis=0)
     edge_low = permute(both[:, -1:], [(s, s, 1) for s in every])
@@ -256,83 +274,81 @@
     low0, high0 = edge_low[:FRAMES], edge_high[:FRAMES]
     act6 = jnp.concatenate([edge_low[FRAMES:], acts[0], edge_high[FRAMES:]], axis=1)
 
+    w = kernels[0].reshape(27 * CH, CH)
     slope = slope_of(acts[0])
-    none = jnp.zeros((FRAMES, 2, COLS, CH), BF)
-    state = lax.cond(
+    result, top, bottom = lax.cond(
         me == 7,
-        lambda: tuple(single(low0, cotangent, high0, w, slope)),
-        lambda: (cotangent, none, none),
-    )
-
-    def hop(state, target):
-        result, top, bottom = state
-        own = permute(result, [(target + 2, target, 0)])
-        low = permute(bottom, [(target + 2, target, 1)])
-        high = permute(top, [(target + 2, target, -1)])
+        lambda: tuple(single(low0, cotangent, high0, w, slope, 1)),
+        lambda: (blank(ROWS), blank(1), blank(1)),
+    )
+
+    def hop(result, top, bottom, source, target):
+        own = permute(result, [(source, target, 0)])
+        low = permute(bottom, [(source, target, 1)])
+        high = permute(top, [(source, target, -1)])
         return low, own, high
 
-    act6, state = barrier((act6, state))
-    act_next = permute(act6, [(s + 1, s, 0) for s in pair])
-    arrived, w_half = barrier((hop(state, 5), w_half))
-    w_other = lax.ppermute(
-        w_half, AXES, [(s * DP + d, s * DP + (d ^ 1)) for s in pair for d in range(DP)]
-    )
+    w_next = permute(w, [(s + 1, s, 0) for s in pairs])
+    act6, result = barrier((act6, result))
+    act_next = permute(act6, [(s + 1, s, 0) for s in pairs])
     row = lax.broadcasted_iota(jnp.int32, act_next.shape, 1) + dp * ROWS - 1
     inside = (row >= 0) & (row < DP * ROWS)
     slope_next = jnp.where(inside, slope_of(act_next), 0.0)
 
-    def stage(state, arrived, section):
-        low, own, high = arrived
-        return lax.cond(
+    low, own, high = hop(result, top, bottom, 7, 6)
+    result, top, bottom = lax.cond(
+        me == 6,
+        lambda: tuple(single(low, own, high, w, slope, 2)),
+        lambda: (result, blank(2), blank(2)),
+    )
+    act6, own, result = barrier((act6, own, result))
+    grad = jnp.where(me == 7, cotangent, own)
+    ut = tap_rows(act6, jnp.asarray(channel_order(), BF))
+
+    low, own, high = hop(result, top, bottom, 6, 4)
+    ut, grad, low = barrier((ut, grad, low))
+    for section in (4, 2):
+        result, top, bottom, grad = lax.cond(
             me == section,
-            lambda: tuple(
-                double(core, low, own, high, w_half, w_other, slope_next, w, slope)
+            lambda low=low, own=own, high=high: tuple(
+                double(low, own, high, w_next, slope_next, w, slope)
             ),
-            lambda: state,
+            lambda result=result, top=top, bottom=bottom, grad=grad: (
+                result,
+                top,
+                bottom,
+                grad,
+            ),
         )
-
-    def even(result, sections):
-        hops = [(s + 1, s) for s in sections]
-        own = permute(result, [(a, b, 0) for a, b in hops])
-        low = permute(result[:, -1:], [(a, b, 1) for a, b in hops])
-        high = permute(result[:, :1], [(a, b, -1) for a, b in hops])
-        live = functools.reduce(jnp.logical_or, [me == s for s in sections])
-        return lax.cond(
-            live,
-            lambda: single(low, own, high, w, slope)[0],
-            lambda: result,
-        )
-
-    state = stage(state, arrived, 5)
-    act6, state = barrier((act6, state))
-    arrived = hop(state, 3)
-    act_prev = permute(act6, [(s, (s + 1) % SEC, 0) for s in every])
-    ut = tap_rows(act_prev, jnp.asarray(channel_order(), BF))
-    ut, arrived = barrier((ut, arrived))
-    state = stage(state, arrived, 3)
-    arrived = hop(state, 1)
-    result = even(state[0], (6, 4, 2))
-    result, arrived = barrier((result, arrived))
-    result, _, _ = stage((result, state[1], state[2]), arrived, 1)
-    final = even(result, (0,))
-
-    part = taps(ut, jnp.where(me == 0, cotangent, result), scale)
+        low, own, high = hop(result, top, bottom, section, section - 2)
+
+    grad = grad + permute(result, [(s + 1, s, 0) for s in (5, 3, 1)])
+    grad, low = barrier((grad, low))
+
+    grad, low, high = lax.cond(
+        me == 0,
+        lambda: tuple(wide(low, own, high, w_next, slope_next)),
+        lambda: (grad, blank(1), blank(1)),
+    )
+    part = taps(ut, grad, scale)
+    grad, low, high, part = barrier((grad, low, high, part))
+    result = result + permute(grad, [(s - 1, s, 0) for s in (5, 3, 1)])
+    final = lax.cond(
+        me == 0,
+        lambda: single(low, grad, high, w, slope, 1)[0],
+        lambda: result,
+    )
+
     for bit in HALVING:
         size = part.shape[1] // 2
         mine = (dp // bit) % 2
         keep = lax.dynamic_slice_in_dim(part, mine * size, size, 1)
         give = lax.dynamic_slice_in_dim(part, (1 - mine) * size, size, 1)
-        shift = 0
-        if bit == HALVING[-1]:
-            keep = permute(keep, [((s + 1) % SEC, s, 0) for s in every])
-            shift = 1
         got = lax.ppermute(
-            give,
-            AXES,
-            [((s + shift) % SEC * DP + d, s * DP + (d ^ bit)) for s in every for d in range(DP)],
+            give, AXES, [(s * DP + d, s * DP + (d ^ bit)) for s in every for d in range(DP)]
         )
         part = keep.astype(F32) + got.astype(F32)
-        if not shift:
+        if bit != HALVING[-1]:
             part = part.astype(BF)
     share = CH // DP
     kernel_part = jnp.transpose(part.reshape(9, share, 3, CH), (1, 2, 0, 3)).reshape(share, 27, CH)

time: 137 us -> 141 us (1.029)
  the two profiles are of different devices: /device:TPU:8 before, /device:TPU:32 now
where the time goes in v6:
time: 141 us; the launch traced here: 140 us
  waiting for transfers between devices  82.4 us (58%)
  starting transfers between devices  34.7 us (25%)
  Pallas kernels  11.8 us (8%)
  other arithmetic  7.32 us (5%)
  local copies, waits for them, and re-layouts  2.33 us (2%)
    ppermute x18, waiting for transfers between devices, permute(): return lax.ppermute(value, AXES, pairs)  66.2 us
    ppermute x18, starting transfers between devices, permute(): return lax.ppermute(value, AXES, pairs)  25.1 us
    ppermute x5, waiting for transfers between devices, local(): lax.ppermute(give, AXES, [(s * DP + d, s * DP + (d ^ bit)) for s in every...  16.2 us
    ppermute x5, starting transfers between devices, local(): lax.ppermute(give, AXES, [(s * DP + d, s * DP + (d ^ bit)) for s in every...  9.64 us
    pallas_call x2, Pallas kernels, block_call(): pl.pallas_call(kernel, out_shape=[rows_shape(r) for r in outs], in_specs=...  8.07 us
  transfers between devices with their start and end apart: 23, of which 7 were waited for; matrix products, arithmetic and copies ran while one was open for 5% of the time, Pallas kernels for 3%

profile of v6, /device:TPU:32, one launch (start us, length us, event | category | flops | bytes accessed | tf_op | source)
XLA Modules:
  0.0 140.0 jit_solution(492168382934620747)
XLA Ops:
  0.6 0.0 copy-start.2
  0.6 1.1 pad_maximum_fusion.2
  1.7 1.9 %collective-permute-start = (bf16[18,1,32,128]{3,2,1,0:T(8,128)(2,1)S(1)}, bf16[18,1,32,128]{3,2,1,0:T(8,128)(2,1)S(1)}, u32[]{:S(2)}, u32[]{:S(2)}) collective-permute-start(bf16[18,1,32,128]{3,2,1,0:T(8,128)(2,1)S(1)} %get-tuple-element.197), channel_id=1, source_target_pairs={{0,1},{1,2},{2,3},{3,4},{4,5},{5,6},{6,7},{7,8},{8,9},{9,10},{10,1... | collective-permute-start | bytes 442376 | tf_op jit(solution)/shard_map/ppermute | solution.py:31
  3.6 6.0 %collective-permute-start.1 = (bf16[18,1,32,128]{3,2,1,0:T(8,128)(2,1)S(1)}, bf16[18,1,32,128]{3,2,1,0:T(8,128)(2,1)S(1)}, u32[]{:S(2)}, u32[]{:S(2)}) collective-permute-start(bf16[18,1,32,128]{3,2,1,0:T(8,128)(2,1)S(1)} %get-tuple-element.198), channel_id=1, source_target_pairs={{1,0},{2,1},{3,2},{4,3},{5,4},{6,5},{7,6},{8,7},{9,8},{10,9},{11,1... | collective-permute-start | bytes 442376 | tf_op jit(solution)/shard_map/ppermute | solution.py:31
  9.7 1.3 collective-permute-start.8
  11.0 2.0 %fusion.10 = f32[9,4,32,128]{3,2,1,0:T(8,128)} fusion(bf16[1,9,4,32,128]{4,3,2,1,0:T(8,128)(2,1)} %param.16), kind=kLoop, calls=%fused_computation.16 | loop fusion | flops 1179648 | bytes 884736 | tf_op jit(solution)/shard_map/mul | solution.py:257
  13.0 0.0 collective-permute-done
  13.0 0.0 collective-permute-done.1
  13.0 0.8 conditional.6
  13.0 0.8 broadcast.33
  13.8 0.0 copy-start.3
  13.8 0.0 copy-start
  13.9 0.1 pad_maximum_fusion.act_ref
  13.9 0.7 collective-permute-start.2
  14.6 1.3 collective-permute-start.9
  15.9 0.7 collective-permute-start.3
  16.6 0.7 collective-permute-start.4
  17.3 0.0 collective-permute-done.3
  17.3 0.0 collective-permute-done.4
  17.3 0.0 collective-permute-done.2
  17.3 0.7 conditional.7
  17.3 0.7 broadcast.35
  18.1 0.7 collective-permute-start.5
  18.7 0.7 collective-permute-start.6
  19.4 0.7 broadcast_select_fusion
  20.2 0.7 collective-permute-start.7
  20.9 1.1 tap_rows.1.ut_ref
  22.0 21.7 %collective-permute-done.9 = bf16[9,6,32,128]{3,2,1,0:T(8,128)(2,1)} collective-permute-done((bf16[9,6,32,128]{3,2,1,0:T(8,128)(2,1)S(1)}, bf16[9,6,32,128]{3,2,1,0:T(8,128)(2,1)}, u32[]{:S(2)}, u32[]{:S(2)}) %collective-permute-start.9) | collective-permute-done | bytes 442400 | tf_op jit(solution)/shard_map/ppermute | solution.py:31
  43.7 1.3 fusion.5
  45.0 0.0 collective-permute-done.7
  45.1 0.0 collective-permute-done.6
  45.1 1.4 collective-permute-start.11
  46.5 1.3 collective-permute-start.10
  47.8 1.3 collective-permute-start.12
  49.1 0.2 conditional.9
  49.3 1.4 collective-permute-start.13
  50.7 1.3 collective-permute-start.15
  52.0 1.3 collective-permute-start.14
  53.3 1.3 collective-permute-start.16
  54.6 1.9 %add.102 = bf16[9,4,32,128]{3,2,1,0:T(8,128)(2,1)} add(bf16[9,4,32,128]{3,2,1,0:T(8,128)(2,1)} %get-tuple-element.184, bf16[9,4,32,128]{3,2,1,0:T(8,128)(2,1)} %collective-permute-done.13) | non-fusion elementwise | flops 147456 | bytes 884736 | tf_op jit(solution)/shard_map/add | solution.py:325
  56.4 29.0 %collective-permute-done.14 = bf16[9,2,32,128]{3,2,1,0:T(8,128)(2,1)} collective-permute-done((bf16[9,2,32,128]{3,2,1,0:T(8,128)(2,1)}, bf16[9,2,32,128]{3,2,1,0:T(8,128)(2,1)}, u32[]{:S(2)}, u32[]{:S(2)}) %collective-permute-start.14) | collective-permute-done | bytes 147488 | tf_op jit(solution)/shard_map/ppermute | solution.py:31
  85.5 15.5 %collective-permute-done.16 = bf16[9,2,32,128]{3,2,1,0:T(8,128)(2,1)} collective-permute-done((bf16[9,2,32,128]{3,2,1,0:T(8,128)(2,1)}, bf16[9,2,32,128]{3,2,1,0:T(8,128)(2,1)}, u32[]{:S(2)}, u32[]{:S(2)}) %collective-permute-start.16) | collective-permute-done | bytes 147488 | tf_op jit(solution)/shard_map/ppermute | solution.py:31
  101.0 4.5 %conditional.10 = ((bf16[9,4,32,128]{3,2,1,0:T(8,128)(2,1)}, bf16[9,1,32,128]{3,2,1,0:T(8,128)(2,1)}, bf16[9,1,32,128]{3,2,1,0:T(8,128)(2,1)})) conditional(s32[]{:T(128)} %convert_element_type.64, bf16[9,4,32,128]{3,2,1,0:T(8,128)(2,1)} %add.102, (bf16[9,2,32,128]{3,2,1,0:T(8,128)(2,1)}, bf16[9,4,32,128]{3,2,1,0:T(8,128)(2,1)}, ...), branch_computations={%region_8.9_spmd, %region_9.10_spmd} | conditional | bytes 147492 | solution.py:328
  101.0 4.5 %wide_block.1 = (bf16[9,4,32,128]{3,2,1,0:T(8,128)(2,1)}, bf16[9,1,32,128]{3,2,1,0:T(8,128)(2,1)}, bf16[9,1,32,128]{3,2,1,0:T(8,128)(2,1)}) custom-call(bf16[9,2,32,128]{3,2,1,0:T(8,128)(2,1)} %get-tuple-element.122.low_ref, bf16[9,4,32,128]{3,2,1,0:T(8,128)(2,1)} %get-tuple-element.123.own_ref, bf16[9,2,32,128]{3,2,1,0:T(8,128)(2,1)} %get-tuple-element.124.high_ref, ...), custom_call_target="tpu_custom_call" | custom-call | tf_op jit(solution)/shard_map/cond/branch_1_fun/wide_block/pallas_call | solution.py:144
  105.5 2.6 %kernel_taps.1 = bf16[9,128,384]{2,1,0:T(8,128)(2,1)S(1)} custom-call(bf16[9,128,1152]{2,1,0:T(8,128)(2,1)S(1)} %tap_rows.1.ut_ref, bf16[9,4,32,128]{3,2,1,0:T(8,128)(2,1)} %get-tuple-element.193.g_ref), custom_call_target="tpu_custom_call" | custom-call | tf_op jit(solution)/shard_map/kernel_taps/pallas_call | solution.py:229
  108.1 0.0 copy-start.4
  108.1 0.0 copy-start.1
  108.1 0.1 constant_dynamic-slice_fusion.4
  108.2 0.2 collective-permute-start.18
  108.4 1.7 %collective-permute-done.18 = bf16[9,64,384]{2,1,0:T(8,128)(2,1)S(1)} collective-permute-done((bf16[9,64,384]{2,1,0:T(8,128)(2,1)S(1)}, bf16[9,64,384]{2,1,0:T(8,128)(2,1)S(1)}, u32[]{:S(2)}, u32[]{:S(2)}) %collective-permute-start.18) | collective-permute-done | bytes 442400 | tf_op jit(solution)/shard_map/ppermute | solution.py:347
  110.0 0.1 add_convert_fusion
  110.2 0.1 collective-permute-start.19
  110.4 8.9 %collective-permute-done.19 = bf16[9,32,384]{2,1,0:T(8,128)(2,1)S(1)} collective-permute-done((bf16[9,32,384]{2,1,0:T(8,128)(2,1)S(1)}, bf16[9,32,384]{2,1,0:T(8,128)(2,1)S(1)}, u32[]{:S(2)}, u32[]{:S(2)}) %collective-permute-start.19) | collective-permute-done | bytes 221216 | tf_op jit(solution)/shard_map/ppermute | solution.py:347
  119.3 0.1 add_convert_fusion.1
  119.4 0.1 collective-permute-start.20
  119.5 4.7 %collective-permute-done.20 = bf16[9,16,384]{2,1,0:T(8,128)(2,1)S(1)} collective-permute-done((bf16[9,16,384]{2,1,0:T(8,128)(2,1)S(1)}, bf16[9,16,384]{2,1,0:T(8,128)(2,1)S(1)}, u32[]{:S(2)}, u32[]{:S(2)}) %collective-permute-start.20) | collective-permute-done | bytes 110624 | tf_op jit(solution)/shard_map/ppermute | solution.py:347
  124.3 3.0 %collective-permute-start.21 = (bf16[9,8,384]{2,1,0:T(8,128)(2,1)S(1)}, bf16[9,8,384]{2,1,0:T(8,128)(2,1)S(1)}, u32[]{:S(2)}, u32[]{:S(2)}) collective-permute-start(bf16[9,8,384]{2,1,0:T(8,128)(2,1)S(1)} %constant_dynamic-slice_fusion.1), channel_id=1, source_target_pairs={{0,8},{1,9},{2,10},{3,11},{4,12},{5,13},{6,14},{7,15},{8,0},{9,1},... | collective-permute-start | bytes 165896 | tf_op jit(solution)/shard_map/ppermute | solution.py:347
  127.3 1.3 collective-permute-start.17
  128.6 0.9 collective-permute-done.21
  129.5 6.2 %collective-permute-start.22 = (bf16[9,4,384]{2,1,0:T(4,128)(2,1)S(1)}, bf16[9,4,384]{2,1,0:T(4,128)(2,1)S(1)}, u32[]{:S(2)}, u32[]{:S(2)}) collective-permute-start(bf16[9,4,384]{2,1,0:T(4,128)(2,1)S(1)} %constant_dynamic-slice_fusion), channel_id=1, source_target_pairs={{0,16},{1,17},{2,18},{3,19},{4,20},{5,21},{6,22},{7,23},{8,24},{9,... | collective-permute-start | bytes 82952 | tf_op jit(solution)/shard_map/ppermute | solution.py:347
  135.8 3.6 %conditional.11 = (bf16[1,9,4,32,128]{4,3,2,1,0:T(8,128)(2,1)}) conditional(s32[]{:T(128)} %convert_element_type.64, (bf16[9,4,32,128]{3,2,1,0:T(8,128)(2,1)}, bf16[9,4,32,128]{3,2,1,0:T(8,128)(2,1)S(1)}) %tuple.66, (bf16[9,1,32,128]{3,2,1,0:T(8,128)(2,1)}, bf16[9,4,32,128]{3,2,1,0:T(8,128)(2,1)S(1)}, bf16[9,1,32,128]{3,2,1,0:T(8,128)(2,1)}, ...), branch_computations={%region_10.11_spmd, %region_11.12_spmd} | conditional | flops 147456 | bytes 884744 | solution.py:336
  135.8 3.6 %one_block_1.3 = (bf16[9,4,32,128]{3,2,1,0:T(8,128)(2,1)}, bf16[9,1,32,128]{3,2,1,0:T(8,128)(2,1)}, bf16[9,1,32,128]{3,2,1,0:T(8,128)(2,1)}) custom-call(bf16[9,1,32,128]{3,2,1,0:T(8,128)(2,1)} %get-tuple-element.129.low_ref, bf16[9,4,32,128]{3,2,1,0:T(8,128)(2,1)S(1)} %get-tuple-element.130.own_ref, bf16[9,1,32,128]{3,2,1,0:T(8,128)(2,1)} %get-tuple-element.131.high_ref, ...), custom_call_target="tpu_custom_call" | custom-call | tf_op jit(solution)/shard_map/cond/branch_1_fun/one_block_1/pallas_call | solution.py:144
  139.3 0.0 collective-permute-done.22
  139.4 0.6 copy.7
  (29 shorter events, 0.3 us)
Async XLA Ops:
  0.6 13.2 %copy-start.2 = (bf16[1,9,4,32,128]{4,3,2,1,0:T(8,128)(2,1)S(1)}, bf16[1,9,4,32,128]{4,3,2,1,0:T(8,128)(2,1)}, u32[]{:S(2)}) copy-start(bf16[1,9,4,32,128]{4,3,2,1,0:T(8,128)(2,1)} %param.16) | copy-start | bytes 884740
  1.7 11.3 %collective-permute-start = (bf16[18,1,32,128]{3,2,1,0:T(8,128)(2,1)S(1)}, bf16[18,1,32,128]{3,2,1,0:T(8,128)(2,1)S(1)}, u32[]{:S(2)}, u32[]{:S(2)}) collective-permute-start(bf16[18,1,32,128]{3,2,1,0:T(8,128)(2,1)S(1)} %get-tuple-element.197), channel_id=1, source_target_pairs={{0,1},{1,2},{2,3},{3,4},{4,5},{5,6},{6,7},{7,8},{8,9},{9,10},{10,1... | collective-permute-start | bytes 442376 | tf_op jit(solution)/shard_map/ppermute | solution.py:31
  3.6 9.3 %collective-permute-start.1 = (bf16[18,1,32,128]{3,2,1,0:T(8,128)(2,1)S(1)}, bf16[18,1,32,128]{3,2,1,0:T(8,128)(2,1)S(1)}, u32[]{:S(2)}, u32[]{:S(2)}) collective-permute-start(bf16[18,1,32,128]{3,2,1,0:T(8,128)(2,1)S(1)} %get-tuple-element.198), channel_id=1, source_target_pairs={{1,0},{2,1},{3,2},{4,3},{5,4},{6,5},{7,6},{8,7},{9,8},{10,9},{11,1... | collective-permute-start | bytes 442376 | tf_op jit(solution)/shard_map/ppermute | solution.py:31
  9.7 35.4 %collective-permute-start.8 = (bf16[3456,128]{1,0:T(8,128)(2,1)}, bf16[3456,128]{1,0:T(8,128)(2,1)}, u32[]{:S(2)}, u32[]{:S(2)}) collective-permute-start(bf16[3456,128]{1,0:T(8,128)(2,1)} %bitcast.11), channel_id=1, source_target_pairs={{160,128},{161,129},{162,130},{163,131},{164,132},{165,133},{166,1... | collective-permute-start | bytes 2654216 | tf_op jit(solution)/shard_map/ppermute | solution.py:31
  13.8 5.6 %copy-start.3 = (bf16[9,4,32,128]{3,2,1,0:T(8,128)(2,1)S(1)}, bf16[9,4,32,128]{3,2,1,0:T(8,128)(2,1)}, u32[]{:S(2)}) copy-start(bf16[9,4,32,128]{3,2,1,0:T(8,128)(2,1)} %param.18) | copy-start | bytes 884740
  13.8 7.0 %copy-start = (bf16[128,128]{1,0:T(8,128)(2,1)S(1)}, bf16[128,128]{1,0:T(8,128)(2,1)}, u32[]{:S(2)}) copy-start(bf16[128,128]{1,0:T(8,128)(2,1)} %constant.119.clone.order_ref) | copy-start | bytes 98308
  13.9 3.4 %collective-permute-start.2 = (bf16[9,4,32,128]{3,2,1,0:T(8,128)(2,1)}, bf16[9,4,32,128]{3,2,1,0:T(8,128)(2,1)S(1)}, u32[]{:S(2)}, u32[]{:S(2)}) collective-permute-start(bf16[9,4,32,128]{3,2,1,0:T(8,128)(2,1)} %get-tuple-element.169), channel_id=1, source_target_pairs={{224,192},{225,193},{226,194},{227,195},{228,196},{229,197},{230,1... | collective-permute-start | bytes 884744 | tf_op jit(solution)/shard_map/ppermute | solution.py:31
  14.6 29.1 %collective-permute-start.9 = (bf16[9,6,32,128]{3,2,1,0:T(8,128)(2,1)S(1)}, bf16[9,6,32,128]{3,2,1,0:T(8,128)(2,1)}, u32[]{:S(2)}, u32[]{:S(2)}) collective-permute-start(bf16[9,6,32,128]{3,2,1,0:T(8,128)(2,1)S(1)} %pad_maximum_fusion.act_ref), channel_id=1, source_target_pairs={{160,128},{161,129},{162,130},{163,131},{164,132},{165,133},{166,1... | collective-permute-start | bytes 1327112 | tf_op jit(solution)/shard_map/ppermute | solution.py:31
  15.9 1.4 collective-permute-start.3
  16.6 0.7 collective-permute-start.4
  18.1 4.0 %copy-start.5 = (bf16[9,2,32,128]{3,2,1,0:T(8,128)(2,1)}, bf16[9,2,32,128]{3,2,1,0:T(8,128)(2,1)S(1)}, u32[]{:S(2)}) copy-start(bf16[9,2,32,128]{3,2,1,0:T(8,128)(2,1)S(1)} %get-tuple-element.175) | copy-start | bytes 442372
  18.1 3.9 %collective-permute-start.5 = (bf16[9,2,32,128]{3,2,1,0:T(8,128)(2,1)S(1)}, bf16[9,2,32,128]{3,2,1,0:T(8,128)(2,1)S(1)}, u32[]{:S(2)}, u32[]{:S(2)}) collective-permute-start(bf16[9,2,32,128]{3,2,1,0:T(8,128)(2,1)S(1)} %get-tuple-element.175), channel_id=1, source_target_pairs={{192,129},{193,130},{194,131},{195,132},{196,133},{197,134},{198,1... | collective-permute-start | bytes 442376 | tf_op jit(solution)/shard_map/ppermute | solution.py:31
  18.7 26.3 %collective-permute-start.6 = (bf16[9,4,32,128]{3,2,1,0:T(8,128)(2,1)}, bf16[9,4,32,128]{3,2,1,0:T(8,128)(2,1)S(1)}, u32[]{:S(2)}, u32[]{:S(2)}) collective-permute-start(bf16[9,4,32,128]{3,2,1,0:T(8,128)(2,1)} %get-tuple-element.173), channel_id=1, source_target_pairs={{192,128},{193,129},{194,130},{195,131},{196,132},{197,133},{198,1... | collective-permute-start | bytes 884744 | tf_op jit(solution)/shard_map/ppermute | solution.py:31
  20.2 24.9 %collective-permute-start.7 = (bf16[9,2,32,128]{3,2,1,0:T(8,128)(2,1)}, bf16[9,2,32,128]{3,2,1,0:T(8,128)(2,1)S(1)}, u32[]{:S(2)}, u32[]{:S(2)}) collective-permute-start(bf16[9,2,32,128]{3,2,1,0:T(8,128)(2,1)} %get-tuple-element.174), channel_id=1, source_target_pairs={{193,128},{194,129},{195,130},{196,131},{197,132},{198,133},{199,1... | collective-permute-start | bytes 442376 | tf_op jit(solution)/shard_map/ppermute | solution.py:31
  45.1 4.0 %collective-permute-start.11 = (bf16[9,4,32,128]{3,2,1,0:T(8,128)(2,1)}, bf16[9,4,32,128]{3,2,1,0:T(8,128)(2,1)}, u32[]{:S(2)}, u32[]{:S(2)}) collective-permute-start(bf16[9,4,32,128]{3,2,1,0:T(8,128)(2,1)} %get-tuple-element.181), channel_id=1, source_target_pairs={{128,64},{129,65},{130,66},{131,67},{132,68},{133,69},{134,70},{13... | collective-permute-start | bytes 884744 | tf_op jit(solution)/shard_map/ppermute | solution.py:31
  46.5 2.6 %collective-permute-start.10 = (bf16[9,2,32,128]{3,2,1,0:T(8,128)(2,1)}, bf16[9,2,32,128]{3,2,1,0:T(8,128)(2,1)}, u32[]{:S(2)}, u32[]{:S(2)}) collective-permute-start(bf16[9,2,32,128]{3,2,1,0:T(8,128)(2,1)} %get-tuple-element.180), channel_id=1, source_target_pairs={{128,65},{129,66},{130,67},{131,68},{132,69},{133,70},{134,71},{13... | collective-permute-start | bytes 442376 | tf_op jit(solution)/shard_map/ppermute | solution.py:31
  47.8 1.3 collective-permute-start.12
  49.3 5.3 %collective-permute-start.13 = (bf16[9,4,32,128]{3,2,1,0:T(8,128)(2,1)}, bf16[9,4,32,128]{3,2,1,0:T(8,128)(2,1)}, u32[]{:S(2)}, u32[]{:S(2)}) collective-permute-start(bf16[9,4,32,128]{3,2,1,0:T(8,128)(2,1)} %get-tuple-element.183), channel_id=1, source_target_pairs={{192,160},{193,161},{194,162},{195,163},{196,164},{197,165},{198,1... | collective-permute-start | bytes 884744 | tf_op jit(solution)/shard_map/ppermute | solution.py:31
  50.7 50.3 %collective-permute-start.15 = (bf16[9,4,32,128]{3,2,1,0:T(8,128)(2,1)}, bf16[9,4,32,128]{3,2,1,0:T(8,128)(2,1)}, u32[]{:S(2)}, u32[]{:S(2)}) collective-permute-start(bf16[9,4,32,128]{3,2,1,0:T(8,128)(2,1)} %get-tuple-element.183), channel_id=1, source_target_pairs={{64,0},{65,1},{66,2},{67,3},{68,4},{69,5},{70,6},{71,7},{72,8},{73... | collective-permute-start | bytes 884744 | tf_op jit(solution)/shard_map/ppermute | solution.py:31
  52.0 33.5 %collective-permute-start.14 = (bf16[9,2,32,128]{3,2,1,0:T(8,128)(2,1)}, bf16[9,2,32,128]{3,2,1,0:T(8,128)(2,1)}, u32[]{:S(2)}, u32[]{:S(2)}) collective-permute-start(bf16[9,2,32,128]{3,2,1,0:T(8,128)(2,1)} %get-tuple-element.185), channel_id=1, source_target_pairs={{64,1},{65,2},{66,3},{67,4},{68,5},{69,6},{70,7},{71,8},{72,9},{73... | collective-permute-start | bytes 442376 | tf_op jit(solution)/shard_map/ppermute | solution.py:31
  53.3 47.7 %collective-permute-start.16 = (bf16[9,2,32,128]{3,2,1,0:T(8,128)(2,1)}, bf16[9,2,32,128]{3,2,1,0:T(8,128)(2,1)}, u32[]{:S(2)}, u32[]{:S(2)}) collective-permute-start(bf16[9,2,32,128]{3,2,1,0:T(8,128)(2,1)} %get-tuple-element.188), channel_id=1, source_target_pairs={{65,0},{66,1},{67,2},{68,3},{69,4},{70,5},{71,6},{72,7},{73,8},{74... | collective-permute-start | bytes 442376 | tf_op jit(solution)/shard_map/ppermute | solution.py:31
  108.1 19.2 %copy-start.4 = (bf16[9,4,32,128]{3,2,1,0:T(8,128)(2,1)S(1)}, bf16[9,4,32,128]{3,2,1,0:T(8,128)(2,1)}, u32[]{:S(2)}) copy-start(bf16[9,4,32,128]{3,2,1,0:T(8,128)(2,1)} %get-tuple-element.193.g_ref) | copy-start | bytes 884740
  108.1 27.7 %copy-start.1 = (bf16[1,3,3,3,128,128]{5,4,3,2,1,0:T(8,128)(2,1)S(1)}, bf16[1,3,3,3,128,128]{5,4,3,2,1,0:T(8,128)(2,1)}, u32[]{:S(2)}) copy-start(bf16[1,3,3,3,128,128]{5,4,3,2,1,0:T(8,128)(2,1)} %param.17) | copy-start | bytes 2654212
  108.2 1.9 %collective-permute-start.18 = (bf16[9,64,384]{2,1,0:T(8,128)(2,1)S(1)}, bf16[9,64,384]{2,1,0:T(8,128)(2,1)S(1)}, u32[]{:S(2)}, u32[]{:S(2)}) collective-permute-start(bf16[9,64,384]{2,1,0:T(8,128)(2,1)S(1)} %constant_dynamic-slice_fusion.4), channel_id=1, source_target_pairs={{0,1},{1,0},{2,3},{3,2},{4,5},{5,4},{6,7},{7,6},{8,9},{9,8},{10,11... | collective-permute-start | bytes 1327112 | tf_op jit(solution)/shard_map/ppermute | solution.py:347
  110.2 9.1 %collective-permute-start.19 = (bf16[9,32,384]{2,1,0:T(8,128)(2,1)S(1)}, bf16[9,32,384]{2,1,0:T(8,128)(2,1)S(1)}, u32[]{:S(2)}, u32[]{:S(2)}) collective-permute-start(bf16[9,32,384]{2,1,0:T(8,128)(2,1)S(1)} %constant_dynamic-slice_fusion.3), channel_id=1, source_target_pairs={{0,2},{1,3},{2,0},{3,1},{4,6},{5,7},{6,4},{7,5},{8,10},{9,11},{10,... | collective-permute-start | bytes 663560 | tf_op jit(solution)/shard_map/ppermute | solution.py:347
  119.4 4.8 %collective-permute-start.20 = (bf16[9,16,384]{2,1,0:T(8,128)(2,1)S(1)}, bf16[9,16,384]{2,1,0:T(8,128)(2,1)S(1)}, u32[]{:S(2)}, u32[]{:S(2)}) collective-permute-start(bf16[9,16,384]{2,1,0:T(8,128)(2,1)S(1)} %constant_dynamic-slice_fusion.2), channel_id=1, source_target_pairs={{0,4},{1,5},{2,6},{3,7},{4,0},{5,1},{6,2},{7,3},{8,12},{9,13},{10,... | collective-permute-start | bytes 331784 | tf_op jit(solution)/shard_map/ppermute | solution.py:347
  124.3 5.2 %collective-permute-start.21 = (bf16[9,8,384]{2,1,0:T(8,128)(2,1)S(1)}, bf16[9,8,384]{2,1,0:T(8,128)(2,1)S(1)}, u32[]{:S(2)}, u32[]{:S(2)}) collective-permute-start(bf16[9,8,384]{2,1,0:T(8,128)(2,1)S(1)} %constant_dynamic-slice_fusion.1), channel_id=1, source_target_pairs={{0,8},{1,9},{2,10},{3,11},{4,12},{5,13},{6,14},{7,15},{8,0},{9,1},... | collective-permute-start | bytes 165896 | tf_op jit(solution)/shard_map/ppermute | solution.py:347
  127.3 8.5 %collective-permute-start.17 = (bf16[9,4,32,128]{3,2,1,0:T(8,128)(2,1)S(1)}, bf16[9,4,32,128]{3,2,1,0:T(8,128)(2,1)S(1)}, u32[]{:S(2)}, u32[]{:S(2)}) collective-permute-start(bf16[9,4,32,128]{3,2,1,0:T(8,128)(2,1)S(1)} %copy-done.4), channel_id=1, source_target_pairs={{128,160},{129,161},{130,162},{131,163},{132,164},{133,165},{134,1... | collective-permute-start | bytes 884744 | tf_op jit(solution)/shard_map/ppermute | solution.py:31
  129.5 9.8 %collective-permute-start.22 = (bf16[9,4,384]{2,1,0:T(4,128)(2,1)S(1)}, bf16[9,4,384]{2,1,0:T(4,128)(2,1)S(1)}, u32[]{:S(2)}, u32[]{:S(2)}) collective-permute-start(bf16[9,4,384]{2,1,0:T(4,128)(2,1)S(1)} %constant_dynamic-slice_fusion), channel_id=1, source_target_pairs={{0,16},{1,17},{2,18},{3,19},{4,20},{5,21},{6,22},{7,23},{8,24},{9,... | collective-permute-start | bytes 82952 | tf_op jit(solution)/shard_map/ppermute | solution.py:347

commit v7 on v6

--- a/solution.py
+++ b/solution.py
@@ -7,6 +7,7 @@
 from jax import lax
 from jax.experimental import pallas as pl
 from jax.experimental.pallas import tpu as pltpu
+from jax.sharding import Mesh
 from jax.sharding import PartitionSpec as P
 
 BF = jnp.bfloat16
@@ -17,8 +18,8 @@
 ROWS = 4
 COLS = 32
 CH = 128
-AXES = ("section", "dp")
-HALVING = (1, 2, 4, 8, 16)
+PEERS = 16
+AXES = ("section", "z", "y", "core")
 
 
 def permute(value, hops):
@@ -55,7 +56,7 @@
     )
 
 
-def back_pass(x_ref, rhs, slope_ref, rows, emit):
+def back_pass(x_ref, rhs, slope_ref, rows, emit, rhs_dim=1):
     group = 3
     size = rows * COLS
     one_later = None
@@ -65,7 +66,7 @@
             [x_ref[start : start + group, 2 - j : 2 - j + rows] for j in range(3)], axis=-1
         ).reshape(group * size, 9 * CH)
         part = lax.dot_general(
-            lhs, rhs, (((1,), (1,)), ((), ())), preferred_element_type=F32
+            lhs, rhs, (((1,), (rhs_dim,)), ((), ())), preferred_element_type=F32
         )
         for t in range(group - 1, -1, -1):
             here = part[t * size : (t + 1) * size]
@@ -101,10 +102,22 @@
     return emit
 
 
-def single_kernel(low_ref, own_ref, high_ref, w_ref, slope_ref, *rest):
-    *outs, x_ref = rest
+def single_kernel(low_ref, own_ref, high_ref, slope_ref, w_ref, *rest):
+    *outs, x_ref, held_ref, sem = rest
+    copy = pltpu.make_async_copy(w_ref, held_ref, sem)
+    copy.start()
     load(low_ref, own_ref, high_ref, x_ref)
-    back_pass(x_ref, weights(w_ref), slope_ref, ROWS, emit_to(outs))
+    copy.wait()
+    back_pass(x_ref, weights(held_ref), slope_ref, ROWS, emit_to(outs))
+
+
+def last_kernel(low_ref, own_ref, high_ref, slope_ref, w_ref, out_ref, x_ref):
+    load(low_ref, own_ref, high_ref, x_ref)
+
+    def emit(frame, value):
+        out_ref[frame] = value.reshape(ROWS, COLS, CH)
+
+    back_pass(x_ref, w_ref[...], slope_ref, ROWS, emit, 0)
 
 
 def wide_kernel(low_ref, own_ref, high_ref, w_ref, slope_ref, *rest):
@@ -117,7 +130,7 @@
         own_out[frame] = whole[1 : 1 + ROWS]
         high_out[frame] = whole[1 + ROWS :]
 
-    back_pass(x_ref, weights(w_ref), slope_ref, ROWS + 2, emit)
+    back_pass(x_ref, w_ref[...], slope_ref, ROWS + 2, emit, 0)
 
 
 def double_kernel(low_ref, own_ref, high_ref, w1_ref, slope1_ref, w0_ref, slope0_ref, *rest):
@@ -128,8 +141,8 @@
         fill(x0_ref, frame, 0, value.astype(F32))
         middle_ref[frame] = value.reshape(ROWS + 2, COLS, CH)[1 : 1 + ROWS]
 
-    back_pass(x1_ref, weights(w1_ref), slope1_ref, ROWS + 2, emit_middle)
-    back_pass(x0_ref, weights(w0_ref), slope0_ref, ROWS, emit_to(outs))
+    back_pass(x1_ref, w1_ref[...], slope1_ref, ROWS + 2, emit_middle, 0)
+    back_pass(x0_ref, w0_ref[...], slope0_ref, ROWS, emit_to(outs), 0)
 
 
 def in_vmem(count):
@@ -140,13 +153,19 @@
     return jax.ShapeDtypeStruct((FRAMES, rows, COLS, CH), BF)
 
 
-def block_call(kernel, name, operands, outs, halos):
+def block_call(kernel, name, operands, outs, halos, held=None):
+    scratch = [pltpu.VMEM((FRAMES, r, COLS, 3 * CH), BF) for r in halos]
+    specs = in_vmem(len(operands))
+    if held is not None:
+        operands = (*operands, held)
+        specs.append(pl.BlockSpec(memory_space=pl.ANY))
+        scratch += [pltpu.VMEM(held.shape, BF), pltpu.SemaphoreType.DMA]
     return pl.pallas_call(
         kernel,
         out_shape=[rows_shape(r) for r in outs],
-        in_specs=in_vmem(len(operands)),
+        in_specs=specs,
         out_specs=in_vmem(len(outs)),
-        scratch_shapes=[pltpu.VMEM((FRAMES, r, COLS, 3 * CH), BF) for r in halos],
+        scratch_shapes=scratch,
         compiler_params=pltpu.CompilerParams(vmem_limit_bytes=24 << 20),
         name=name,
     )(*operands)
@@ -156,10 +175,17 @@
     return block_call(
         single_kernel,
         f"one_block_{edge}",
-        (low, own, high, w, slope),
+        (low, own, high, slope),
         (ROWS, edge, edge),
         (ROWS + 2,),
-    )
+        w,
+    )
+
+
+def last(low, own, high, w, slope):
+    return block_call(
+        last_kernel, "last_block", (low, own, high, slope, w), (ROWS,), (ROWS + 2,)
+    )[0]
 
 
 def wide(low, own, high, w, slope):
@@ -238,14 +264,12 @@
 
 def channel_order():
     share = CH // DP
-    order = []
-    for n in range(CH):
-        slot, rest = divmod(n, share)
-        d = 0
-        for place, bit in enumerate(HALVING):
-            if (slot >> (len(HALVING) - 1 - place)) & 1:
-                d |= bit
-        order.append(d * share + rest)
+    order = [
+        (chip * 2 + core) * share + rest
+        for core in range(2)
+        for chip in range(PEERS)
+        for rest in range(share)
+    ]
     matrix = np.zeros((CH, CH), np.float32)
     matrix[np.arange(CH), order] = 1.0
     return matrix
@@ -257,9 +281,15 @@
     return sig * (1.0 + x * (1.0 - sig))
 
 
+def as_matrix(w):
+    kern = w.reshape(3, 3, 3, CH, CH)
+    return jnp.transpose(kern, (1, 2, 4, 0, 3)).reshape(9 * CH, 3 * CH)
+
+
 def local(acts, kernels, cotangent):
     me = lax.axis_index("section")
-    dp = lax.axis_index("dp")
+    dp = lax.axis_index(AXES[1:])
+    core = lax.axis_index("core")
     scale = 1.0 / math.sqrt(FRAMES * ROWS * DP * COLS)
     every = range(SEC)
     pairs = (4, 2, 0)
@@ -301,12 +331,12 @@
         lambda: tuple(single(low, own, high, w, slope, 2)),
         lambda: (result, blank(2), blank(2)),
     )
-    act6, own, result = barrier((act6, own, result))
+    w, own, result = barrier((w, own, result))
     grad = jnp.where(me == 7, cotangent, own)
-    ut = tap_rows(act6, jnp.asarray(channel_order(), BF))
+    w_next, w = as_matrix(w_next), as_matrix(w)
 
     low, own, high = hop(result, top, bottom, 6, 4)
-    ut, grad, low = barrier((ut, grad, low))
+    w, w_next, grad, low = barrier((w, w_next, grad, low))
     for section in (4, 2):
         result, top, bottom, grad = lax.cond(
             me == section,
@@ -323,7 +353,9 @@
         low, own, high = hop(result, top, bottom, section, section - 2)
 
     grad = grad + permute(result, [(s + 1, s, 0) for s in (5, 3, 1)])
-    grad, low = barrier((grad, low))
+    act6, grad = barrier((act6, grad))
+    ut = tap_rows(act6, jnp.asarray(channel_order(), BF))
+    ut, grad, low = barrier((ut, grad, low))
 
     grad, low, high = lax.cond(
         me == 0,
@@ -335,35 +367,36 @@
     result = result + permute(grad, [(s - 1, s, 0) for s in (5, 3, 1)])
     final = lax.cond(
         me == 0,
-        lambda: single(low, grad, high, w, slope, 1)[0],
+        lambda: last(low, grad, high, w, slope),
         lambda: result,
     )
 
-    for bit in HALVING:
-        size = part.shape[1] // 2
-        mine = (dp // bit) % 2
-        keep = lax.dynamic_slice_in_dim(part, mine * size, size, 1)
-        give = lax.dynamic_slice_in_dim(part, (1 - mine) * size, size, 1)
-        got = lax.ppermute(
-            give, AXES, [(s * DP + d, s * DP + (d ^ bit)) for s in every for d in range(DP)]
-        )
-        part = keep.astype(F32) + got.astype(F32)
-        if bit != HALVING[-1]:
-            part = part.astype(BF)
+    half = CH // 2
+    keep = lax.dynamic_slice_in_dim(part, core * half, half, 1)
+    give = lax.dynamic_slice_in_dim(part, (1 - core) * half, half, 1)
+    got = lax.ppermute(
+        give, AXES, [(s * DP + d, s * DP + (d ^ 1)) for s in every for d in range(DP)]
+    )
+    part = (keep.astype(F32) + got.astype(F32)).astype(BF)
+    part = jnp.transpose(part.reshape(9, PEERS, CH // DP, 3 * CH), (1, 0, 2, 3))
+    part = lax.all_to_all(part, ("z", "y"), 0, 0, tiled=True)
+    part = jnp.sum(part.astype(F32), axis=0)
     share = CH // DP
     kernel_part = jnp.transpose(part.reshape(9, share, 3, CH), (1, 2, 0, 3)).reshape(share, 27, CH)
     return (final[None], kernel_part[None])
 
 
 def solution(mesh):
+    parts = Mesh(mesh.devices.reshape(SEC, DP // 4, 2, 2), AXES)
+    rows = AXES[1:]
     return jax.shard_map(
         local,
-        mesh=mesh,
+        mesh=parts,
         in_specs=(
-            P("section", None, "dp", None, None),
+            P("section", None, rows, None, None),
             P("section", None, None, None, None, None),
-            P(None, "dp", None, None),
+            P(None, rows, None, None),
         ),
-        out_specs=(P("section", None, "dp", None, None), P("section", "dp", None, None)),
+        out_specs=(P("section", None, rows, None, None), P("section", rows, None, None)),
         check_vma=False,
     )

time: 141 us -> 141 us (level)
  the two profiles are of different devices: /device:TPU:32 before, /device:TPU:1 now
where the time goes in v7:
time: 141 us; the launch traced here: 140 us
  waiting for transfers between devices  70.7 us (50%)
  starting transfers between devices  41.1 us (29%)
  local copies, waits for them, and re-layouts  12.4 us (9%)
  Pallas kernels  10 us (7%)
  other arithmetic  4.83 us (3%)
    ppermute x18, waiting for transfers between devices, permute(): return lax.ppermute(value, AXES, pairs)  64.1 us
    ppermute x18, starting transfers between devices, permute(): return lax.ppermute(value, AXES, pairs)  26.6 us
    all_to_all x1, starting transfers between devices, local(): part = lax.all_to_all(part, ('z', 'y'), 0, 0, tiled=True)  10.9 us
    pallas_call x2, Pallas kernels, block_call(): pl.pallas_call(kernel, out_shape=[rows_shape(r) for r in outs], in_specs=...  6.36 us
    reshape x2, local copies, waits for them, and re-layouts, as_matrix(): kern = w.reshape(3, 3, 3, CH, CH)  5.51 us
    all_to_all x1, waiting for transfers between devices, local(): part = lax.all_to_all(part, ('z', 'y'), 0, 0, tiled=True)  5.1 us
    ppermute x1, starting transfers between devices, local(): lax.ppermute(give, AXES, [(s * DP + d, s * DP + (d ^ 1)) for s in every f...  3.55 us
    reshape x1, local copies, waits for them, and re-layouts, as_matrix(): return jnp.transpose(kern, (1, 2, 4, 0, 3)).reshape(9 * CH, 3 * CH)  2.84 us
  transfers between devices with their start and end apart: 20, of which 6 were waited for; matrix products, arithmetic and copies ran while one was open for 10% of the time, Pallas kernels for 2%

profile of v7, /device:TPU:1, one launch (start us, length us, event | category | flops | bytes accessed | tf_op | source)
XLA Modules:
  0.0 140.4 jit_solution(1125076890877814330)
XLA Ops:
  0.6 0.0 copy-start.6
  0.7 1.1 pad_maximum_fusion.2
  1.8 6.2 %collective-permute-start = (bf16[18,1,32,128]{3,2,1,0:T(8,128)(2,1)S(1)}, bf16[18,1,32,128]{3,2,1,0:T(8,128)(2,1)S(1)}, u32[]{:S(2)}, u32[]{:S(2)}) collective-permute-start(bf16[18,1,32,128]{3,2,1,0:T(8,128)(2,1)S(1)} %get-tuple-element.204), channel_id=1, source_target_pairs={{0,1},{1,2},{2,3},{3,4},{4,5},{5,6},{6,7},{7,8},{8,9},{9,10},{10,1... | collective-permute-start | bytes 442376 | tf_op jit(solution)/shard_map/ppermute | solution.py:32
  8.0 1.9 %collective-permute-start.1 = (bf16[18,1,32,128]{3,2,1,0:T(8,128)(2,1)S(1)}, bf16[18,1,32,128]{3,2,1,0:T(8,128)(2,1)S(1)}, u32[]{:S(2)}, u32[]{:S(2)}) collective-permute-start(bf16[18,1,32,128]{3,2,1,0:T(8,128)(2,1)S(1)} %get-tuple-element.205), channel_id=1, source_target_pairs={{1,0},{2,1},{3,2},{4,3},{5,4},{6,5},{7,6},{8,7},{9,8},{10,9},{11,1... | collective-permute-start | bytes 442376 | tf_op jit(solution)/shard_map/ppermute | solution.py:32
  9.9 1.3 collective-permute-start.5
  11.2 1.2 fusion.10
  12.4 3.5 %collective-permute-done.1 = bf16[18,1,32,128]{3,2,1,0:T(8,128)(2,1)S(1)} collective-permute-done((bf16[18,1,32,128]{3,2,1,0:T(8,128)(2,1)S(1)}, bf16[18,1,32,128]{3,2,1,0:T(8,128)(2,1)S(1)}, u32[]{:S(2)}, u32[]{:S(2)}) %collective-permute-start.1) | collective-permute-done | bytes 147488 | tf_op jit(solution)/shard_map/ppermute | solution.py:32
  16.0 0.7 conditional.6
  16.1 0.6 broadcast.24.clone
  16.7 0.2 copy-done.7
  16.9 0.1 pad_maximum_fusion.act_ref
  17.0 0.7 collective-permute-start.2
  17.7 1.3 collective-permute-start.9
  19.0 0.7 collective-permute-start.3
  19.7 0.7 collective-permute-start.4
  20.4 0.0 collective-permute-done.2
  20.4 1.4 conditional.7
  20.4 0.7 broadcast.25
  21.1 0.7 broadcast.25.clone
  21.8 2.0 %copy.13 = bf16[3,3,3,128,128]{3,0,4,2,1:T(4,128)(2,1)} copy(bf16[3,3,3,128,128]{4,3,2,1,0:T(8,128)(2,1)S(1)} %bitcast.28) | data formatting | bytes 1769472 | tf_op jit(solution)/shard_map/reshape | solution.py:285
  23.8 1.3 collective-permute-start.6
  25.1 1.4 collective-permute-start.7
  26.5 1.3 collective-permute-start.8
  27.8 14.9 %collective-permute-done.9 = bf16[9,6,32,128]{3,2,1,0:T(8,128)(2,1)} collective-permute-done((bf16[9,6,32,128]{3,2,1,0:T(8,128)(2,1)S(1)}, bf16[9,6,32,128]{3,2,1,0:T(8,128)(2,1)}, u32[]{:S(2)}, u32[]{:S(2)}) %collective-permute-start.9) | collective-permute-done | bytes 442400 | tf_op jit(solution)/shard_map/ppermute | solution.py:32
  42.7 1.3 fusion.5
  44.1 0.0 collective-permute-done.5
  44.1 3.5 %copy.14 = bf16[3,3,3,128,128]{3,0,4,2,1:T(4,128)(2,1)} copy(bf16[3,3,3,128,128]{4,3,2,1,0:T(8,128)(2,1)} %bitcast.6) | data formatting | bytes 1769472 | tf_op jit(solution)/shard_map/reshape | solution.py:285
  47.6 2.8 %copy_bitcast_fusion = (bf16[1152,384]{1,0:T(8,128)(2,1)}, bf16[1152,384]{1,0:T(8,128)(2,1)S(1)}) fusion(bf16[144,8,3,128]{3,2,1,0:T(4,128)(2,1)} %bitcast.30, bf16[144,8,3,128]{3,2,1,0:T(4,128)(2,1)} %bitcast.29), kind=kLoop, calls=%fused_computation.9 | loop fusion | bytes 3538944 | tf_op jit(solution)/shard_map/reshape | solution.py:286
  50.5 0.0 collective-permute-done.7
  50.5 1.4 collective-permute-start.11
  51.9 1.3 collective-permute-start.10
  53.2 1.3 collective-permute-start.12
  54.5 0.0 collective-permute-done.10
  54.5 0.0 collective-permute-done.12
  54.5 0.0 collective-permute-done.11
  54.6 0.0 copy-start
  54.6 0.2 conditional.9
  54.8 0.0 copy-start.10
  54.8 0.7 collective-permute-start.13
  55.5 1.3 collective-permute-start.15
  56.8 1.3 collective-permute-start.14
  58.1 1.3 collective-permute-start.16
  59.4 0.8 add.53
  60.2 1.1 tap_rows.1.ut_ref
  61.3 37.9 %collective-permute-done.14 = bf16[9,2,32,128]{3,2,1,0:T(8,128)(2,1)} collective-permute-done((bf16[9,2,32,128]{3,2,1,0:T(8,128)(2,1)}, bf16[9,2,32,128]{3,2,1,0:T(8,128)(2,1)}, u32[]{:S(2)}, u32[]{:S(2)}) %collective-permute-start.14) | collective-permute-done | bytes 147488 | tf_op jit(solution)/shard_map/ppermute | solution.py:32
  99.2 4.7 %conditional.10 = ((bf16[9,4,32,128]{3,2,1,0:T(8,128)(2,1)}, bf16[9,1,32,128]{3,2,1,0:T(8,128)(2,1)}, bf16[9,1,32,128]{3,2,1,0:T(8,128)(2,1)})) conditional(s32[]{:T(128)} %convert_element_type.34, bf16[9,4,32,128]{3,2,1,0:T(8,128)(2,1)} %add.53, (bf16[9,2,32,128]{3,2,1,0:T(8,128)(2,1)}, bf16[9,4,32,128]{3,2,1,0:T(8,128)(2,1)}, ...), branch_computations={%region_8.9_spmd, %region_9.10_spmd} | conditional | bytes 147492 | solution.py:360
  99.2 4.7 %wide_block.1 = (bf16[9,4,32,128]{3,2,1,0:T(8,128)(2,1)}, bf16[9,1,32,128]{3,2,1,0:T(8,128)(2,1)}, bf16[9,1,32,128]{3,2,1,0:T(8,128)(2,1)}) custom-call(bf16[9,2,32,128]{3,2,1,0:T(8,128)(2,1)} %get-tuple-element.122.low_ref, bf16[9,4,32,128]{3,2,1,0:T(8,128)(2,1)} %get-tuple-element.123.own_ref, bf16[9,2,32,128]{3,2,1,0:T(8,128)(2,1)} %get-tuple-element.124.high_ref, ...), custom_call_target="tpu_custom_call" | custom-call | tf_op jit(solution)/shard_map/cond/branch_1_fun/wide_block/pallas_call | solution.py:163
  104.0 2.6 %kernel_taps.1 = bf16[9,128,384]{2,1,0:T(8,128)(2,1)S(1)} custom-call(bf16[9,128,1152]{2,1,0:T(8,128)(2,1)S(1)} %tap_rows.1.ut_ref, bf16[9,4,32,128]{3,2,1,0:T(8,128)(2,1)} %get-tuple-element.200.g_ref), custom_call_target="tpu_custom_call" | custom-call | tf_op jit(solution)/shard_map/kernel_taps/pallas_call | solution.py:255
  106.5 0.1 constant_dynamic-slice_fusion
  106.6 3.5 %collective-permute-start.18 = (bf16[9,64,384]{2,1,0:T(8,128)(2,1)S(1)}, bf16[9,64,384]{2,1,0:T(8,128)(2,1)S(1)}, u32[]{:S(2)}, u32[]{:S(2)}) collective-permute-start(bf16[9,64,384]{2,1,0:T(8,128)(2,1)S(1)} %constant_dynamic-slice_fusion), channel_id=1, source_target_pairs={{0,1},{1,0},{2,3},{3,2},{4,5},{5,4},{6,7},{7,6},{8,9},{9,8},{10,11... | collective-permute-start | bytes 1327112 | tf_op jit(solution)/shard_map/ppermute | solution.py:377
  110.1 1.4 %collective-permute-done.18 = bf16[9,64,384]{2,1,0:T(8,128)(2,1)S(1)} collective-permute-done((bf16[9,64,384]{2,1,0:T(8,128)(2,1)S(1)}, bf16[9,64,384]{2,1,0:T(8,128)(2,1)S(1)}, u32[]{:S(2)}, u32[]{:S(2)}) %collective-permute-start.18) | collective-permute-done | bytes 442400 | tf_op jit(solution)/shard_map/ppermute | solution.py:377
  111.6 0.1 add_convert_fusion
  111.7 0.0 copy-start.11
  111.8 0.1 reshape.26
  111.9 0.9 copy.22
  112.8 10.9 %all-to-all-start = ((bf16[16,9,4,384]{3,2,1,0:T(4,128)(2,1)}), bf16[16,9,4,384]{3,2,1,0:T(4,128)(2,1)S(1)}, u32[]{:S(2)}, u32[]{:S(2)}) async-start(bf16[16,9,4,384]{3,2,1,0:T(4,128)(2,1)} %bitcast.24), calls=%async_computation | async-start | bytes 884736 | tf_op jit(solution)/shard_map/all_to_all | solution.py:382
  123.7 1.3 collective-permute-start.17
  125.0 7.8 %collective-permute-done.17 = bf16[9,4,32,128]{3,2,1,0:T(8,128)(2,1)S(1)} collective-permute-done((bf16[9,4,32,128]{3,2,1,0:T(8,128)(2,1)S(1)}, bf16[9,4,32,128]{3,2,1,0:T(8,128)(2,1)S(1)}, u32[]{:S(2)}, u32[]{:S(2)}) %collective-permute-start.17) | collective-permute-done | bytes 294944 | tf_op jit(solution)/shard_map/ppermute | solution.py:32
  132.8 1.7 %conditional.11 = (bf16[1,9,4,32,128]{4,3,2,1,0:T(8,128)(2,1)S(1)}) conditional(s32[]{:T(128)} %convert_element_type.34, (bf16[9,4,32,128]{3,2,1,0:T(8,128)(2,1)S(1)}, bf16[9,4,32,128]{3,2,1,0:T(8,128)(2,1)S(1)}) %tuple.102, (bf16[9,1,32,128]{3,2,1,0:T(8,128)(2,1)S(1)}, bf16[9,4,32,128]{3,2,1,0:T(8,128)(2,1)S(1)}, ...), branch_computations={%region_10.11_spmd, %region_11.12_spmd} | conditional | flops 147456 | bytes 884744 | solution.py:368
  132.8 1.6 %last_block.1 = bf16[9,4,32,128]{3,2,1,0:T(8,128)(2,1)S(1)} custom-call(bf16[9,1,32,128]{3,2,1,0:T(8,128)(2,1)S(1)} %get-tuple-element.129.low_ref, bf16[9,4,32,128]{3,2,1,0:T(8,128)(2,1)S(1)} %get-tuple-element.130.own_ref, bf16[9,1,32,128]{3,2,1,0:T(8,128)(2,1)S(1)} %get-tuple-element.131.high_ref, f32[9,4,32,128]{3,2,1,0:T(8,128)S(1)} %get-tuple-element.132.slope_ref, ...), custom_call_target="tpu_custom_call" | custom-call | tf_op jit(solution)/shard_map/cond/branch_1_fun/last_block/pallas_call | solution.py:163
  134.5 0.0 copy-start.14
  134.5 5.1 %all-to-all-done = bf16[16,9,4,384]{3,2,1,0:T(4,128)(2,1)S(1)} async-done(((bf16[16,9,4,384]{3,2,1,0:T(4,128)(2,1)}), bf16[16,9,4,384]{3,2,1,0:T(4,128)(2,1)S(1)}, u32[]{:S(2)}, u32[]{:S(2)}) %all-to-all-start) | async-done | bytes 442400 | tf_op jit(solution)/shard_map/all_to_all | solution.py:382
  139.6 0.2 convert_reduce_fusion
  139.8 0.6 copy.16
  (39 shorter events, 0.2 us)
Async XLA Ops:
  0.6 15.3 %copy-start.8 = (bf16[9,4,32,128]{3,2,1,0:T(8,128)(2,1)S(1)}, bf16[9,4,32,128]{3,2,1,0:T(8,128)(2,1)}, u32[]{:S(2)}) copy-start(bf16[9,4,32,128]{3,2,1,0:T(8,128)(2,1)} %param.18) | copy-start | bytes 884740
  0.6 15.3 %copy-start.6 = (bf16[1,3,3,3,128,128]{5,4,3,2,1,0:T(8,128)(2,1)S(1)}, bf16[1,3,3,3,128,128]{5,4,3,2,1,0:T(8,128)(2,1)}, u32[]{:S(2)}) copy-start(bf16[1,3,3,3,128,128]{5,4,3,2,1,0:T(8,128)(2,1)} %param.17) | copy-start | bytes 2654212
  1.8 10.6 %collective-permute-start = (bf16[18,1,32,128]{3,2,1,0:T(8,128)(2,1)S(1)}, bf16[18,1,32,128]{3,2,1,0:T(8,128)(2,1)S(1)}, u32[]{:S(2)}, u32[]{:S(2)}) collective-permute-start(bf16[18,1,32,128]{3,2,1,0:T(8,128)(2,1)S(1)} %get-tuple-element.204), channel_id=1, source_target_pairs={{0,1},{1,2},{2,3},{3,4},{4,5},{5,6},{6,7},{7,8},{8,9},{9,10},{10,1... | collective-permute-start | bytes 442376 | tf_op jit(solution)/shard_map/ppermute | solution.py:32
  8.0 8.0 %collective-permute-start.1 = (bf16[18,1,32,128]{3,2,1,0:T(8,128)(2,1)S(1)}, bf16[18,1,32,128]{3,2,1,0:T(8,128)(2,1)S(1)}, u32[]{:S(2)}, u32[]{:S(2)}) collective-permute-start(bf16[18,1,32,128]{3,2,1,0:T(8,128)(2,1)S(1)} %get-tuple-element.205), channel_id=1, source_target_pairs={{1,0},{2,1},{3,2},{4,3},{5,4},{6,5},{7,6},{8,7},{9,8},{10,9},{11,1... | collective-permute-start | bytes 442376 | tf_op jit(solution)/shard_map/ppermute | solution.py:32
  9.9 34.2 %collective-permute-start.5 = (bf16[3456,128]{1,0:T(8,128)(2,1)}, bf16[3456,128]{1,0:T(8,128)(2,1)}, u32[]{:S(2)}, u32[]{:S(2)}) collective-permute-start(bf16[3456,128]{1,0:T(8,128)(2,1)} %bitcast.25), channel_id=1, source_target_pairs={{160,128},{161,129},{162,130},{163,131},{164,132},{165,133},{166,1... | collective-permute-start | bytes 2654216 | tf_op jit(solution)/shard_map/ppermute | solution.py:32
  12.4 42.1 %copy-start.1 = (f32[9,4,32,128]{3,2,1,0:T(8,128)}, f32[9,4,32,128]{3,2,1,0:T(8,128)S(1)}, u32[]{:S(2)}) copy-start(f32[9,4,32,128]{3,2,1,0:T(8,128)S(1)} %fusion.10) | copy-start | bytes 1769476
  16.0 1.0 copy-start.7
  17.0 3.4 %collective-permute-start.2 = (bf16[9,4,32,128]{3,2,1,0:T(8,128)(2,1)S(1)}, bf16[9,4,32,128]{3,2,1,0:T(8,128)(2,1)S(1)}, u32[]{:S(2)}, u32[]{:S(2)}) collective-permute-start(bf16[9,4,32,128]{3,2,1,0:T(8,128)(2,1)S(1)} %get-tuple-element.171), channel_id=1, source_target_pairs={{224,192},{225,193},{226,194},{227,195},{228,196},{229,197},{230,1... | collective-permute-start | bytes 884744 | tf_op jit(solution)/shard_map/ppermute | solution.py:32
  17.7 25.1 %collective-permute-start.9 = (bf16[9,6,32,128]{3,2,1,0:T(8,128)(2,1)S(1)}, bf16[9,6,32,128]{3,2,1,0:T(8,128)(2,1)}, u32[]{:S(2)}, u32[]{:S(2)}) collective-permute-start(bf16[9,6,32,128]{3,2,1,0:T(8,128)(2,1)S(1)} %pad_maximum_fusion.act_ref), channel_id=1, source_target_pairs={{160,128},{161,129},{162,130},{163,131},{164,132},{165,133},{166,1... | collective-permute-start | bytes 1327112 | tf_op jit(solution)/shard_map/ppermute | solution.py:32
  19.0 1.4 collective-permute-start.3
  19.7 0.7 collective-permute-start.4
  23.8 26.7 %collective-permute-start.6 = (bf16[9,2,32,128]{3,2,1,0:T(8,128)(2,1)}, bf16[9,2,32,128]{3,2,1,0:T(8,128)(2,1)}, u32[]{:S(2)}, u32[]{:S(2)}) collective-permute-start(bf16[9,2,32,128]{3,2,1,0:T(8,128)(2,1)} %get-tuple-element.177), channel_id=1, source_target_pairs={{192,129},{193,130},{194,131},{195,132},{196,133},{197,134},{198,1... | collective-permute-start | bytes 442376 | tf_op jit(solution)/shard_map/ppermute | solution.py:32
  25.1 25.4 %collective-permute-start.7 = (bf16[9,4,32,128]{3,2,1,0:T(8,128)(2,1)S(1)}, bf16[9,4,32,128]{3,2,1,0:T(8,128)(2,1)}, u32[]{:S(2)}, u32[]{:S(2)}) collective-permute-start(bf16[9,4,32,128]{3,2,1,0:T(8,128)(2,1)S(1)} %get-tuple-element.175), channel_id=1, source_target_pairs={{192,128},{193,129},{194,130},{195,131},{196,132},{197,133},{198,1... | collective-permute-start | bytes 884744 | tf_op jit(solution)/shard_map/ppermute | solution.py:32
  26.5 24.0 %collective-permute-start.8 = (bf16[9,2,32,128]{3,2,1,0:T(8,128)(2,1)}, bf16[9,2,32,128]{3,2,1,0:T(8,128)(2,1)}, u32[]{:S(2)}, u32[]{:S(2)}) collective-permute-start(bf16[9,2,32,128]{3,2,1,0:T(8,128)(2,1)} %get-tuple-element.176), channel_id=1, source_target_pairs={{193,128},{194,129},{195,130},{196,131},{197,132},{198,133},{199,1... | collective-permute-start | bytes 442376 | tf_op jit(solution)/shard_map/ppermute | solution.py:32
  44.1 10.5 %copy-start.3 = (f32[9,6,32,128]{3,2,1,0:T(8,128)}, f32[9,6,32,128]{3,2,1,0:T(8,128)S(1)}, u32[]{:S(2)}) copy-start(f32[9,6,32,128]{3,2,1,0:T(8,128)S(1)} %fusion.5) | copy-start | bytes 2654212
  50.5 4.1 %copy-start.4 = (bf16[1152,384]{1,0:T(8,128)(2,1)}, bf16[1152,384]{1,0:T(8,128)(2,1)S(1)}, u32[]{:S(2)}) copy-start(bf16[1152,384]{1,0:T(8,128)(2,1)S(1)} %get-tuple-element.184) | copy-start | bytes 2654212
  50.5 4.0 %collective-permute-start.11 = (bf16[9,4,32,128]{3,2,1,0:T(8,128)(2,1)S(1)}, bf16[9,4,32,128]{3,2,1,0:T(8,128)(2,1)}, u32[]{:S(2)}, u32[]{:S(2)}) collective-permute-start(bf16[9,4,32,128]{3,2,1,0:T(8,128)(2,1)S(1)} %get-tuple-element.186), channel_id=1, source_target_pairs={{128,64},{129,65},{130,66},{131,67},{132,68},{133,69},{134,70},{13... | collective-permute-start | bytes 884744 | tf_op jit(solution)/shard_map/ppermute | solution.py:32
  51.9 2.6 %collective-permute-start.10 = (bf16[9,2,32,128]{3,2,1,0:T(8,128)(2,1)}, bf16[9,2,32,128]{3,2,1,0:T(8,128)(2,1)}, u32[]{:S(2)}, u32[]{:S(2)}) collective-permute-start(bf16[9,2,32,128]{3,2,1,0:T(8,128)(2,1)} %get-tuple-element.185), channel_id=1, source_target_pairs={{128,65},{129,66},{130,67},{131,68},{132,69},{133,70},{134,71},{13... | collective-permute-start | bytes 442376 | tf_op jit(solution)/shard_map/ppermute | solution.py:32
  53.2 1.3 collective-permute-start.12
  54.6 5.6 %copy-start = (bf16[128,128]{1,0:T(8,128)(2,1)S(1)}, bf16[128,128]{1,0:T(8,128)(2,1)}, u32[]{:S(2)}) copy-start(bf16[128,128]{1,0:T(8,128)(2,1)} %constant.51.clone.order_ref) | copy-start | bytes 98308
  54.8 6.6 %copy-start.10 = (bf16[9,4,32,128]{3,2,1,0:T(8,128)(2,1)}, bf16[9,4,32,128]{3,2,1,0:T(8,128)(2,1)S(1)}, u32[]{:S(2)}) copy-start(bf16[9,4,32,128]{3,2,1,0:T(8,128)(2,1)S(1)} %get-tuple-element.188) | copy-start | bytes 884740
  54.8 4.6 %collective-permute-start.13 = (bf16[9,4,32,128]{3,2,1,0:T(8,128)(2,1)S(1)}, bf16[9,4,32,128]{3,2,1,0:T(8,128)(2,1)S(1)}, u32[]{:S(2)}, u32[]{:S(2)}) collective-permute-start(bf16[9,4,32,128]{3,2,1,0:T(8,128)(2,1)S(1)} %get-tuple-element.188), channel_id=1, source_target_pairs={{192,160},{193,161},{194,162},{195,163},{196,164},{197,165},{198,1... | collective-permute-start | bytes 884744 | tf_op jit(solution)/shard_map/ppermute | solution.py:32
  55.5 43.8 %collective-permute-start.15 = (bf16[9,4,32,128]{3,2,1,0:T(8,128)(2,1)S(1)}, bf16[9,4,32,128]{3,2,1,0:T(8,128)(2,1)}, u32[]{:S(2)}, u32[]{:S(2)}) collective-permute-start(bf16[9,4,32,128]{3,2,1,0:T(8,128)(2,1)S(1)} %get-tuple-element.188), channel_id=1, source_target_pairs={{64,0},{65,1},{66,2},{67,3},{68,4},{69,5},{70,6},{71,7},{72,8},{73... | collective-permute-start | bytes 884744 | tf_op jit(solution)/shard_map/ppermute | solution.py:32
  56.8 42.5 %collective-permute-start.14 = (bf16[9,2,32,128]{3,2,1,0:T(8,128)(2,1)}, bf16[9,2,32,128]{3,2,1,0:T(8,128)(2,1)}, u32[]{:S(2)}, u32[]{:S(2)}) collective-permute-start(bf16[9,2,32,128]{3,2,1,0:T(8,128)(2,1)} %get-tuple-element.192), channel_id=1, source_target_pairs={{64,1},{65,2},{66,3},{67,4},{68,5},{69,6},{70,7},{71,8},{72,9},{73... | collective-permute-start | bytes 442376 | tf_op jit(solution)/shard_map/ppermute | solution.py:32
  58.1 41.2 %collective-permute-start.16 = (bf16[9,2,32,128]{3,2,1,0:T(8,128)(2,1)}, bf16[9,2,32,128]{3,2,1,0:T(8,128)(2,1)}, u32[]{:S(2)}, u32[]{:S(2)}) collective-permute-start(bf16[9,2,32,128]{3,2,1,0:T(8,128)(2,1)} %get-tuple-element.195), channel_id=1, source_target_pairs={{65,0},{66,1},{67,2},{68,3},{69,4},{70,5},{71,6},{72,7},{73,8},{74... | collective-permute-start | bytes 442376 | tf_op jit(solution)/shard_map/ppermute | solution.py:32
  106.6 5.0 %collective-permute-start.18 = (bf16[9,64,384]{2,1,0:T(8,128)(2,1)S(1)}, bf16[9,64,384]{2,1,0:T(8,128)(2,1)S(1)}, u32[]{:S(2)}, u32[]{:S(2)}) collective-permute-start(bf16[9,64,384]{2,1,0:T(8,128)(2,1)S(1)} %constant_dynamic-slice_fusion), channel_id=1, source_target_pairs={{0,1},{1,0},{2,3},{3,2},{4,5},{5,4},{6,7},{7,6},{8,9},{9,8},{10,11... | collective-permute-start | bytes 1327112 | tf_op jit(solution)/shard_map/ppermute | solution.py:377
  111.7 12.0 %copy-start.9 = (bf16[9,4,32,128]{3,2,1,0:T(8,128)(2,1)S(1)}, bf16[9,4,32,128]{3,2,1,0:T(8,128)(2,1)}, u32[]{:S(2)}) copy-start(bf16[9,4,32,128]{3,2,1,0:T(8,128)(2,1)} %get-tuple-element.200.g_ref) | copy-start | bytes 884740
  111.7 21.1 %copy-start.2 = (f32[9,4,32,128]{3,2,1,0:T(8,128)S(1)}, f32[9,4,32,128]{3,2,1,0:T(8,128)}, u32[]{:S(2)}) copy-start(f32[9,4,32,128]{3,2,1,0:T(8,128)} %copy-done.1) | copy-start | bytes 1769476
  111.7 21.1 %copy-start.5 = (bf16[1152,384]{1,0:T(8,128)(2,1)S(1)}, bf16[1152,384]{1,0:T(8,128)(2,1)}, u32[]{:S(2)}) copy-start(bf16[1152,384]{1,0:T(8,128)(2,1)} %copy-done.4) | copy-start | bytes 2654212
  111.7 21.1 %copy-start.11 = (bf16[9,4,32,128]{3,2,1,0:T(8,128)(2,1)S(1)}, bf16[9,4,32,128]{3,2,1,0:T(8,128)(2,1)}, u32[]{:S(2)}) copy-start(bf16[9,4,32,128]{3,2,1,0:T(8,128)(2,1)} %copy-done.10) | copy-start | bytes 884740
  111.7 21.1 %copy-start.12 = (bf16[9,1,32,128]{3,2,1,0:T(8,128)(2,1)S(1)}, bf16[9,1,32,128]{3,2,1,0:T(8,128)(2,1)}, u32[]{:S(2)}) copy-start(bf16[9,1,32,128]{3,2,1,0:T(8,128)(2,1)} %get-tuple-element.201) | copy-start | bytes 221188
  111.7 21.1 %copy-start.13 = (bf16[9,1,32,128]{3,2,1,0:T(8,128)(2,1)S(1)}, bf16[9,1,32,128]{3,2,1,0:T(8,128)(2,1)}, u32[]{:S(2)}) copy-start(bf16[9,1,32,128]{3,2,1,0:T(8,128)(2,1)} %get-tuple-element.202) | copy-start | bytes 221188
  112.8 26.8 %all-to-all-start = ((bf16[16,9,4,384]{3,2,1,0:T(4,128)(2,1)}), bf16[16,9,4,384]{3,2,1,0:T(4,128)(2,1)S(1)}, u32[]{:S(2)}, u32[]{:S(2)}) async-start(bf16[16,9,4,384]{3,2,1,0:T(4,128)(2,1)} %bitcast.24), calls=%async_computation | async-start | bytes 884736 | tf_op jit(solution)/shard_map/all_to_all | solution.py:382
  123.7 9.1 %collective-permute-start.17 = (bf16[9,4,32,128]{3,2,1,0:T(8,128)(2,1)S(1)}, bf16[9,4,32,128]{3,2,1,0:T(8,128)(2,1)S(1)}, u32[]{:S(2)}, u32[]{:S(2)}) collective-permute-start(bf16[9,4,32,128]{3,2,1,0:T(8,128)(2,1)S(1)} %copy-done.9), channel_id=1, source_target_pairs={{128,160},{129,161},{130,162},{131,163},{132,164},{133,165},{134,1... | collective-permute-start | bytes 884744 | tf_op jit(solution)/shard_map/ppermute | solution.py:32
  134.5 5.9 %copy-start.14 = (bf16[1,9,4,32,128]{4,3,2,1,0:T(8,128)(2,1)}, bf16[1,9,4,32,128]{4,3,2,1,0:T(8,128)(2,1)S(1)}, u32[]{:S(2)}) copy-start(bf16[1,9,4,32,128]{4,3,2,1,0:T(8,128)(2,1)S(1)} %get-tuple-element.247) | copy-start | bytes 884740

commit v8 on v7

--- a/solution.py
+++ b/solution.py
@@ -56,7 +56,7 @@
     )
 
 
-def back_pass(x_ref, rhs, slope_ref, rows, emit, rhs_dim=1):
+def back_pass(x_ref, rhs, slope_ref, rows, emit):
     group = 3
     size = rows * COLS
     one_later = None
@@ -66,7 +66,7 @@
             [x_ref[start : start + group, 2 - j : 2 - j + rows] for j in range(3)], axis=-1
         ).reshape(group * size, 9 * CH)
         part = lax.dot_general(
-            lhs, rhs, (((1,), (rhs_dim,)), ((), ())), preferred_element_type=F32
+            lhs, rhs, (((1,), (1,)), ((), ())), preferred_element_type=F32
         )
         for t in range(group - 1, -1, -1):
             here = part[t * size : (t + 1) * size]
@@ -117,7 +117,7 @@
     def emit(frame, value):
         out_ref[frame] = value.reshape(ROWS, COLS, CH)
 
-    back_pass(x_ref, w_ref[...], slope_ref, ROWS, emit, 0)
+    back_pass(x_ref, weights(w_ref), slope_ref, ROWS, emit)
 
 
 def wide_kernel(low_ref, own_ref, high_ref, w_ref, slope_ref, *rest):
@@ -130,7 +130,7 @@
         own_out[frame] = whole[1 : 1 + ROWS]
         high_out[frame] = whole[1 + ROWS :]
 
-    back_pass(x_ref, w_ref[...], slope_ref, ROWS + 2, emit, 0)
+    back_pass(x_ref, weights(w_ref), slope_ref, ROWS + 2, emit)
 
 
 def double_kernel(low_ref, own_ref, high_ref, w1_ref, slope1_ref, w0_ref, slope0_ref, *rest):
@@ -141,8 +141,8 @@
         fill(x0_ref, frame, 0, value.astype(F32))
         middle_ref[frame] = value.reshape(ROWS + 2, COLS, CH)[1 : 1 + ROWS]
 
-    back_pass(x1_ref, w1_ref[...], slope1_ref, ROWS + 2, emit_middle, 0)
-    back_pass(x0_ref, w0_ref[...], slope0_ref, ROWS, emit_to(outs), 0)
+    back_pass(x1_ref, weights(w1_ref), slope1_ref, ROWS + 2, emit_middle)
+    back_pass(x0_ref, weights(w0_ref), slope0_ref, ROWS, emit_to(outs))
 
 
 def in_vmem(count):
@@ -238,8 +238,8 @@
     )(act6, order)
 
 
-def taps_kernel(scale, ut_ref, g_ref, out_ref):
-    grad = g_ref[...].reshape(FRAMES, ROWS * COLS, CH)
+def taps_kernel(scale, ut_ref, g_ref, more_ref, out_ref):
+    grad = (g_ref[...] + more_ref[...]).reshape(FRAMES, ROWS * COLS, CH)
     padded = jnp.concatenate([grad, jnp.zeros((2, ROWS * COLS, CH), BF)], axis=0)
     rhs = jnp.concatenate([padded[2 - i : 2 - i + FRAMES] for i in range(3)], axis=-1).reshape(
         FRAMES * ROWS * COLS, 3 * CH
@@ -251,15 +251,15 @@
         out_ref[taps_here] = (part * scale).astype(BF).reshape(3, CH, 3 * CH)
 
 
-def taps(ut, grad, scale):
+def taps(ut, grad, more, scale):
     return pl.pallas_call(
         functools.partial(taps_kernel, scale),
         out_shape=jax.ShapeDtypeStruct((9, CH, 3 * CH), BF),
-        in_specs=in_vmem(2),
+        in_specs=in_vmem(3),
         out_specs=pl.BlockSpec(memory_space=pltpu.VMEM),
         compiler_params=pltpu.CompilerParams(vmem_limit_bytes=24 << 20),
         name="kernel_taps",
-    )(ut, grad)
+    )(ut, grad, more)
 
 
 def channel_order():
@@ -281,11 +281,6 @@
     return sig * (1.0 + x * (1.0 - sig))
 
 
-def as_matrix(w):
-    kern = w.reshape(3, 3, 3, CH, CH)
-    return jnp.transpose(kern, (1, 2, 4, 0, 3)).reshape(9 * CH, 3 * CH)
-
-
 def local(acts, kernels, cotangent):
     me = lax.axis_index("section")
     dp = lax.axis_index(AXES[1:])
@@ -331,12 +326,12 @@
         lambda: tuple(single(low, own, high, w, slope, 2)),
         lambda: (result, blank(2), blank(2)),
     )
-    w, own, result = barrier((w, own, result))
+    own, result = barrier((own, result))
     grad = jnp.where(me == 7, cotangent, own)
-    w_next, w = as_matrix(w_next), as_matrix(w)
 
     low, own, high = hop(result, top, bottom, 6, 4)
-    w, w_next, grad, low = barrier((w, w_next, grad, low))
+    grad, low = barrier((grad, low))
+    came = own
     for section in (4, 2):
         result, top, bottom, grad = lax.cond(
             me == section,
@@ -351,20 +346,23 @@
             ),
         )
         low, own, high = hop(result, top, bottom, section, section - 2)
-
-    grad = grad + permute(result, [(s + 1, s, 0) for s in (5, 3, 1)])
-    act6, grad = barrier((act6, grad))
+        if section == 4:
+            came = came + own
+    act6, grad, came = barrier((act6, grad, came))
     ut = tap_rows(act6, jnp.asarray(channel_order(), BF))
-    ut, grad, low = barrier((ut, grad, low))
+    ut, grad, low, own, high, came = barrier((ut, grad, low, own, high, came))
+
+    forward = [(s - 1, s, 0) for s in (5, 3, 1)]
+    passed = permute(came + own, forward)
 
     grad, low, high = lax.cond(
         me == 0,
         lambda: tuple(wide(low, own, high, w_next, slope_next)),
         lambda: (grad, blank(1), blank(1)),
     )
-    part = taps(ut, grad, scale)
+    part = taps(ut, grad, passed, scale)
     grad, low, high, part = barrier((grad, low, high, part))
-    result = result + permute(grad, [(s - 1, s, 0) for s in (5, 3, 1)])
+    result = result + permute(grad, forward)
     final = lax.cond(
         me == 0,
         lambda: last(low, grad, high, w, slope),

time: 141 us -> 140 us (level)
  the two profiles are of different devices: /device:TPU:1 before, /device:TPU:8 now
where the time goes in v8:
time: 140 us
  waiting for transfers between devices  83 us (59%)
  starting transfers between devices  38.1 us (27%)
  local copies, waits for them, and re-layouts  7.02 us (5%)
  other arithmetic  6.47 us (5%)
  Pallas kernels  3.68 us (3%)
    ppermute x18, waiting for transfers between devices, permute(): return lax.ppermute(value, AXES, pairs)  79.7 us
    ppermute x18, starting transfers between devices, permute(): return lax.ppermute(value, AXES, pairs)  19.8 us
    all_to_all x1, starting transfers between devices, local(): part = lax.all_to_all(part, ('z', 'y'), 0, 0, tiled=True)  16.1 us
    another operation x7, local copies, waits for them, and re-layouts  3.55 us
  transfers between devices with their start and end apart: 20, of which 5 were waited for; matrix products, arithmetic and copies ran while one was open for 6% of the time, Pallas kernels for 1%

profile of v8, /device:TPU:8, one launch (start us, length us, event | category | flops | bytes accessed | tf_op | source)
XLA Modules:
  0.0 139.5 jit_solution(11513826060304949584)
XLA Ops:
  0.6 0.0 copy-start.6
  0.6 1.1 pad_maximum_fusion.2
  1.7 1.7 %collective-permute-start = (bf16[18,1,32,128]{3,2,1,0:T(8,128)(2,1)S(1)}, bf16[18,1,32,128]{3,2,1,0:T(8,128)(2,1)S(1)}, u32[]{:S(2)}, u32[]{:S(2)}) collective-permute-start(bf16[18,1,32,128]{3,2,1,0:T(8,128)(2,1)S(1)} %get-tuple-element.206), channel_id=1, source_target_pairs={{0,1},{1,2},{2,3},{3,4},{4,5},{5,6},{6,7},{7,8},{8,9},{9,10},{10,1... | collective-permute-start | bytes 442376 | tf_op jit(solution)/shard_map/ppermute | solution.py:32
  3.5 1.3 collective-permute-start.1
  4.8 4.6 %collective-permute-start.8 = (bf16[3456,128]{1,0:T(8,128)(2,1)}, bf16[3456,128]{1,0:T(8,128)(2,1)}, u32[]{:S(2)}, u32[]{:S(2)}) collective-permute-start(bf16[3456,128]{1,0:T(8,128)(2,1)} %bitcast.13), channel_id=1, source_target_pairs={{160,128},{161,129},{162,130},{163,131},{164,132},{165,133},{166,1... | collective-permute-start | bytes 2654216 | tf_op jit(solution)/shard_map/ppermute | solution.py:32
  9.4 1.2 fusion.10
  10.5 0.0 collective-permute-done.1
  10.6 0.9 conditional.6
  10.6 0.9 broadcast.23
  11.5 0.0 copy-start.7
  11.6 0.1 pad_maximum_fusion.act_ref
  11.6 0.7 collective-permute-start.2
  12.3 1.4 %collective-permute-start.9 = (bf16[9,6,32,128]{3,2,1,0:T(8,128)(2,1)S(1)}, bf16[9,6,32,128]{3,2,1,0:T(8,128)(2,1)S(1)}, u32[]{:S(2)}, u32[]{:S(2)}) collective-permute-start(bf16[9,6,32,128]{3,2,1,0:T(8,128)(2,1)S(1)} %pad_maximum_fusion.act_ref), channel_id=1, source_target_pairs={{160,128},{161,129},{162,130},{163,131},{164,132},{165,133},{166,1... | collective-permute-start | bytes 1327112 | tf_op jit(solution)/shard_map/ppermute | solution.py:32
  13.7 0.7 collective-permute-start.3
  14.4 0.7 collective-permute-start.4
  15.1 0.0 collective-permute-done.3
  15.1 0.0 collective-permute-done.2
  15.1 1.4 conditional.7
  15.1 0.7 broadcast.25
  15.8 0.7 broadcast.25.clone
  16.5 0.7 collective-permute-start.5
  17.2 0.7 collective-permute-start.6
  17.8 0.7 broadcast_select_fusion
  18.6 0.7 collective-permute-start.7
  19.3 0.0 collective-permute-done.5
  19.3 18.5 %collective-permute-done.9 = bf16[9,6,32,128]{3,2,1,0:T(8,128)(2,1)S(1)} collective-permute-done((bf16[9,6,32,128]{3,2,1,0:T(8,128)(2,1)S(1)}, bf16[9,6,32,128]{3,2,1,0:T(8,128)(2,1)S(1)}, u32[]{:S(2)}, u32[]{:S(2)}) %collective-permute-start.9) | collective-permute-done | bytes 442400 | tf_op jit(solution)/shard_map/ppermute | solution.py:32
  37.8 1.2 fusion.5
  39.0 0.0 collective-permute-done.7
  39.1 0.0 collective-permute-done.6
  39.1 0.0 collective-permute-done.8
  39.1 0.0 copy-start.2
  39.1 0.7 collective-permute-start.11
  39.8 0.7 collective-permute-start.10
  40.5 0.7 collective-permute-start.12
  41.2 0.7 collective-permute-start.14
  41.9 0.7 collective-permute-start.13
  42.6 0.9 collective-permute-start.15
  43.4 0.1 add.56
  43.5 1.1 tap_rows.1.ut_ref
  44.7 0.8 add.57
  45.5 1.3 collective-permute-start.16
  46.8 1.3 conditional.10
  46.8 0.6 broadcast.26
  47.5 0.6 broadcast.26.clone
  48.1 47.7 %collective-permute-done.16.more_ref = bf16[9,4,32,128]{3,2,1,0:T(8,128)(2,1)S(1)} collective-permute-done((bf16[9,4,32,128]{3,2,1,0:T(8,128)(2,1)}, bf16[9,4,32,128]{3,2,1,0:T(8,128)(2,1)S(1)}, u32[]{:S(2)}, u32[]{:S(2)}) %collective-permute-start.16) | collective-permute-done | bytes 294944 | tf_op jit(solution)/shard_map/ppermute | solution.py:32
  95.9 0.7 copy-done
  96.6 1.0 copy-done.1
  97.5 2.6 %kernel_taps.1 = bf16[9,128,384]{2,1,0:T(8,128)(2,1)S(1)} custom-call(bf16[9,128,1152]{2,1,0:T(8,128)(2,1)S(1)} %tap_rows.1.ut_ref, bf16[9,4,32,128]{3,2,1,0:T(8,128)(2,1)} %get-tuple-element.202.g_ref, bf16[9,4,32,128]{3,2,1,0:T(8,128)(2,1)S(1)} %copy-done.1), custom_call_target="tpu_custom_call" | custom-call | tf_op jit(solution)/shard_map/kernel_taps/pallas_call | solution.py:255
  100.1 0.0 copy-start.3
  100.1 0.1 constant_dynamic-slice_fusion
  100.2 2.2 %collective-permute-start.18 = (bf16[9,64,384]{2,1,0:T(8,128)(2,1)S(1)}, bf16[9,64,384]{2,1,0:T(8,128)(2,1)S(1)}, u32[]{:S(2)}, u32[]{:S(2)}) collective-permute-start(bf16[9,64,384]{2,1,0:T(8,128)(2,1)S(1)} %constant_dynamic-slice_fusion), channel_id=1, source_target_pairs={{0,1},{1,0},{2,3},{3,2},{4,5},{5,4},{6,7},{7,6},{8,9},{9,8},{10,11... | collective-permute-start | bytes 1327112 | tf_op jit(solution)/shard_map/ppermute | solution.py:375
  102.4 1.4 %collective-permute-done.18 = bf16[9,64,384]{2,1,0:T(8,128)(2,1)S(1)} collective-permute-done((bf16[9,64,384]{2,1,0:T(8,128)(2,1)S(1)}, bf16[9,64,384]{2,1,0:T(8,128)(2,1)S(1)}, u32[]{:S(2)}, u32[]{:S(2)}) %collective-permute-start.18) | collective-permute-done | bytes 442400 | tf_op jit(solution)/shard_map/ppermute | solution.py:375
  103.8 0.1 add_convert_fusion
  103.9 0.1 reshape.10
  104.0 0.9 copy.10
  104.9 16.1 %all-to-all-start = ((bf16[16,9,4,384]{3,2,1,0:T(4,128)(2,1)}), bf16[16,9,4,384]{3,2,1,0:T(4,128)(2,1)S(1)}, u32[]{:S(2)}, u32[]{:S(2)}) async-start(bf16[16,9,4,384]{3,2,1,0:T(4,128)(2,1)} %bitcast.12), calls=%async_computation | async-start | bytes 884736 | tf_op jit(solution)/shard_map/all_to_all | solution.py:380
  121.1 1.3 collective-permute-start.17
  122.4 13.4 %collective-permute-done.17 = bf16[9,4,32,128]{3,2,1,0:T(8,128)(2,1)S(1)} collective-permute-done((bf16[9,4,32,128]{3,2,1,0:T(8,128)(2,1)}, bf16[9,4,32,128]{3,2,1,0:T(8,128)(2,1)S(1)}, u32[]{:S(2)}, u32[]{:S(2)}) %collective-permute-start.17) | collective-permute-done | bytes 294944 | tf_op jit(solution)/shard_map/ppermute | solution.py:32
  135.8 1.0 conditional.11
  135.8 1.0 add_bitcast_fusion
  136.8 0.0 copy-start.10
  136.8 1.9 %all-to-all-done = bf16[16,9,4,384]{3,2,1,0:T(4,128)(2,1)S(1)} async-done(((bf16[16,9,4,384]{3,2,1,0:T(4,128)(2,1)}), bf16[16,9,4,384]{3,2,1,0:T(4,128)(2,1)S(1)}, u32[]{:S(2)}, u32[]{:S(2)}) %all-to-all-start) | async-done | bytes 442400 | tf_op jit(solution)/shard_map/all_to_all | solution.py:380
  138.7 0.2 convert_reduce_fusion
  138.9 0.6 copy.8
  (34 shorter events, 0.1 us)
Async XLA Ops:
  0.6 10.9 %copy-start.6 = (bf16[1,9,4,32,128]{4,3,2,1,0:T(8,128)(2,1)S(1)}, bf16[1,9,4,32,128]{4,3,2,1,0:T(8,128)(2,1)}, u32[]{:S(2)}) copy-start(bf16[1,9,4,32,128]{4,3,2,1,0:T(8,128)(2,1)} %param.16) | copy-start | bytes 884740
  1.7 8.8 %collective-permute-start = (bf16[18,1,32,128]{3,2,1,0:T(8,128)(2,1)S(1)}, bf16[18,1,32,128]{3,2,1,0:T(8,128)(2,1)S(1)}, u32[]{:S(2)}, u32[]{:S(2)}) collective-permute-start(bf16[18,1,32,128]{3,2,1,0:T(8,128)(2,1)S(1)} %get-tuple-element.206), channel_id=1, source_target_pairs={{0,1},{1,2},{2,3},{3,4},{4,5},{5,6},{6,7},{7,8},{8,9},{9,10},{10,1... | collective-permute-start | bytes 442376 | tf_op jit(solution)/shard_map/ppermute | solution.py:32
  3.5 7.1 %collective-permute-start.1 = (bf16[18,1,32,128]{3,2,1,0:T(8,128)(2,1)S(1)}, bf16[18,1,32,128]{3,2,1,0:T(8,128)(2,1)S(1)}, u32[]{:S(2)}, u32[]{:S(2)}) collective-permute-start(bf16[18,1,32,128]{3,2,1,0:T(8,128)(2,1)S(1)} %get-tuple-element.207), channel_id=1, source_target_pairs={{1,0},{2,1},{3,2},{4,3},{5,4},{6,5},{7,6},{8,7},{9,8},{10,9},{11,1... | collective-permute-start | bytes 442376 | tf_op jit(solution)/shard_map/ppermute | solution.py:32
  4.8 34.3 %collective-permute-start.8 = (bf16[3456,128]{1,0:T(8,128)(2,1)}, bf16[3456,128]{1,0:T(8,128)(2,1)}, u32[]{:S(2)}, u32[]{:S(2)}) collective-permute-start(bf16[3456,128]{1,0:T(8,128)(2,1)} %bitcast.13), channel_id=1, source_target_pairs={{160,128},{161,129},{162,130},{163,131},{164,132},{165,133},{166,1... | collective-permute-start | bytes 2654216 | tf_op jit(solution)/shard_map/ppermute | solution.py:32
  10.5 30.7 %copy-start.4 = (f32[9,4,32,128]{3,2,1,0:T(8,128)}, f32[9,4,32,128]{3,2,1,0:T(8,128)S(1)}, u32[]{:S(2)}) copy-start(f32[9,4,32,128]{3,2,1,0:T(8,128)S(1)} %fusion.10) | copy-start | bytes 1769476
  11.5 6.3 %copy-start.7 = (bf16[9,4,32,128]{3,2,1,0:T(8,128)(2,1)S(1)}, bf16[9,4,32,128]{3,2,1,0:T(8,128)(2,1)}, u32[]{:S(2)}) copy-start(bf16[9,4,32,128]{3,2,1,0:T(8,128)(2,1)} %param.18) | copy-start | bytes 884740
  11.6 3.5 %collective-permute-start.2 = (bf16[9,4,32,128]{3,2,1,0:T(8,128)(2,1)}, bf16[9,4,32,128]{3,2,1,0:T(8,128)(2,1)S(1)}, u32[]{:S(2)}, u32[]{:S(2)}) collective-permute-start(bf16[9,4,32,128]{3,2,1,0:T(8,128)(2,1)} %get-tuple-element.172), channel_id=1, source_target_pairs={{224,192},{225,193},{226,194},{227,195},{228,196},{229,197},{230,1... | collective-permute-start | bytes 884744 | tf_op jit(solution)/shard_map/ppermute | solution.py:32
  12.3 25.5 %collective-permute-start.9 = (bf16[9,6,32,128]{3,2,1,0:T(8,128)(2,1)S(1)}, bf16[9,6,32,128]{3,2,1,0:T(8,128)(2,1)S(1)}, u32[]{:S(2)}, u32[]{:S(2)}) collective-permute-start(bf16[9,6,32,128]{3,2,1,0:T(8,128)(2,1)S(1)} %pad_maximum_fusion.act_ref), channel_id=1, source_target_pairs={{160,128},{161,129},{162,130},{163,131},{164,132},{165,133},{166,1... | collective-permute-start | bytes 1327112 | tf_op jit(solution)/shard_map/ppermute | solution.py:32
  13.7 1.4 collective-permute-start.3
  14.4 0.7 collective-permute-start.4
  16.5 2.8 %collective-permute-start.5 = (bf16[9,2,32,128]{3,2,1,0:T(8,128)(2,1)}, bf16[9,2,32,128]{3,2,1,0:T(8,128)(2,1)S(1)}, u32[]{:S(2)}, u32[]{:S(2)}) collective-permute-start(bf16[9,2,32,128]{3,2,1,0:T(8,128)(2,1)} %get-tuple-element.178), channel_id=1, source_target_pairs={{192,129},{193,130},{194,131},{195,132},{196,133},{197,134},{198,1... | collective-permute-start | bytes 442376 | tf_op jit(solution)/shard_map/ppermute | solution.py:32
  17.2 21.9 %collective-permute-start.6 = (bf16[9,4,32,128]{3,2,1,0:T(8,128)(2,1)}, bf16[9,4,32,128]{3,2,1,0:T(8,128)(2,1)S(1)}, u32[]{:S(2)}, u32[]{:S(2)}) collective-permute-start(bf16[9,4,32,128]{3,2,1,0:T(8,128)(2,1)} %get-tuple-element.176), channel_id=1, source_target_pairs={{192,128},{193,129},{194,130},{195,131},{196,132},{197,133},{198,1... | collective-permute-start | bytes 884744 | tf_op jit(solution)/shard_map/ppermute | solution.py:32
  18.6 20.5 %collective-permute-start.7 = (bf16[9,2,32,128]{3,2,1,0:T(8,128)(2,1)}, bf16[9,2,32,128]{3,2,1,0:T(8,128)(2,1)S(1)}, u32[]{:S(2)}, u32[]{:S(2)}) collective-permute-start(bf16[9,2,32,128]{3,2,1,0:T(8,128)(2,1)} %get-tuple-element.177), channel_id=1, source_target_pairs={{193,128},{194,129},{195,130},{196,131},{197,132},{198,133},{199,1... | collective-permute-start | bytes 442376 | tf_op jit(solution)/shard_map/ppermute | solution.py:32
  39.1 4.4 %copy-start.2 = (bf16[128,128]{1,0:T(8,128)(2,1)S(1)}, bf16[128,128]{1,0:T(8,128)(2,1)}, u32[]{:S(2)}) copy-start(bf16[128,128]{1,0:T(8,128)(2,1)} %constant.51.clone.order_ref) | copy-start | bytes 98308
  39.1 2.1 %collective-permute-start.11 = (bf16[9,4,32,128]{3,2,1,0:T(8,128)(2,1)}, bf16[9,4,32,128]{3,2,1,0:T(8,128)(2,1)S(1)}, u32[]{:S(2)}, u32[]{:S(2)}) collective-permute-start(bf16[9,4,32,128]{3,2,1,0:T(8,128)(2,1)} %get-tuple-element.184), channel_id=1, source_target_pairs={{128,64},{129,65},{130,66},{131,67},{132,68},{133,69},{134,70},{13... | collective-permute-start | bytes 884744 | tf_op jit(solution)/shard_map/ppermute | solution.py:32
  39.8 1.4 collective-permute-start.10
  40.5 0.7 collective-permute-start.12
  41.2 3.5 %collective-permute-start.14 = (bf16[9,4,32,128]{3,2,1,0:T(8,128)(2,1)}, bf16[9,4,32,128]{3,2,1,0:T(8,128)(2,1)S(1)}, u32[]{:S(2)}, u32[]{:S(2)}) collective-permute-start(bf16[9,4,32,128]{3,2,1,0:T(8,128)(2,1)} %get-tuple-element.186), channel_id=1, source_target_pairs={{64,0},{65,1},{66,2},{67,3},{68,4},{69,5},{70,6},{71,7},{72,8},{73... | collective-permute-start | bytes 884744 | tf_op jit(solution)/shard_map/ppermute | solution.py:32
  41.9 2.8 %collective-permute-start.13 = (bf16[9,2,32,128]{3,2,1,0:T(8,128)(2,1)}, bf16[9,2,32,128]{3,2,1,0:T(8,128)(2,1)S(1)}, u32[]{:S(2)}, u32[]{:S(2)}) collective-permute-start(bf16[9,2,32,128]{3,2,1,0:T(8,128)(2,1)} %get-tuple-element.190), channel_id=1, source_target_pairs={{64,1},{65,2},{66,3},{67,4},{68,5},{69,6},{70,7},{71,8},{72,9},{73... | collective-permute-start | bytes 442376 | tf_op jit(solution)/shard_map/ppermute | solution.py:32
  42.6 2.1 %collective-permute-start.15 = (bf16[9,2,32,128]{3,2,1,0:T(8,128)(2,1)}, bf16[9,2,32,128]{3,2,1,0:T(8,128)(2,1)S(1)}, u32[]{:S(2)}, u32[]{:S(2)}) collective-permute-start(bf16[9,2,32,128]{3,2,1,0:T(8,128)(2,1)} %get-tuple-element.191), channel_id=1, source_target_pairs={{65,0},{66,1},{67,2},{68,3},{69,4},{70,5},{71,6},{72,7},{73,8},{74... | collective-permute-start | bytes 442376 | tf_op jit(solution)/shard_map/ppermute | solution.py:32
  44.7 0.8 copy-start.11
  44.7 0.8 copy-start.12
  45.5 50.3 %collective-permute-start.16 = (bf16[9,4,32,128]{3,2,1,0:T(8,128)(2,1)}, bf16[9,4,32,128]{3,2,1,0:T(8,128)(2,1)S(1)}, u32[]{:S(2)}, u32[]{:S(2)}) collective-permute-start(bf16[9,4,32,128]{3,2,1,0:T(8,128)(2,1)} %add.57), channel_id=1, source_target_pairs={{128,160},{129,161},{130,162},{131,163},{132,164},{133,165},{134,1... | collective-permute-start | bytes 884744 | tf_op jit(solution)/shard_map/ppermute | solution.py:32
  95.9 0.7 copy-start
  96.6 1.0 copy-start.1
  100.1 35.7 %copy-start.3 = (bf16[1,3,3,3,128,128]{5,4,3,2,1,0:T(8,128)(2,1)S(1)}, bf16[1,3,3,3,128,128]{5,4,3,2,1,0:T(8,128)(2,1)}, u32[]{:S(2)}) copy-start(bf16[1,3,3,3,128,128]{5,4,3,2,1,0:T(8,128)(2,1)} %param.17) | copy-start | bytes 2654212
  100.1 35.7 %copy-start.5 = (f32[9,4,32,128]{3,2,1,0:T(8,128)S(1)}, f32[9,4,32,128]{3,2,1,0:T(8,128)}, u32[]{:S(2)}) copy-start(f32[9,4,32,128]{3,2,1,0:T(8,128)} %copy-done.4) | copy-start | bytes 1769476
  100.1 35.7 %copy-start.8 = (bf16[9,1,32,128]{3,2,1,0:T(8,128)(2,1)S(1)}, bf16[9,1,32,128]{3,2,1,0:T(8,128)(2,1)}, u32[]{:S(2)}) copy-start(bf16[9,1,32,128]{3,2,1,0:T(8,128)(2,1)} %get-tuple-element.203) | copy-start | bytes 221188
  100.1 35.7 %copy-start.9 = (bf16[9,1,32,128]{3,2,1,0:T(8,128)(2,1)S(1)}, bf16[9,1,32,128]{3,2,1,0:T(8,128)(2,1)}, u32[]{:S(2)}) copy-start(bf16[9,1,32,128]{3,2,1,0:T(8,128)(2,1)} %get-tuple-element.204) | copy-start | bytes 221188
  100.2 3.6 %collective-permute-start.18 = (bf16[9,64,384]{2,1,0:T(8,128)(2,1)S(1)}, bf16[9,64,384]{2,1,0:T(8,128)(2,1)S(1)}, u32[]{:S(2)}, u32[]{:S(2)}) collective-permute-start(bf16[9,64,384]{2,1,0:T(8,128)(2,1)S(1)} %constant_dynamic-slice_fusion), channel_id=1, source_target_pairs={{0,1},{1,0},{2,3},{3,2},{4,5},{5,4},{6,7},{7,6},{8,9},{9,8},{10,11... | collective-permute-start | bytes 1327112 | tf_op jit(solution)/shard_map/ppermute | solution.py:375
  104.9 33.8 %all-to-all-start = ((bf16[16,9,4,384]{3,2,1,0:T(4,128)(2,1)}), bf16[16,9,4,384]{3,2,1,0:T(4,128)(2,1)S(1)}, u32[]{:S(2)}, u32[]{:S(2)}) async-start(bf16[16,9,4,384]{3,2,1,0:T(4,128)(2,1)} %bitcast.12), calls=%async_computation | async-start | bytes 884736 | tf_op jit(solution)/shard_map/all_to_all | solution.py:380
  121.1 14.7 %collective-permute-start.17 = (bf16[9,4,32,128]{3,2,1,0:T(8,128)(2,1)}, bf16[9,4,32,128]{3,2,1,0:T(8,128)(2,1)S(1)}, u32[]{:S(2)}, u32[]{:S(2)}) collective-permute-start(bf16[9,4,32,128]{3,2,1,0:T(8,128)(2,1)} %get-tuple-element.202.g_ref), channel_id=1, source_target_pairs={{128,160},{129,161},{130,162},{131,163},{132,164},{133,165},{134,1... | collective-permute-start | bytes 884744 | tf_op jit(solution)/shard_map/ppermute | solution.py:32
  136.8 2.7 %copy-start.10 = (bf16[1,9,4,32,128]{4,3,2,1,0:T(8,128)(2,1)}, bf16[1,9,4,32,128]{4,3,2,1,0:T(8,128)(2,1)S(1)}, u32[]{:S(2)}) copy-start(bf16[1,9,4,32,128]{4,3,2,1,0:T(8,128)(2,1)S(1)} %get-tuple-element.247) | copy-start | bytes 884740

commit v9 on v8

--- a/solution.py
+++ b/solution.py
@@ -102,26 +102,53 @@
     return emit
 
 
-def single_kernel(low_ref, own_ref, high_ref, slope_ref, w_ref, *rest):
-    *outs, x_ref, held_ref, sem = rest
-    copy = pltpu.make_async_copy(w_ref, held_ref, sem)
-    copy.start()
+PIECES = 3
+
+
+class Stream:
+    def __init__(self, source, held, sems):
+        size = source.shape[0] // PIECES
+        self.held = held
+        self.copies = [
+            pltpu.make_async_copy(
+                source.at[pl.ds(n * size, size)], held.at[pl.ds(n * size, size)], sems.at[n]
+            )
+            for n in range(PIECES)
+        ]
+        for copy in self.copies:
+            copy.start()
+
+    def get(self):
+        for copy in self.copies:
+            copy.wait()
+        return self.held
+
+
+def streams(rest, count):
+    sources, middle, buffers = rest[:count], rest[count : len(rest) - 2 * count], rest[-2 * count :]
+    return middle, [
+        Stream(source, buffers[2 * n], buffers[2 * n + 1]) for n, source in enumerate(sources)
+    ]
+
+
+def single_kernel(low_ref, own_ref, high_ref, *rest):
+    (*outs, x_ref), (w, slope) = streams(rest, 2)
     load(low_ref, own_ref, high_ref, x_ref)
-    copy.wait()
-    back_pass(x_ref, weights(held_ref), slope_ref, ROWS, emit_to(outs))
-
-
-def last_kernel(low_ref, own_ref, high_ref, slope_ref, w_ref, out_ref, x_ref):
+    back_pass(x_ref, weights(w.get()), slope.get(), ROWS, emit_to(outs))
+
+
+def last_kernel(low_ref, own_ref, high_ref, *rest):
+    (out_ref, x_ref), (w, slope) = streams(rest, 2)
     load(low_ref, own_ref, high_ref, x_ref)
 
     def emit(frame, value):
         out_ref[frame] = value.reshape(ROWS, COLS, CH)
 
-    back_pass(x_ref, weights(w_ref), slope_ref, ROWS, emit)
-
-
-def wide_kernel(low_ref, own_ref, high_ref, w_ref, slope_ref, *rest):
-    own_out, low_out, high_out, x_ref = rest
+    back_pass(x_ref, weights(w.get()), slope.get(), ROWS, emit)
+
+
+def wide_kernel(scale, low_ref, own_ref, high_ref, *rest):
+    (own_out, low_out, high_out, part_ref, x_ref), (w, slope, ut) = streams(rest, 3)
     load(low_ref, own_ref, high_ref, x_ref)
 
     def emit(frame, value):
@@ -130,19 +157,33 @@
         own_out[frame] = whole[1 : 1 + ROWS]
         high_out[frame] = whole[1 + ROWS :]
 
-    back_pass(x_ref, weights(w_ref), slope_ref, ROWS + 2, emit)
-
-
-def double_kernel(low_ref, own_ref, high_ref, w1_ref, slope1_ref, w0_ref, slope0_ref, *rest):
-    *outs, middle_ref, x1_ref, x0_ref = rest
+    back_pass(x_ref, weights(w.get()), slope.get(), ROWS + 2, emit)
+    tap_terms(ut.get(), own_out[...], scale, part_ref)
+
+
+def double_kernel(low_ref, own_ref, high_ref, *rest):
+    (*outs, middle_ref, x1_ref, x0_ref), (w1, slope1, w0, slope0) = streams(rest, 4)
     load(low_ref, own_ref, high_ref, x1_ref)
 
     def emit_middle(frame, value):
         fill(x0_ref, frame, 0, value.astype(F32))
         middle_ref[frame] = value.reshape(ROWS + 2, COLS, CH)[1 : 1 + ROWS]
 
-    back_pass(x1_ref, weights(w1_ref), slope1_ref, ROWS + 2, emit_middle)
-    back_pass(x0_ref, weights(w0_ref), slope0_ref, ROWS, emit_to(outs))
+    back_pass(x1_ref, weights(w1.get()), slope1.get(), ROWS + 2, emit_middle)
+    back_pass(x0_ref, weights(w0.get()), slope0.get(), ROWS, emit_to(outs))
+
+
+def tap_terms(ut_ref, grad, scale, out_ref):
+    grad = grad.reshape(FRAMES, ROWS * COLS, CH)
+    padded = jnp.concatenate([grad, jnp.zeros((2, ROWS * COLS, CH), BF)], axis=0)
+    rhs = jnp.concatenate([padded[2 - i : 2 - i + FRAMES] for i in range(3)], axis=-1).reshape(
+        FRAMES * ROWS * COLS, 3 * CH
+    )
+    for n in range(3):
+        taps_here = slice(3 * n, 3 * n + 3)
+        lhs = ut_ref[taps_here].reshape(3 * CH, FRAMES * ROWS * COLS)
+        part = jnp.dot(lhs, rhs, preferred_element_type=F32)
+        out_ref[taps_here] = (part * scale).astype(BF).reshape(3, CH, 3 * CH)
 
 
 def in_vmem(count):
@@ -153,47 +194,48 @@
     return jax.ShapeDtypeStruct((FRAMES, rows, COLS, CH), BF)
 
 
-def block_call(kernel, name, operands, outs, halos, held=None):
+PART = jax.ShapeDtypeStruct((9, CH, 3 * CH), BF)
+
+
+def block_call(kernel, name, operands, streamed, outs, halos):
     scratch = [pltpu.VMEM((FRAMES, r, COLS, 3 * CH), BF) for r in halos]
-    specs = in_vmem(len(operands))
-    if held is not None:
-        operands = (*operands, held)
-        specs.append(pl.BlockSpec(memory_space=pl.ANY))
-        scratch += [pltpu.VMEM(held.shape, BF), pltpu.SemaphoreType.DMA]
+    for value in streamed:
+        scratch += [pltpu.VMEM(value.shape, value.dtype), pltpu.SemaphoreType.DMA((PIECES,))]
     return pl.pallas_call(
         kernel,
-        out_shape=[rows_shape(r) for r in outs],
-        in_specs=specs,
+        out_shape=[rows_shape(r) if isinstance(r, int) else r for r in outs],
+        in_specs=in_vmem(len(operands)) + [pl.BlockSpec(memory_space=pl.ANY)] * len(streamed),
         out_specs=in_vmem(len(outs)),
         scratch_shapes=scratch,
         compiler_params=pltpu.CompilerParams(vmem_limit_bytes=24 << 20),
         name=name,
-    )(*operands)
+    )(*operands, *streamed)
 
 
 def single(low, own, high, w, slope, edge):
     return block_call(
         single_kernel,
         f"one_block_{edge}",
-        (low, own, high, slope),
+        (low, own, high),
+        (w, slope),
         (ROWS, edge, edge),
         (ROWS + 2,),
-        w,
     )
 
 
 def last(low, own, high, w, slope):
     return block_call(
-        last_kernel, "last_block", (low, own, high, slope, w), (ROWS,), (ROWS + 2,)
+        last_kernel, "last_block", (low, own, high), (w, slope), (ROWS,), (ROWS + 2,)
     )[0]
 
 
-def wide(low, own, high, w, slope):
+def wide(low, own, high, w, slope, ut, scale):
     return block_call(
-        wide_kernel,
+        functools.partial(wide_kernel, scale),
         "wide_block",
-        (low, own, high, w, slope),
-        (ROWS, 1, 1),
+        (low, own, high),
+        (w, slope, ut),
+        (ROWS, 1, 1, PART),
         (ROWS + 4,),
     )
 
@@ -202,7 +244,8 @@
     return block_call(
         double_kernel,
         "two_blocks",
-        (low, own, high, w1, slope1, w0, slope0),
+        (low, own, high),
+        (w1, slope1, w0, slope0),
         (ROWS, 2, 2, ROWS),
         (ROWS + 4, ROWS + 2),
     )
@@ -239,16 +282,7 @@
 
 
 def taps_kernel(scale, ut_ref, g_ref, more_ref, out_ref):
-    grad = (g_ref[...] + more_ref[...]).reshape(FRAMES, ROWS * COLS, CH)
-    padded = jnp.concatenate([grad, jnp.zeros((2, ROWS * COLS, CH), BF)], axis=0)
-    rhs = jnp.concatenate([padded[2 - i : 2 - i + FRAMES] for i in range(3)], axis=-1).reshape(
-        FRAMES * ROWS * COLS, 3 * CH
-    )
-    for n in range(3):
-        taps_here = slice(3 * n, 3 * n + 3)
-        lhs = ut_ref[taps_here].reshape(3 * CH, FRAMES * ROWS * COLS)
-        part = jnp.dot(lhs, rhs, preferred_element_type=F32)
-        out_ref[taps_here] = (part * scale).astype(BF).reshape(3, CH, 3 * CH)
+    tap_terms(ut_ref, g_ref[...] + more_ref[...], scale, out_ref)
 
 
 def taps(ut, grad, more, scale):
@@ -294,10 +328,10 @@
         return jnp.zeros((FRAMES, rows, COLS, CH), BF)
 
     both = jnp.concatenate([cotangent, acts[0]], axis=0)
-    edge_low = permute(both[:, -1:], [(s, s, 1) for s in every])
-    edge_high = permute(both[:, :1], [(s, s, -1) for s in every])
+    last_row, first_row, own_acts = barrier((both[:, -1:], both[:, :1], acts[0]))
+    edge_low = permute(last_row, [(7, 7, 1)])
+    edge_high = permute(first_row, [(7, 7, -1)])
     low0, high0 = edge_low[:FRAMES], edge_high[:FRAMES]
-    act6 = jnp.concatenate([edge_low[FRAMES:], acts[0], edge_high[FRAMES:]], axis=1)
 
     w = kernels[0].reshape(27 * CH, CH)
     slope = slope_of(acts[0])
@@ -314,7 +348,10 @@
         return low, own, high
 
     w_next = permute(w, [(s + 1, s, 0) for s in pairs])
-    act6, result = barrier((act6, result))
+
+    act_low = edge_low[FRAMES:] + permute(own_acts[:, -1:], [(s, s, 1) for s in range(6)])
+    act_high = edge_high[FRAMES:] + permute(own_acts[:, :1], [(s, s, -1) for s in range(6)])
+    act6 = jnp.concatenate([act_low, own_acts, act_high], axis=1)
     act_next = permute(act6, [(s + 1, s, 0) for s in pairs])
     row = lax.broadcasted_iota(jnp.int32, act_next.shape, 1) + dp * ROWS - 1
     inside = (row >= 0) & (row < DP * ROWS)
@@ -348,26 +385,28 @@
         low, own, high = hop(result, top, bottom, section, section - 2)
         if section == 4:
             came = came + own
-    act6, grad, came = barrier((act6, grad, came))
+    own_acts, grad, came = barrier((own_acts, grad, came))
+    act_low = act_low + permute(own_acts[:, -1:], [(6, 6, 1)])
+    act_high = act_high + permute(own_acts[:, :1], [(6, 6, -1)])
+    act6 = jnp.concatenate([act_low, own_acts, act_high], axis=1)
     ut = tap_rows(act6, jnp.asarray(channel_order(), BF))
     ut, grad, low, own, high, came = barrier((ut, grad, low, own, high, came))
 
     forward = [(s - 1, s, 0) for s in (5, 3, 1)]
     passed = permute(came + own, forward)
 
-    grad, low, high = lax.cond(
+    grad, low, high, part = lax.cond(
         me == 0,
-        lambda: tuple(wide(low, own, high, w_next, slope_next)),
-        lambda: (grad, blank(1), blank(1)),
-    )
-    part = taps(ut, grad, passed, scale)
-    grad, low, high, part = barrier((grad, low, high, part))
-    result = result + permute(grad, forward)
+        lambda: tuple(wide(low, own, high, w_next, slope_next, ut, scale)),
+        lambda: (grad, blank(1), blank(1), jnp.zeros(PART.shape, BF)),
+    )
+    part = lax.cond(me == 0, lambda: part, lambda: taps(ut, grad, passed, scale))
     final = lax.cond(
         me == 0,
         lambda: last(low, grad, high, w, slope),
         lambda: result,
     )
+    final = final + permute(grad, forward)
 
     half = CH // 2
     keep = lax.dynamic_slice_in_dim(part, core * half, half, 1)

time: 140 us -> 141 us (level)
  waiting for transfers between devices: 83 us -> 79.5 us
  other arithmetic: 6.47 us -> 8.34 us
    all_to_all x1, starting transfers between devices: 16.1 us -> 11.7 us  [local(): part = lax.all_to_all(part, ('z', 'y'), 0, 0, tiled=True)]
    ppermute x18 -> x22, starting transfers between devices: 19.8 us -> 24.1 us  [permute(): return lax.ppermute(value, AXES, pairs)]
    ppermute x18 -> x22, waiting for transfers between devices: 79.7 us -> 76.3 us  [permute(): return lax.ppermute(value, AXES, pairs)]
    another operation x7 -> x8, local copies, waits for them, and re-layouts: 3.55 us -> 3.8 us
  transfers between devices with their start and end apart: 20 -> 24, of which waited for: 5 -> 5; matrix products, arithmetic and copies ran while one was open for 6% -> 7% of each run, Pallas kernels for 1% -> 1%
where the time goes in v9:
time: 141 us; the launch traced here: 140 us
  waiting for transfers between devices  79.5 us (56%)
  starting transfers between devices  37.8 us (27%)
  local copies, waits for them, and re-layouts  8.37 us (6%)
  other arithmetic  8.34 us (6%)
  Pallas kernels  4.63 us (3%)
    ppermute x22, waiting for transfers between devices, permute(): return lax.ppermute(value, AXES, pairs)  76.3 us
    ppermute x22, starting transfers between devices, permute(): return lax.ppermute(value, AXES, pairs)  24.1 us
    all_to_all x1, starting transfers between devices, local(): part = lax.all_to_all(part, ('z', 'y'), 0, 0, tiled=True)  11.7 us
    another operation x8, local copies, waits for them, and re-layouts  3.8 us
    pallas_call x1, Pallas kernels, taps(): pl.pallas_call(functools.partial(taps_kernel, scale), out_shape=jax.Shape...  3.5 us
  transfers between devices with their start and end apart: 24, of which 5 were waited for; matrix products, arithmetic and copies ran while one was open for 7% of the time, Pallas kernels for 1%

profile of v9, /device:TPU:8, one launch (start us, length us, event | category | flops | bytes accessed | tf_op | source)
XLA Modules:
  0.0 140.1 jit_solution(1749649289553512979)
XLA Ops:
  0.6 0.0 copy-start.2
  0.6 1.1 pad_maximum_fusion.2
  1.7 0.7 collective-permute-start
  2.4 0.7 collective-permute-start.1
  3.1 0.9 fusion.12
  4.0 1.3 collective-permute-start.10
  5.3 3.0 %collective-permute-start.9 = (bf16[9,1,32,128]{3,2,1,0:T(8,128)(2,1)S(1)}, bf16[9,1,32,128]{3,2,1,0:T(8,128)(2,1)S(1)}, u32[]{:S(2)}, u32[]{:S(2)}) collective-permute-start(bf16[9,1,32,128]{3,2,1,0:T(8,128)(2,1)S(1)} %get-tuple-element.284), channel_id=1, source_target_pairs={{0,1},{1,2},{2,3},{3,4},{4,5},{5,6},{6,7},{7,8},{8,9},{9,10},{10,1... | collective-permute-start | bytes 221192 | tf_op jit(solution)/shard_map/ppermute | solution.py:32
  8.4 5.0 %collective-permute-start.8 = (bf16[3456,128]{1,0:T(8,128)(2,1)}, bf16[3456,128]{1,0:T(8,128)(2,1)}, u32[]{:S(2)}, u32[]{:S(2)}) collective-permute-start(bf16[3456,128]{1,0:T(8,128)(2,1)} %bitcast.10), channel_id=1, source_target_pairs={{160,128},{161,129},{162,130},{163,131},{164,132},{165,133},{166,1... | collective-permute-start | bytes 2654216 | tf_op jit(solution)/shard_map/ppermute | solution.py:32
  13.4 1.2 fusion.10
  14.6 0.0 collective-permute-done
  14.6 0.0 collective-permute-done.1
  14.6 0.8 conditional.7
  14.6 0.8 broadcast.36
  15.4 0.0 copy-start.3
  15.4 0.8 collective-permute-start.2
  16.3 0.0 collective-permute-done.10
  16.3 0.1 pad_maximum_fusion
  16.4 1.3 collective-permute-start.11
  17.7 0.7 collective-permute-start.3
  18.4 0.7 collective-permute-start.4
  19.1 0.7 conditional.8
  19.2 0.7 broadcast.27.clone
  19.8 0.7 collective-permute-start.5
  20.5 0.7 collective-permute-start.6
  21.2 0.7 broadcast_select_fusion
  21.9 0.7 collective-permute-start.7
  22.6 19.4 %collective-permute-done.11 = bf16[9,6,32,128]{3,2,1,0:T(8,128)(2,1)S(1)} collective-permute-done((bf16[9,6,32,128]{3,2,1,0:T(8,128)(2,1)S(1)}, bf16[9,6,32,128]{3,2,1,0:T(8,128)(2,1)S(1)}, u32[]{:S(2)}, u32[]{:S(2)}) %collective-permute-start.11) | collective-permute-done | bytes 442400 | tf_op jit(solution)/shard_map/ppermute | solution.py:32
  42.1 1.3 fusion.5
  43.4 0.7 collective-permute-start.13
  44.0 0.7 collective-permute-start.12
  44.7 0.7 collective-permute-start.14
  45.4 0.0 copy-start
  45.4 0.2 conditional.10
  45.6 0.1 add.67
  45.7 0.7 collective-permute-start.18
  46.4 0.7 collective-permute-start.15
  47.1 0.7 collective-permute-start.16
  47.8 0.7 collective-permute-start.17
  48.5 0.7 collective-permute-start.19
  49.2 0.1 pad_maximum_fusion.1.act_ref
  49.3 1.1 tap_rows.1
  50.5 0.8 copy-done.4
  51.3 0.8 add.71
  52.1 1.3 collective-permute-start.21
  53.4 2.3 %conditional.11 = ((bf16[9,4,32,128]{3,2,1,0:T(8,128)(2,1)}, bf16[9,1,32,128]{3,2,1,0:T(8,128)(2,1)}, bf16[9,1,32,128]{3,2,1,0:T(8,128)(2,1)}, bf16[9,128,384]{2,1,0:T(8,128)(2,1)})) conditional(s32[]{:T(128)} %convert_element_type.35, bf16[9,4,32,128]{3,2,1,0:T(8,128)(2,1)} %get-tuple-element.233, (bf16[9,2,32,128]{3,2,1,0:T(8,128)(2,1)}, ...), branch_computations={%region_8.9_spmd, %region_9.10_spmd} | conditional | bytes 1032238 | solution.py:398
  53.4 1.0 broadcast.29
  54.4 0.6 broadcast.28
  55.0 0.6 broadcast.28.clone
  55.7 43.5 %collective-permute-done.21 = bf16[9,4,32,128]{3,2,1,0:T(8,128)(2,1)S(1)} collective-permute-done((bf16[9,4,32,128]{3,2,1,0:T(8,128)(2,1)}, bf16[9,4,32,128]{3,2,1,0:T(8,128)(2,1)S(1)}, u32[]{:S(2)}, u32[]{:S(2)}) %collective-permute-start.21) | collective-permute-done | bytes 294944 | tf_op jit(solution)/shard_map/ppermute | solution.py:32
  99.2 3.5 %conditional.13 = (bf16[9,128,384]{2,1,0:T(8,128)(2,1)}) conditional(s32[]{:T(128)} %convert_element_type.35, (bf16[9,128,1152]{2,1,0:T(8,128)(2,1)S(1)}, bf16[9,4,32,128]{3,2,1,0:T(8,128)(2,1)}, bf16[9,4,32,128]{3,2,1,0:T(8,128)(2,1)S(1)}) %tuple.85, bf16[9,128,384]{2,1,0:T(8,128)(2,1)} %get-tuple-element.242), branch_computations={%region_12.13_spmd, %region_13.14_spmd} | conditional | bytes 8 | solution.py:403
  99.2 3.5 %kernel_taps.1 = bf16[9,128,384]{2,1,0:T(8,128)(2,1)} custom-call(bf16[9,128,1152]{2,1,0:T(8,128)(2,1)S(1)} %get-tuple-element.168.ut_ref, bf16[9,4,32,128]{3,2,1,0:T(8,128)(2,1)} %get-tuple-element.169.g_ref, bf16[9,4,32,128]{3,2,1,0:T(8,128)(2,1)S(1)} %get-tuple-element.170.more_ref), custom_call_target="tpu_custom_call" | custom-call | tf_op jit(solution)/shard_map/cond/branch_0_fun/kernel_taps/pallas_call | solution.py:289
  102.7 1.1 constant_dynamic-slice_fusion
  103.9 2.0 %collective-permute-start.22 = (bf16[9,64,384]{2,1,0:T(8,128)(2,1)S(1)}, bf16[9,64,384]{2,1,0:T(8,128)(2,1)S(1)}, u32[]{:S(2)}, u32[]{:S(2)}) collective-permute-start(bf16[9,64,384]{2,1,0:T(8,128)(2,1)S(1)} %constant_dynamic-slice_fusion), channel_id=1, source_target_pairs={{0,1},{1,0},{2,3},{3,2},{4,5},{5,4},{6,7},{7,6},{8,9},{9,8},{10,11... | collective-permute-start | bytes 1327112 | tf_op jit(solution)/shard_map/ppermute | solution.py:414
  105.9 1.4 %collective-permute-done.22 = bf16[9,64,384]{2,1,0:T(8,128)(2,1)S(1)} collective-permute-done((bf16[9,64,384]{2,1,0:T(8,128)(2,1)S(1)}, bf16[9,64,384]{2,1,0:T(8,128)(2,1)S(1)}, u32[]{:S(2)}, u32[]{:S(2)}) %collective-permute-start.22) | collective-permute-done | bytes 442400 | tf_op jit(solution)/shard_map/ppermute | solution.py:414
  107.3 1.1 add_convert_fusion
  108.4 0.1 reshape.10
  108.5 0.9 copy.8
  109.5 11.7 %all-to-all-start = ((bf16[16,9,4,384]{3,2,1,0:T(4,128)(2,1)}), bf16[16,9,4,384]{3,2,1,0:T(4,128)(2,1)S(1)}, u32[]{:S(2)}, u32[]{:S(2)}) async-start(bf16[16,9,4,384]{3,2,1,0:T(4,128)(2,1)} %copy.8), calls=%async_computation | async-start | bytes 884736 | tf_op jit(solution)/shard_map/all_to_all | solution.py:419
  121.2 1.3 collective-permute-start.20
  122.5 13.2 %collective-permute-done.20 = bf16[9,4,32,128]{3,2,1,0:T(8,128)(2,1)S(1)} collective-permute-done((bf16[9,4,32,128]{3,2,1,0:T(8,128)(2,1)}, bf16[9,4,32,128]{3,2,1,0:T(8,128)(2,1)S(1)}, u32[]{:S(2)}, u32[]{:S(2)}) %collective-permute-start.20) | collective-permute-done | bytes 294944 | tf_op jit(solution)/shard_map/ppermute | solution.py:32
  135.8 1.7 %add_bitcast_fusion = bf16[1,9,4,32,128]{4,3,2,1,0:T(8,128)(2,1)} fusion(bf16[9,4,32,128]{3,2,1,0:T(8,128)(2,1)} %get-tuple-element.327, bf16[9,4,32,128]{3,2,1,0:T(8,128)(2,1)S(1)} %collective-permute-done.20), kind=kLoop, calls=%fused_computation.19 | loop fusion | flops 147456 | bytes 884736 | tf_op jit(solution)/shard_map/broadcast_in_dim | solution.py:423
  137.5 1.8 %all-to-all-done = bf16[16,9,4,384]{3,2,1,0:T(4,128)(2,1)S(1)} async-done(((bf16[16,9,4,384]{3,2,1,0:T(4,128)(2,1)}), bf16[16,9,4,384]{3,2,1,0:T(4,128)(2,1)S(1)}, u32[]{:S(2)}, u32[]{:S(2)}) %all-to-all-start) | async-done | bytes 442400 | tf_op jit(solution)/shard_map/all_to_all | solution.py:419
  139.3 0.2 convert_reduce_fusion
  139.5 0.6 copy.9
  (41 shorter events, 0.2 us)
Async XLA Ops:
  0.6 15.7 %copy-start.2 = (bf16[1,9,4,32,128]{4,3,2,1,0:T(8,128)(2,1)S(1)}, bf16[1,9,4,32,128]{4,3,2,1,0:T(8,128)(2,1)}, u32[]{:S(2)}) copy-start(bf16[1,9,4,32,128]{4,3,2,1,0:T(8,128)(2,1)} %param.18) | copy-start | bytes 884740
  1.7 12.9 %collective-permute-start = (bf16[18,1,32,128]{3,2,1,0:T(8,128)(2,1)S(1)}, bf16[18,1,32,128]{3,2,1,0:T(8,128)(2,1)S(1)}, u32[]{:S(2)}, u32[]{:S(2)}) collective-permute-start(bf16[18,1,32,128]{3,2,1,0:T(8,128)(2,1)S(1)} %get-tuple-element.208), channel_id=1, source_target_pairs={{224,225},{225,226},{226,227},{227,228},{228,229},{229,230},{230,2... | collective-permute-start | bytes 442376 | tf_op jit(solution)/shard_map/ppermute | solution.py:32
  2.4 12.2 %collective-permute-start.1 = (bf16[18,1,32,128]{3,2,1,0:T(8,128)(2,1)S(1)}, bf16[18,1,32,128]{3,2,1,0:T(8,128)(2,1)S(1)}, u32[]{:S(2)}, u32[]{:S(2)}) collective-permute-start(bf16[18,1,32,128]{3,2,1,0:T(8,128)(2,1)S(1)} %get-tuple-element.209), channel_id=1, source_target_pairs={{225,224},{226,225},{227,226},{228,227},{229,228},{230,229},{231,2... | collective-permute-start | bytes 442376 | tf_op jit(solution)/shard_map/ppermute | solution.py:32
  4.0 12.2 %collective-permute-start.10 = (bf16[9,1,32,128]{3,2,1,0:T(8,128)(2,1)S(1)}, bf16[9,1,32,128]{3,2,1,0:T(8,128)(2,1)S(1)}, u32[]{:S(2)}, u32[]{:S(2)}) collective-permute-start(bf16[9,1,32,128]{3,2,1,0:T(8,128)(2,1)S(1)} %get-tuple-element.285), channel_id=1, source_target_pairs={{1,0},{2,1},{3,2},{4,3},{5,4},{6,5},{7,6},{8,7},{9,8},{10,9},{11,1... | collective-permute-start | bytes 221192 | tf_op jit(solution)/shard_map/ppermute | solution.py:32
  5.3 11.0 %collective-permute-start.9 = (bf16[9,1,32,128]{3,2,1,0:T(8,128)(2,1)S(1)}, bf16[9,1,32,128]{3,2,1,0:T(8,128)(2,1)S(1)}, u32[]{:S(2)}, u32[]{:S(2)}) collective-permute-start(bf16[9,1,32,128]{3,2,1,0:T(8,128)(2,1)S(1)} %get-tuple-element.284), channel_id=1, source_target_pairs={{0,1},{1,2},{2,3},{3,4},{4,5},{5,6},{6,7},{7,8},{8,9},{9,10},{10,1... | collective-permute-start | bytes 221192 | tf_op jit(solution)/shard_map/ppermute | solution.py:32
  8.4 35.0 %collective-permute-start.8 = (bf16[3456,128]{1,0:T(8,128)(2,1)}, bf16[3456,128]{1,0:T(8,128)(2,1)}, u32[]{:S(2)}, u32[]{:S(2)}) collective-permute-start(bf16[3456,128]{1,0:T(8,128)(2,1)} %bitcast.10), channel_id=1, source_target_pairs={{160,128},{161,129},{162,130},{163,131},{164,132},{165,133},{166,1... | collective-permute-start | bytes 2654216 | tf_op jit(solution)/shard_map/ppermute | solution.py:32
  15.4 5.8 %copy-start.3 = (bf16[9,4,32,128]{3,2,1,0:T(8,128)(2,1)S(1)}, bf16[9,4,32,128]{3,2,1,0:T(8,128)(2,1)}, u32[]{:S(2)}) copy-start(bf16[9,4,32,128]{3,2,1,0:T(8,128)(2,1)} %param.20) | copy-start | bytes 884740
  15.4 3.7 %collective-permute-start.2 = (bf16[9,4,32,128]{3,2,1,0:T(8,128)(2,1)}, bf16[9,4,32,128]{3,2,1,0:T(8,128)(2,1)S(1)}, u32[]{:S(2)}, u32[]{:S(2)}) collective-permute-start(bf16[9,4,32,128]{3,2,1,0:T(8,128)(2,1)} %get-tuple-element.210), channel_id=1, source_target_pairs={{224,192},{225,193},{226,194},{227,195},{228,196},{229,197},{230,1... | collective-permute-start | bytes 884744 | tf_op jit(solution)/shard_map/ppermute | solution.py:32
  16.4 25.7 %collective-permute-start.11 = (bf16[9,6,32,128]{3,2,1,0:T(8,128)(2,1)S(1)}, bf16[9,6,32,128]{3,2,1,0:T(8,128)(2,1)S(1)}, u32[]{:S(2)}, u32[]{:S(2)}) collective-permute-start(bf16[9,6,32,128]{3,2,1,0:T(8,128)(2,1)S(1)} %pad_maximum_fusion), channel_id=1, source_target_pairs={{160,128},{161,129},{162,130},{163,131},{164,132},{165,133},{166,1... | collective-permute-start | bytes 1327112 | tf_op jit(solution)/shard_map/ppermute | solution.py:32
  17.7 1.4 collective-permute-start.3
  18.4 0.7 collective-permute-start.4
  19.8 2.8 %collective-permute-start.5 = (bf16[9,2,32,128]{3,2,1,0:T(8,128)(2,1)}, bf16[9,2,32,128]{3,2,1,0:T(8,128)(2,1)S(1)}, u32[]{:S(2)}, u32[]{:S(2)}) collective-permute-start(bf16[9,2,32,128]{3,2,1,0:T(8,128)(2,1)} %get-tuple-element.217), channel_id=1, source_target_pairs={{192,129},{193,130},{194,131},{195,132},{196,133},{197,134},{198,1... | collective-permute-start | bytes 442376 | tf_op jit(solution)/shard_map/ppermute | solution.py:32
  20.5 22.8 %collective-permute-start.6 = (bf16[9,4,32,128]{3,2,1,0:T(8,128)(2,1)}, bf16[9,4,32,128]{3,2,1,0:T(8,128)(2,1)S(1)}, u32[]{:S(2)}, u32[]{:S(2)}) collective-permute-start(bf16[9,4,32,128]{3,2,1,0:T(8,128)(2,1)} %get-tuple-element.215), channel_id=1, source_target_pairs={{192,128},{193,129},{194,130},{195,131},{196,132},{197,133},{198,1... | collective-permute-start | bytes 884744 | tf_op jit(solution)/shard_map/ppermute | solution.py:32
  21.9 21.4 %collective-permute-start.7 = (bf16[9,2,32,128]{3,2,1,0:T(8,128)(2,1)S(1)}, bf16[9,2,32,128]{3,2,1,0:T(8,128)(2,1)S(1)}, u32[]{:S(2)}, u32[]{:S(2)}) collective-permute-start(bf16[9,2,32,128]{3,2,1,0:T(8,128)(2,1)S(1)} %get-tuple-element.216), channel_id=1, source_target_pairs={{193,128},{194,129},{195,130},{196,131},{197,132},{198,133},{199,1... | collective-permute-start | bytes 442376 | tf_op jit(solution)/shard_map/ppermute | solution.py:32
  43.4 2.1 %collective-permute-start.13 = (bf16[9,4,32,128]{3,2,1,0:T(8,128)(2,1)}, bf16[9,4,32,128]{3,2,1,0:T(8,128)(2,1)S(1)}, u32[]{:S(2)}, u32[]{:S(2)}) collective-permute-start(bf16[9,4,32,128]{3,2,1,0:T(8,128)(2,1)} %get-tuple-element.223), channel_id=1, source_target_pairs={{128,64},{129,65},{130,66},{131,67},{132,68},{133,69},{134,70},{13... | collective-permute-start | bytes 884744 | tf_op jit(solution)/shard_map/ppermute | solution.py:32
  44.0 1.4 collective-permute-start.12
  44.7 0.7 collective-permute-start.14
  45.4 3.9 %copy-start = (bf16[128,128]{1,0:T(8,128)(2,1)S(1)}, bf16[128,128]{1,0:T(8,128)(2,1)}, u32[]{:S(2)}) copy-start(bf16[128,128]{1,0:T(8,128)(2,1)} %constant.52.clone.order_ref) | copy-start | bytes 98308
  45.7 4.8 %collective-permute-start.18 = (bf16[9,4,32,128]{3,2,1,0:T(8,128)(2,1)}, bf16[9,4,32,128]{3,2,1,0:T(8,128)(2,1)S(1)}, u32[]{:S(2)}, u32[]{:S(2)}) collective-permute-start(bf16[9,4,32,128]{3,2,1,0:T(8,128)(2,1)} %get-tuple-element.225), channel_id=1, source_target_pairs={{64,0},{65,1},{66,2},{67,3},{68,4},{69,5},{70,6},{71,7},{72,8},{73... | collective-permute-start | bytes 884744 | tf_op jit(solution)/shard_map/ppermute | solution.py:32
  46.4 2.7 %collective-permute-start.15 = (bf16[9,1,32,128]{3,2,1,0:T(8,128)(2,1)S(1)}, bf16[9,1,32,128]{3,2,1,0:T(8,128)(2,1)S(1)}, u32[]{:S(2)}, u32[]{:S(2)}) collective-permute-start(bf16[9,1,32,128]{3,2,1,0:T(8,128)(2,1)S(1)} %get-tuple-element.282), channel_id=1, source_target_pairs={{192,193},{193,194},{194,195},{195,196},{196,197},{197,198},{198,1... | collective-permute-start | bytes 221192 | tf_op jit(solution)/shard_map/ppermute | solution.py:32
  47.1 2.1 %collective-permute-start.16 = (bf16[9,1,32,128]{3,2,1,0:T(8,128)(2,1)S(1)}, bf16[9,1,32,128]{3,2,1,0:T(8,128)(2,1)S(1)}, u32[]{:S(2)}, u32[]{:S(2)}) collective-permute-start(bf16[9,1,32,128]{3,2,1,0:T(8,128)(2,1)S(1)} %get-tuple-element.283), channel_id=1, source_target_pairs={{193,192},{194,193},{195,194},{196,195},{197,196},{198,197},{199,1... | collective-permute-start | bytes 221192 | tf_op jit(solution)/shard_map/ppermute | solution.py:32
  47.8 2.7 %collective-permute-start.17 = (bf16[9,2,32,128]{3,2,1,0:T(8,128)(2,1)}, bf16[9,2,32,128]{3,2,1,0:T(8,128)(2,1)S(1)}, u32[]{:S(2)}, u32[]{:S(2)}) collective-permute-start(bf16[9,2,32,128]{3,2,1,0:T(8,128)(2,1)} %get-tuple-element.229), channel_id=1, source_target_pairs={{64,1},{65,2},{66,3},{67,4},{68,5},{69,6},{70,7},{71,8},{72,9},{73... | collective-permute-start | bytes 442376 | tf_op jit(solution)/shard_map/ppermute | solution.py:32
  48.5 2.0 %collective-permute-start.19 = (bf16[9,2,32,128]{3,2,1,0:T(8,128)(2,1)S(1)}, bf16[9,2,32,128]{3,2,1,0:T(8,128)(2,1)S(1)}, u32[]{:S(2)}, u32[]{:S(2)}) collective-permute-start(bf16[9,2,32,128]{3,2,1,0:T(8,128)(2,1)S(1)} %get-tuple-element.231), channel_id=1, source_target_pairs={{65,0},{66,1},{67,2},{68,3},{69,4},{70,5},{71,6},{72,7},{73,8},{74... | collective-permute-start | bytes 442376 | tf_op jit(solution)/shard_map/ppermute | solution.py:32
  50.4 1.6 %copy-start.7 = (bf16[9,2,32,128]{3,2,1,0:T(8,128)(2,1)}, bf16[9,2,32,128]{3,2,1,0:T(8,128)(2,1)S(1)}, u32[]{:S(2)}) copy-start(bf16[9,2,32,128]{3,2,1,0:T(8,128)(2,1)S(1)} %collective-permute-done.17) | copy-start | bytes 442372
  50.5 1.6 %copy-start.8 = (bf16[9,2,32,128]{3,2,1,0:T(8,128)(2,1)}, bf16[9,2,32,128]{3,2,1,0:T(8,128)(2,1)S(1)}, u32[]{:S(2)}) copy-start(bf16[9,2,32,128]{3,2,1,0:T(8,128)(2,1)S(1)} %collective-permute-done.19) | copy-start | bytes 442372
  50.5 0.8 copy-start.4
  52.1 47.2 %collective-permute-start.21 = (bf16[9,4,32,128]{3,2,1,0:T(8,128)(2,1)}, bf16[9,4,32,128]{3,2,1,0:T(8,128)(2,1)S(1)}, u32[]{:S(2)}, u32[]{:S(2)}) collective-permute-start(bf16[9,4,32,128]{3,2,1,0:T(8,128)(2,1)} %add.71), channel_id=1, source_target_pairs={{128,160},{129,161},{130,162},{131,163},{132,164},{133,165},{134,1... | collective-permute-start | bytes 884744 | tf_op jit(solution)/shard_map/ppermute | solution.py:32
  102.7 19.8 %copy-start.1 = (bf16[1,3,3,3,128,128]{5,4,3,2,1,0:T(8,128)(2,1)S(1)}, bf16[1,3,3,3,128,128]{5,4,3,2,1,0:T(8,128)(2,1)}, u32[]{:S(2)}) copy-start(bf16[1,3,3,3,128,128]{5,4,3,2,1,0:T(8,128)(2,1)} %param.19) | copy-start | bytes 2654212
  102.7 19.8 %copy-start.5 = (bf16[9,1,32,128]{3,2,1,0:T(8,128)(2,1)S(1)}, bf16[9,1,32,128]{3,2,1,0:T(8,128)(2,1)}, u32[]{:S(2)}) copy-start(bf16[9,1,32,128]{3,2,1,0:T(8,128)(2,1)} %get-tuple-element.238) | copy-start | bytes 221188
  102.7 19.8 %copy-start.6 = (bf16[9,1,32,128]{3,2,1,0:T(8,128)(2,1)S(1)}, bf16[9,1,32,128]{3,2,1,0:T(8,128)(2,1)}, u32[]{:S(2)}) copy-start(bf16[9,1,32,128]{3,2,1,0:T(8,128)(2,1)} %get-tuple-element.240) | copy-start | bytes 221188
  103.9 3.4 %collective-permute-start.22 = (bf16[9,64,384]{2,1,0:T(8,128)(2,1)S(1)}, bf16[9,64,384]{2,1,0:T(8,128)(2,1)S(1)}, u32[]{:S(2)}, u32[]{:S(2)}) collective-permute-start(bf16[9,64,384]{2,1,0:T(8,128)(2,1)S(1)} %constant_dynamic-slice_fusion), channel_id=1, source_target_pairs={{0,1},{1,0},{2,3},{3,2},{4,5},{5,4},{6,7},{7,6},{8,9},{9,8},{10,11... | collective-permute-start | bytes 1327112 | tf_op jit(solution)/shard_map/ppermute | solution.py:414
  109.5 29.8 %all-to-all-start = ((bf16[16,9,4,384]{3,2,1,0:T(4,128)(2,1)}), bf16[16,9,4,384]{3,2,1,0:T(4,128)(2,1)S(1)}, u32[]{:S(2)}, u32[]{:S(2)}) async-start(bf16[16,9,4,384]{3,2,1,0:T(4,128)(2,1)} %copy.8), calls=%async_computation | async-start | bytes 884736 | tf_op jit(solution)/shard_map/all_to_all | solution.py:419
  121.2 14.6 %collective-permute-start.20 = (bf16[9,4,32,128]{3,2,1,0:T(8,128)(2,1)}, bf16[9,4,32,128]{3,2,1,0:T(8,128)(2,1)S(1)}, u32[]{:S(2)}, u32[]{:S(2)}) collective-permute-start(bf16[9,4,32,128]{3,2,1,0:T(8,128)(2,1)} %get-tuple-element.239), channel_id=1, source_target_pairs={{128,160},{129,161},{130,162},{131,163},{132,164},{133,165},{134,1... | collective-permute-start | bytes 884744 | tf_op jit(solution)/shard_map/ppermute | solution.py:32

commit v10 on v2

--- a/solution.py
+++ b/solution.py
@@ -7,6 +7,7 @@
 from jax import lax
 from jax.experimental import pallas as pl
 from jax.experimental.pallas import tpu as pltpu
+from jax.sharding import Mesh
 from jax.sharding import PartitionSpec as P
 
 BF = jnp.bfloat16
@@ -17,8 +18,8 @@
 ROWS = 4
 COLS = 32
 CH = 128
-AXES = ("section", "dp")
-HALVING = (1, 2, 4, 8, 16)
+PEERS = 16
+AXES = ("section", "z", "y", "core")
 
 
 def permute(value, hops):
@@ -194,14 +195,12 @@
 
 def channel_order():
     share = CH // DP
-    order = []
-    for n in range(CH):
-        slot, rest = divmod(n, share)
-        d = 0
-        for place, bit in enumerate(HALVING):
-            if (slot >> (len(HALVING) - 1 - place)) & 1:
-                d |= bit
-        order.append(d * share + rest)
+    order = [
+        (chip * 2 + core) * share + rest
+        for core in range(2)
+        for chip in range(PEERS)
+        for rest in range(share)
+    ]
     matrix = np.zeros((CH, CH), np.float32)
     matrix[np.arange(CH), order] = 1.0
     return matrix
@@ -219,8 +218,8 @@
 
 def local(acts, kernels, cotangent):
     me = lax.axis_index("section")
-    dp = lax.axis_index("dp")
-    core = dp % 2
+    dp = lax.axis_index(AXES[1:])
+    core = lax.axis_index("core")
     scale = 1.0 / math.sqrt(FRAMES * ROWS * DP * COLS)
     odd = [s for s in range(SEC) if s % 2 == 1]
     every = range(SEC)
@@ -301,37 +300,33 @@
 
     grad = jnp.where(me == 0, cotangent, result)
     part = taps(ut, grad, scale)
-    for bit in HALVING:
-        size = part.shape[1] // 2
-        mine = (dp // bit) % 2
-        keep = lax.dynamic_slice_in_dim(part, mine * size, size, 1)
-        give = lax.dynamic_slice_in_dim(part, (1 - mine) * size, size, 1)
-        shift = 0
-        if bit == HALVING[-1]:
-            keep = permute(keep, [((s + 1) % SEC, s, 0) for s in every])
-            shift = 1
-        got = lax.ppermute(
-            give,
-            AXES,
-            [((s + shift) % SEC * DP + d, s * DP + (d ^ bit)) for s in every for d in range(DP)],
-        )
-        part = keep.astype(F32) + got.astype(F32)
-        if not shift:
-            part = part.astype(BF)
+    half = CH // 2
+    keep = lax.dynamic_slice_in_dim(part, core * half, half, 1)
+    give = lax.dynamic_slice_in_dim(part, (1 - core) * half, half, 1)
+    got = lax.ppermute(
+        give, AXES, [(s * DP + d, s * DP + (d ^ 1)) for s in every for d in range(DP)]
+    )
+    part = (keep.astype(F32) + got.astype(F32)).astype(BF)
+    part = jnp.transpose(part.reshape(9, PEERS, CH // DP, 3 * CH), (1, 0, 2, 3))
+    part = lax.all_to_all(part, ("z", "y"), 0, 0, tiled=True)
+    part = jnp.sum(part.astype(F32), axis=0)
+    part = permute(part.astype(BF), [((s + 1) % SEC, s, 0) for s in every]).astype(F32)
     share = CH // DP
     kernel_part = jnp.transpose(part.reshape(9, share, 3, CH), (1, 2, 0, 3)).reshape(share, 27, CH)
     return (final[None], kernel_part[None])
 
 
 def solution(mesh):
+    parts = Mesh(mesh.devices.reshape(SEC, DP // 4, 2, 2), AXES)
+    rows = AXES[1:]
     return jax.shard_map(
         local,
-        mesh=mesh,
+        mesh=parts,
         in_specs=(
-            P("section", None, "dp", None, None),
+            P("section", None, rows, None, None),
             P("section", None, None, None, None, None),
-            P(None, "dp", None, None),
+            P(None, rows, None, None),
         ),
-        out_specs=(P("section", None, "dp", None, None), P("section", "dp", None, None)),
+        out_specs=(P("section", None, rows, None, None), P("section", rows, None, None)),
         check_vma=False,
     )

time: 136 us -> 143 us (1.051)
  starting transfers between devices: 33.6 us -> 39.7 us
  local copies, waits for them, and re-layouts: 7.46 us -> 10.2 us
  waiting for transfers between devices: 76.6 us -> 74.5 us
    ppermute x5 -> x1, waiting for transfers between devices: 16.6 us -> 1.67 us  [local(): lax.ppermute(give, AXES, [(s * DP + d, s * DP + (d ^ 1)) for s in every f...]
    all_to_all x0 -> x1, waiting for transfers between devices: none -> 14.1 us  [local(): part = lax.all_to_all(part, ('z', 'y'), 0, 0, tiled=True)]
    all_to_all x0 -> x1, starting transfers between devices: none -> 12.7 us  [local(): part = lax.all_to_all(part, ('z', 'y'), 0, 0, tiled=True)]
    ppermute x5 -> x1, starting transfers between devices: 8.76 us -> 0.21 us  [local(): lax.ppermute(give, AXES, [(s * DP + d, s * DP + (d ^ 1)) for s in every f...]
  transfers between devices with their start and end apart: 27 -> 24, of which waited for: 11 -> 7; matrix products, arithmetic and copies ran while one was open for 6% -> 9% of each run, Pallas kernels for 1% -> 1%
where the time goes in v10:
time: 143 us; the launch traced here: 141 us
  waiting for transfers between devices  74.5 us (52%)
  starting transfers between devices  39.7 us (28%)
  local copies, waits for them, and re-layouts  10.2 us (7%)
  Pallas kernels  9.57 us (7%)
  other arithmetic  6.32 us (4%)
    ppermute x21, waiting for transfers between devices, permute(): return lax.ppermute(value, AXES, pairs)  58.7 us
    ppermute x21, starting transfers between devices, permute(): return lax.ppermute(value, AXES, pairs)  21.7 us
    all_to_all x1, waiting for transfers between devices, local(): part = lax.all_to_all(part, ('z', 'y'), 0, 0, tiled=True)  14.1 us
    all_to_all x1, starting transfers between devices, local(): part = lax.all_to_all(part, ('z', 'y'), 0, 0, tiled=True)  12.7 us
    pallas_call x1, Pallas kernels, double(): pl.pallas_call(double_kernel, out_shape=gradient_shapes(), in_specs=in_vm...  6.84 us
    ppermute x1, starting transfers between devices, local(): lax.ppermute(w_half, AXES, [(s * DP + d, s * DP + (d ^ 1)) for s in pair...  5.05 us
  transfers between devices with their start and end apart: 24, of which 7 were waited for; matrix products, arithmetic and copies ran while one was open for 9% of the time, Pallas kernels for 1%

profile of v10, /device:TPU:8, one launch (start us, length us, event | category | flops | bytes accessed | tf_op | source)
XLA Modules:
  0.0 141.5 jit_solution(1984798225603745097)
XLA Ops:
  0.6 1.0 pad_maximum_fusion.2
  1.7 2.4 %collective-permute-start = (bf16[18,1,32,128]{3,2,1,0:T(8,128)(2,1)S(1)}, bf16[18,1,32,128]{3,2,1,0:T(8,128)(2,1)}, u32[]{:S(2)}, u32[]{:S(2)}) collective-permute-start(bf16[18,1,32,128]{3,2,1,0:T(8,128)(2,1)S(1)} %get-tuple-element.190), channel_id=1, source_target_pairs={{0,1},{1,2},{2,3},{3,4},{4,5},{5,6},{6,7},{7,8},{8,9},{9,10},{10,1... | collective-permute-start | bytes 442376 | tf_op jit(solution)/shard_map/ppermute | solution.py:32
  4.1 1.3 collective-permute-start.1
  5.4 2.4 %copy.10 = bf16[3,3,128,3,128]{4,3,2,1,0:T(4,128)(2,1)S(1)} copy(bf16[3,3,128,3,128]{2,4,1,0,3:T(8,128)(2,1)} %bitcast.30) | data formatting | bytes 1769472 | tf_op jit(solution)/shard_map/transpose | solution.py:216
  7.8 0.0 copy-start.6
  7.8 0.0 copy-start.5
  7.8 0.1 copy.16
  8.0 0.1 constant_dynamic-slice_fusion.1
  8.1 1.3 collective-permute-start.5
  9.4 0.2 fusion.10
  9.6 0.0 collective-permute-done
  9.6 2.2 %conditional.6 = ((bf16[9,4,32,128]{3,2,1,0:T(8,128)(2,1)}, bf16[9,2,32,128]{3,2,1,0:T(8,128)(2,1)}, bf16[9,2,32,128]{3,2,1,0:T(8,128)(2,1)})) conditional(s32[]{:T(128)} %convert_element_type.39, bf16[9,4,32,128]{3,2,1,0:T(8,128)(2,1)S(1)} %copy-done.5, (bf16[18,1,32,128]{3,2,1,0:T(8,128)(2,1)}, bf16[18,1,32,128]{3,2,1,0:T(8,128)(2,1)}, ...), branch_computations={%region_0.0_spmd, %region_1.0_spmd} | conditional | bytes 884772 | solution.py:242
  9.7 0.8 copy.18
  10.5 0.7 broadcast_in_dim.13
  11.1 0.7 broadcast_in_dim.13.clone
  11.8 0.9 slice.40
  12.7 0.9 slice.41
  13.6 0.1 pad_maximum_fusion
  13.7 1.3 collective-permute-start.7
  15.0 7.6 %collective-permute-done.5 = bf16[576,384]{1,0:T(8,128)(2,1)} collective-permute-done((bf16[576,384]{1,0:T(8,128)(2,1)S(1)}, bf16[576,384]{1,0:T(8,128)(2,1)}, u32[]{:S(2)}, u32[]{:S(2)}) %collective-permute-start.5) | collective-permute-done | bytes 442400 | tf_op jit(solution)/shard_map/ppermute | solution.py:32
  22.5 5.0 %collective-permute-start.6 = (bf16[576,384]{1,0:T(8,128)(2,1)}, bf16[576,384]{1,0:T(8,128)(2,1)S(1)}, u32[]{:S(2)}, u32[]{:S(2)}) collective-permute-start(bf16[576,384]{1,0:T(8,128)(2,1)} %collective-permute-done.5), channel_id=1, source_target_pairs={{32,33},{33,32},{34,35},{35,34},{36,37},{37,36},{38,39},{39,38},{4... | collective-permute-start | bytes 1327112 | tf_op jit(solution)/shard_map/ppermute | solution.py:250
  27.6 0.7 collective-permute-start.3
  28.3 1.3 collective-permute-start.2
  29.6 1.3 collective-permute-start.4
  31.0 0.9 collective-permute-done.7
  31.9 1.3 fusion.5
  33.2 2.4 %maximum_select_fusion = bf16[1152,384]{1,0:T(8,128)(2,1)} fusion(bf16[576,384]{1,0:T(8,128)(2,1)S(1)} %collective-permute-done.6, bf16[576,384]{1,0:T(8,128)(2,1)} %collective-permute-done.5, pred[]{:T(512)S(6)} %eq.36), kind=kLoop, calls=%fused_computation.9 | loop fusion | flops 3981312 | bytes 1769473 | tf_op jit(solution)/shard_map/jit(_where)/select_n | solution.py:253
  35.6 0.0 collective-permute-done.2
  35.6 0.7 collective-permute-start.9
  36.3 0.7 collective-permute-start.10
  37.0 0.7 collective-permute-start.8
  37.7 0.0 collective-permute-done.10
  37.7 0.0 copy-start
  37.8 0.1 collective-permute-start.11
  37.9 1.3 collective-permute-start.13
  39.2 1.3 collective-permute-start.12
  40.5 1.5 %collective-permute-start.14 = (bf16[9,2,32,128]{3,2,1,0:T(8,128)(2,1)}, bf16[9,2,32,128]{3,2,1,0:T(8,128)(2,1)}, u32[]{:S(2)}, u32[]{:S(2)}) collective-permute-start(bf16[9,2,32,128]{3,2,1,0:T(8,128)(2,1)} %get-tuple-element.183), channel_id=1, source_target_pairs={{97,32},{98,33},{99,34},{100,35},{101,36},{102,37},{103,38},{104,3... | collective-permute-start | bytes 442376 | tf_op jit(solution)/shard_map/ppermute | solution.py:32
  41.9 8.6 %collective-permute-done.11.act_ref = bf16[9,6,32,128]{3,2,1,0:T(8,128)(2,1)S(1)} collective-permute-done((bf16[9,6,32,128]{3,2,1,0:T(8,128)(2,1)S(1)}, bf16[9,6,32,128]{3,2,1,0:T(8,128)(2,1)S(1)}, u32[]{:S(2)}, u32[]{:S(2)}) %collective-permute-start.11) | collective-permute-done | bytes 442400 | tf_op jit(solution)/shard_map/ppermute | solution.py:32
  50.5 1.1 tap_rows.1.ut_ref
  51.7 36.9 %collective-permute-done.14 = bf16[9,2,32,128]{3,2,1,0:T(8,128)(2,1)} collective-permute-done((bf16[9,2,32,128]{3,2,1,0:T(8,128)(2,1)}, bf16[9,2,32,128]{3,2,1,0:T(8,128)(2,1)}, u32[]{:S(2)}, u32[]{:S(2)}) %collective-permute-start.14) | collective-permute-done | bytes 147488 | tf_op jit(solution)/shard_map/ppermute | solution.py:32
  88.6 6.8 %conditional.9 = (bf16[9,4,32,128]{3,2,1,0:T(8,128)(2,1)}) conditional(s32[]{:T(128)} %convert_element_type.38, bf16[9,4,32,128]{3,2,1,0:T(8,128)(2,1)} %get-tuple-element.180, (bf16[9,2,32,128]{3,2,1,0:T(8,128)(2,1)}, bf16[9,4,32,128]{3,2,1,0:T(8,128)(2,1)}, bf16[9,2,32,128]{3,2,1,0:T(8,128)(2,1)}, bf16[1152,384]{1,0:T(8,128)(2,1)}, ...), branch_computations={%region_6.7_spmd, %region_7.8_spmd} | conditional | bytes 8 | solution.py:271
  88.6 6.8 %two_blocks.5 = (bf16[9,4,32,128]{3,2,1,0:T(8,128)(2,1)}, bf16[9,2,32,128]{3,2,1,0:T(8,128)(2,1)}, bf16[9,2,32,128]{3,2,1,0:T(8,128)(2,1)}) custom-call(bf16[9,2,32,128]{3,2,1,0:T(8,128)(2,1)} %get-tuple-element.124.low_ref, bf16[9,4,32,128]{3,2,1,0:T(8,128)(2,1)} %get-tuple-element.125.own_ref, bf16[9,2,32,128]{3,2,1,0:T(8,128)(2,1)} %get-tuple-element.126.high_ref, ...), custom_call_target="tpu_custom_call" | custom-call | tf_op jit(solution)/shard_map/cond/branch_1_fun/two_blocks/pallas_call | solution.py:128
  95.4 0.7 collective-permute-start.16
  96.1 0.9 fusion.12
  97.0 0.7 collective-permute-start.15
  97.7 1.3 collective-permute-start.17
  99.0 1.0 broadcast_select_fusion.g_ref
  100.0 1.6 %kernel_taps.1 = bf16[9,128,384]{2,1,0:T(8,128)(2,1)S(1)} custom-call(bf16[9,128,1152]{2,1,0:T(8,128)(2,1)S(1)} %tap_rows.1.ut_ref, bf16[9,4,32,128]{3,2,1,0:T(8,128)(2,1)S(1)} %broadcast_select_fusion.g_ref), custom_call_target="tpu_custom_call" | custom-call | tf_op jit(solution)/shard_map/kernel_taps/pallas_call | solution.py:186
  101.6 0.1 constant_dynamic-slice_fusion
  101.7 0.2 collective-permute-start.21
  101.9 1.7 %collective-permute-done.21 = bf16[9,64,384]{2,1,0:T(8,128)(2,1)S(1)} collective-permute-done((bf16[9,64,384]{2,1,0:T(8,128)(2,1)S(1)}, bf16[9,64,384]{2,1,0:T(8,128)(2,1)S(1)}, u32[]{:S(2)}, u32[]{:S(2)}) %collective-permute-start.21) | collective-permute-done | bytes 442400 | tf_op jit(solution)/shard_map/ppermute | solution.py:306
  103.6 0.1 add_convert_fusion
  103.7 0.1 reshape.15
  103.8 0.9 copy.17
  104.7 12.7 %all-to-all-start = ((bf16[16,9,4,384]{3,2,1,0:T(4,128)(2,1)}), bf16[16,9,4,384]{3,2,1,0:T(4,128)(2,1)S(1)}, u32[]{:S(2)}, u32[]{:S(2)}) async-start(bf16[16,9,4,384]{3,2,1,0:T(4,128)(2,1)} %bitcast.19), calls=%async_computation | async-start | bytes 884736 | tf_op jit(solution)/shard_map/all_to_all | solution.py:311
  117.4 1.3 collective-permute-start.19
  118.8 0.9 fusion.11
  119.7 1.3 collective-permute-start.18
  121.0 0.7 collective-permute-start.20
  121.7 14.1 %all-to-all-done = bf16[16,9,4,384]{3,2,1,0:T(4,128)(2,1)S(1)} async-done(((bf16[16,9,4,384]{3,2,1,0:T(4,128)(2,1)}), bf16[16,9,4,384]{3,2,1,0:T(4,128)(2,1)S(1)}, u32[]{:S(2)}, u32[]{:S(2)}) %all-to-all-start) | async-done | bytes 442400 | tf_op jit(solution)/shard_map/all_to_all | solution.py:311
  135.8 0.2 reduce_sum.12
  136.0 0.1 collective-permute-start.22
  136.1 4.7 %collective-permute-done.22 = bf16[9,4,384]{2,1,0:T(4,128)(2,1)S(1)} collective-permute-done((bf16[9,4,384]{2,1,0:T(4,128)(2,1)S(1)}, bf16[9,4,384]{2,1,0:T(4,128)(2,1)S(1)}, u32[]{:S(2)}, u32[]{:S(2)}) %collective-permute-start.22) | collective-permute-done | bytes 27680 | tf_op jit(solution)/shard_map/ppermute | solution.py:32
  140.9 0.6 copy.12
  (31 shorter events, 0.1 us)
Async XLA Ops:
  1.7 7.9 %collective-permute-start = (bf16[18,1,32,128]{3,2,1,0:T(8,128)(2,1)S(1)}, bf16[18,1,32,128]{3,2,1,0:T(8,128)(2,1)}, u32[]{:S(2)}, u32[]{:S(2)}) collective-permute-start(bf16[18,1,32,128]{3,2,1,0:T(8,128)(2,1)S(1)} %get-tuple-element.190), channel_id=1, source_target_pairs={{0,1},{1,2},{2,3},{3,4},{4,5},{5,6},{6,7},{7,8},{8,9},{9,10},{10,1... | collective-permute-start | bytes 442376 | tf_op jit(solution)/shard_map/ppermute | solution.py:32
  4.1 5.6 %collective-permute-start.1 = (bf16[18,1,32,128]{3,2,1,0:T(8,128)(2,1)S(1)}, bf16[18,1,32,128]{3,2,1,0:T(8,128)(2,1)}, u32[]{:S(2)}, u32[]{:S(2)}) collective-permute-start(bf16[18,1,32,128]{3,2,1,0:T(8,128)(2,1)S(1)} %get-tuple-element.191), channel_id=1, source_target_pairs={{1,0},{2,1},{3,2},{4,3},{5,4},{6,5},{7,6},{8,7},{9,8},{10,9},{11,1... | collective-permute-start | bytes 442376 | tf_op jit(solution)/shard_map/ppermute | solution.py:32
  7.8 1.6 %copy-start.6 = (bf16[1,9,4,32,128]{4,3,2,1,0:T(8,128)(2,1)S(1)}, bf16[1,9,4,32,128]{4,3,2,1,0:T(8,128)(2,1)}, u32[]{:S(2)}) copy-start(bf16[1,9,4,32,128]{4,3,2,1,0:T(8,128)(2,1)} %param.16) | copy-start | bytes 884740
  7.8 1.8 %copy-start.5 = (bf16[9,4,32,128]{3,2,1,0:T(8,128)(2,1)S(1)}, bf16[9,4,32,128]{3,2,1,0:T(8,128)(2,1)}, u32[]{:S(2)}) copy-start(bf16[9,4,32,128]{3,2,1,0:T(8,128)(2,1)} %param.18) | copy-start | bytes 884740
  8.0 29.7 %copy-start.1 = (bf16[144,8,3,128]{3,1,2,0:T(8,128)(2,1)}, bf16[144,8,3,128]{3,1,2,0:T(8,128)(2,1)S(1)}, u32[]{:S(2)}) copy-start(bf16[144,8,3,128]{3,1,2,0:T(8,128)(2,1)S(1)} %copy.16) | copy-start | bytes 2654212
  8.1 14.5 %collective-permute-start.5 = (bf16[576,384]{1,0:T(8,128)(2,1)S(1)}, bf16[576,384]{1,0:T(8,128)(2,1)}, u32[]{:S(2)}, u32[]{:S(2)}) collective-permute-start(bf16[576,384]{1,0:T(8,128)(2,1)S(1)} %constant_dynamic-slice_fusion.1), channel_id=1, source_target_pairs={{64,32},{65,33},{66,34},{67,35},{68,36},{69,37},{70,38},{71,39},{7... | collective-permute-start | bytes 1327112 | tf_op jit(solution)/shard_map/ppermute | solution.py:32
  9.6 28.1 %copy-start.3 = (f32[9,4,32,128]{3,2,1,0:T(8,128)}, f32[9,4,32,128]{3,2,1,0:T(8,128)S(1)}, u32[]{:S(2)}) copy-start(f32[9,4,32,128]{3,2,1,0:T(8,128)S(1)} %fusion.10) | copy-start | bytes 1769476
  13.7 18.2 %collective-permute-start.7 = (bf16[9,6,32,128]{3,2,1,0:T(8,128)(2,1)S(1)}, bf16[9,6,32,128]{3,2,1,0:T(8,128)(2,1)S(1)}, u32[]{:S(2)}, u32[]{:S(2)}) collective-permute-start(bf16[9,6,32,128]{3,2,1,0:T(8,128)(2,1)S(1)} %pad_maximum_fusion), channel_id=1, source_target_pairs={{64,32},{65,33},{66,34},{67,35},{68,36},{69,37},{70,38},{71,39},{7... | collective-permute-start | bytes 1327112 | tf_op jit(solution)/shard_map/ppermute | solution.py:32
  22.5 10.6 %collective-permute-start.6 = (bf16[576,384]{1,0:T(8,128)(2,1)}, bf16[576,384]{1,0:T(8,128)(2,1)S(1)}, u32[]{:S(2)}, u32[]{:S(2)}) collective-permute-start(bf16[576,384]{1,0:T(8,128)(2,1)} %collective-permute-done.5), channel_id=1, source_target_pairs={{32,33},{33,32},{34,35},{35,34},{36,37},{37,36},{38,39},{39,38},{4... | collective-permute-start | bytes 1327112 | tf_op jit(solution)/shard_map/ppermute | solution.py:250
  27.6 8.0 %collective-permute-start.3 = (bf16[9,4,32,128]{3,2,1,0:T(8,128)(2,1)}, bf16[9,4,32,128]{3,2,1,0:T(8,128)(2,1)S(1)}, u32[]{:S(2)}, u32[]{:S(2)}) collective-permute-start(bf16[9,4,32,128]{3,2,1,0:T(8,128)(2,1)} %get-tuple-element.171), channel_id=1, source_target_pairs={{224,160},{225,161},{226,162},{227,163},{228,164},{229,165},{230,1... | collective-permute-start | bytes 884744 | tf_op jit(solution)/shard_map/ppermute | solution.py:32
  28.3 7.3 %collective-permute-start.2 = (bf16[9,2,32,128]{3,2,1,0:T(8,128)(2,1)}, bf16[9,2,32,128]{3,2,1,0:T(8,128)(2,1)}, u32[]{:S(2)}, u32[]{:S(2)}) collective-permute-start(bf16[9,2,32,128]{3,2,1,0:T(8,128)(2,1)} %get-tuple-element.173), channel_id=1, source_target_pairs={{224,161},{225,162},{226,163},{227,164},{228,165},{229,166},{230,1... | collective-permute-start | bytes 442376 | tf_op jit(solution)/shard_map/ppermute | solution.py:32
  29.6 6.0 %collective-permute-start.4 = (bf16[9,2,32,128]{3,2,1,0:T(8,128)(2,1)}, bf16[9,2,32,128]{3,2,1,0:T(8,128)(2,1)}, u32[]{:S(2)}, u32[]{:S(2)}) collective-permute-start(bf16[9,2,32,128]{3,2,1,0:T(8,128)(2,1)} %get-tuple-element.172), channel_id=1, source_target_pairs={{225,160},{226,161},{227,162},{228,163},{229,164},{230,165},{231,1... | collective-permute-start | bytes 442376 | tf_op jit(solution)/shard_map/ppermute | solution.py:32
  35.6 2.1 %collective-permute-start.9 = (bf16[9,4,32,128]{3,2,1,0:T(8,128)(2,1)}, bf16[9,4,32,128]{3,2,1,0:T(8,128)(2,1)S(1)}, u32[]{:S(2)}, u32[]{:S(2)}) collective-permute-start(bf16[9,4,32,128]{3,2,1,0:T(8,128)(2,1)} %get-tuple-element.175), channel_id=1, source_target_pairs={{160,96},{161,97},{162,98},{163,99},{164,100},{165,101},{166,102},... | collective-permute-start | bytes 884744 | tf_op jit(solution)/shard_map/ppermute | solution.py:32
  36.3 1.4 collective-permute-start.10
  37.0 0.7 collective-permute-start.8
  37.7 12.8 %copy-start = (bf16[128,128]{1,0:T(8,128)(2,1)S(1)}, bf16[128,128]{1,0:T(8,128)(2,1)}, u32[]{:S(2)}) copy-start(bf16[128,128]{1,0:T(8,128)(2,1)} %constant.56.clone.order_ref) | copy-start | bytes 98308
  37.8 12.7 %collective-permute-start.11 = (bf16[9,6,32,128]{3,2,1,0:T(8,128)(2,1)S(1)}, bf16[9,6,32,128]{3,2,1,0:T(8,128)(2,1)S(1)}, u32[]{:S(2)}, u32[]{:S(2)}) collective-permute-start(bf16[9,6,32,128]{3,2,1,0:T(8,128)(2,1)S(1)} %pad_maximum_fusion), channel_id=1, source_target_pairs={{0,32},{1,33},{2,34},{3,35},{4,36},{5,37},{6,38},{7,39},{8,40},{9,... | collective-permute-start | bytes 1327112 | tf_op jit(solution)/shard_map/ppermute | solution.py:32
  37.9 50.7 %collective-permute-start.13 = (bf16[9,4,32,128]{3,2,1,0:T(8,128)(2,1)}, bf16[9,4,32,128]{3,2,1,0:T(8,128)(2,1)}, u32[]{:S(2)}, u32[]{:S(2)}) collective-permute-start(bf16[9,4,32,128]{3,2,1,0:T(8,128)(2,1)} %get-tuple-element.180), channel_id=1, source_target_pairs={{96,32},{97,33},{98,34},{99,35},{100,36},{101,37},{102,38},{103,39... | collective-permute-start | bytes 884744 | tf_op jit(solution)/shard_map/ppermute | solution.py:32
  39.2 12.5 %collective-permute-start.12 = (bf16[9,2,32,128]{3,2,1,0:T(8,128)(2,1)}, bf16[9,2,32,128]{3,2,1,0:T(8,128)(2,1)}, u32[]{:S(2)}, u32[]{:S(2)}) collective-permute-start(bf16[9,2,32,128]{3,2,1,0:T(8,128)(2,1)} %get-tuple-element.182), channel_id=1, source_target_pairs={{96,33},{97,34},{98,35},{99,36},{100,37},{101,38},{102,39},{103,40... | collective-permute-start | bytes 442376 | tf_op jit(solution)/shard_map/ppermute | solution.py:32
  40.5 48.1 %collective-permute-start.14 = (bf16[9,2,32,128]{3,2,1,0:T(8,128)(2,1)}, bf16[9,2,32,128]{3,2,1,0:T(8,128)(2,1)}, u32[]{:S(2)}, u32[]{:S(2)}) collective-permute-start(bf16[9,2,32,128]{3,2,1,0:T(8,128)(2,1)} %get-tuple-element.183), channel_id=1, source_target_pairs={{97,32},{98,33},{99,34},{100,35},{101,36},{102,37},{103,38},{104,3... | collective-permute-start | bytes 442376 | tf_op jit(solution)/shard_map/ppermute | solution.py:32
  95.4 3.6 %collective-permute-start.16 = (bf16[9,4,32,128]{3,2,1,0:T(8,128)(2,1)}, bf16[9,4,32,128]{3,2,1,0:T(8,128)(2,1)S(1)}, u32[]{:S(2)}, u32[]{:S(2)}) collective-permute-start(bf16[9,4,32,128]{3,2,1,0:T(8,128)(2,1)} %get-tuple-element.219), channel_id=1, source_target_pairs={{224,192},{225,193},{226,194},{227,195},{228,196},{229,197},{230,1... | collective-permute-start | bytes 884744 | tf_op jit(solution)/shard_map/ppermute | solution.py:32
  97.0 2.0 %collective-permute-start.15 = (bf16[9,1,32,128]{3,2,1,0:T(8,128)(2,1)S(1)}, bf16[9,1,32,128]{3,2,1,0:T(8,128)(2,1)S(1)}, u32[]{:S(2)}, u32[]{:S(2)}) collective-permute-start(bf16[9,1,32,128]{3,2,1,0:T(8,128)(2,1)S(1)} %get-tuple-element.195), channel_id=1, source_target_pairs={{224,193},{225,194},{226,195},{227,196},{228,197},{229,198},{230,1... | collective-permute-start | bytes 221192 | tf_op jit(solution)/shard_map/ppermute | solution.py:32
  97.7 1.3 collective-permute-start.17
  101.7 1.9 %collective-permute-start.21 = (bf16[9,64,384]{2,1,0:T(8,128)(2,1)S(1)}, bf16[9,64,384]{2,1,0:T(8,128)(2,1)S(1)}, u32[]{:S(2)}, u32[]{:S(2)}) collective-permute-start(bf16[9,64,384]{2,1,0:T(8,128)(2,1)S(1)} %constant_dynamic-slice_fusion), channel_id=1, source_target_pairs={{0,1},{1,0},{2,3},{3,2},{4,5},{5,4},{6,7},{7,6},{8,9},{9,8},{10,11... | collective-permute-start | bytes 1327112 | tf_op jit(solution)/shard_map/ppermute | solution.py:306
  103.7 32.4 %copy-start.2 = (bf16[144,8,3,128]{3,1,2,0:T(8,128)(2,1)S(1)}, bf16[144,8,3,128]{3,1,2,0:T(8,128)(2,1)}, u32[]{:S(2)}) copy-start(bf16[144,8,3,128]{3,1,2,0:T(8,128)(2,1)} %copy-done.1) | copy-start | bytes 2654212
  103.7 32.4 %copy-start.4 = (f32[9,4,32,128]{3,2,1,0:T(8,128)S(1)}, f32[9,4,32,128]{3,2,1,0:T(8,128)}, u32[]{:S(2)}) copy-start(f32[9,4,32,128]{3,2,1,0:T(8,128)} %copy-done.3) | copy-start | bytes 1769476
  104.7 31.1 %all-to-all-start = ((bf16[16,9,4,384]{3,2,1,0:T(4,128)(2,1)}), bf16[16,9,4,384]{3,2,1,0:T(4,128)(2,1)S(1)}, u32[]{:S(2)}, u32[]{:S(2)}) async-start(bf16[16,9,4,384]{3,2,1,0:T(4,128)(2,1)} %bitcast.19), calls=%async_computation | async-start | bytes 884736 | tf_op jit(solution)/shard_map/all_to_all | solution.py:311
  117.4 18.7 %collective-permute-start.19 = (bf16[9,4,32,128]{3,2,1,0:T(8,128)(2,1)}, bf16[9,4,32,128]{3,2,1,0:T(8,128)(2,1)S(1)}, u32[]{:S(2)}, u32[]{:S(2)}) collective-permute-start(bf16[9,4,32,128]{3,2,1,0:T(8,128)(2,1)} %get-tuple-element.220), channel_id=1, source_target_pairs={{32,0},{33,1},{34,2},{35,3},{36,4},{37,5},{38,6},{39,7},{40,8},{41... | collective-permute-start | bytes 884744 | tf_op jit(solution)/shard_map/ppermute | solution.py:32
  119.7 16.4 %collective-permute-start.18 = (bf16[9,1,32,128]{3,2,1,0:T(8,128)(2,1)S(1)}, bf16[9,1,32,128]{3,2,1,0:T(8,128)(2,1)S(1)}, u32[]{:S(2)}, u32[]{:S(2)}) collective-permute-start(bf16[9,1,32,128]{3,2,1,0:T(8,128)(2,1)S(1)} %get-tuple-element.193), channel_id=1, source_target_pairs={{32,1},{33,2},{34,3},{35,4},{36,5},{37,6},{38,7},{39,8},{40,9},{41... | collective-permute-start | bytes 221192 | tf_op jit(solution)/shard_map/ppermute | solution.py:32
  121.0 15.1 %collective-permute-start.20 = (bf16[9,1,32,128]{3,2,1,0:T(8,128)(2,1)S(1)}, bf16[9,1,32,128]{3,2,1,0:T(8,128)(2,1)S(1)}, u32[]{:S(2)}, u32[]{:S(2)}) collective-permute-start(bf16[9,1,32,128]{3,2,1,0:T(8,128)(2,1)S(1)} %get-tuple-element.192), channel_id=1, source_target_pairs={{33,0},{34,1},{35,2},{36,3},{37,4},{38,5},{39,6},{40,7},{41,8},{42... | collective-permute-start | bytes 221192 | tf_op jit(solution)/shard_map/ppermute | solution.py:32
  136.0 4.9 %collective-permute-start.22 = (bf16[9,4,384]{2,1,0:T(4,128)(2,1)S(1)}, bf16[9,4,384]{2,1,0:T(4,128)(2,1)S(1)}, u32[]{:S(2)}, u32[]{:S(2)}) collective-permute-start(bf16[9,4,384]{2,1,0:T(4,128)(2,1)S(1)} %reduce_sum.12), channel_id=1, source_target_pairs={{32,0},{33,1},{34,2},{35,3},{36,4},{37,5},{38,6},{39,7},{40,8},{41... | collective-permute-start | bytes 82952 | tf_op jit(solution)/shard_map/ppermute | solution.py:32

commit v11 on v9

--- a/solution.py
+++ b/solution.py
@@ -102,53 +102,24 @@
     return emit
 
 
-PIECES = 3
-
-
-class Stream:
-    def __init__(self, source, held, sems):
-        size = source.shape[0] // PIECES
-        self.held = held
-        self.copies = [
-            pltpu.make_async_copy(
-                source.at[pl.ds(n * size, size)], held.at[pl.ds(n * size, size)], sems.at[n]
-            )
-            for n in range(PIECES)
-        ]
-        for copy in self.copies:
-            copy.start()
-
-    def get(self):
-        for copy in self.copies:
-            copy.wait()
-        return self.held
-
-
-def streams(rest, count):
-    sources, middle, buffers = rest[:count], rest[count : len(rest) - 2 * count], rest[-2 * count :]
-    return middle, [
-        Stream(source, buffers[2 * n], buffers[2 * n + 1]) for n, source in enumerate(sources)
-    ]
-
-
 def single_kernel(low_ref, own_ref, high_ref, *rest):
-    (*outs, x_ref), (w, slope) = streams(rest, 2)
+    w_ref, slope_ref, *outs, x_ref = rest
     load(low_ref, own_ref, high_ref, x_ref)
-    back_pass(x_ref, weights(w.get()), slope.get(), ROWS, emit_to(outs))
+    back_pass(x_ref, weights(w_ref), slope_ref, ROWS, emit_to(outs))
 
 
 def last_kernel(low_ref, own_ref, high_ref, *rest):
-    (out_ref, x_ref), (w, slope) = streams(rest, 2)
+    w_ref, slope_ref, out_ref, x_ref = rest
     load(low_ref, own_ref, high_ref, x_ref)
 
     def emit(frame, value):
         out_ref[frame] = value.reshape(ROWS, COLS, CH)
 
-    back_pass(x_ref, weights(w.get()), slope.get(), ROWS, emit)
+    back_pass(x_ref, weights(w_ref), slope_ref, ROWS, emit)
 
 
 def wide_kernel(scale, low_ref, own_ref, high_ref, *rest):
-    (own_out, low_out, high_out, part_ref, x_ref), (w, slope, ut) = streams(rest, 3)
+    w_ref, slope_ref, ut_ref, own_out, low_out, high_out, keep_ref, give_ref, x_ref = rest
     load(low_ref, own_ref, high_ref, x_ref)
 
     def emit(frame, value):
@@ -157,23 +128,23 @@
         own_out[frame] = whole[1 : 1 + ROWS]
         high_out[frame] = whole[1 + ROWS :]
 
-    back_pass(x_ref, weights(w.get()), slope.get(), ROWS + 2, emit)
-    tap_terms(ut.get(), own_out[...], scale, part_ref)
+    back_pass(x_ref, weights(w_ref), slope_ref, ROWS + 2, emit)
+    tap_terms(ut_ref, own_out[...], scale, keep_ref, give_ref)
 
 
 def double_kernel(low_ref, own_ref, high_ref, *rest):
-    (*outs, middle_ref, x1_ref, x0_ref), (w1, slope1, w0, slope0) = streams(rest, 4)
+    w1_ref, slope1_ref, w0_ref, slope0_ref, *outs, middle_ref, x1_ref, x0_ref = rest
     load(low_ref, own_ref, high_ref, x1_ref)
 
     def emit_middle(frame, value):
         fill(x0_ref, frame, 0, value.astype(F32))
         middle_ref[frame] = value.reshape(ROWS + 2, COLS, CH)[1 : 1 + ROWS]
 
-    back_pass(x1_ref, weights(w1.get()), slope1.get(), ROWS + 2, emit_middle)
-    back_pass(x0_ref, weights(w0.get()), slope0.get(), ROWS, emit_to(outs))
-
-
-def tap_terms(ut_ref, grad, scale, out_ref):
+    back_pass(x1_ref, weights(w1_ref), slope1_ref, ROWS + 2, emit_middle)
+    back_pass(x0_ref, weights(w0_ref), slope0_ref, ROWS, emit_to(outs))
+
+
+def tap_terms(ut_ref, grad, scale, keep_ref, give_ref):
     grad = grad.reshape(FRAMES, ROWS * COLS, CH)
     padded = jnp.concatenate([grad, jnp.zeros((2, ROWS * COLS, CH), BF)], axis=0)
     rhs = jnp.concatenate([padded[2 - i : 2 - i + FRAMES] for i in range(3)], axis=-1).reshape(
@@ -183,7 +154,9 @@
         taps_here = slice(3 * n, 3 * n + 3)
         lhs = ut_ref[taps_here].reshape(3 * CH, FRAMES * ROWS * COLS)
         part = jnp.dot(lhs, rhs, preferred_element_type=F32)
-        out_ref[taps_here] = (part * scale).astype(BF).reshape(3, CH, 3 * CH)
+        part = (part * scale).astype(BF).reshape(3, CH, 3 * CH)
+        keep_ref[taps_here] = part[:, : CH // 2]
+        give_ref[taps_here] = part[:, CH // 2 :]
 
 
 def in_vmem(count):
@@ -194,30 +167,27 @@
     return jax.ShapeDtypeStruct((FRAMES, rows, COLS, CH), BF)
 
 
-PART = jax.ShapeDtypeStruct((9, CH, 3 * CH), BF)
-
-
-def block_call(kernel, name, operands, streamed, outs, halos):
+PART = jax.ShapeDtypeStruct((9, CH // 2, 3 * CH), BF)
+
+
+def block_call(kernel, name, operands, outs, halos):
     scratch = [pltpu.VMEM((FRAMES, r, COLS, 3 * CH), BF) for r in halos]
-    for value in streamed:
-        scratch += [pltpu.VMEM(value.shape, value.dtype), pltpu.SemaphoreType.DMA((PIECES,))]
     return pl.pallas_call(
         kernel,
         out_shape=[rows_shape(r) if isinstance(r, int) else r for r in outs],
-        in_specs=in_vmem(len(operands)) + [pl.BlockSpec(memory_space=pl.ANY)] * len(streamed),
+        in_specs=in_vmem(len(operands)),
         out_specs=in_vmem(len(outs)),
         scratch_shapes=scratch,
         compiler_params=pltpu.CompilerParams(vmem_limit_bytes=24 << 20),
         name=name,
-    )(*operands, *streamed)
+    )(*operands)
 
 
 def single(low, own, high, w, slope, edge):
     return block_call(
         single_kernel,
         f"one_block_{edge}",
-        (low, own, high),
-        (w, slope),
+        (low, own, high, w, slope),
         (ROWS, edge, edge),
         (ROWS + 2,),
     )
@@ -225,7 +195,7 @@
 
 def last(low, own, high, w, slope):
     return block_call(
-        last_kernel, "last_block", (low, own, high), (w, slope), (ROWS,), (ROWS + 2,)
+        last_kernel, "last_block", (low, own, high, w, slope), (ROWS,), (ROWS + 2,)
     )[0]
 
 
@@ -233,9 +203,8 @@
     return block_call(
         functools.partial(wide_kernel, scale),
         "wide_block",
-        (low, own, high),
-        (w, slope, ut),
-        (ROWS, 1, 1, PART),
+        (low, own, high, w, slope, ut),
+        (ROWS, 1, 1, PART, PART),
         (ROWS + 4,),
     )
 
@@ -244,8 +213,7 @@
     return block_call(
         double_kernel,
         "two_blocks",
-        (low, own, high),
-        (w1, slope1, w0, slope0),
+        (low, own, high, w1, slope1, w0, slope0),
         (ROWS, 2, 2, ROWS),
         (ROWS + 4, ROWS + 2),
     )
@@ -281,16 +249,16 @@
     )(act6, order)
 
 
-def taps_kernel(scale, ut_ref, g_ref, more_ref, out_ref):
-    tap_terms(ut_ref, g_ref[...] + more_ref[...], scale, out_ref)
+def taps_kernel(scale, ut_ref, g_ref, more_ref, keep_ref, give_ref):
+    tap_terms(ut_ref, g_ref[...] + more_ref[...], scale, keep_ref, give_ref)
 
 
 def taps(ut, grad, more, scale):
     return pl.pallas_call(
         functools.partial(taps_kernel, scale),
-        out_shape=jax.ShapeDtypeStruct((9, CH, 3 * CH), BF),
+        out_shape=[PART, PART],
         in_specs=in_vmem(3),
-        out_specs=pl.BlockSpec(memory_space=pltpu.VMEM),
+        out_specs=in_vmem(2),
         compiler_params=pltpu.CompilerParams(vmem_limit_bytes=24 << 20),
         name="kernel_taps",
     )(ut, grad, more)
@@ -298,14 +266,15 @@
 
 def channel_order():
     share = CH // DP
-    order = [
-        (chip * 2 + core) * share + rest
-        for core in range(2)
-        for chip in range(PEERS)
-        for rest in range(share)
-    ]
-    matrix = np.zeros((CH, CH), np.float32)
-    matrix[np.arange(CH), order] = 1.0
+    matrix = np.zeros((2, CH, CH), np.float32)
+    for own in range(2):
+        order = [
+            (chip * 2 + core) * share + rest
+            for core in (own, 1 - own)
+            for chip in range(PEERS)
+            for rest in range(share)
+        ]
+        matrix[own, np.arange(CH), order] = 1.0
     return matrix
 
 
@@ -349,8 +318,8 @@
 
     w_next = permute(w, [(s + 1, s, 0) for s in pairs])
 
-    act_low = edge_low[FRAMES:] + permute(own_acts[:, -1:], [(s, s, 1) for s in range(6)])
-    act_high = edge_high[FRAMES:] + permute(own_acts[:, :1], [(s, s, -1) for s in range(6)])
+    act_low = edge_low[FRAMES:] + permute(own_acts[:, -1:], [(s, s, 1) for s in range(7)])
+    act_high = edge_high[FRAMES:] + permute(own_acts[:, :1], [(s, s, -1) for s in range(7)])
     act6 = jnp.concatenate([act_low, own_acts, act_high], axis=1)
     act_next = permute(act6, [(s + 1, s, 0) for s in pairs])
     row = lax.broadcasted_iota(jnp.int32, act_next.shape, 1) + dp * ROWS - 1
@@ -385,22 +354,23 @@
         low, own, high = hop(result, top, bottom, section, section - 2)
         if section == 4:
             came = came + own
-    own_acts, grad, came = barrier((own_acts, grad, came))
-    act_low = act_low + permute(own_acts[:, -1:], [(6, 6, 1)])
-    act_high = act_high + permute(own_acts[:, :1], [(6, 6, -1)])
-    act6 = jnp.concatenate([act_low, own_acts, act_high], axis=1)
-    ut = tap_rows(act6, jnp.asarray(channel_order(), BF))
+    act6, grad, came = barrier((act6, grad, came))
+    both_orders = jnp.asarray(channel_order(), BF)
+    ut = tap_rows(act6, jnp.where(core == 0, both_orders[0], both_orders[1]))
     ut, grad, low, own, high, came = barrier((ut, grad, low, own, high, came))
 
     forward = [(s - 1, s, 0) for s in (5, 3, 1)]
     passed = permute(came + own, forward)
 
-    grad, low, high, part = lax.cond(
+    none = jnp.zeros(PART.shape, BF)
+    grad, low, high, keep, give = lax.cond(
         me == 0,
         lambda: tuple(wide(low, own, high, w_next, slope_next, ut, scale)),
-        lambda: (grad, blank(1), blank(1), jnp.zeros(PART.shape, BF)),
-    )
-    part = lax.cond(me == 0, lambda: part, lambda: taps(ut, grad, passed, scale))
+        lambda: (grad, blank(1), blank(1), none, none),
+    )
+    keep, give = lax.cond(
+        me == 0, lambda: (keep, give), lambda: tuple(taps(ut, grad, passed, scale))
+    )
     final = lax.cond(
         me == 0,
         lambda: last(low, grad, high, w, slope),
@@ -408,9 +378,6 @@
     )
     final = final + permute(grad, forward)
 
-    half = CH // 2
-    keep = lax.dynamic_slice_in_dim(part, core * half, half, 1)
-    give = lax.dynamic_slice_in_dim(part, (1 - core) * half, half, 1)
     got = lax.ppermute(
         give, AXES, [(s * DP + d, s * DP + (d ^ 1)) for s in every for d in range(DP)]
     )

time: 141 us -> 140 us (level)
  local copies, waits for them, and re-layouts: 8.37 us -> 4.81 us
  waiting for transfers between devices: 79.5 us -> 82.4 us
    all_to_all x1, starting transfers between devices: 11.7 us -> 15.6 us  [local(): part = lax.all_to_all(part, ('z', 'y'), 0, 0, tiled=True)]
    ppermute x22 -> x20, starting transfers between devices: 24.1 us -> 21.9 us  [permute(): return lax.ppermute(value, AXES, pairs)]
    ppermute x22 -> x20, waiting for transfers between devices: 76.3 us -> 78.1 us  [permute(): return lax.ppermute(value, AXES, pairs)]
    another operation x8 -> x7, local copies, waits for them, and re-layouts: 3.8 us -> 2.05 us
  transfers between devices with their start and end apart: 24 -> 22, of which waited for: 5 -> 5; matrix products, arithmetic and copies ran while one was open for 7% -> 4% of each run, Pallas kernels for 1% -> 1%
where the time goes in v11:
time: 140 us; the launch traced here: 139 us
  waiting for transfers between devices  82.4 us (59%)
  starting transfers between devices  39.1 us (28%)
  other arithmetic  7.32 us (5%)
  local copies, waits for them, and re-layouts  4.81 us (3%)
  Pallas kernels  3.77 us (3%)
    ppermute x20, waiting for transfers between devices, permute(): return lax.ppermute(value, AXES, pairs)  78.1 us
    ppermute x20, starting transfers between devices, permute(): return lax.ppermute(value, AXES, pairs)  21.9 us
    all_to_all x1, starting transfers between devices, local(): part = lax.all_to_all(part, ('z', 'y'), 0, 0, tiled=True)  15.6 us
    all_to_all x1, waiting for transfers between devices, local(): part = lax.all_to_all(part, ('z', 'y'), 0, 0, tiled=True)  2.96 us
  transfers between devices with their start and end apart: 22, of which 5 were waited for; matrix products, arithmetic and copies ran while one was open for 4% of the time, Pallas kernels for 1%

profile of v11, /device:TPU:8, one launch (start us, length us, event | category | flops | bytes accessed | tf_op | source)
XLA Modules:
  0.0 138.8 jit_solution(723284900318847026)
XLA Ops:
  0.6 0.0 copy-start.3
  0.6 1.1 pad_maximum_fusion.1
  1.7 0.9 fusion.11
  2.7 1.7 %collective-permute-start.9 = (bf16[9,1,32,128]{3,2,1,0:T(8,128)(2,1)S(1)}, bf16[9,1,32,128]{3,2,1,0:T(8,128)(2,1)S(1)}, u32[]{:S(2)}, u32[]{:S(2)}) collective-permute-start(bf16[9,1,32,128]{3,2,1,0:T(8,128)(2,1)S(1)} %get-tuple-element.293), channel_id=1, source_target_pairs={{0,1},{1,2},{2,3},{3,4},{4,5},{5,6},{6,7},{7,8},{8,9},{9,10},{10,1... | collective-permute-start | bytes 221192 | tf_op jit(solution)/shard_map/ppermute | solution.py:32
  4.4 1.3 collective-permute-start.10
  5.7 0.7 collective-permute-start
  6.4 0.7 collective-permute-start.1
  7.1 4.6 %collective-permute-start.8 = (bf16[3456,128]{1,0:T(8,128)(2,1)}, bf16[3456,128]{1,0:T(8,128)(2,1)}, u32[]{:S(2)}, u32[]{:S(2)}) collective-permute-start(bf16[3456,128]{1,0:T(8,128)(2,1)} %bitcast.12), channel_id=1, source_target_pairs={{160,128},{161,129},{162,130},{163,131},{164,132},{165,133},{166,1... | collective-permute-start | bytes 2654216 | tf_op jit(solution)/shard_map/ppermute | solution.py:32
  11.7 1.2 fusion.10
  12.9 0.0 collective-permute-done
  12.9 0.1 conditional.13
  13.0 0.0 copy-start.4
  13.0 0.8 collective-permute-start.2
  13.8 0.0 collective-permute-done.10
  13.9 0.1 pad_maximum_fusion.act_ref
  13.9 1.3 collective-permute-start.11
  15.3 0.7 collective-permute-start.4
  16.0 0.7 collective-permute-start.3
  16.7 0.0 collective-permute-done.4
  16.7 0.0 collective-permute-done.2
  16.7 0.7 conditional.14
  16.7 0.7 broadcast.27
  17.4 0.7 collective-permute-start.5
  18.1 0.7 collective-permute-start.6
  18.8 0.7 broadcast_select_fusion
  19.5 0.7 collective-permute-start.7
  20.2 0.0 collective-permute-done.5
  20.2 19.8 %collective-permute-done.11 = bf16[9,6,32,128]{3,2,1,0:T(8,128)(2,1)S(1)} collective-permute-done((bf16[9,6,32,128]{3,2,1,0:T(8,128)(2,1)S(1)}, bf16[9,6,32,128]{3,2,1,0:T(8,128)(2,1)S(1)}, u32[]{:S(2)}, u32[]{:S(2)}) %collective-permute-start.11) | collective-permute-done | bytes 442400 | tf_op jit(solution)/shard_map/ppermute | solution.py:32
  40.0 1.2 fusion.5
  41.2 0.0 collective-permute-done.6
  41.2 0.0 collective-permute-done.8
  41.3 0.0 copy-start.11
  41.3 0.0 copy-start.12
  41.3 0.7 collective-permute-start.13
  42.0 0.7 collective-permute-start.12
  42.7 0.7 collective-permute-start.14
  43.3 0.0 collective-permute-done.12
  43.4 0.0 collective-permute-done.14
  43.4 1.4 collective-permute-start.16
  44.8 0.7 collective-permute-start.15
  45.4 0.9 collective-permute-start.17
  46.3 0.1 add.55
  46.4 1.1 tap_rows.1
  47.6 1.9 %add.57 = bf16[9,4,32,128]{3,2,1,0:T(8,128)(2,1)} add(bf16[9,4,32,128]{3,2,1,0:T(8,128)(2,1)S(1)} %add.55, bf16[9,4,32,128]{3,2,1,0:T(8,128)(2,1)} %collective-permute-done.16) | non-fusion elementwise | flops 147456 | bytes 884736 | tf_op jit(solution)/shard_map/add | solution.py:363
  49.5 1.3 collective-permute-start.19
  50.8 1.4 conditional.17
  50.8 0.6 broadcast.28.clone
  51.4 0.6 broadcast.28
  52.2 45.6 %collective-permute-done.19 = bf16[9,4,32,128]{3,2,1,0:T(8,128)(2,1)} collective-permute-done((bf16[9,4,32,128]{3,2,1,0:T(8,128)(2,1)}, bf16[9,4,32,128]{3,2,1,0:T(8,128)(2,1)}, u32[]{:S(2)}, u32[]{:S(2)}) %collective-permute-start.19) | collective-permute-done | bytes 294944 | tf_op jit(solution)/shard_map/ppermute | solution.py:32
  97.8 2.7 %conditional.19 = (bf16[9,64,384]{2,1,0:T(8,128)(2,1)S(1)}, bf16[9,64,384]{2,1,0:T(8,128)(2,1)S(1)}) conditional(s32[]{:T(128)} %convert_element_type.38, (bf16[9,128,1152]{2,1,0:T(8,128)(2,1)S(1)}, bf16[9,4,32,128]{3,2,1,0:T(8,128)(2,1)}, bf16[9,4,32,128]{3,2,1,0:T(8,128)(2,1)}) %tuple.87, (bf16[9,64,384]{2,1,0:T(8,128)(2,1)S(1)}, ...), branch_computations={%region_12.13_spmd, %region_13.14_spmd} | conditional | bytes 884752
  97.8 2.6 %kernel_taps.1 = (bf16[9,64,384]{2,1,0:T(8,128)(2,1)S(1)}, bf16[9,64,384]{2,1,0:T(8,128)(2,1)S(1)}) custom-call(bf16[9,128,1152]{2,1,0:T(8,128)(2,1)S(1)} %get-tuple-element.171.ut_ref, bf16[9,4,32,128]{3,2,1,0:T(8,128)(2,1)} %get-tuple-element.172.g_ref, bf16[9,4,32,128]{3,2,1,0:T(8,128)(2,1)} %get-tuple-element.173.more_ref), custom_call_target="tpu_custom_call" | custom-call | tf_op jit(solution)/shard_map/cond/branch_0_fun/kernel_taps/pallas_call | solution.py:257
  100.5 0.0 copy-start
  100.5 1.6 %collective-permute-start.20 = (bf16[9,64,384]{2,1,0:T(8,128)(2,1)S(1)}, bf16[9,64,384]{2,1,0:T(8,128)(2,1)S(1)}, u32[]{:S(2)}, u32[]{:S(2)}) collective-permute-start(bf16[9,64,384]{2,1,0:T(8,128)(2,1)S(1)} %get-tuple-element.253), channel_id=1, source_target_pairs={{0,1},{1,0},{2,3},{3,2},{4,5},{5,4},{6,7},{7,6},{8,9},{9,8},{10,11... | collective-permute-start | bytes 1327112 | tf_op jit(solution)/shard_map/ppermute | solution.py:381
  102.2 1.4 %collective-permute-done.20 = bf16[9,64,384]{2,1,0:T(8,128)(2,1)S(1)} collective-permute-done((bf16[9,64,384]{2,1,0:T(8,128)(2,1)S(1)}, bf16[9,64,384]{2,1,0:T(8,128)(2,1)S(1)}, u32[]{:S(2)}, u32[]{:S(2)}) %collective-permute-start.20) | collective-permute-done | bytes 442400 | tf_op jit(solution)/shard_map/ppermute | solution.py:381
  103.6 0.1 add_convert_fusion
  103.7 0.1 reshape.12
  103.8 0.9 copy.8
  104.7 15.6 %all-to-all-start = ((bf16[16,9,4,384]{3,2,1,0:T(4,128)(2,1)}), bf16[16,9,4,384]{3,2,1,0:T(4,128)(2,1)S(1)}, u32[]{:S(2)}, u32[]{:S(2)}) async-start(bf16[16,9,4,384]{3,2,1,0:T(4,128)(2,1)} %copy.8), calls=%async_computation | async-start | bytes 884736 | tf_op jit(solution)/shard_map/all_to_all | solution.py:386
  120.3 1.3 collective-permute-start.18
  121.7 12.6 %collective-permute-done.18 = bf16[9,4,32,128]{3,2,1,0:T(8,128)(2,1)S(1)} collective-permute-done((bf16[9,4,32,128]{3,2,1,0:T(8,128)(2,1)}, bf16[9,4,32,128]{3,2,1,0:T(8,128)(2,1)S(1)}, u32[]{:S(2)}, u32[]{:S(2)}) %collective-permute-start.18) | collective-permute-done | bytes 294944 | tf_op jit(solution)/shard_map/ppermute | solution.py:32
  134.2 0.7 add_bitcast_fusion
  135.0 3.0 %all-to-all-done = bf16[16,9,4,384]{3,2,1,0:T(4,128)(2,1)S(1)} async-done(((bf16[16,9,4,384]{3,2,1,0:T(4,128)(2,1)}), bf16[16,9,4,384]{3,2,1,0:T(4,128)(2,1)S(1)}, u32[]{:S(2)}, u32[]{:S(2)}) %all-to-all-start) | async-done | bytes 442400 | tf_op jit(solution)/shard_map/all_to_all | solution.py:386
  138.0 0.2 convert_reduce_fusion
  138.1 0.6 copy.9
  (42 shorter events, 0.3 us)
Async XLA Ops:
  0.6 13.3 %copy-start.3 = (bf16[1,9,4,32,128]{4,3,2,1,0:T(8,128)(2,1)S(1)}, bf16[1,9,4,32,128]{4,3,2,1,0:T(8,128)(2,1)}, u32[]{:S(2)}) copy-start(bf16[1,9,4,32,128]{4,3,2,1,0:T(8,128)(2,1)} %param.18) | copy-start | bytes 884740
  2.7 11.2 %collective-permute-start.9 = (bf16[9,1,32,128]{3,2,1,0:T(8,128)(2,1)S(1)}, bf16[9,1,32,128]{3,2,1,0:T(8,128)(2,1)S(1)}, u32[]{:S(2)}, u32[]{:S(2)}) collective-permute-start(bf16[9,1,32,128]{3,2,1,0:T(8,128)(2,1)S(1)} %get-tuple-element.293), channel_id=1, source_target_pairs={{0,1},{1,2},{2,3},{3,4},{4,5},{5,6},{6,7},{7,8},{8,9},{9,10},{10,1... | collective-permute-start | bytes 221192 | tf_op jit(solution)/shard_map/ppermute | solution.py:32
  4.4 9.4 %collective-permute-start.10 = (bf16[9,1,32,128]{3,2,1,0:T(8,128)(2,1)S(1)}, bf16[9,1,32,128]{3,2,1,0:T(8,128)(2,1)S(1)}, u32[]{:S(2)}, u32[]{:S(2)}) collective-permute-start(bf16[9,1,32,128]{3,2,1,0:T(8,128)(2,1)S(1)} %get-tuple-element.294), channel_id=1, source_target_pairs={{1,0},{2,1},{3,2},{4,3},{5,4},{6,5},{7,6},{8,7},{9,8},{10,9},{11,1... | collective-permute-start | bytes 221192 | tf_op jit(solution)/shard_map/ppermute | solution.py:32
  5.7 7.1 %collective-permute-start = (bf16[18,1,32,128]{3,2,1,0:T(8,128)(2,1)S(1)}, bf16[18,1,32,128]{3,2,1,0:T(8,128)(2,1)S(1)}, u32[]{:S(2)}, u32[]{:S(2)}) collective-permute-start(bf16[18,1,32,128]{3,2,1,0:T(8,128)(2,1)S(1)} %get-tuple-element.216), channel_id=1, source_target_pairs={{224,225},{225,226},{226,227},{227,228},{228,229},{229,230},{230,2... | collective-permute-start | bytes 442376 | tf_op jit(solution)/shard_map/ppermute | solution.py:32
  6.4 6.5 %collective-permute-start.1 = (bf16[18,1,32,128]{3,2,1,0:T(8,128)(2,1)S(1)}, bf16[18,1,32,128]{3,2,1,0:T(8,128)(2,1)S(1)}, u32[]{:S(2)}, u32[]{:S(2)}) collective-permute-start(bf16[18,1,32,128]{3,2,1,0:T(8,128)(2,1)S(1)} %get-tuple-element.217), channel_id=1, source_target_pairs={{225,224},{226,225},{227,226},{228,227},{229,228},{230,229},{231,2... | collective-permute-start | bytes 442376 | tf_op jit(solution)/shard_map/ppermute | solution.py:32
  7.1 34.2 %collective-permute-start.8 = (bf16[3456,128]{1,0:T(8,128)(2,1)}, bf16[3456,128]{1,0:T(8,128)(2,1)}, u32[]{:S(2)}, u32[]{:S(2)}) collective-permute-start(bf16[3456,128]{1,0:T(8,128)(2,1)} %bitcast.12), channel_id=1, source_target_pairs={{160,128},{161,129},{162,130},{163,131},{164,132},{165,133},{166,1... | collective-permute-start | bytes 2654216 | tf_op jit(solution)/shard_map/ppermute | solution.py:32
  12.8 30.5 %copy-start.1 = (f32[9,4,32,128]{3,2,1,0:T(8,128)}, f32[9,4,32,128]{3,2,1,0:T(8,128)S(1)}, u32[]{:S(2)}) copy-start(f32[9,4,32,128]{3,2,1,0:T(8,128)S(1)} %fusion.10) | copy-start | bytes 1769476
  13.0 5.8 %copy-start.4 = (bf16[9,4,32,128]{3,2,1,0:T(8,128)(2,1)S(1)}, bf16[9,4,32,128]{3,2,1,0:T(8,128)(2,1)}, u32[]{:S(2)}) copy-start(bf16[9,4,32,128]{3,2,1,0:T(8,128)(2,1)} %param.20) | copy-start | bytes 884740
  13.0 3.7 %collective-permute-start.2 = (bf16[9,4,32,128]{3,2,1,0:T(8,128)(2,1)S(1)}, bf16[9,4,32,128]{3,2,1,0:T(8,128)(2,1)S(1)}, u32[]{:S(2)}, u32[]{:S(2)}) collective-permute-start(bf16[9,4,32,128]{3,2,1,0:T(8,128)(2,1)S(1)} %get-tuple-element.218), channel_id=1, source_target_pairs={{224,192},{225,193},{226,194},{227,195},{228,196},{229,197},{230,1... | collective-permute-start | bytes 884744 | tf_op jit(solution)/shard_map/ppermute | solution.py:32
  13.9 26.0 %collective-permute-start.11 = (bf16[9,6,32,128]{3,2,1,0:T(8,128)(2,1)S(1)}, bf16[9,6,32,128]{3,2,1,0:T(8,128)(2,1)S(1)}, u32[]{:S(2)}, u32[]{:S(2)}) collective-permute-start(bf16[9,6,32,128]{3,2,1,0:T(8,128)(2,1)S(1)} %pad_maximum_fusion.act_ref), channel_id=1, source_target_pairs={{160,128},{161,129},{162,130},{163,131},{164,132},{165,133},{166,1... | collective-permute-start | bytes 1327112 | tf_op jit(solution)/shard_map/ppermute | solution.py:32
  15.3 1.4 collective-permute-start.4
  16.0 0.7 collective-permute-start.3
  17.4 2.8 %collective-permute-start.5 = (bf16[9,2,32,128]{3,2,1,0:T(8,128)(2,1)S(1)}, bf16[9,2,32,128]{3,2,1,0:T(8,128)(2,1)S(1)}, u32[]{:S(2)}, u32[]{:S(2)}) collective-permute-start(bf16[9,2,32,128]{3,2,1,0:T(8,128)(2,1)S(1)} %get-tuple-element.225), channel_id=1, source_target_pairs={{192,129},{193,130},{194,131},{195,132},{196,133},{197,134},{198,1... | collective-permute-start | bytes 442376 | tf_op jit(solution)/shard_map/ppermute | solution.py:32
  18.1 23.2 %collective-permute-start.6 = (bf16[9,4,32,128]{3,2,1,0:T(8,128)(2,1)S(1)}, bf16[9,4,32,128]{3,2,1,0:T(8,128)(2,1)S(1)}, u32[]{:S(2)}, u32[]{:S(2)}) collective-permute-start(bf16[9,4,32,128]{3,2,1,0:T(8,128)(2,1)S(1)} %get-tuple-element.223), channel_id=1, source_target_pairs={{192,128},{193,129},{194,130},{195,131},{196,132},{197,133},{198,1... | collective-permute-start | bytes 884744 | tf_op jit(solution)/shard_map/ppermute | solution.py:32
  19.5 21.7 %collective-permute-start.7 = (bf16[9,2,32,128]{3,2,1,0:T(8,128)(2,1)}, bf16[9,2,32,128]{3,2,1,0:T(8,128)(2,1)S(1)}, u32[]{:S(2)}, u32[]{:S(2)}) collective-permute-start(bf16[9,2,32,128]{3,2,1,0:T(8,128)(2,1)} %get-tuple-element.224), channel_id=1, source_target_pairs={{193,128},{194,129},{195,130},{196,131},{197,132},{198,133},{199,1... | collective-permute-start | bytes 442376 | tf_op jit(solution)/shard_map/ppermute | solution.py:32
  41.3 5.0 %copy-start.11 = (bf16[1,128,128]{2,1,0:T(8,128)(2,1)S(1)}, bf16[1,128,128]{2,1,0:T(8,128)(2,1)}, u32[]{:S(2)}) copy-start(bf16[1,128,128]{2,1,0:T(8,128)(2,1)} %constant.52) | copy-start | bytes 98308
  41.3 5.0 %copy-start.12 = (bf16[1,128,128]{2,1,0:T(8,128)(2,1)S(1)}, bf16[1,128,128]{2,1,0:T(8,128)(2,1)}, u32[]{:S(2)}) copy-start(bf16[1,128,128]{2,1,0:T(8,128)(2,1)} %constant.51) | copy-start | bytes 98308
  41.3 2.1 %collective-permute-start.13 = (bf16[9,4,32,128]{3,2,1,0:T(8,128)(2,1)S(1)}, bf16[9,4,32,128]{3,2,1,0:T(8,128)(2,1)S(1)}, u32[]{:S(2)}, u32[]{:S(2)}) collective-permute-start(bf16[9,4,32,128]{3,2,1,0:T(8,128)(2,1)S(1)} %get-tuple-element.231), channel_id=1, source_target_pairs={{128,64},{129,65},{130,66},{131,67},{132,68},{133,69},{134,70},{13... | collective-permute-start | bytes 884744 | tf_op jit(solution)/shard_map/ppermute | solution.py:32
  42.0 1.4 collective-permute-start.12
  42.7 0.7 collective-permute-start.14
  43.4 7.4 %copy-start.5 = (bf16[9,4,32,128]{3,2,1,0:T(8,128)(2,1)}, bf16[9,4,32,128]{3,2,1,0:T(8,128)(2,1)S(1)}, u32[]{:S(2)}) copy-start(bf16[9,4,32,128]{3,2,1,0:T(8,128)(2,1)S(1)} %get-tuple-element.233) | copy-start | bytes 884740
  43.4 4.2 %collective-permute-start.16 = (bf16[9,4,32,128]{3,2,1,0:T(8,128)(2,1)S(1)}, bf16[9,4,32,128]{3,2,1,0:T(8,128)(2,1)}, u32[]{:S(2)}, u32[]{:S(2)}) collective-permute-start(bf16[9,4,32,128]{3,2,1,0:T(8,128)(2,1)S(1)} %get-tuple-element.233), channel_id=1, source_target_pairs={{64,0},{65,1},{66,2},{67,3},{68,4},{69,5},{70,6},{71,7},{72,8},{73... | collective-permute-start | bytes 884744 | tf_op jit(solution)/shard_map/ppermute | solution.py:32
  44.8 2.8 %collective-permute-start.15 = (bf16[9,2,32,128]{3,2,1,0:T(8,128)(2,1)S(1)}, bf16[9,2,32,128]{3,2,1,0:T(8,128)(2,1)S(1)}, u32[]{:S(2)}, u32[]{:S(2)}) collective-permute-start(bf16[9,2,32,128]{3,2,1,0:T(8,128)(2,1)S(1)} %get-tuple-element.237), channel_id=1, source_target_pairs={{64,1},{65,2},{66,3},{67,4},{68,5},{69,6},{70,7},{71,8},{72,9},{73... | collective-permute-start | bytes 442376 | tf_op jit(solution)/shard_map/ppermute | solution.py:32
  45.4 2.1 %collective-permute-start.17 = (bf16[9,2,32,128]{3,2,1,0:T(8,128)(2,1)}, bf16[9,2,32,128]{3,2,1,0:T(8,128)(2,1)S(1)}, u32[]{:S(2)}, u32[]{:S(2)}) collective-permute-start(bf16[9,2,32,128]{3,2,1,0:T(8,128)(2,1)} %get-tuple-element.239), channel_id=1, source_target_pairs={{65,0},{66,1},{67,2},{68,3},{69,4},{70,5},{71,6},{72,7},{73,8},{74... | collective-permute-start | bytes 442376 | tf_op jit(solution)/shard_map/ppermute | solution.py:32
  47.6 1.9 %copy-start.9 = (bf16[9,2,32,128]{3,2,1,0:T(8,128)(2,1)}, bf16[9,2,32,128]{3,2,1,0:T(8,128)(2,1)S(1)}, u32[]{:S(2)}) copy-start(bf16[9,2,32,128]{3,2,1,0:T(8,128)(2,1)S(1)} %collective-permute-done.15) | copy-start | bytes 442372
  47.6 1.9 %copy-start.10 = (bf16[9,2,32,128]{3,2,1,0:T(8,128)(2,1)}, bf16[9,2,32,128]{3,2,1,0:T(8,128)(2,1)S(1)}, u32[]{:S(2)}) copy-start(bf16[9,2,32,128]{3,2,1,0:T(8,128)(2,1)S(1)} %collective-permute-done.17) | copy-start | bytes 442372
  49.5 48.3 %collective-permute-start.19 = (bf16[9,4,32,128]{3,2,1,0:T(8,128)(2,1)}, bf16[9,4,32,128]{3,2,1,0:T(8,128)(2,1)}, u32[]{:S(2)}, u32[]{:S(2)}) collective-permute-start(bf16[9,4,32,128]{3,2,1,0:T(8,128)(2,1)} %add.57), channel_id=1, source_target_pairs={{128,160},{129,161},{130,162},{131,163},{132,164},{133,165},{134,1... | collective-permute-start | bytes 884744 | tf_op jit(solution)/shard_map/ppermute | solution.py:32
  100.5 21.1 %copy-start = (bf16[1,3,3,3,128,128]{5,4,3,2,1,0:T(8,128)(2,1)S(1)}, bf16[1,3,3,3,128,128]{5,4,3,2,1,0:T(8,128)(2,1)}, u32[]{:S(2)}) copy-start(bf16[1,3,3,3,128,128]{5,4,3,2,1,0:T(8,128)(2,1)} %param.19) | copy-start | bytes 2654212
  100.5 21.1 %copy-start.2 = (f32[9,4,32,128]{3,2,1,0:T(8,128)S(1)}, f32[9,4,32,128]{3,2,1,0:T(8,128)}, u32[]{:S(2)}) copy-start(f32[9,4,32,128]{3,2,1,0:T(8,128)} %copy-done.1) | copy-start | bytes 1769476
  100.5 21.1 %copy-start.6 = (bf16[9,4,32,128]{3,2,1,0:T(8,128)(2,1)S(1)}, bf16[9,4,32,128]{3,2,1,0:T(8,128)(2,1)}, u32[]{:S(2)}) copy-start(bf16[9,4,32,128]{3,2,1,0:T(8,128)(2,1)} %copy-done.5) | copy-start | bytes 884740
  100.5 21.1 %copy-start.7 = (bf16[9,1,32,128]{3,2,1,0:T(8,128)(2,1)S(1)}, bf16[9,1,32,128]{3,2,1,0:T(8,128)(2,1)}, u32[]{:S(2)}) copy-start(bf16[9,1,32,128]{3,2,1,0:T(8,128)(2,1)} %get-tuple-element.248) | copy-start | bytes 221188
  100.5 21.1 %copy-start.8 = (bf16[9,1,32,128]{3,2,1,0:T(8,128)(2,1)S(1)}, bf16[9,1,32,128]{3,2,1,0:T(8,128)(2,1)}, u32[]{:S(2)}) copy-start(bf16[9,1,32,128]{3,2,1,0:T(8,128)(2,1)} %get-tuple-element.246) | copy-start | bytes 221188
  100.5 3.1 %collective-permute-start.20 = (bf16[9,64,384]{2,1,0:T(8,128)(2,1)S(1)}, bf16[9,64,384]{2,1,0:T(8,128)(2,1)S(1)}, u32[]{:S(2)}, u32[]{:S(2)}) collective-permute-start(bf16[9,64,384]{2,1,0:T(8,128)(2,1)S(1)} %get-tuple-element.253), channel_id=1, source_target_pairs={{0,1},{1,0},{2,3},{3,2},{4,5},{5,4},{6,7},{7,6},{8,9},{9,8},{10,11... | collective-permute-start | bytes 1327112 | tf_op jit(solution)/shard_map/ppermute | solution.py:381
  104.7 33.2 %all-to-all-start = ((bf16[16,9,4,384]{3,2,1,0:T(4,128)(2,1)}), bf16[16,9,4,384]{3,2,1,0:T(4,128)(2,1)S(1)}, u32[]{:S(2)}, u32[]{:S(2)}) async-start(bf16[16,9,4,384]{3,2,1,0:T(4,128)(2,1)} %copy.8), calls=%async_computation | async-start | bytes 884736 | tf_op jit(solution)/shard_map/all_to_all | solution.py:386
  120.3 14.0 %collective-permute-start.18 = (bf16[9,4,32,128]{3,2,1,0:T(8,128)(2,1)}, bf16[9,4,32,128]{3,2,1,0:T(8,128)(2,1)S(1)}, u32[]{:S(2)}, u32[]{:S(2)}) collective-permute-start(bf16[9,4,32,128]{3,2,1,0:T(8,128)(2,1)} %get-tuple-element.247), channel_id=1, source_target_pairs={{128,160},{129,161},{130,162},{131,163},{132,164},{133,165},{134,1... | collective-permute-start | bytes 884744 | tf_op jit(solution)/shard_map/ppermute | solution.py:32

commit v12 on v4

--- a/solution.py
+++ b/solution.py
@@ -7,6 +7,7 @@
 from jax import lax
 from jax.experimental import pallas as pl
 from jax.experimental.pallas import tpu as pltpu
+from jax.sharding import Mesh
 from jax.sharding import PartitionSpec as P
 
 BF = jnp.bfloat16
@@ -17,8 +18,8 @@
 ROWS = 4
 COLS = 32
 CH = 128
-AXES = ("section", "dp")
-HALVING = (1, 4, 2, 8, 16)
+PEERS = 16
+AXES = ("section", "z", "y", "core")
 
 
 def permute(value, hops):
@@ -215,14 +216,12 @@
 
 def channel_order():
     share = CH // DP
-    order = []
-    for n in range(CH):
-        slot, rest = divmod(n, share)
-        d = 0
-        for place, bit in enumerate(HALVING):
-            if (slot >> (len(HALVING) - 1 - place)) & 1:
-                d |= bit
-        order.append(d * share + rest)
+    order = [
+        (chip * 2 + core) * share + rest
+        for core in range(2)
+        for chip in range(PEERS)
+        for rest in range(share)
+    ]
     matrix = np.zeros((CH, CH), np.float32)
     matrix[np.arange(CH), order] = 1.0
     return matrix
@@ -236,8 +235,8 @@
 
 def local(acts, kernels, cotangent):
     me = lax.axis_index("section")
-    dp = lax.axis_index("dp")
-    core = dp % 2
+    dp = lax.axis_index(AXES[1:])
+    core = lax.axis_index("core")
     scale = 1.0 / math.sqrt(FRAMES * ROWS * DP * COLS)
     odd = [s for s in range(SEC) if s % 2 == 1]
     every = range(SEC)
@@ -317,37 +316,33 @@
     final = even(result, (0,))
 
     part = taps(ut, jnp.where(me == 0, cotangent, result), scale)
-    for bit in HALVING:
-        size = part.shape[1] // 2
-        mine = (dp // bit) % 2
-        keep = lax.dynamic_slice_in_dim(part, mine * size, size, 1)
-        give = lax.dynamic_slice_in_dim(part, (1 - mine) * size, size, 1)
-        shift = 0
-        if bit == HALVING[-1]:
-            keep = permute(keep, [((s + 1) % SEC, s, 0) for s in every])
-            shift = 1
-        got = lax.ppermute(
-            give,
-            AXES,
-            [((s + shift) % SEC * DP + d, s * DP + (d ^ bit)) for s in every for d in range(DP)],
-        )
-        part = keep.astype(F32) + got.astype(F32)
-        if not shift:
-            part = part.astype(BF)
+    half = CH // 2
+    keep = lax.dynamic_slice_in_dim(part, core * half, half, 1)
+    give = lax.dynamic_slice_in_dim(part, (1 - core) * half, half, 1)
+    got = lax.ppermute(
+        give, AXES, [(s * DP + d, s * DP + (d ^ 1)) for s in every for d in range(DP)]
+    )
+    part = (keep.astype(F32) + got.astype(F32)).astype(BF)
+    part = jnp.transpose(part.reshape(9, PEERS, CH // DP, 3 * CH), (1, 0, 2, 3))
+    part = lax.all_to_all(part, ("z", "y"), 0, 0, tiled=True)
+    part = jnp.sum(part.astype(F32), axis=0)
+    part = permute(part.astype(BF), [((s + 1) % SEC, s, 0) for s in every]).astype(F32)
     share = CH // DP
     kernel_part = jnp.transpose(part.reshape(9, share, 3, CH), (1, 2, 0, 3)).reshape(share, 27, CH)
     return (final[None], kernel_part[None])
 
 
 def solution(mesh):
+    parts = Mesh(mesh.devices.reshape(SEC, DP // 4, 2, 2), AXES)
+    rows = AXES[1:]
     return jax.shard_map(
         local,
-        mesh=mesh,
+        mesh=parts,
         in_specs=(
-            P("section", None, "dp", None, None),
+            P("section", None, rows, None, None),
             P("section", None, None, None, None, None),
-            P(None, "dp", None, None),
+            P(None, rows, None, None),
         ),
-        out_specs=(P("section", None, "dp", None, None), P("section", "dp", None, None)),
+        out_specs=(P("section", None, rows, None, None), P("section", rows, None, None)),
         check_vma=False,
     )

time: 137 us -> 133 us (0.971)
  starting transfers between devices: 41.5 us -> 39 us
  waiting for transfers between devices: 72.3 us -> 70.8 us
    ppermute x5 -> x1, waiting for transfers between devices: 18.4 us -> 1.78 us  [local(): lax.ppermute(give, AXES, [(s * DP + d, s * DP + (d ^ 1)) for s in every f...]
    all_to_all x0 -> x1, waiting for transfers between devices: none -> 15.1 us  [local(): part = lax.all_to_all(part, ('z', 'y'), 0, 0, tiled=True)]
    ppermute x5 -> x1, starting transfers between devices: 12.1 us -> 0.09 us  [local(): lax.ppermute(give, AXES, [(s * DP + d, s * DP + (d ^ 1)) for s in every f...]
    all_to_all x0 -> x1, starting transfers between devices: none -> 11 us  [local(): part = lax.all_to_all(part, ('z', 'y'), 0, 0, tiled=True)]
    ppermute x1, starting transfers between devices: 7.46 us -> 6.05 us  [local(): lax.ppermute(w_half, AXES, [(s * DP + d, s * DP + (d ^ 1)) for s in pair...]
  transfers between devices with their start and end apart: 27 -> 24, of which waited for: 12 -> 8; matrix products, arithmetic and copies ran while one was open for 6% -> 6% of each run, Pallas kernels for 1% -> 1%
where the time goes in v12:
time: 133 us; the launch traced here: 132 us
  waiting for transfers between devices  70.8 us (53%)
  starting transfers between devices  39 us (29%)
  Pallas kernels  9.49 us (7%)
  local copies, waits for them, and re-layouts  7.53 us (6%)
  other arithmetic  3.98 us (3%)
    ppermute x21, waiting for transfers between devices, permute(): return lax.ppermute(value, AXES, pairs)  54 us
    ppermute x21, starting transfers between devices, permute(): return lax.ppermute(value, AXES, pairs)  21.9 us
    all_to_all x1, waiting for transfers between devices, local(): part = lax.all_to_all(part, ('z', 'y'), 0, 0, tiled=True)  15.1 us
    all_to_all x1, starting transfers between devices, local(): part = lax.all_to_all(part, ('z', 'y'), 0, 0, tiled=True)  11 us
    pallas_call x1, Pallas kernels, double(): pl.pallas_call(double_kernel, out_shape=gradient_shapes(), in_specs=[pl.B...  6.76 us
    ppermute x1, starting transfers between devices, local(): lax.ppermute(w_half, AXES, [(s * DP + d, s * DP + (d ^ 1)) for s in pair...  6.05 us
  transfers between devices with their start and end apart: 24, of which 8 were waited for; matrix products, arithmetic and copies ran while one was open for 6% of the time, Pallas kernels for 1%

profile of v12, /device:TPU:8, one launch (start us, length us, event | category | flops | bytes accessed | tf_op | source)
XLA Modules:
  0.0 132.1 jit_solution(8681528482046285180)
XLA Ops:
  0.6 0.0 copy-start.1
  0.7 1.1 pad_maximum_fusion.2
  1.8 0.0 copy-start.6
  1.8 1.9 %collective-permute-start = (bf16[18,1,32,128]{3,2,1,0:T(8,128)(2,1)S(1)}, bf16[18,1,32,128]{3,2,1,0:T(8,128)(2,1)S(1)}, u32[]{:S(2)}, u32[]{:S(2)}) collective-permute-start(bf16[18,1,32,128]{3,2,1,0:T(8,128)(2,1)S(1)} %get-tuple-element.224), channel_id=1, source_target_pairs={{0,1},{1,2},{2,3},{3,4},{4,5},{5,6},{6,7},{7,8},{8,9},{9,10},{10,1... | collective-permute-start | bytes 442376 | tf_op jit(solution)/shard_map/ppermute | solution.py:32
  3.7 1.3 collective-permute-start.1
  5.0 1.0 constant_dynamic-slice_fusion.1
  6.0 1.3 collective-permute-start.5
  7.3 1.2 fusion.10
  8.5 0.5 collective-permute-done.1
  9.0 2.1 %conditional.6 = ((bf16[9,4,32,128]{3,2,1,0:T(8,128)(2,1)}, bf16[9,2,32,128]{3,2,1,0:T(8,128)(2,1)}, bf16[9,2,32,128]{3,2,1,0:T(8,128)(2,1)})) conditional(s32[]{:T(128)} %convert_element_type.40, bf16[9,4,32,128]{3,2,1,0:T(8,128)(2,1)S(1)} %copy-done.5, (bf16[18,1,32,128]{3,2,1,0:T(8,128)(2,1)S(1)}, bf16[18,1,32,128]{3,2,1,0:T(8,128)(2,1)S(1)}, ...), branch_computations={%region_0.0_spmd, %region_1.0_spmd} | conditional | bytes 884772 | solution.py:260
  9.0 0.7 copy.11
  9.7 0.7 broadcast_in_dim.13
  10.4 0.7 broadcast_in_dim.13.clone
  11.1 0.1 pad_maximum_fusion
  11.2 0.0 copy-start
  11.2 0.7 collective-permute-start.3
  11.9 1.3 collective-permute-start.7
  13.2 1.3 %collective-permute-start.2 = (bf16[9,2,32,128]{3,2,1,0:T(8,128)(2,1)}, bf16[9,2,32,128]{3,2,1,0:T(8,128)(2,1)}, u32[]{:S(2)}, u32[]{:S(2)}) collective-permute-start(bf16[9,2,32,128]{3,2,1,0:T(8,128)(2,1)} %get-tuple-element.199), channel_id=1, source_target_pairs={{224,161},{225,162},{226,163},{227,164},{228,165},{229,166},{230,1... | collective-permute-start | bytes 442376 | tf_op jit(solution)/shard_map/ppermute | solution.py:32
  14.5 0.7 collective-permute-start.4
  15.2 0.0 collective-permute-done.4
  15.2 0.0 collective-permute-done.3
  15.2 6.2 %collective-permute-done.5 = bf16[1728,128]{1,0:T(8,128)(2,1)} collective-permute-done((bf16[1728,128]{1,0:T(8,128)(2,1)S(1)}, bf16[1728,128]{1,0:T(8,128)(2,1)}, u32[]{:S(2)}, u32[]{:S(2)}) %collective-permute-start.5) | collective-permute-done | bytes 442400 | tf_op jit(solution)/shard_map/ppermute | solution.py:32
  21.5 6.0 %collective-permute-start.6 = (bf16[1728,128]{1,0:T(8,128)(2,1)}, bf16[1728,128]{1,0:T(8,128)(2,1)}, u32[]{:S(2)}, u32[]{:S(2)}) collective-permute-start(bf16[1728,128]{1,0:T(8,128)(2,1)} %collective-permute-done.5), channel_id=1, source_target_pairs={{32,33},{33,32},{34,35},{35,34},{36,37},{37,36},{38,39},{39,38},{4... | collective-permute-start | bytes 1327112 | tf_op jit(solution)/shard_map/ppermute | solution.py:276
  27.5 3.3 %collective-permute-done.7 = bf16[9,6,32,128]{3,2,1,0:T(8,128)(2,1)S(1)} collective-permute-done((bf16[9,6,32,128]{3,2,1,0:T(8,128)(2,1)S(1)}, bf16[9,6,32,128]{3,2,1,0:T(8,128)(2,1)S(1)}, u32[]{:S(2)}, u32[]{:S(2)}) %collective-permute-start.7) | collective-permute-done | bytes 442400 | tf_op jit(solution)/shard_map/ppermute | solution.py:32
  30.8 1.3 fusion.5
  32.1 0.0 collective-permute-start.8
  32.1 1.4 %collective-permute-start.10 = (bf16[9,4,32,128]{3,2,1,0:T(8,128)(2,1)}, bf16[9,4,32,128]{3,2,1,0:T(8,128)(2,1)}, u32[]{:S(2)}, u32[]{:S(2)}) collective-permute-start(bf16[9,4,32,128]{3,2,1,0:T(8,128)(2,1)} %get-tuple-element.207), channel_id=1, source_target_pairs={{160,96},{161,97},{162,98},{163,99},{164,100},{165,101},{166,102},... | collective-permute-start | bytes 884744 | tf_op jit(solution)/shard_map/ppermute | solution.py:32
  33.5 1.3 collective-permute-start.11
  34.8 1.3 collective-permute-start.9
  36.1 8.1 %collective-permute-done.8.act_ref = bf16[9,6,32,128]{3,2,1,0:T(8,128)(2,1)S(1)} collective-permute-done((bf16[9,6,32,128]{3,2,1,0:T(8,128)(2,1)S(1)}, bf16[9,6,32,128]{3,2,1,0:T(8,128)(2,1)S(1)}, u32[]{:S(2)}, u32[]{:S(2)}) %collective-permute-start.8) | collective-permute-done | bytes 442400 | tf_op jit(solution)/shard_map/ppermute | solution.py:32
  44.2 1.1 tap_rows.1.ut_ref
  45.4 0.0 collective-permute-done.9
  45.4 0.0 collective-permute-done.10
  45.4 1.4 %collective-permute-start.13 = (bf16[9,4,32,128]{3,2,1,0:T(8,128)(2,1)}, bf16[9,4,32,128]{3,2,1,0:T(8,128)(2,1)}, u32[]{:S(2)}, u32[]{:S(2)}) collective-permute-start(bf16[9,4,32,128]{3,2,1,0:T(8,128)(2,1)} %get-tuple-element.214), channel_id=1, source_target_pairs={{224,192},{225,193},{226,194},{227,195},{228,196},{229,197},{230,1... | collective-permute-start | bytes 884744 | tf_op jit(solution)/shard_map/ppermute | solution.py:32
  46.8 1.5 %collective-permute-start.16 = (bf16[9,4,32,128]{3,2,1,0:T(8,128)(2,1)}, bf16[9,4,32,128]{3,2,1,0:T(8,128)(2,1)}, u32[]{:S(2)}, u32[]{:S(2)}) collective-permute-start(bf16[9,4,32,128]{3,2,1,0:T(8,128)(2,1)} %get-tuple-element.214), channel_id=1, source_target_pairs={{96,32},{97,33},{98,34},{99,35},{100,36},{101,37},{102,38},{103,39... | collective-permute-start | bytes 884744 | tf_op jit(solution)/shard_map/ppermute | solution.py:32
  48.3 0.9 fusion.12
  49.2 0.7 collective-permute-start.12
  49.9 0.7 collective-permute-start.15
  50.6 1.3 collective-permute-start.17
  51.9 0.7 collective-permute-start.14
  52.6 1.0 conditional.9
  52.6 1.0 copy.29
  53.6 31.2 %collective-permute-done.17 = bf16[9,2,32,128]{3,2,1,0:T(8,128)(2,1)} collective-permute-done((bf16[9,2,32,128]{3,2,1,0:T(8,128)(2,1)}, bf16[9,2,32,128]{3,2,1,0:T(8,128)(2,1)}, u32[]{:S(2)}, u32[]{:S(2)}) %collective-permute-start.17) | collective-permute-done | bytes 147488 | tf_op jit(solution)/shard_map/ppermute | solution.py:32
  84.7 6.8 %conditional.10 = (bf16[9,4,32,128]{3,2,1,0:T(8,128)(2,1)S(1)}) conditional(s32[]{:T(128)} %convert_element_type.37, bf16[9,4,32,128]{3,2,1,0:T(8,128)(2,1)S(1)} %get-tuple-element.253, (s32[]{:T(128)}, bf16[9,2,32,128]{3,2,1,0:T(8,128)(2,1)S(1)}, bf16[9,4,32,128]{3,2,1,0:T(8,128)(2,1)}, bf16[9,2,32,128]{3,2,1,0:T(8,128)(2,1)}, ...), branch_computations={%region_8.9_spmd, %region_9.10_spmd} | conditional | bytes 8 | solution.py:285
  84.7 6.8 %two_blocks.5 = (bf16[9,4,32,128]{3,2,1,0:T(8,128)(2,1)S(1)}, bf16[9,2,32,128]{3,2,1,0:T(8,128)(2,1)}, bf16[9,2,32,128]{3,2,1,0:T(8,128)(2,1)}) custom-call(s32[1]{0:T(128)} %bitcast.2.core_ref, bf16[9,2,32,128]{3,2,1,0:T(8,128)(2,1)S(1)} %get-tuple-element.147.low_ref, bf16[9,4,32,128]{3,2,1,0:T(8,128)(2,1)} %get-tuple-element.148.own_ref, ...), custom_call_target="tpu_custom_call" | custom-call | tf_op jit(solution)/shard_map/cond/branch_1_fun/two_blocks/pallas_call | solution.py:148
  91.5 0.7 copy-done.7
  92.3 1.6 %kernel_taps.1 = bf16[9,128,384]{2,1,0:T(8,128)(2,1)S(1)} custom-call(bf16[9,128,1152]{2,1,0:T(8,128)(2,1)S(1)} %tap_rows.1.ut_ref, bf16[9,4,32,128]{3,2,1,0:T(8,128)(2,1)S(1)} %broadcast_select_fusion.g_ref), custom_call_target="tpu_custom_call" | custom-call | tf_op jit(solution)/shard_map/kernel_taps/pallas_call | solution.py:207
  93.9 0.0 copy-start.8
  93.9 0.0 copy-start.2
  93.9 0.1 constant_dynamic-slice_fusion
  94.0 0.1 collective-permute-start.21
  94.1 1.8 %collective-permute-done.21 = bf16[9,64,384]{2,1,0:T(8,128)(2,1)S(1)} collective-permute-done((bf16[9,64,384]{2,1,0:T(8,128)(2,1)S(1)}, bf16[9,64,384]{2,1,0:T(8,128)(2,1)S(1)}, u32[]{:S(2)}, u32[]{:S(2)}) %collective-permute-start.21) | collective-permute-done | bytes 442400 | tf_op jit(solution)/shard_map/ppermute | solution.py:322
  95.8 0.1 add_convert_fusion
  96.0 0.1 reshape.20
  96.1 0.9 copy.10
  97.0 11.0 %all-to-all-start = ((bf16[16,9,4,384]{3,2,1,0:T(4,128)(2,1)}), bf16[16,9,4,384]{3,2,1,0:T(4,128)(2,1)S(1)}, u32[]{:S(2)}, u32[]{:S(2)}) async-start(bf16[16,9,4,384]{3,2,1,0:T(4,128)(2,1)} %bitcast.15), calls=%async_computation | async-start | bytes 884736 | tf_op jit(solution)/shard_map/all_to_all | solution.py:327
  108.0 1.3 collective-permute-start.19
  109.4 1.3 collective-permute-start.18
  110.7 0.7 collective-permute-start.20
  111.3 15.1 %all-to-all-done = bf16[16,9,4,384]{3,2,1,0:T(4,128)(2,1)S(1)} async-done(((bf16[16,9,4,384]{3,2,1,0:T(4,128)(2,1)}), bf16[16,9,4,384]{3,2,1,0:T(4,128)(2,1)S(1)}, u32[]{:S(2)}, u32[]{:S(2)}) %all-to-all-start) | async-done | bytes 442400 | tf_op jit(solution)/shard_map/all_to_all | solution.py:327
  126.4 0.2 reduce_sum.12
  126.6 0.1 collective-permute-start.22
  126.7 4.7 %collective-permute-done.22 = bf16[9,4,384]{2,1,0:T(4,128)(2,1)S(1)} collective-permute-done((bf16[9,4,384]{2,1,0:T(4,128)(2,1)S(1)}, bf16[9,4,384]{2,1,0:T(4,128)(2,1)S(1)}, u32[]{:S(2)}, u32[]{:S(2)}) %collective-permute-start.22) | collective-permute-done | bytes 27680 | tf_op jit(solution)/shard_map/ppermute | solution.py:32
  131.4 0.6 copy.8
  (35 shorter events, 0.1 us)
Async XLA Ops:
  0.6 8.4 %copy-start.5 = (bf16[9,4,32,128]{3,2,1,0:T(8,128)(2,1)S(1)}, bf16[9,4,32,128]{3,2,1,0:T(8,128)(2,1)}, u32[]{:S(2)}) copy-start(bf16[9,4,32,128]{3,2,1,0:T(8,128)(2,1)} %param.18) | copy-start | bytes 884740
  0.6 8.4 %copy-start.1 = (bf16[1,3,3,3,128,128]{5,4,3,2,1,0:T(8,128)(2,1)S(1)}, bf16[1,3,3,3,128,128]{5,4,3,2,1,0:T(8,128)(2,1)}, u32[]{:S(2)}) copy-start(bf16[1,3,3,3,128,128]{5,4,3,2,1,0:T(8,128)(2,1)} %param.17) | copy-start | bytes 2654212
  1.8 9.3 %copy-start.6 = (bf16[1,9,4,32,128]{4,3,2,1,0:T(8,128)(2,1)S(1)}, bf16[1,9,4,32,128]{4,3,2,1,0:T(8,128)(2,1)}, u32[]{:S(2)}) copy-start(bf16[1,9,4,32,128]{4,3,2,1,0:T(8,128)(2,1)} %param.16) | copy-start | bytes 884740
  1.8 6.7 %collective-permute-start = (bf16[18,1,32,128]{3,2,1,0:T(8,128)(2,1)S(1)}, bf16[18,1,32,128]{3,2,1,0:T(8,128)(2,1)S(1)}, u32[]{:S(2)}, u32[]{:S(2)}) collective-permute-start(bf16[18,1,32,128]{3,2,1,0:T(8,128)(2,1)S(1)} %get-tuple-element.224), channel_id=1, source_target_pairs={{0,1},{1,2},{2,3},{3,4},{4,5},{5,6},{6,7},{7,8},{8,9},{9,10},{10,1... | collective-permute-start | bytes 442376 | tf_op jit(solution)/shard_map/ppermute | solution.py:32
  3.7 5.3 %collective-permute-start.1 = (bf16[18,1,32,128]{3,2,1,0:T(8,128)(2,1)S(1)}, bf16[18,1,32,128]{3,2,1,0:T(8,128)(2,1)S(1)}, u32[]{:S(2)}, u32[]{:S(2)}) collective-permute-start(bf16[18,1,32,128]{3,2,1,0:T(8,128)(2,1)S(1)} %get-tuple-element.225), channel_id=1, source_target_pairs={{1,0},{2,1},{3,2},{4,3},{5,4},{6,5},{7,6},{8,7},{9,8},{10,9},{11,1... | collective-permute-start | bytes 442376 | tf_op jit(solution)/shard_map/ppermute | solution.py:32
  6.0 15.4 %collective-permute-start.5 = (bf16[1728,128]{1,0:T(8,128)(2,1)S(1)}, bf16[1728,128]{1,0:T(8,128)(2,1)}, u32[]{:S(2)}, u32[]{:S(2)}) collective-permute-start(bf16[1728,128]{1,0:T(8,128)(2,1)S(1)} %constant_dynamic-slice_fusion.1), channel_id=1, source_target_pairs={{64,32},{65,33},{66,34},{67,35},{68,36},{69,37},{70,38},{71,39},{7... | collective-permute-start | bytes 1327112 | tf_op jit(solution)/shard_map/ppermute | solution.py:32
  8.5 23.6 %copy-start.3 = (f32[9,4,32,128]{3,2,1,0:T(8,128)}, f32[9,4,32,128]{3,2,1,0:T(8,128)S(1)}, u32[]{:S(2)}) copy-start(f32[9,4,32,128]{3,2,1,0:T(8,128)S(1)} %fusion.10) | copy-start | bytes 1769476
  11.2 33.1 %copy-start = (bf16[128,128]{1,0:T(8,128)(2,1)S(1)}, bf16[128,128]{1,0:T(8,128)(2,1)}, u32[]{:S(2)}) copy-start(bf16[128,128]{1,0:T(8,128)(2,1)} %constant.56.clone.order_ref) | copy-start | bytes 98308
  11.2 4.0 %collective-permute-start.3 = (bf16[9,4,32,128]{3,2,1,0:T(8,128)(2,1)}, bf16[9,4,32,128]{3,2,1,0:T(8,128)(2,1)S(1)}, u32[]{:S(2)}, u32[]{:S(2)}) collective-permute-start(bf16[9,4,32,128]{3,2,1,0:T(8,128)(2,1)} %get-tuple-element.197), channel_id=1, source_target_pairs={{224,160},{225,161},{226,162},{227,163},{228,164},{229,165},{230,1... | collective-permute-start | bytes 884744 | tf_op jit(solution)/shard_map/ppermute | solution.py:32
  11.9 19.0 %collective-permute-start.7 = (bf16[9,6,32,128]{3,2,1,0:T(8,128)(2,1)S(1)}, bf16[9,6,32,128]{3,2,1,0:T(8,128)(2,1)S(1)}, u32[]{:S(2)}, u32[]{:S(2)}) collective-permute-start(bf16[9,6,32,128]{3,2,1,0:T(8,128)(2,1)S(1)} %pad_maximum_fusion), channel_id=1, source_target_pairs={{64,32},{65,33},{66,34},{67,35},{68,36},{69,37},{70,38},{71,39},{7... | collective-permute-start | bytes 1327112 | tf_op jit(solution)/shard_map/ppermute | solution.py:32
  13.2 2.0 %collective-permute-start.2 = (bf16[9,2,32,128]{3,2,1,0:T(8,128)(2,1)}, bf16[9,2,32,128]{3,2,1,0:T(8,128)(2,1)}, u32[]{:S(2)}, u32[]{:S(2)}) collective-permute-start(bf16[9,2,32,128]{3,2,1,0:T(8,128)(2,1)} %get-tuple-element.199), channel_id=1, source_target_pairs={{224,161},{225,162},{226,163},{227,164},{228,165},{229,166},{230,1... | collective-permute-start | bytes 442376 | tf_op jit(solution)/shard_map/ppermute | solution.py:32
  14.5 0.7 collective-permute-start.4
  15.2 6.3 %copy-start.9 = (bf16[9,2,32,128]{3,2,1,0:T(8,128)(2,1)}, bf16[9,2,32,128]{3,2,1,0:T(8,128)(2,1)S(1)}, u32[]{:S(2)}) copy-start(bf16[9,2,32,128]{3,2,1,0:T(8,128)(2,1)S(1)} %collective-permute-done.4) | copy-start | bytes 442372
  21.5 10.7 %collective-permute-start.6 = (bf16[1728,128]{1,0:T(8,128)(2,1)}, bf16[1728,128]{1,0:T(8,128)(2,1)}, u32[]{:S(2)}, u32[]{:S(2)}) collective-permute-start(bf16[1728,128]{1,0:T(8,128)(2,1)} %collective-permute-done.5), channel_id=1, source_target_pairs={{32,33},{33,32},{34,35},{35,34},{36,37},{37,36},{38,39},{39,38},{4... | collective-permute-start | bytes 1327112 | tf_op jit(solution)/shard_map/ppermute | solution.py:276
  32.1 12.1 %collective-permute-start.8 = (bf16[9,6,32,128]{3,2,1,0:T(8,128)(2,1)S(1)}, bf16[9,6,32,128]{3,2,1,0:T(8,128)(2,1)S(1)}, u32[]{:S(2)}, u32[]{:S(2)}) collective-permute-start(bf16[9,6,32,128]{3,2,1,0:T(8,128)(2,1)S(1)} %pad_maximum_fusion), channel_id=1, source_target_pairs={{0,32},{1,33},{2,34},{3,35},{4,36},{5,37},{6,38},{7,39},{8,40},{9,... | collective-permute-start | bytes 1327112 | tf_op jit(solution)/shard_map/ppermute | solution.py:32
  32.1 13.3 %collective-permute-start.10 = (bf16[9,4,32,128]{3,2,1,0:T(8,128)(2,1)}, bf16[9,4,32,128]{3,2,1,0:T(8,128)(2,1)}, u32[]{:S(2)}, u32[]{:S(2)}) collective-permute-start(bf16[9,4,32,128]{3,2,1,0:T(8,128)(2,1)} %get-tuple-element.207), channel_id=1, source_target_pairs={{160,96},{161,97},{162,98},{163,99},{164,100},{165,101},{166,102},... | collective-permute-start | bytes 884744 | tf_op jit(solution)/shard_map/ppermute | solution.py:32
  33.5 11.9 %collective-permute-start.11 = (bf16[9,2,32,128]{3,2,1,0:T(8,128)(2,1)}, bf16[9,2,32,128]{3,2,1,0:T(8,128)(2,1)}, u32[]{:S(2)}, u32[]{:S(2)}) collective-permute-start(bf16[9,2,32,128]{3,2,1,0:T(8,128)(2,1)} %get-tuple-element.208), channel_id=1, source_target_pairs={{161,96},{162,97},{163,98},{164,99},{165,100},{166,101},{167,102},... | collective-permute-start | bytes 442376 | tf_op jit(solution)/shard_map/ppermute | solution.py:32
  34.8 10.6 %collective-permute-start.9 = (bf16[9,2,32,128]{3,2,1,0:T(8,128)(2,1)}, bf16[9,2,32,128]{3,2,1,0:T(8,128)(2,1)}, u32[]{:S(2)}, u32[]{:S(2)}) collective-permute-start(bf16[9,2,32,128]{3,2,1,0:T(8,128)(2,1)} %get-tuple-element.209), channel_id=1, source_target_pairs={{160,97},{161,98},{162,99},{163,100},{164,101},{165,102},{166,103}... | collective-permute-start | bytes 442376 | tf_op jit(solution)/shard_map/ppermute | solution.py:32
  45.4 7.2 %collective-permute-start.13 = (bf16[9,4,32,128]{3,2,1,0:T(8,128)(2,1)}, bf16[9,4,32,128]{3,2,1,0:T(8,128)(2,1)}, u32[]{:S(2)}, u32[]{:S(2)}) collective-permute-start(bf16[9,4,32,128]{3,2,1,0:T(8,128)(2,1)} %get-tuple-element.214), channel_id=1, source_target_pairs={{224,192},{225,193},{226,194},{227,195},{228,196},{229,197},{230,1... | collective-permute-start | bytes 884744 | tf_op jit(solution)/shard_map/ppermute | solution.py:32
  46.8 38.0 %collective-permute-start.16 = (bf16[9,4,32,128]{3,2,1,0:T(8,128)(2,1)}, bf16[9,4,32,128]{3,2,1,0:T(8,128)(2,1)}, u32[]{:S(2)}, u32[]{:S(2)}) collective-permute-start(bf16[9,4,32,128]{3,2,1,0:T(8,128)(2,1)} %get-tuple-element.214), channel_id=1, source_target_pairs={{96,32},{97,33},{98,34},{99,35},{100,36},{101,37},{102,38},{103,39... | collective-permute-start | bytes 884744 | tf_op jit(solution)/shard_map/ppermute | solution.py:32
  49.2 2.7 %collective-permute-start.12 = (bf16[9,1,32,128]{3,2,1,0:T(8,128)(2,1)S(1)}, bf16[9,1,32,128]{3,2,1,0:T(8,128)(2,1)S(1)}, u32[]{:S(2)}, u32[]{:S(2)}) collective-permute-start(bf16[9,1,32,128]{3,2,1,0:T(8,128)(2,1)S(1)} %get-tuple-element.229), channel_id=1, source_target_pairs={{224,193},{225,194},{226,195},{227,196},{228,197},{229,198},{230,1... | collective-permute-start | bytes 221192 | tf_op jit(solution)/shard_map/ppermute | solution.py:32
  49.9 3.7 %collective-permute-start.15 = (bf16[9,2,32,128]{3,2,1,0:T(8,128)(2,1)}, bf16[9,2,32,128]{3,2,1,0:T(8,128)(2,1)S(1)}, u32[]{:S(2)}, u32[]{:S(2)}) collective-permute-start(bf16[9,2,32,128]{3,2,1,0:T(8,128)(2,1)} %get-tuple-element.215), channel_id=1, source_target_pairs={{96,33},{97,34},{98,35},{99,36},{100,37},{101,38},{102,39},{103,40... | collective-permute-start | bytes 442376 | tf_op jit(solution)/shard_map/ppermute | solution.py:32
  50.6 34.2 %collective-permute-start.17 = (bf16[9,2,32,128]{3,2,1,0:T(8,128)(2,1)}, bf16[9,2,32,128]{3,2,1,0:T(8,128)(2,1)}, u32[]{:S(2)}, u32[]{:S(2)}) collective-permute-start(bf16[9,2,32,128]{3,2,1,0:T(8,128)(2,1)} %get-tuple-element.216), channel_id=1, source_target_pairs={{97,32},{98,33},{99,34},{100,35},{101,36},{102,37},{103,38},{104,3... | collective-permute-start | bytes 442376 | tf_op jit(solution)/shard_map/ppermute | solution.py:32
  51.9 0.7 collective-permute-start.14
  91.5 0.7 copy-start.7
  93.9 14.1 %copy-start.8 = (bf16[9,4,32,128]{3,2,1,0:T(8,128)(2,1)S(1)}, bf16[9,4,32,128]{3,2,1,0:T(8,128)(2,1)}, u32[]{:S(2)}) copy-start(bf16[9,4,32,128]{3,2,1,0:T(8,128)(2,1)} %copy-done.7) | copy-start | bytes 884740
  93.9 32.8 %copy-start.2 = (bf16[1,3,3,3,128,128]{5,4,3,2,1,0:T(8,128)(2,1)S(1)}, bf16[1,3,3,3,128,128]{5,4,3,2,1,0:T(8,128)(2,1)}, u32[]{:S(2)}) copy-start(bf16[1,3,3,3,128,128]{5,4,3,2,1,0:T(8,128)(2,1)} %param.17) | copy-start | bytes 2654212
  93.9 32.8 %copy-start.4 = (f32[9,4,32,128]{3,2,1,0:T(8,128)S(1)}, f32[9,4,32,128]{3,2,1,0:T(8,128)}, u32[]{:S(2)}) copy-start(f32[9,4,32,128]{3,2,1,0:T(8,128)} %copy-done.3) | copy-start | bytes 1769476
  94.0 1.9 %collective-permute-start.21 = (bf16[9,64,384]{2,1,0:T(8,128)(2,1)S(1)}, bf16[9,64,384]{2,1,0:T(8,128)(2,1)S(1)}, u32[]{:S(2)}, u32[]{:S(2)}) collective-permute-start(bf16[9,64,384]{2,1,0:T(8,128)(2,1)S(1)} %constant_dynamic-slice_fusion), channel_id=1, source_target_pairs={{0,1},{1,0},{2,3},{3,2},{4,5},{5,4},{6,7},{7,6},{8,9},{9,8},{10,11... | collective-permute-start | bytes 1327112 | tf_op jit(solution)/shard_map/ppermute | solution.py:322
  97.0 29.4 %all-to-all-start = ((bf16[16,9,4,384]{3,2,1,0:T(4,128)(2,1)}), bf16[16,9,4,384]{3,2,1,0:T(4,128)(2,1)S(1)}, u32[]{:S(2)}, u32[]{:S(2)}) async-start(bf16[16,9,4,384]{3,2,1,0:T(4,128)(2,1)} %bitcast.15), calls=%async_computation | async-start | bytes 884736 | tf_op jit(solution)/shard_map/all_to_all | solution.py:327
  108.0 18.7 %collective-permute-start.19 = (bf16[9,4,32,128]{3,2,1,0:T(8,128)(2,1)S(1)}, bf16[9,4,32,128]{3,2,1,0:T(8,128)(2,1)S(1)}, u32[]{:S(2)}, u32[]{:S(2)}) collective-permute-start(bf16[9,4,32,128]{3,2,1,0:T(8,128)(2,1)S(1)} %copy-done.8), channel_id=1, source_target_pairs={{32,0},{33,1},{34,2},{35,3},{36,4},{37,5},{38,6},{39,7},{40,8},{41... | collective-permute-start | bytes 884744 | tf_op jit(solution)/shard_map/ppermute | solution.py:32
  109.4 17.3 %collective-permute-start.18 = (bf16[9,1,32,128]{3,2,1,0:T(8,128)(2,1)S(1)}, bf16[9,1,32,128]{3,2,1,0:T(8,128)(2,1)S(1)}, u32[]{:S(2)}, u32[]{:S(2)}) collective-permute-start(bf16[9,1,32,128]{3,2,1,0:T(8,128)(2,1)S(1)} %get-tuple-element.227), channel_id=1, source_target_pairs={{32,1},{33,2},{34,3},{35,4},{36,5},{37,6},{38,7},{39,8},{40,9},{41... | collective-permute-start | bytes 221192 | tf_op jit(solution)/shard_map/ppermute | solution.py:32
  110.7 16.0 %collective-permute-start.20 = (bf16[9,1,32,128]{3,2,1,0:T(8,128)(2,1)S(1)}, bf16[9,1,32,128]{3,2,1,0:T(8,128)(2,1)S(1)}, u32[]{:S(2)}, u32[]{:S(2)}) collective-permute-start(bf16[9,1,32,128]{3,2,1,0:T(8,128)(2,1)S(1)} %get-tuple-element.226), channel_id=1, source_target_pairs={{33,0},{34,1},{35,2},{36,3},{37,4},{38,5},{39,6},{40,7},{41,8},{42... | collective-permute-start | bytes 221192 | tf_op jit(solution)/shard_map/ppermute | solution.py:32
  126.6 4.8 %collective-permute-start.22 = (bf16[9,4,384]{2,1,0:T(4,128)(2,1)S(1)}, bf16[9,4,384]{2,1,0:T(4,128)(2,1)S(1)}, u32[]{:S(2)}, u32[]{:S(2)}) collective-permute-start(bf16[9,4,384]{2,1,0:T(4,128)(2,1)S(1)} %reduce_sum.12), channel_id=1, source_target_pairs={{32,0},{33,1},{34,2},{35,3},{36,4},{37,5},{38,6},{39,7},{40,8},{41... | collective-permute-start | bytes 82952 | tf_op jit(solution)/shard_map/ppermute | solution.py:32

commit v13 on v12

--- a/solution.py
+++ b/solution.py
@@ -272,7 +272,9 @@
 
     act6, state = barrier((act6, state))
     act_next = permute(act6, [(s + 1, s, 0) for s in pair])
-    arrived, w_half = barrier((hop(state, 5), w_half))
+    low5, own5, high5 = hop(state, 5)
+    low5, own5, w_half = barrier((low5, own5, w_half))
+    arrived = (low5, own5, high5)
     w_other = lax.ppermute(
         w_half, AXES, [(s * DP + d, s * DP + (d ^ 1)) for s in pair for d in range(DP)]
     )

time: 133 us -> 135 us (1.015)
  starting transfers between devices: 39 us -> 45 us
  waiting for transfers between devices: 70.8 us -> 66.8 us
    ppermute x21, waiting for transfers between devices: 54 us -> 50.3 us  [permute(): return lax.ppermute(value, AXES, pairs)]
    ppermute x1, starting transfers between devices: 0.09 us -> 3.61 us  [local(): lax.ppermute(give, AXES, [(s * DP + d, s * DP + (d ^ 1)) for s in every f...]
    all_to_all x1, starting transfers between devices: 11 us -> 13.4 us  [local(): part = lax.all_to_all(part, ('z', 'y'), 0, 0, tiled=True)]
where the time goes in v13:
time: 135 us; the launch traced here: 134 us
  waiting for transfers between devices  66.8 us (49%)
  starting transfers between devices  45 us (33%)
  Pallas kernels  9.49 us (7%)
  local copies, waits for them, and re-layouts  7.53 us (6%)
  other arithmetic  3.97 us (3%)
    ppermute x21, waiting for transfers between devices, permute(): return lax.ppermute(value, AXES, pairs)  50.3 us
    ppermute x21, starting transfers between devices, permute(): return lax.ppermute(value, AXES, pairs)  22 us
    all_to_all x1, waiting for transfers between devices, local(): part = lax.all_to_all(part, ('z', 'y'), 0, 0, tiled=True)  15.1 us
    all_to_all x1, starting transfers between devices, local(): part = lax.all_to_all(part, ('z', 'y'), 0, 0, tiled=True)  13.4 us
    pallas_call x1, Pallas kernels, double(): pl.pallas_call(double_kernel, out_shape=gradient_shapes(), in_specs=[pl.B...  6.76 us
    ppermute x1, starting transfers between devices, local(): lax.ppermute(w_half, AXES, [(s * DP + d, s * DP + (d ^ 1)) for s in pair...  6.05 us
    ppermute x1, starting transfers between devices, local(): lax.ppermute(give, AXES, [(s * DP + d, s * DP + (d ^ 1)) for s in every f...  3.61 us
  transfers between devices with their start and end apart: 24, of which 8 were waited for; matrix products, arithmetic and copies ran while one was open for 6% of the time, Pallas kernels for 1%

profile of v13, /device:TPU:8, one launch (start us, length us, event | category | flops | bytes accessed | tf_op | source)
XLA Modules:
  0.0 134.0 jit_solution(12980485911911849201)
XLA Ops:
  0.6 0.0 copy-start.1
  0.7 1.1 pad_maximum_fusion.2
  1.8 0.0 copy-start.6
  1.8 1.9 %collective-permute-start = (bf16[18,1,32,128]{3,2,1,0:T(8,128)(2,1)S(1)}, bf16[18,1,32,128]{3,2,1,0:T(8,128)(2,1)S(1)}, u32[]{:S(2)}, u32[]{:S(2)}) collective-permute-start(bf16[18,1,32,128]{3,2,1,0:T(8,128)(2,1)S(1)} %get-tuple-element.222), channel_id=1, source_target_pairs={{0,1},{1,2},{2,3},{3,4},{4,5},{5,6},{6,7},{7,8},{8,9},{9,10},{10,1... | collective-permute-start | bytes 442376 | tf_op jit(solution)/shard_map/ppermute | solution.py:32
  3.7 1.3 collective-permute-start.1
  5.0 1.0 constant_dynamic-slice_fusion.1
  6.0 1.3 collective-permute-start.4
  7.3 1.2 fusion.10
  8.5 0.5 collective-permute-done.1
  9.0 2.1 %conditional.6 = ((bf16[9,4,32,128]{3,2,1,0:T(8,128)(2,1)}, bf16[9,2,32,128]{3,2,1,0:T(8,128)(2,1)}, bf16[9,2,32,128]{3,2,1,0:T(8,128)(2,1)})) conditional(s32[]{:T(128)} %convert_element_type.40, bf16[9,4,32,128]{3,2,1,0:T(8,128)(2,1)S(1)} %copy-done.5, (bf16[18,1,32,128]{3,2,1,0:T(8,128)(2,1)S(1)}, bf16[18,1,32,128]{3,2,1,0:T(8,128)(2,1)S(1)}, ...), branch_computations={%region_0.0_spmd, %region_1.0_spmd} | conditional | bytes 884772 | solution.py:260
  9.0 0.7 copy.11
  9.7 0.7 broadcast_in_dim.13
  10.4 0.7 broadcast_in_dim.13.clone
  11.1 0.1 pad_maximum_fusion
  11.2 0.0 copy-start
  11.2 0.7 collective-permute-start.3
  11.9 1.3 collective-permute-start.7
  13.2 1.3 collective-permute-start.2
  14.5 0.0 collective-permute-done.2
  14.5 0.0 collective-permute-done.3
  14.5 6.9 %collective-permute-done.4 = bf16[1728,128]{1,0:T(8,128)(2,1)} collective-permute-done((bf16[1728,128]{1,0:T(8,128)(2,1)S(1)}, bf16[1728,128]{1,0:T(8,128)(2,1)}, u32[]{:S(2)}, u32[]{:S(2)}) %collective-permute-start.4) | collective-permute-done | bytes 442400 | tf_op jit(solution)/shard_map/ppermute | solution.py:32
  21.5 6.0 %collective-permute-start.6 = (bf16[1728,128]{1,0:T(8,128)(2,1)}, bf16[1728,128]{1,0:T(8,128)(2,1)}, u32[]{:S(2)}, u32[]{:S(2)}) collective-permute-start(bf16[1728,128]{1,0:T(8,128)(2,1)} %collective-permute-done.4), channel_id=1, source_target_pairs={{32,33},{33,32},{34,35},{35,34},{36,37},{37,36},{38,39},{39,38},{4... | collective-permute-start | bytes 1327112 | tf_op jit(solution)/shard_map/ppermute | solution.py:278
  27.5 0.7 collective-permute-start.5
  28.2 2.6 %collective-permute-done.7 = bf16[9,6,32,128]{3,2,1,0:T(8,128)(2,1)S(1)} collective-permute-done((bf16[9,6,32,128]{3,2,1,0:T(8,128)(2,1)S(1)}, bf16[9,6,32,128]{3,2,1,0:T(8,128)(2,1)S(1)}, u32[]{:S(2)}, u32[]{:S(2)}) %collective-permute-start.7) | collective-permute-done | bytes 442400 | tf_op jit(solution)/shard_map/ppermute | solution.py:32
  30.8 1.3 fusion.5
  32.1 0.0 collective-permute-done.5
  32.1 0.0 collective-permute-done.6
  32.1 0.1 collective-permute-start.8
  32.2 1.4 %collective-permute-start.10 = (bf16[9,4,32,128]{3,2,1,0:T(8,128)(2,1)}, bf16[9,4,32,128]{3,2,1,0:T(8,128)(2,1)}, u32[]{:S(2)}, u32[]{:S(2)}) collective-permute-start(bf16[9,4,32,128]{3,2,1,0:T(8,128)(2,1)} %get-tuple-element.205), channel_id=1, source_target_pairs={{160,96},{161,97},{162,98},{163,99},{164,100},{165,101},{166,102},... | collective-permute-start | bytes 884744 | tf_op jit(solution)/shard_map/ppermute | solution.py:32
  33.6 1.3 collective-permute-start.11
  34.9 1.3 collective-permute-start.9
  36.2 8.1 %collective-permute-done.8.act_ref = bf16[9,6,32,128]{3,2,1,0:T(8,128)(2,1)S(1)} collective-permute-done((bf16[9,6,32,128]{3,2,1,0:T(8,128)(2,1)S(1)}, bf16[9,6,32,128]{3,2,1,0:T(8,128)(2,1)S(1)}, u32[]{:S(2)}, u32[]{:S(2)}) %collective-permute-start.8) | collective-permute-done | bytes 442400 | tf_op jit(solution)/shard_map/ppermute | solution.py:32
  44.3 1.1 tap_rows.1.ut_ref
  45.5 1.4 %collective-permute-start.13 = (bf16[9,4,32,128]{3,2,1,0:T(8,128)(2,1)}, bf16[9,4,32,128]{3,2,1,0:T(8,128)(2,1)}, u32[]{:S(2)}, u32[]{:S(2)}) collective-permute-start(bf16[9,4,32,128]{3,2,1,0:T(8,128)(2,1)} %get-tuple-element.212), channel_id=1, source_target_pairs={{224,192},{225,193},{226,194},{227,195},{228,196},{229,197},{230,1... | collective-permute-start | bytes 884744 | tf_op jit(solution)/shard_map/ppermute | solution.py:32
  46.9 1.5 %collective-permute-start.16 = (bf16[9,4,32,128]{3,2,1,0:T(8,128)(2,1)}, bf16[9,4,32,128]{3,2,1,0:T(8,128)(2,1)}, u32[]{:S(2)}, u32[]{:S(2)}) collective-permute-start(bf16[9,4,32,128]{3,2,1,0:T(8,128)(2,1)} %get-tuple-element.212), channel_id=1, source_target_pairs={{96,32},{97,33},{98,34},{99,35},{100,36},{101,37},{102,38},{103,39... | collective-permute-start | bytes 884744 | tf_op jit(solution)/shard_map/ppermute | solution.py:32
  48.3 0.9 fusion.12
  49.3 0.7 collective-permute-start.12
  50.0 0.7 collective-permute-start.15
  50.6 1.3 collective-permute-start.17
  51.9 0.7 collective-permute-start.14
  52.7 1.0 conditional.9
  52.7 1.0 copy.29
  53.6 27.5 %collective-permute-done.17 = bf16[9,2,32,128]{3,2,1,0:T(8,128)(2,1)} collective-permute-done((bf16[9,2,32,128]{3,2,1,0:T(8,128)(2,1)}, bf16[9,2,32,128]{3,2,1,0:T(8,128)(2,1)}, u32[]{:S(2)}, u32[]{:S(2)}) %collective-permute-start.17) | collective-permute-done | bytes 147488 | tf_op jit(solution)/shard_map/ppermute | solution.py:32
  81.1 6.8 %conditional.10 = (bf16[9,4,32,128]{3,2,1,0:T(8,128)(2,1)S(1)}) conditional(s32[]{:T(128)} %convert_element_type.37, bf16[9,4,32,128]{3,2,1,0:T(8,128)(2,1)S(1)} %get-tuple-element.251, (s32[]{:T(128)}, bf16[9,2,32,128]{3,2,1,0:T(8,128)(2,1)S(1)}, bf16[9,4,32,128]{3,2,1,0:T(8,128)(2,1)}, bf16[9,2,32,128]{3,2,1,0:T(8,128)(2,1)}, ...), branch_computations={%region_8.9_spmd, %region_9.10_spmd} | conditional | bytes 8 | solution.py:287
  81.1 6.8 %two_blocks.5 = (bf16[9,4,32,128]{3,2,1,0:T(8,128)(2,1)S(1)}, bf16[9,2,32,128]{3,2,1,0:T(8,128)(2,1)}, bf16[9,2,32,128]{3,2,1,0:T(8,128)(2,1)}) custom-call(s32[1]{0:T(128)} %bitcast.2.core_ref, bf16[9,2,32,128]{3,2,1,0:T(8,128)(2,1)S(1)} %get-tuple-element.147.low_ref, bf16[9,4,32,128]{3,2,1,0:T(8,128)(2,1)} %get-tuple-element.148.own_ref, ...), custom_call_target="tpu_custom_call" | custom-call | tf_op jit(solution)/shard_map/cond/branch_1_fun/two_blocks/pallas_call | solution.py:148
  87.9 0.7 copy-done.7
  88.6 1.6 %kernel_taps.1 = bf16[9,128,384]{2,1,0:T(8,128)(2,1)S(1)} custom-call(bf16[9,128,1152]{2,1,0:T(8,128)(2,1)S(1)} %tap_rows.1.ut_ref, bf16[9,4,32,128]{3,2,1,0:T(8,128)(2,1)S(1)} %broadcast_select_fusion.g_ref), custom_call_target="tpu_custom_call" | custom-call | tf_op jit(solution)/shard_map/kernel_taps/pallas_call | solution.py:207
  90.3 0.0 copy-start.8
  90.3 0.0 copy-start.2
  90.3 0.1 constant_dynamic-slice_fusion
  90.4 3.6 %collective-permute-start.21 = (bf16[9,64,384]{2,1,0:T(8,128)(2,1)S(1)}, bf16[9,64,384]{2,1,0:T(8,128)(2,1)S(1)}, u32[]{:S(2)}, u32[]{:S(2)}) collective-permute-start(bf16[9,64,384]{2,1,0:T(8,128)(2,1)S(1)} %constant_dynamic-slice_fusion), channel_id=1, source_target_pairs={{0,1},{1,0},{2,3},{3,2},{4,5},{5,4},{6,7},{7,6},{8,9},{9,8},{10,11... | collective-permute-start | bytes 1327112 | tf_op jit(solution)/shard_map/ppermute | solution.py:324
  94.0 1.4 %collective-permute-done.21 = bf16[9,64,384]{2,1,0:T(8,128)(2,1)S(1)} collective-permute-done((bf16[9,64,384]{2,1,0:T(8,128)(2,1)S(1)}, bf16[9,64,384]{2,1,0:T(8,128)(2,1)S(1)}, u32[]{:S(2)}, u32[]{:S(2)}) %collective-permute-start.21) | collective-permute-done | bytes 442400 | tf_op jit(solution)/shard_map/ppermute | solution.py:324
  95.4 0.1 add_convert_fusion
  95.5 0.1 reshape.20
  95.6 0.9 copy.10
  96.6 13.4 %all-to-all-start = ((bf16[16,9,4,384]{3,2,1,0:T(4,128)(2,1)}), bf16[16,9,4,384]{3,2,1,0:T(4,128)(2,1)S(1)}, u32[]{:S(2)}, u32[]{:S(2)}) async-start(bf16[16,9,4,384]{3,2,1,0:T(4,128)(2,1)} %bitcast.15), calls=%async_computation | async-start | bytes 884736 | tf_op jit(solution)/shard_map/all_to_all | solution.py:329
  109.9 1.3 collective-permute-start.19
  111.3 1.3 collective-permute-start.18
  112.6 0.7 collective-permute-start.20
  113.2 15.1 %all-to-all-done = bf16[16,9,4,384]{3,2,1,0:T(4,128)(2,1)S(1)} async-done(((bf16[16,9,4,384]{3,2,1,0:T(4,128)(2,1)}), bf16[16,9,4,384]{3,2,1,0:T(4,128)(2,1)S(1)}, u32[]{:S(2)}, u32[]{:S(2)}) %all-to-all-start) | async-done | bytes 442400 | tf_op jit(solution)/shard_map/all_to_all | solution.py:329
  128.3 0.2 reduce_sum.12
  128.5 0.1 collective-permute-start.22
  128.7 4.7 %collective-permute-done.22 = bf16[9,4,384]{2,1,0:T(4,128)(2,1)S(1)} collective-permute-done((bf16[9,4,384]{2,1,0:T(4,128)(2,1)S(1)}, bf16[9,4,384]{2,1,0:T(4,128)(2,1)S(1)}, u32[]{:S(2)}, u32[]{:S(2)}) %collective-permute-start.22) | collective-permute-done | bytes 27680 | tf_op jit(solution)/shard_map/ppermute | solution.py:32
  133.3 0.6 copy.8
  (33 shorter events, 0.2 us)
Async XLA Ops:
  0.6 8.4 %copy-start.5 = (bf16[9,4,32,128]{3,2,1,0:T(8,128)(2,1)S(1)}, bf16[9,4,32,128]{3,2,1,0:T(8,128)(2,1)}, u32[]{:S(2)}) copy-start(bf16[9,4,32,128]{3,2,1,0:T(8,128)(2,1)} %param.18) | copy-start | bytes 884740
  0.6 8.4 %copy-start.1 = (bf16[1,3,3,3,128,128]{5,4,3,2,1,0:T(8,128)(2,1)S(1)}, bf16[1,3,3,3,128,128]{5,4,3,2,1,0:T(8,128)(2,1)}, u32[]{:S(2)}) copy-start(bf16[1,3,3,3,128,128]{5,4,3,2,1,0:T(8,128)(2,1)} %param.17) | copy-start | bytes 2654212
  1.8 9.3 %copy-start.6 = (bf16[1,9,4,32,128]{4,3,2,1,0:T(8,128)(2,1)S(1)}, bf16[1,9,4,32,128]{4,3,2,1,0:T(8,128)(2,1)}, u32[]{:S(2)}) copy-start(bf16[1,9,4,32,128]{4,3,2,1,0:T(8,128)(2,1)} %param.16) | copy-start | bytes 884740
  1.8 6.7 %collective-permute-start = (bf16[18,1,32,128]{3,2,1,0:T(8,128)(2,1)S(1)}, bf16[18,1,32,128]{3,2,1,0:T(8,128)(2,1)S(1)}, u32[]{:S(2)}, u32[]{:S(2)}) collective-permute-start(bf16[18,1,32,128]{3,2,1,0:T(8,128)(2,1)S(1)} %get-tuple-element.222), channel_id=1, source_target_pairs={{0,1},{1,2},{2,3},{3,4},{4,5},{5,6},{6,7},{7,8},{8,9},{9,10},{10,1... | collective-permute-start | bytes 442376 | tf_op jit(solution)/shard_map/ppermute | solution.py:32
  3.7 5.3 %collective-permute-start.1 = (bf16[18,1,32,128]{3,2,1,0:T(8,128)(2,1)S(1)}, bf16[18,1,32,128]{3,2,1,0:T(8,128)(2,1)S(1)}, u32[]{:S(2)}, u32[]{:S(2)}) collective-permute-start(bf16[18,1,32,128]{3,2,1,0:T(8,128)(2,1)S(1)} %get-tuple-element.223), channel_id=1, source_target_pairs={{1,0},{2,1},{3,2},{4,3},{5,4},{6,5},{7,6},{8,7},{9,8},{10,9},{11,1... | collective-permute-start | bytes 442376 | tf_op jit(solution)/shard_map/ppermute | solution.py:32
  6.0 15.4 %collective-permute-start.4 = (bf16[1728,128]{1,0:T(8,128)(2,1)S(1)}, bf16[1728,128]{1,0:T(8,128)(2,1)}, u32[]{:S(2)}, u32[]{:S(2)}) collective-permute-start(bf16[1728,128]{1,0:T(8,128)(2,1)S(1)} %constant_dynamic-slice_fusion.1), channel_id=1, source_target_pairs={{64,32},{65,33},{66,34},{67,35},{68,36},{69,37},{70,38},{71,39},{7... | collective-permute-start | bytes 1327112 | tf_op jit(solution)/shard_map/ppermute | solution.py:32
  8.5 23.6 %copy-start.3 = (f32[9,4,32,128]{3,2,1,0:T(8,128)}, f32[9,4,32,128]{3,2,1,0:T(8,128)S(1)}, u32[]{:S(2)}) copy-start(f32[9,4,32,128]{3,2,1,0:T(8,128)S(1)} %fusion.10) | copy-start | bytes 1769476
  11.2 33.1 %copy-start = (bf16[128,128]{1,0:T(8,128)(2,1)S(1)}, bf16[128,128]{1,0:T(8,128)(2,1)}, u32[]{:S(2)}) copy-start(bf16[128,128]{1,0:T(8,128)(2,1)} %constant.56.clone.order_ref) | copy-start | bytes 98308
  11.2 3.3 %collective-permute-start.3 = (bf16[9,4,32,128]{3,2,1,0:T(8,128)(2,1)}, bf16[9,4,32,128]{3,2,1,0:T(8,128)(2,1)S(1)}, u32[]{:S(2)}, u32[]{:S(2)}) collective-permute-start(bf16[9,4,32,128]{3,2,1,0:T(8,128)(2,1)} %get-tuple-element.196), channel_id=1, source_target_pairs={{224,160},{225,161},{226,162},{227,163},{228,164},{229,165},{230,1... | collective-permute-start | bytes 884744 | tf_op jit(solution)/shard_map/ppermute | solution.py:32
  11.9 18.9 %collective-permute-start.7 = (bf16[9,6,32,128]{3,2,1,0:T(8,128)(2,1)S(1)}, bf16[9,6,32,128]{3,2,1,0:T(8,128)(2,1)S(1)}, u32[]{:S(2)}, u32[]{:S(2)}) collective-permute-start(bf16[9,6,32,128]{3,2,1,0:T(8,128)(2,1)S(1)} %pad_maximum_fusion), channel_id=1, source_target_pairs={{64,32},{65,33},{66,34},{67,35},{68,36},{69,37},{70,38},{71,39},{7... | collective-permute-start | bytes 1327112 | tf_op jit(solution)/shard_map/ppermute | solution.py:32
  13.2 1.3 collective-permute-start.2
  21.5 10.7 %collective-permute-start.6 = (bf16[1728,128]{1,0:T(8,128)(2,1)}, bf16[1728,128]{1,0:T(8,128)(2,1)}, u32[]{:S(2)}, u32[]{:S(2)}) collective-permute-start(bf16[1728,128]{1,0:T(8,128)(2,1)} %collective-permute-done.4), channel_id=1, source_target_pairs={{32,33},{33,32},{34,35},{35,34},{36,37},{37,36},{38,39},{39,38},{4... | collective-permute-start | bytes 1327112 | tf_op jit(solution)/shard_map/ppermute | solution.py:278
  27.5 4.6 %collective-permute-start.5 = (bf16[9,2,32,128]{3,2,1,0:T(8,128)(2,1)}, bf16[9,2,32,128]{3,2,1,0:T(8,128)(2,1)S(1)}, u32[]{:S(2)}, u32[]{:S(2)}) collective-permute-start(bf16[9,2,32,128]{3,2,1,0:T(8,128)(2,1)} %get-tuple-element.197), channel_id=1, source_target_pairs={{225,160},{226,161},{227,162},{228,163},{229,164},{230,165},{231,1... | collective-permute-start | bytes 442376 | tf_op jit(solution)/shard_map/ppermute | solution.py:32
  32.1 12.2 %collective-permute-start.8 = (bf16[9,6,32,128]{3,2,1,0:T(8,128)(2,1)S(1)}, bf16[9,6,32,128]{3,2,1,0:T(8,128)(2,1)S(1)}, u32[]{:S(2)}, u32[]{:S(2)}) collective-permute-start(bf16[9,6,32,128]{3,2,1,0:T(8,128)(2,1)S(1)} %pad_maximum_fusion), channel_id=1, source_target_pairs={{0,32},{1,33},{2,34},{3,35},{4,36},{5,37},{6,38},{7,39},{8,40},{9,... | collective-permute-start | bytes 1327112 | tf_op jit(solution)/shard_map/ppermute | solution.py:32
  32.2 13.2 %collective-permute-start.10 = (bf16[9,4,32,128]{3,2,1,0:T(8,128)(2,1)}, bf16[9,4,32,128]{3,2,1,0:T(8,128)(2,1)}, u32[]{:S(2)}, u32[]{:S(2)}) collective-permute-start(bf16[9,4,32,128]{3,2,1,0:T(8,128)(2,1)} %get-tuple-element.205), channel_id=1, source_target_pairs={{160,96},{161,97},{162,98},{163,99},{164,100},{165,101},{166,102},... | collective-permute-start | bytes 884744 | tf_op jit(solution)/shard_map/ppermute | solution.py:32
  33.6 11.8 %collective-permute-start.11 = (bf16[9,2,32,128]{3,2,1,0:T(8,128)(2,1)}, bf16[9,2,32,128]{3,2,1,0:T(8,128)(2,1)}, u32[]{:S(2)}, u32[]{:S(2)}) collective-permute-start(bf16[9,2,32,128]{3,2,1,0:T(8,128)(2,1)} %get-tuple-element.206), channel_id=1, source_target_pairs={{161,96},{162,97},{163,98},{164,99},{165,100},{166,101},{167,102},... | collective-permute-start | bytes 442376 | tf_op jit(solution)/shard_map/ppermute | solution.py:32
  34.9 10.6 %collective-permute-start.9 = (bf16[9,2,32,128]{3,2,1,0:T(8,128)(2,1)}, bf16[9,2,32,128]{3,2,1,0:T(8,128)(2,1)}, u32[]{:S(2)}, u32[]{:S(2)}) collective-permute-start(bf16[9,2,32,128]{3,2,1,0:T(8,128)(2,1)} %get-tuple-element.207), channel_id=1, source_target_pairs={{160,97},{161,98},{162,99},{163,100},{164,101},{165,102},{166,103}... | collective-permute-start | bytes 442376 | tf_op jit(solution)/shard_map/ppermute | solution.py:32
  45.5 7.2 %collective-permute-start.13 = (bf16[9,4,32,128]{3,2,1,0:T(8,128)(2,1)}, bf16[9,4,32,128]{3,2,1,0:T(8,128)(2,1)}, u32[]{:S(2)}, u32[]{:S(2)}) collective-permute-start(bf16[9,4,32,128]{3,2,1,0:T(8,128)(2,1)} %get-tuple-element.212), channel_id=1, source_target_pairs={{224,192},{225,193},{226,194},{227,195},{228,196},{229,197},{230,1... | collective-permute-start | bytes 884744 | tf_op jit(solution)/shard_map/ppermute | solution.py:32
  46.9 34.3 %collective-permute-start.16 = (bf16[9,4,32,128]{3,2,1,0:T(8,128)(2,1)}, bf16[9,4,32,128]{3,2,1,0:T(8,128)(2,1)}, u32[]{:S(2)}, u32[]{:S(2)}) collective-permute-start(bf16[9,4,32,128]{3,2,1,0:T(8,128)(2,1)} %get-tuple-element.212), channel_id=1, source_target_pairs={{96,32},{97,33},{98,34},{99,35},{100,36},{101,37},{102,38},{103,39... | collective-permute-start | bytes 884744 | tf_op jit(solution)/shard_map/ppermute | solution.py:32
  49.3 2.7 %collective-permute-start.12 = (bf16[9,1,32,128]{3,2,1,0:T(8,128)(2,1)S(1)}, bf16[9,1,32,128]{3,2,1,0:T(8,128)(2,1)S(1)}, u32[]{:S(2)}, u32[]{:S(2)}) collective-permute-start(bf16[9,1,32,128]{3,2,1,0:T(8,128)(2,1)S(1)} %get-tuple-element.227), channel_id=1, source_target_pairs={{224,193},{225,194},{226,195},{227,196},{228,197},{229,198},{230,1... | collective-permute-start | bytes 221192 | tf_op jit(solution)/shard_map/ppermute | solution.py:32
  50.0 3.7 %collective-permute-start.15 = (bf16[9,2,32,128]{3,2,1,0:T(8,128)(2,1)}, bf16[9,2,32,128]{3,2,1,0:T(8,128)(2,1)S(1)}, u32[]{:S(2)}, u32[]{:S(2)}) collective-permute-start(bf16[9,2,32,128]{3,2,1,0:T(8,128)(2,1)} %get-tuple-element.213), channel_id=1, source_target_pairs={{96,33},{97,34},{98,35},{99,36},{100,37},{101,38},{102,39},{103,40... | collective-permute-start | bytes 442376 | tf_op jit(solution)/shard_map/ppermute | solution.py:32
  50.6 30.5 %collective-permute-start.17 = (bf16[9,2,32,128]{3,2,1,0:T(8,128)(2,1)}, bf16[9,2,32,128]{3,2,1,0:T(8,128)(2,1)}, u32[]{:S(2)}, u32[]{:S(2)}) collective-permute-start(bf16[9,2,32,128]{3,2,1,0:T(8,128)(2,1)} %get-tuple-element.214), channel_id=1, source_target_pairs={{97,32},{98,33},{99,34},{100,35},{101,36},{102,37},{103,38},{104,3... | collective-permute-start | bytes 442376 | tf_op jit(solution)/shard_map/ppermute | solution.py:32
  51.9 0.7 collective-permute-start.14
  87.9 0.7 copy-start.7
  90.3 19.7 %copy-start.8 = (bf16[9,4,32,128]{3,2,1,0:T(8,128)(2,1)S(1)}, bf16[9,4,32,128]{3,2,1,0:T(8,128)(2,1)}, u32[]{:S(2)}) copy-start(bf16[9,4,32,128]{3,2,1,0:T(8,128)(2,1)} %copy-done.7) | copy-start | bytes 884740
  90.3 38.4 %copy-start.2 = (bf16[1,3,3,3,128,128]{5,4,3,2,1,0:T(8,128)(2,1)S(1)}, bf16[1,3,3,3,128,128]{5,4,3,2,1,0:T(8,128)(2,1)}, u32[]{:S(2)}) copy-start(bf16[1,3,3,3,128,128]{5,4,3,2,1,0:T(8,128)(2,1)} %param.17) | copy-start | bytes 2654212
  90.3 38.4 %copy-start.4 = (f32[9,4,32,128]{3,2,1,0:T(8,128)S(1)}, f32[9,4,32,128]{3,2,1,0:T(8,128)}, u32[]{:S(2)}) copy-start(f32[9,4,32,128]{3,2,1,0:T(8,128)} %copy-done.3) | copy-start | bytes 1769476
  90.4 5.0 %collective-permute-start.21 = (bf16[9,64,384]{2,1,0:T(8,128)(2,1)S(1)}, bf16[9,64,384]{2,1,0:T(8,128)(2,1)S(1)}, u32[]{:S(2)}, u32[]{:S(2)}) collective-permute-start(bf16[9,64,384]{2,1,0:T(8,128)(2,1)S(1)} %constant_dynamic-slice_fusion), channel_id=1, source_target_pairs={{0,1},{1,0},{2,3},{3,2},{4,5},{5,4},{6,7},{7,6},{8,9},{9,8},{10,11... | collective-permute-start | bytes 1327112 | tf_op jit(solution)/shard_map/ppermute | solution.py:324
  96.6 31.8 %all-to-all-start = ((bf16[16,9,4,384]{3,2,1,0:T(4,128)(2,1)}), bf16[16,9,4,384]{3,2,1,0:T(4,128)(2,1)S(1)}, u32[]{:S(2)}, u32[]{:S(2)}) async-start(bf16[16,9,4,384]{3,2,1,0:T(4,128)(2,1)} %bitcast.15), calls=%async_computation | async-start | bytes 884736 | tf_op jit(solution)/shard_map/all_to_all | solution.py:329
  109.9 18.7 %collective-permute-start.19 = (bf16[9,4,32,128]{3,2,1,0:T(8,128)(2,1)S(1)}, bf16[9,4,32,128]{3,2,1,0:T(8,128)(2,1)S(1)}, u32[]{:S(2)}, u32[]{:S(2)}) collective-permute-start(bf16[9,4,32,128]{3,2,1,0:T(8,128)(2,1)S(1)} %copy-done.8), channel_id=1, source_target_pairs={{32,0},{33,1},{34,2},{35,3},{36,4},{37,5},{38,6},{39,7},{40,8},{41... | collective-permute-start | bytes 884744 | tf_op jit(solution)/shard_map/ppermute | solution.py:32
  111.3 17.3 %collective-permute-start.18 = (bf16[9,1,32,128]{3,2,1,0:T(8,128)(2,1)S(1)}, bf16[9,1,32,128]{3,2,1,0:T(8,128)(2,1)S(1)}, u32[]{:S(2)}, u32[]{:S(2)}) collective-permute-start(bf16[9,1,32,128]{3,2,1,0:T(8,128)(2,1)S(1)} %get-tuple-element.225), channel_id=1, source_target_pairs={{32,1},{33,2},{34,3},{35,4},{36,5},{37,6},{38,7},{39,8},{40,9},{41... | collective-permute-start | bytes 221192 | tf_op jit(solution)/shard_map/ppermute | solution.py:32
  112.6 16.0 %collective-permute-start.20 = (bf16[9,1,32,128]{3,2,1,0:T(8,128)(2,1)S(1)}, bf16[9,1,32,128]{3,2,1,0:T(8,128)(2,1)S(1)}, u32[]{:S(2)}, u32[]{:S(2)}) collective-permute-start(bf16[9,1,32,128]{3,2,1,0:T(8,128)(2,1)S(1)} %get-tuple-element.224), channel_id=1, source_target_pairs={{33,0},{34,1},{35,2},{36,3},{37,4},{38,5},{39,6},{40,7},{41,8},{42... | collective-permute-start | bytes 221192 | tf_op jit(solution)/shard_map/ppermute | solution.py:32
  128.5 4.8 %collective-permute-start.22 = (bf16[9,4,384]{2,1,0:T(4,128)(2,1)S(1)}, bf16[9,4,384]{2,1,0:T(4,128)(2,1)S(1)}, u32[]{:S(2)}, u32[]{:S(2)}) collective-permute-start(bf16[9,4,384]{2,1,0:T(4,128)(2,1)S(1)} %reduce_sum.12), channel_id=1, source_target_pairs={{32,0},{33,1},{34,2},{35,3},{36,4},{37,5},{38,6},{39,7},{40,8},{41... | collective-permute-start | bytes 82952 | tf_op jit(solution)/shard_map/ppermute | solution.py:32
